TPU v7x, 32 devices: a whole 2x2x4 slice. The times are simulated.
32 devices in a mesh: dp: 4 (over z), ctx: 8 (over y, x, core).
Axes of the slice: x: 2, y: 2, z: 4, core: 2. Of those that a mesh axis runs over, the one named last changes fastest.
Arguments:
- x_in: bfloat16 [4, 1024, 1024], P('dp', 'ctx'), may hold values from -6 to 6
- doc_ids: int32 [4, 1024], P('dp'), may hold values from 0 to 7, never falling along the last dimension, each value on 1 to 512 neighbouring positions
- routes: int32 [2, 4, 1024, 8], P(None, 'dp', 'ctx'), may hold values from 0 to 31, all different within a row; in each aligned block of 128 rows (0 to 127, 128 to 255, ..., all dimensions but the last counted through in order) at most 40 rows name the same one
- gain_attn: bfloat16 [2, 1024], P(None, 'ctx'), may hold values from 0.5 to 1.5
- w_qkv: bfloat16 [2, 1024, 2048], P(None, 'ctx'), may hold values from -0.1875 to 0.1875
- w_out: bfloat16 [2, 1024, 1024], P(None, 'ctx'), may hold values from -1.5 to 1.5
- gain_moe: bfloat16 [2, 1024], P(None, 'ctx'), may hold values from 0.5 to 1.5
- w_router: bfloat16 [2, 1024, 32], P(None, 'ctx'), may hold values from -0.09375 to 0.09375
- w_expert: bfloat16 [2, 32, 1024, 1536], P(None, 'ctx'), may hold values from -0.375 to 0.375
- cotangent: bfloat16 [4, 1024, 1024], P('dp', 'ctx'), may hold values from -6 to 6
Outputs:
- y_out: bfloat16 [4, 1024, 1024], P('dp', 'ctx')
- x_grad: float32 [4, 1024, 1024], P('dp', 'ctx')
- gain_attn_grad: float32 [2, 1024], P(None, 'ctx')
- qkv_grad: float32 [2, 1024, 2048], P(None, 'ctx')
- out_grad: float32 [2, 1024, 1024], P(None, 'ctx')
- gain_moe_grad: float32 [2, 1024], P(None, 'ctx')
- router_grad: float32 [2, 1024, 32], P(None, 'ctx')
- expert_grad: float32 [2, 32, 1024, 1536], P(None, 'ctx')
Inputs may be any that keep to these rules, and one draw needn't show every extreme that they name: `doc_ids`: document numbers never fall along a stream; each document has 1 to 512 tokens and one has exactly 512. A token's 8 routes in a layer are different experts. In each layer, the 128 tokens of one device (aligned blocks of a stream) name no expert more than 40 times, and some device's tokens name some expert exactly 40 times.
All inputs are finite; a program needn't handle non-finite values.
Results may differ from a plain program's by a relative error of at most 0.03.
Values may be sent and summed in bfloat16 or wider, within the bound.
No kernel may reach another device: no remote copies, remote signals or barrier semaphores. Data moves between devices by JAX's collectives and lax.ppermute only.
A program may use at most 320 MiB of HBM per device.

v0:
```python
import math

import jax
import jax.numpy as jnp
from jax import lax
from jax.sharding import PartitionSpec as P

HEADS = 16
KVH = 8
HD = 64
TOP = 8
FE = 512
CAP = 40


epsilon = 1e-06


def norm_scale(values):
    return lax.rsqrt(jnp.mean(values * values, axis=-1, keepdims=True) + epsilon)


def angles(positions, head_width):
    frequency = 10000.0 ** (-jnp.arange(0, head_width, 2).astype(jnp.float32) / head_width)
    turned = positions[:, None] * frequency[None, :]
    return (jnp.cos(turned)[:, None, :], jnp.sin(turned)[:, None, :])


def rotate(values, cosine, sine_vals):
    half_width = values.shape[-1] // 2
    first_half = values[..., :half_width]
    second_half = values[..., half_width:]
    return jnp.concatenate(
        [
            first_half * cosine - second_half * sine_vals,
            second_half * cosine + first_half * sine_vals,
        ],
        axis=-1,
    )


def unrotate(values, cosine, sine_vals):
    half_width = values.shape[-1] // 2
    first_half = values[..., :half_width]
    second_half = values[..., half_width:]
    return jnp.concatenate(
        [
            first_half * cosine + second_half * sine_vals,
            second_half * cosine - first_half * sine_vals,
        ],
        axis=-1,
    )


def doc_positions(doc_row):
    length = doc_row.shape[0]
    index_row = jnp.arange(length, dtype=jnp.int32)
    previous = jnp.concatenate([jnp.full((1,), -1, jnp.int32), doc_row[:-1]])
    starts = lax.cummax(jnp.where(doc_row != previous, index_row, 0), axis=0)
    return (index_row, (index_row - starts).astype(jnp.float32))


def slot_plan(route_rows, capacity, expert_count):
    flat_route = route_rows.reshape(-1)
    onehot = (flat_route[:, None] == jnp.arange(expert_count, dtype=jnp.int32)[None, :]).astype(
        jnp.int32
    )
    running = jnp.cumsum(onehot, axis=0)
    slot_rank = jnp.sum(onehot * running, axis=1) - 1
    destination = flat_route * capacity + slot_rank
    slot_table = (
        jnp.zeros((expert_count * capacity,), jnp.int32)
        .at[destination]
        .set(jnp.arange(flat_route.shape[0], dtype=jnp.int32) + 1)
    )
    return (destination, slot_table)


def local(x_in, doc_ids, routes, gain_attn, w_qkv, w_out, gain_moe, w_router, w_expert, cotangent):
    ctx_size = lax.axis_size("ctx")
    ctx_rank = lax.axis_index("ctx")
    local_tokens = x_in.shape[1]
    model_width = x_in.shape[2]
    length = local_tokens * ctx_size
    layer_count = w_qkv.shape[0]
    expert_count = w_router.shape[2]
    query_width = HEADS * HD
    key_width = KVH * HD
    group_size = HEADS // KVH
    pair_width = 2 * FE
    score_scale = 1.0 / math.sqrt(HD)
    doc_row = doc_ids[0]
    index_row, positions = doc_positions(doc_row)
    offset = ctx_rank * local_tokens
    query_index = offset + jnp.arange(local_tokens, dtype=jnp.int32)
    query_doc = lax.dynamic_slice_in_dim(doc_row, offset, local_tokens)
    cosine, sine_vals = angles(lax.dynamic_slice_in_dim(positions, offset, local_tokens), HD)
    key_block = min(512, length)
    key_blocks = length // key_block
    block_index = index_row.reshape(key_blocks, key_block)
    block_doc = doc_row.reshape(key_blocks, key_block)

    def visible_mask(index_piece, doc_piece):
        return (
            (index_piece[None, :] <= query_index[:, None])
            & (doc_piece[None, :] == query_doc[:, None])
        )[:, None, None, :]

    def block_needed(index_piece, doc_piece):
        return (
            (index_piece[0] <= query_index[-1])
            & (doc_piece[-1] >= query_doc[0])
            & (doc_piece[0] <= query_doc[-1])
        )

    residual = x_in[0].astype(jnp.float32)
    layer_store = []
    for layer_idx in range(layer_count):
        gain_one, qkv_weight, out_weight, gain_two, router_weight = (
            lax.all_gather(gain_attn[layer_idx], "ctx", axis=0, tiled=True),
            lax.all_gather(w_qkv[layer_idx], "ctx", axis=0, tiled=True),
            lax.all_gather(w_out[layer_idx], "ctx", axis=0, tiled=True),
            lax.all_gather(gain_moe[layer_idx], "ctx", axis=0, tiled=True),
            lax.all_gather(w_router[layer_idx], "ctx", axis=0, tiled=True),
        )
        scale_one = norm_scale(residual)
        attn_in = (residual * scale_one * gain_one.astype(jnp.float32)).astype(jnp.bfloat16)
        projected = jnp.dot(attn_in, qkv_weight, preferred_element_type=jnp.float32)
        queries = rotate(
            projected[:, :query_width].reshape(local_tokens, HEADS, HD), cosine, sine_vals
        ).astype(jnp.bfloat16)
        keys_local = rotate(
            projected[:, query_width : query_width + key_width].reshape(local_tokens, KVH, HD),
            cosine,
            sine_vals,
        ).astype(jnp.bfloat16)
        pair_local = jnp.concatenate(
            [
                keys_local.reshape(local_tokens, key_width),
                projected[:, query_width + key_width :].astype(jnp.bfloat16),
            ],
            axis=1,
        )
        pair_all = lax.all_gather(pair_local, "ctx", axis=0, tiled=True)
        query_four = queries.reshape(local_tokens, KVH, group_size, HD)

        def forward_block(state_pair, block_piece):
            pair_block, index_piece, doc_piece = block_piece

            def add_block(state_in):
                totals, denominator = state_in
                scores = (
                    jnp.einsum(
                        "tgrd,sgd->tgrs",
                        query_four,
                        pair_block[:, 0],
                        preferred_element_type=jnp.float32,
                    )
                    * score_scale
                )
                weights_exp = jnp.where(visible_mask(index_piece, doc_piece), jnp.exp(scores), 0.0)
                denominator = denominator + jnp.sum(weights_exp, axis=-1)
                totals = totals + jnp.einsum(
                    "tgrs,sgd->tgrd",
                    weights_exp.astype(jnp.bfloat16),
                    pair_block[:, 1],
                    preferred_element_type=jnp.float32,
                )
                return (totals, denominator)

            return (
                lax.cond(
                    block_needed(index_piece, doc_piece),
                    add_block,
                    lambda state_in: state_in,
                    state_pair,
                ),
                None,
            )

        init_carry = (
            jnp.zeros((local_tokens, KVH, group_size, HD), jnp.float32),
            jnp.zeros((local_tokens, KVH, group_size), jnp.float32),
        )
        (totals, denominator), unused = lax.scan(
            forward_block,
            init_carry,
            (pair_all.reshape(key_blocks, key_block, 2, KVH, HD), block_index, block_doc),
        )
        heads_out = (
            (totals / denominator[..., None])
            .astype(jnp.bfloat16)
            .reshape(local_tokens, query_width)
        )
        attn_out = jnp.dot(heads_out, out_weight, preferred_element_type=jnp.float32)
        mid_stream = residual + attn_out
        scale_two = norm_scale(mid_stream)
        moe_in = (mid_stream * scale_two * gain_two.astype(jnp.float32)).astype(jnp.bfloat16)
        logits = jnp.dot(moe_in, router_weight, preferred_element_type=jnp.float32)
        route_rows = routes[layer_idx, 0]
        gate_vals = jax.nn.softmax(jnp.take_along_axis(logits, route_rows, axis=1), axis=-1)
        destination, slot_table = slot_plan(route_rows, CAP, expert_count)
        filled = slot_table > 0
        source = jnp.maximum(slot_table - 1, 0) // TOP
        outgoing = jnp.where(filled[:, None], moe_in[source], jnp.zeros((), jnp.bfloat16)).reshape(
            expert_count, CAP, model_width
        )
        arrived = lax.all_to_all(outgoing, "ctx", split_axis=0, concat_axis=1, tiled=True)
        expert_weight = w_expert[layer_idx]
        hidden_pair = jnp.einsum(
            "ecd,edf->ecf",
            arrived,
            expert_weight[..., :pair_width],
            preferred_element_type=jnp.float32,
        )
        hidden = (jax.nn.silu(hidden_pair[..., :FE]) * hidden_pair[..., FE:]).astype(jnp.bfloat16)
        expert_out = jnp.einsum(
            "ecf,edf->ecd",
            hidden,
            expert_weight[..., pair_width:],
            preferred_element_type=jnp.float32,
        ).astype(jnp.bfloat16)
        returned = lax.all_to_all(expert_out, "ctx", split_axis=1, concat_axis=0, tiled=True)
        picked = returned.reshape(expert_count * CAP, model_width)[destination].reshape(
            local_tokens, TOP, model_width
        )
        layer_store.append(
            (
                residual,
                scale_one,
                attn_in,
                query_four,
                pair_local,
                pair_all,
                totals,
                denominator,
                heads_out,
                mid_stream,
                scale_two,
                moe_in,
                gate_vals,
                route_rows,
                destination,
                slot_table,
                arrived,
                hidden_pair,
                hidden,
                picked,
                gain_one,
                qkv_weight,
                out_weight,
                gain_two,
                router_weight,
            )
        )
        residual = mid_stream + jnp.sum(gate_vals[..., None] * picked.astype(jnp.float32), axis=1)
    out_stream = residual.astype(jnp.bfloat16)[None]
    grad_stream = cotangent[0].astype(jnp.float32)
    layer_grads = []
    for layer_idx in reversed(range(layer_count)):
        (
            layer_input,
            scale_one,
            attn_in,
            query_four,
            pair_local,
            pair_all,
            totals,
            denominator,
            heads_out,
            mid_stream,
            scale_two,
            moe_in,
            gate_vals,
            route_rows,
            destination,
            slot_table,
            arrived,
            hidden_pair,
            hidden,
            picked,
            gain_one,
            qkv_weight,
            out_weight,
            gain_two,
            router_weight,
        ) = layer_store[layer_idx]
        gain_one, qkv_weight, out_weight, gain_two, router_weight = (
            lax.all_gather(gain_attn[layer_idx], "ctx", axis=0, tiled=True),
            lax.all_gather(w_qkv[layer_idx], "ctx", axis=0, tiled=True),
            lax.all_gather(w_out[layer_idx], "ctx", axis=0, tiled=True),
            lax.all_gather(gain_moe[layer_idx], "ctx", axis=0, tiled=True),
            lax.all_gather(w_router[layer_idx], "ctx", axis=0, tiled=True),
        )
        pair_all = lax.all_gather(pair_local, "ctx", axis=0, tiled=True)
        expert_weight = w_expert[layer_idx]
        gate_grad = jnp.sum(grad_stream[:, None, :] * picked.astype(jnp.float32), axis=-1)
        routed_grad = (
            (gate_vals[..., None] * grad_stream[:, None, :])
            .astype(jnp.bfloat16)
            .reshape(local_tokens * TOP, model_width)
        )
        filled = slot_table > 0
        outgoing_grad = jnp.where(
            filled[:, None],
            routed_grad[jnp.maximum(slot_table - 1, 0)],
            jnp.zeros((), jnp.bfloat16),
        ).reshape(expert_count, CAP, model_width)
        arrived_grad = lax.all_to_all(outgoing_grad, "ctx", split_axis=0, concat_axis=1, tiled=True)
        down_grad = jnp.einsum(
            "ecd,ecf->edf", arrived_grad, hidden, preferred_element_type=jnp.float32
        )
        hidden_grad = jnp.einsum(
            "ecd,edf->ecf",
            arrived_grad,
            expert_weight[..., pair_width:],
            preferred_element_type=jnp.float32,
        )
        gate_part = hidden_pair[..., :FE]
        up_part = hidden_pair[..., FE:]
        sigmoid_vals = jax.nn.sigmoid(gate_part)
        silu_vals = gate_part * sigmoid_vals
        silu_slope = sigmoid_vals * (1.0 + gate_part * (1.0 - sigmoid_vals))
        pair_grads = jnp.concatenate(
            [hidden_grad * up_part * silu_slope, hidden_grad * silu_vals], axis=-1
        ).astype(jnp.bfloat16)
        up_grad = jnp.einsum(
            "ecd,ecf->edf", arrived, pair_grads, preferred_element_type=jnp.float32
        )
        row_grad = jnp.einsum(
            "ecf,edf->ecd",
            pair_grads,
            expert_weight[..., :pair_width],
            preferred_element_type=jnp.float32,
        ).astype(jnp.bfloat16)
        returned_grad = lax.all_to_all(row_grad, "ctx", split_axis=1, concat_axis=0, tiled=True)
        moe_grad = jnp.sum(
            returned_grad.reshape(expert_count * CAP, model_width)[destination]
            .reshape(local_tokens, TOP, model_width)
            .astype(jnp.float32),
            axis=1,
        )
        chosen_grad = gate_vals * (
            gate_grad - jnp.sum(gate_vals * gate_grad, axis=-1, keepdims=True)
        )
        onehot_routes = (route_rows[..., None] == jnp.arange(expert_count, dtype=jnp.int32)).astype(
            jnp.float32
        )
        logit_grad = jnp.sum(chosen_grad[..., None] * onehot_routes, axis=1).astype(jnp.bfloat16)
        router_grad = jnp.einsum(
            "td,te->de", moe_in, logit_grad, preferred_element_type=jnp.float32
        )
        moe_grad = moe_grad + jnp.einsum(
            "te,de->td", logit_grad, router_weight, preferred_element_type=jnp.float32
        )
        normed_two = mid_stream * scale_two
        scaled_two = moe_grad * gain_two.astype(jnp.float32)
        gain_two_grad = jnp.sum(moe_grad * normed_two, axis=0)
        mid_grad = grad_stream + scale_two * (
            scaled_two - normed_two * jnp.mean(scaled_two * normed_two, axis=-1, keepdims=True)
        )
        attn_grad = mid_grad.astype(jnp.bfloat16)
        out_grad = jnp.einsum("tc,td->cd", heads_out, attn_grad, preferred_element_type=jnp.float32)
        heads_grad = jnp.einsum(
            "td,cd->tc", attn_grad, out_weight, preferred_element_type=jnp.float32
        ).reshape(local_tokens, KVH, group_size, HD)
        scaled_heads = (heads_grad / denominator[..., None]).astype(jnp.bfloat16)
        denominator_grad = -jnp.sum(heads_grad * totals, axis=-1) / (denominator * denominator)

        def backward_block(query_grad, block_piece):
            pair_block, index_piece, doc_piece = block_piece

            def grad_block(query_in):
                scores = (
                    jnp.einsum(
                        "tgrd,sgd->tgrs",
                        query_four,
                        pair_block[:, 0],
                        preferred_element_type=jnp.float32,
                    )
                    * score_scale
                )
                weights_exp = jnp.where(visible_mask(index_piece, doc_piece), jnp.exp(scores), 0.0)
                prob_grad = jnp.einsum(
                    "tgrd,sgd->tgrs",
                    scaled_heads,
                    pair_block[:, 1],
                    preferred_element_type=jnp.float32,
                )
                score_grad = (weights_exp * (prob_grad + denominator_grad[..., None])).astype(
                    jnp.bfloat16
                )
                query_out = (
                    query_in
                    + jnp.einsum(
                        "tgrs,sgd->tgrd",
                        score_grad,
                        pair_block[:, 0],
                        preferred_element_type=jnp.float32,
                    )
                    * score_scale
                )
                key_grad = (
                    jnp.einsum(
                        "tgrs,tgrd->sgd", score_grad, query_four, preferred_element_type=jnp.float32
                    )
                    * score_scale
                )
                value_grad = jnp.einsum(
                    "tgrs,tgrd->sgd",
                    weights_exp.astype(jnp.bfloat16),
                    scaled_heads,
                    preferred_element_type=jnp.float32,
                )
                return (query_out, jnp.stack([key_grad, value_grad], axis=1))

            def skip_block(query_in):
                return (query_in, jnp.zeros((key_block, 2, KVH, HD), jnp.float32))

            return lax.cond(
                block_needed(index_piece, doc_piece), grad_block, skip_block, query_grad
            )

        query_grad, key_pairs = lax.scan(
            backward_block,
            jnp.zeros((local_tokens, KVH, group_size, HD), jnp.float32),
            (pair_all.reshape(key_blocks, key_block, 2, KVH, HD), block_index, block_doc),
        )
        pair_grad_local = lax.psum_scatter(
            key_pairs.reshape(length, 2 * key_width).astype(jnp.bfloat16),
            "ctx",
            scatter_dimension=0,
            tiled=True,
        ).astype(jnp.float32)
        query_lin = unrotate(query_grad.reshape(local_tokens, HEADS, HD), cosine, sine_vals)
        key_lin = unrotate(
            pair_grad_local[:, :key_width].reshape(local_tokens, KVH, HD), cosine, sine_vals
        )
        projected_grad = jnp.concatenate(
            [
                query_lin.reshape(local_tokens, query_width),
                key_lin.reshape(local_tokens, key_width),
                pair_grad_local[:, key_width:],
            ],
            axis=1,
        ).astype(jnp.bfloat16)
        qkv_grad = jnp.einsum(
            "tc,tf->cf", attn_in, projected_grad, preferred_element_type=jnp.float32
        )
        attn_in_grad = jnp.einsum(
            "tf,cf->tc", projected_grad, qkv_weight, preferred_element_type=jnp.float32
        )
        normed_one = layer_input * scale_one
        scaled_one = attn_in_grad * gain_one.astype(jnp.float32)
        gain_one_grad = jnp.sum(attn_in_grad * normed_one, axis=0)
        grad_stream = mid_grad + scale_one * (
            scaled_one - normed_one * jnp.mean(scaled_one * normed_one, axis=-1, keepdims=True)
        )
        shard_grads = (
            lax.psum_scatter(
                gain_one_grad.astype(jnp.bfloat16), "ctx", scatter_dimension=0, tiled=True
            ).astype(jnp.float32),
            lax.psum_scatter(
                qkv_grad.astype(jnp.bfloat16), "ctx", scatter_dimension=0, tiled=True
            ).astype(jnp.float32),
            lax.psum_scatter(
                out_grad.astype(jnp.bfloat16), "ctx", scatter_dimension=0, tiled=True
            ).astype(jnp.float32),
            lax.psum_scatter(
                gain_two_grad.astype(jnp.bfloat16), "ctx", scatter_dimension=0, tiled=True
            ).astype(jnp.float32),
            lax.psum_scatter(
                router_grad.astype(jnp.bfloat16), "ctx", scatter_dimension=0, tiled=True
            ).astype(jnp.float32),
        )
        expert_grad = jnp.concatenate([up_grad, down_grad], axis=-1)
        summed = (
            lax.psum(shard_grads[0].astype(jnp.bfloat16), "dp").astype(jnp.float32),
            lax.psum(shard_grads[1].astype(jnp.bfloat16), "dp").astype(jnp.float32),
            lax.psum(shard_grads[2].astype(jnp.bfloat16), "dp").astype(jnp.float32),
            lax.psum(shard_grads[3].astype(jnp.bfloat16), "dp").astype(jnp.float32),
            lax.psum(shard_grads[4].astype(jnp.bfloat16), "dp").astype(jnp.float32),
            lax.psum(expert_grad.astype(jnp.bfloat16), "dp").astype(jnp.float32),
        )
        layer_grads.append(summed)
    layer_grads = layer_grads[::-1]
    stacked = [
        jnp.stack([layer_grads[layer_idx][member] for layer_idx in range(layer_count)], axis=0)
        for member in range(6)
    ]
    return (
        out_stream,
        grad_stream[None],
        stacked[0],
        stacked[1],
        stacked[2],
        stacked[3],
        stacked[4],
        stacked[5],
    )


def solution(mesh):
    placed = (
        P("dp", "ctx", None),
        P("dp", None),
        P(None, "dp", "ctx", None),
        P(None, "ctx"),
        P(None, "ctx", None),
        P(None, "ctx", None),
        P(None, "ctx"),
        P(None, "ctx", None),
        P(None, "ctx", None, None),
        P("dp", "ctx", None),
    )
    return jax.shard_map(
        local,
        mesh=mesh,
        in_specs=placed,
        out_specs=(
            P("dp", "ctx", None),
            P("dp", "ctx", None),
            P(None, "ctx"),
            P(None, "ctx", None),
            P(None, "ctx", None),
            P(None, "ctx"),
            P(None, "ctx", None),
            P(None, "ctx", None, None),
        ),
        check_vma=False,
    )
```

profile of v0, /device:TPU:0, one launch (start us, length us, event | category | flops | bytes accessed | tf_op | source)
XLA Modules:
  0.0 2060.4 jit_solution(404911341630574558)
XLA Ops:
  10.2 10.2 all-gather
  21.5 28.4 %all-gather.21.cloned.1.call-done = bf16[1,1024,2048]{2,1,0:T(8,128)(2,1)} async-done(((bf16[1,128,2048]{2,1,0:T(8,128)(2,1)}), bf16[1,1024,2048]{2,1,0:T(8,128)(2,1)}) %all-gather.21.cloned.1.call-update) | async-done | bytes 4194320 | tf_op jit(solution)/shard_map/all_gather | solution.py:121
  56.7 9.0 reduce-window.25
  72.3 8.7 all-gather.3
  82.2 6.3 reshape.883
  93.1 13.5 while.54
  106.7 5.9 all-gather.23.cloned.1.call-done
  115.6 5.1 gather_fusion
  124.4 4.6 all-to-all-start
  129.0 18.8 slice_bitcast_fusion.18
  147.9 24.7 %all-to-all-done = bf16[32,40,1024]{2,1,0:T(8,128)(2,1)} async-done(((bf16[32,40,1024]{2,1,0:T(8,128)(2,1)}), bf16[32,40,1024]{2,1,0:T(8,128)(2,1)}, u32[]{:S(2)}, u32[]{:S(2)}) %all-to-all-start) | async-done | bytes 2621472 | tf_op jit(solution)/shard_map/all_to_all | solution.py:208
  174.5 6.3 fusion.74
  195.4 35.1 %all-gather.5 = bf16[1,1024]{1,0:T(2,128)(2,1)S(1)} all-gather(bf16[1,128]{1,0:T(2,128)(2,1)S(1)} %copy-done.133), channel_id=7, replica_groups=mesh['dp'=4,'ctx'=8] {'ctx'}, dimensions={1}, use_global_device_ids=true | all-gather | bytes 2304 | tf_op jit(solution)/shard_map/all_gather | solution.py:120
  230.7 8.0 all-gather.4
  239.5 7.0 gather_fusion.8
  249.8 5.3 gather_fusion.1
  263.5 9.0 all-gather.8
  272.8 9.0 reduce-window.29
  287.5 9.1 all-gather.9
  298.5 6.4 reshape.884
  309.5 13.4 while.55
  327.2 7.0 gather_fusion.9
  334.9 5.1 gather_fusion.2
  340.7 5.1 gather_fusion.4
  349.7 37.2 %all_to_all.132 = bf16[32,40,1024]{2,1,0:T(8,128)(2,1)} all-to-all(bf16[32,40,1024]{2,1,0:T(8,128)(2,1)S(1)} %get-tuple-element.834), channel_id=1, replica_groups=mesh['dp'=4,'ctx'=8] {'ctx'}, dimensions={0} | all-to-all | bytes 5242880 | tf_op jit(solution)/shard_map/all_to_all | solution.py:309
  393.5 30.2 %all-to-all-done.2 = bf16[32,40,1024]{2,1,0:T(8,128)(2,1)} async-done(((bf16[32,40,1024]{2,1,0:T(8,128)(2,1)}), bf16[32,40,1024]{2,1,0:T(8,128)(2,1)}, u32[]{:S(2)}, u32[]{:S(2)}) %all-to-all-start.2) | async-done | bytes 2621472 | tf_op jit(solution)/shard_map/all_to_all | solution.py:208
  425.9 6.3 fusion.70
  445.4 7.1 fusion.117
  456.0 21.6 %all-to-all-done.3 = bf16[4,320,1024]{2,0,1:T(4,128)(2,1)S(1)} async-done(((bf16[4,320,1024]{2,0,1:T(4,128)(2,1)}), bf16[4,320,1024]{2,0,1:T(4,128)(2,1)S(1)}, u32[]{:S(2)}, u32[]{:S(2)}) %all-to-all-start.3) | async-done | bytes 2621472 | tf_op jit(solution)/shard_map/all_to_all | solution.py:223
  486.4 5.4 gather_fusion.3
  496.2 19.6 all-to-all-done.5
  518.4 5.3 gather_fusion.5
  532.9 17.9 while.56
  538.3 4.8 conditional.10
  550.8 6.2 copy.216
  557.0 6.9 reshape.871
  564.2 44.8 %reduce-scatter.25.cloned.1.call-done = bf16[128,1024]{1,0:T(8,128)(2,1)} async-done(((bf16[1024,1024]{1,0:T(8,128)(2,1)}), bf16[128,1024]{1,0:T(8,128)(2,1)}) %reduce-scatter.25.cloned.1.call-update) | async-done | bytes 262160
  616.1 5.1 gather_fusion.6
  623.4 34.9 %all_to_all.133 = bf16[32,40,1024]{2,1,0:T(8,128)(2,1)S(1)} all-to-all(bf16[32,40,1024]{2,1,0:T(8,128)(2,1)S(1)} %broadcast_select_fusion.2), channel_id=1, replica_groups=mesh['dp'=4,'ctx'=8] {'ctx'}, dimensions={0} | all-to-all | bytes 5242880 | tf_op jit(solution)/shard_map/all_to_all | solution.py:309
  658.6 7.0 multiply_convert_fusion.1
  665.6 6.1 fusion.114
  671.7 5.3 copy.174
  677.0 4.7 all-to-all-start.7
  682.7 31.2 %all-to-all-done.7 = bf16[4,320,1024]{2,0,1:T(4,128)(2,1)} async-done(((bf16[4,320,1024]{2,0,1:T(4,128)(2,1)}), bf16[4,320,1024]{2,0,1:T(4,128)(2,1)}, u32[]{:S(2)}, u32[]{:S(2)}) %all-to-all-start.7) | async-done | bytes 2621472 | tf_op jit(solution)/shard_map/all_to_all | solution.py:336
  716.6 5.3 gather_fusion.7
  730.2 18.6 while.57
  736.0 4.8 conditional.11
  748.8 6.2 copy.217
  755.0 6.6 reshape.873
  770.8 35.9 %reduce-scatter.27.cloned.1.call-done = bf16[128,1024]{1,0:T(8,128)(2,1)} async-done(((bf16[1024,1024]{1,0:T(8,128)(2,1)}), bf16[128,1024]{1,0:T(8,128)(2,1)}) %reduce-scatter.27.cloned.1.call-update) | async-done | bytes 262160
  817.6 8.8 convolution_convert_fusion
  826.4 13.3 maximum_bitcast_fusion.3
  849.0 8.2 convolution_convert_fusion.1
  857.2 13.3 maximum_bitcast_fusion.2
  870.5 35.7 %reduce-scatter.19.cloned.1.call-done = bf16[128,2048]{1,0:T(8,128)(2,1)} async-done(((bf16[1024,2048]{1,0:T(8,128)(2,1)}), bf16[128,2048]{1,0:T(8,128)(2,1)}) %reduce-scatter.19.cloned.1.call-update) | async-done | bytes 524304 | tf_op jit(solution)/shard_map/reduce_scatter | solution.py:463
  906.2 44.5 %reduce-scatter.21.cloned.1.call-done = bf16[128,1024]{1,0:T(8,128)(2,1)} async-done(((bf16[1024,1024]{1,0:T(8,128)(2,1)}), bf16[128,1024]{1,0:T(8,128)(2,1)}) %reduce-scatter.21.cloned.1.call-update) | async-done | bytes 262160 | tf_op jit(solution)/shard_map/reduce_scatter | solution.py:466
  950.7 54.9 %reduce-scatter.17.cloned.1.call-done = bf16[128,2048]{1,0:T(8,128)(2,1)} async-done(((bf16[1024,2048]{1,0:T(8,128)(2,1)}), bf16[128,2048]{1,0:T(8,128)(2,1)}) %reduce-scatter.17.cloned.1.call-update) | async-done | bytes 524304 | tf_op jit(solution)/shard_map/reduce_scatter | solution.py:463
  1007.6 35.3 %reduce-scatter.31.cloned.1.call-done = bf16[128,32]{1,0:T(8,128)(2,1)} async-done(((bf16[1024,32]{1,0:T(8,128)(2,1)}), bf16[128,32]{1,0:T(8,128)(2,1)}) %reduce-scatter.31.cloned.1.call-update) | async-done | bytes 8208
  1043.7 36.6 %reduce-scatter.29.cloned.1.call-done = bf16[128,32]{1,0:T(8,128)(2,1)} async-done(((bf16[1024,32]{1,0:T(8,128)(2,1)}), bf16[128,32]{1,0:T(8,128)(2,1)}) %reduce-scatter.29.cloned.1.call-update) | async-done | bytes 8208
  1085.0 12.9 all-reduce.4
  1098.2 23.6 %all-reduce.5 = (bf16[1,128]{1,0:T(2,128)(2,1)S(1)}, bf16[1,128]{1,0:T(2,128)(2,1)S(1)}, bf16[1,128]{1,0:T(2,128)(2,1)S(1)}, bf16[1,128]{1,0:T(2,128)(2,1)S(1)},...) all-reduce(bf16[1,128]{1,0:T(2,128)(2,1)S(1)} %dynamic-slice_bitcas, ...), channel_id=1, replica_groups=mesh['dp'=4,'ctx'=8] {'dp'}, use_global_device_ids=true, to_apply=%region_59.61 | all-reduce | flops 8704 | bytes 34816 | tf_op jit(solution)/shard_map/psum | solution.py:478
  1124.6 850.3 %all-reduce.9.cloned.1.call-done = (bf16[1,128,2048]{2,1,0:T(8,128)(2,1)}, bf16[1,128,2048]{2,1,0:T(8,128)(2,1)}, bf16[1,128,1024]{2,1,0:T(8,128)(2,1)}, bf16[1,...) async-done(((bf16[1,128,2048]{2,1,0:T(8,128)(2,1)}, bf16[1,128,2048]{2,1,0:T(8,128)(2,1)}, ...) | async-done | bytes 26738704 | tf_op jit(solution)/shard_map/psum | solution.py:479
  1974.8 27.1 %maximum_convert_fusion = f32[2,4,1024,1536]{2,3,1,0:T(8,128)} fusion(bf16[1,4,1024,1536]{2,3,1,0:T(8,128)(2,1)} %get-tuple-element.755, bf16[1,4,1024,1536]{2,3,1,0:T(8,128)(2,1)} %get-tuple-element.756), kind=kLoop, calls=%fused_computation.110 | loop fusion | flops 25165824 | bytes 75497472 | tf_op jit(solution)/shard_map/stack | solution.py:488
  2001.9 49.0 %copy.181 = f32[2,4,1024,1536]{3,2,1,0:T(8,128)} copy(f32[2,4,1024,1536]{2,3,1,0:T(8,128)} %maximum_convert_fusion) | data formatting | bytes 100663296
  (625 shorter events, 231.4 us)
Async XLA Ops:
  7.2 13.3 copy-start.103
  7.2 14.0 copy-start.30
  7.2 42.7 %all-gather.21.cloned.1.call-start = ((), (), s32[]{:S(2)}) async-start(), calls=%async_computation.22 | async-start | bytes 4718592 | tf_op jit(solution)/shard_map/all_gather | solution.py:121
  9.6 72.6 %all-gather.17.cloned.1.call-start = ((), (), s32[]{:S(2)}) async-start(), calls=%async_computation.16 | async-start | bytes 2359296 | tf_op jit(solution)/shard_map/all_gather | solution.py:144
  20.4 32.5 %copy-start.89 = (f32[1,1024]{1,0:T(1,128)}, f32[1,1024]{1,0:T(1,128)S(1)}, u32[]{:S(2)}) copy-start(f32[1,1024]{1,0:T(1,128)S(1)} %convert_element_type.350) | copy-start | bytes 12292
  21.3 31.6 %copy-start.119 = (f32[128]{0:T(128)}, f32[128]{0:T(128)S(1)}, u32[]{:S(2)}) copy-start(f32[128]{0:T(128)S(1)} %add_rsqrt_fusion.3) | copy-start | bytes 1540
  21.5 276.8 %copy-start.57 = (f32[128,32]{0,1:T(8,128)}, f32[128,32]{0,1:T(8,128)S(1)}, u32[]{:S(2)}) copy-start(f32[128,32]{0,1:T(8,128)S(1)} %get-tuple-element.836) | copy-start | bytes 49156
  21.5 276.8 %copy-start.59 = (f32[128,32]{0,1:T(8,128)}, f32[128,32]{0,1:T(8,128)S(1)}, u32[]{:S(2)}) copy-start(f32[128,32]{0,1:T(8,128)S(1)} %get-tuple-element.837) | copy-start | bytes 49156
  53.1 17.4 copy-start.132
  54.1 58.5 %all-gather.23.cloned.1.call-start = ((), (), s32[]{:S(2)}) async-start(), calls=%async_computation.23 | async-start | bytes 2359296 | tf_op jit(solution)/shard_map/all_gather | solution.py:122
  55.0 203.3 %all-gather.25.cloned.1.call-start = ((), (), s32[]{:S(2)}) async-start(), calls=%async_computation.24 | async-start | bytes 4718592 | tf_op jit(solution)/shard_map/all_gather | solution.py:121
  55.6 25.5 %copy-start.130 = (s32[1024]{0:T(1024)}, s32[1024]{0:T(1024)S(1)}, u32[]{:S(2)}) copy-start(s32[1024]{0:T(1024)S(1)} %iota_add_fusion) | copy-start | bytes 12292
  81.0 33.7 %copy-start.97 = (f32[1,1024]{1,0:T(1,128)}, f32[1,1024]{1,0:T(1,128)S(1)}, u32[]{:S(2)}) copy-start(f32[1,1024]{1,0:T(1,128)S(1)} %convert_element_type.351) | copy-start | bytes 12292
  81.1 39.6 %copy-start.104 = (pred[32,40]{1,0:T(8,128)(4,1)}, pred[32,40]{1,0:T(8,128)(4,1)S(1)}, u32[]{:S(2)}) copy-start(pred[32,40]{1,0:T(8,128)(4,1)S(1)} %broadcast_in_dim.196) | copy-start | bytes 3844
  106.6 14.1 copy-start.8
  106.6 14.1 copy-start.10
  106.6 14.1 copy-start.66
  106.7 14.0 copy-start.52
  115.6 123.1 %copy-start = (bf16[128,1024]{1,0:T(8,128)(2,1)}, bf16[128,1024]{1,0:T(8,128)(2,1)S(1)}, u32[]{:S(2)}) copy-start(bf16[128,1024]{1,0:T(8,128)(2,1)S(1)} %multiply_convert_fusion.8) | copy-start | bytes 786436
  124.4 48.1 %all-to-all-start = ((bf16[32,40,1024]{2,1,0:T(8,128)(2,1)}), bf16[32,40,1024]{2,1,0:T(8,128)(2,1)}, u32[]{:S(2)}, u32[]{:S(2)}) async-start(bf16[32,40,1024]{2,1,0:T(8,128)(2,1)} %broadcast_select_fusion.3), calls=%async_computation | async-start | bytes 5242880 | tf_op jit(solution)/shard_map/all_to_all | solution.py:208
  190.8 39.8 %copy-start.115 = (bf16[2,128,32]{1,2,0:T(8,128)(2,1)S(1)}, bf16[2,128,32]{1,2,0:T(8,128)(2,1)}, u32[]{:S(2)}) copy-start(bf16[2,128,32]{1,2,0:T(8,128)(2,1)} %param.35) | copy-start | bytes 49156
  190.8 47.9 %copy-start.114 = (s32[1024,1]{0,1:T(1,128)S(1)}, s32[1024,1]{0,1:T(1,128)}, u32[]{:S(2)}) copy-start(s32[1024,1]{0,1:T(1,128)} %copy-done.113) | copy-start | bytes 12292
  190.8 56.3 %all-to-all-start.1 = ((bf16[4,320,1024]{2,0,1:T(4,128)(2,1)}), bf16[4,320,1024]{2,0,1:T(4,128)(2,1)}, u32[]{:S(2)}, u32[]{:S(2)}) async-start(bf16[4,320,1024]{2,0,1:T(4,128)(2,1)} %copy.152), calls=%async_computation.1 | async-start | bytes 5242880 | tf_op jit(solution)/shard_map/all_to_all | solution.py:223
  195.4 103.1 %all-gather.19.cloned.1.call-start = ((), (), s32[]{:S(2)}) async-start(), calls=%async_computation.17 | async-start | bytes 2359296 | tf_op jit(solution)/shard_map/all_gather | solution.py:144
  230.5 27.8 %copy-start.91 = (f32[1,1024]{1,0:T(1,128)}, f32[1,1024]{1,0:T(1,128)S(1)}, u32[]{:S(2)}) copy-start(f32[1,1024]{1,0:T(1,128)S(1)} %convert_element_type.352) | copy-start | bytes 12292
  258.3 65.5 %copy-start.19 = (f32[128,1024]{1,0:T(8,128)}, f32[128,1024]{1,0:T(8,128)S(1)}, u32[]{:S(2)}) copy-start(f32[128,1024]{1,0:T(8,128)S(1)} %get-tuple-element.758) | copy-start | bytes 1572868
  261.5 35.7 %copy-start.62 = (bf16[1,128,1024]{2,1,0:T(8,128)(2,1)S(1)}, bf16[1,128,1024]{2,1,0:T(8,128)(2,1)}, u32[]{:S(2)}) copy-start(bf16[1,128,1024]{2,1,0:T(8,128)(2,1)} %param.37) | copy-start | bytes 786436
  262.6 61.2 %all-gather.27.cloned.1.call-start = ((), (), s32[]{:S(2)}) async-start(), calls=%async_computation.25 | async-start | bytes 2359296 | tf_op jit(solution)/shard_map/all_gather | solution.py:122
  272.5 53.6 %copy-start.99 = (f32[1,1024]{1,0:T(1,128)}, f32[1,1024]{1,0:T(1,128)S(1)}, u32[]{:S(2)}) copy-start(f32[1,1024]{1,0:T(1,128)S(1)} %convert_element_type.353) | copy-start | bytes 12292
  282.3 16.1 copy-start.111
  386.9 36.9 %all-to-all-start.2 = ((bf16[32,40,1024]{2,1,0:T(8,128)(2,1)}), bf16[32,40,1024]{2,1,0:T(8,128)(2,1)}, u32[]{:S(2)}, u32[]{:S(2)}) async-start(bf16[32,40,1024]{2,1,0:T(8,128)(2,1)} %get-tuple-element.835), calls=%async_computation.2 | async-start | bytes 5242880 | tf_op jit(solution)/shard_map/all_to_all | solution.py:208
  393.5 38.7 %copy-start.25 = (bf16[4,8,40,1024]{3,2,1,0:T(8,128)(2,1)}, bf16[4,8,40,1024]{3,2,1,0:T(8,128)(2,1)S(1)}, u32[]{:S(2)}) copy-start(bf16[4,8,40,1024]{3,2,1,0:T(8,128)(2,1)S(1)} %copy.165) | copy-start | bytes 7864324
  441.8 35.8 %all-to-all-start.3 = ((bf16[4,320,1024]{2,0,1:T(4,128)(2,1)}), bf16[4,320,1024]{2,0,1:T(4,128)(2,1)S(1)}, u32[]{:S(2)}, u32[]{:S(2)}) async-start(bf16[4,320,1024]{2,0,1:T(4,128)(2,1)} %copy.163), calls=%async_computation.3 | async-start | bytes 5242880 | tf_op jit(solution)/shard_map/all_to_all | solution.py:223
  456.0 27.7 %copy-start.112 = (s32[1024,1]{0,1:T(1,128)S(1)}, s32[1024,1]{0,1:T(1,128)}, u32[]{:S(2)}) copy-start(s32[1024,1]{0,1:T(1,128)} %copy-done.111) | copy-start | bytes 12292
  479.1 36.7 %all-to-all-start.5 = ((bf16[4,320,1024]{2,0,1:T(4,128)(2,1)}), bf16[4,320,1024]{2,0,1:T(4,128)(2,1)}, u32[]{:S(2)}, u32[]{:S(2)}) async-start(bf16[4,320,1024]{2,0,1:T(4,128)(2,1)} %copy.166), calls=%async_computation.5 | async-start | bytes 5242880 | tf_op jit(solution)/shard_map/all_to_all | solution.py:336
  483.5 125.5 %reduce-scatter.25.cloned.1.call-start = ((), (), s32[]{:S(2)}) async-start(), calls=%async_computation.26 | async-start | bytes 2359296
  563.9 46.4 %copy-start.20 = (f32[128,1024]{1,0:T(8,128)S(1)}, f32[128,1024]{1,0:T(8,128)}, u32[]{:S(2)}) copy-start(f32[128,1024]{1,0:T(8,128)} %copy-done.19) | copy-start | bytes 1572868
  563.9 46.4 %copy-start.92 = (f32[1,1024]{1,0:T(1,128)S(1)}, f32[1,1024]{1,0:T(1,128)}, u32[]{:S(2)}) copy-start(f32[1,1024]{1,0:T(1,128)} %copy-done.91) | copy-start | bytes 12292
  563.9 46.4 %copy-start.125 = (f32[128]{0:T(128)S(1)}, f32[128]{0:T(128)}, u32[]{:S(2)}) copy-start(f32[128]{0:T(128)} %copy-done.124) | copy-start | bytes 1540
  564.2 50.6 %copy-start.64 = (bf16[128,16,64]{0,2,1:T(8,128)(2,1)}, bf16[128,16,64]{0,2,1:T(8,128)(2,1)S(1)}, u32[]{:S(2)}) copy-start(bf16[128,16,64]{0,2,1:T(8,128)(2,1)S(1)} %pad_maximum_fusion.12) | copy-start | bytes 786436
  621.2 37.3 %slice-start.6 = ((s8[5242880]{0:T(1024)(128)(4,1)}), s8[4194304]{0:T(1024)(128)(4,1)S(1)}, s32[]{:S(2)}) async-start(s8[5242880]{0:T(1024)(128)(4,1)} %bitcast.600), calls=%async_computation.37 | async-start | bytes 8388608
  623.3 35.2 %slice-start.7 = ((s8[5242880]{0:T(1024)(128)(4,1)}), s8[1048576]{0:T(1024)(128)(4,1)S(1)}, s32[]{:S(2)}) async-start(s8[5242880]{0:T(1024)(128)(4,1)} %bitcast.600), calls=%async_computation.38 | async-start | bytes 2097152
  677.0 37.0 %all-to-all-start.7 = ((bf16[4,320,1024]{2,0,1:T(4,128)(2,1)}), bf16[4,320,1024]{2,0,1:T(4,128)(2,1)}, u32[]{:S(2)}, u32[]{:S(2)}) async-start(bf16[4,320,1024]{2,0,1:T(4,128)(2,1)} %copy.174), calls=%async_computation.7 | async-start | bytes 5242880 | tf_op jit(solution)/shard_map/all_to_all | solution.py:336
  681.7 125.1 %reduce-scatter.27.cloned.1.call-start = ((), (), s32[]{:S(2)}) async-start(), calls=%async_computation.27 | async-start | bytes 2359296
  682.7 42.5 %copy-start.95 = (bf16[128,32]{0,1:T(8,128)(2,1)}, bf16[128,32]{0,1:T(8,128)(2,1)S(1)}, u32[]{:S(2)}) copy-start(bf16[128,32]{0,1:T(8,128)(2,1)S(1)} %select_reduce_fusion) | copy-start | bytes 24580
  761.6 108.9 %reduce-scatter.23.cloned.1.call-start = ((), (), s32[]{:S(2)}) async-start(), calls=%async_computation.21 | async-start | bytes 2359296 | tf_op jit(solution)/shard_map/reduce_scatter | solution.py:466
  763.7 142.5 %reduce-scatter.19.cloned.1.call-start = ((), (), s32[]{:S(2)}) async-start(), calls=%async_computation.19 | async-start | bytes 4718592 | tf_op jit(solution)/shard_map/reduce_scatter | solution.py:463
  767.5 183.3 %reduce-scatter.21.cloned.1.call-start = ((), (), s32[]{:S(2)}) async-start(), calls=%async_computation.20 | async-start | bytes 2359296 | tf_op jit(solution)/shard_map/reduce_scatter | solution.py:466
  770.6 38.0 %copy-start.31 = (bf16[1,128,1024]{2,1,0:T(8,128)(2,1)S(1)}, bf16[1,128,1024]{2,1,0:T(8,128)(2,1)}, u32[]{:S(2)}) copy-start(bf16[1,128,1024]{2,1,0:T(8,128)(2,1)} %param.28) | copy-start | bytes 786436
  770.6 38.0 %copy-start.90 = (f32[1,1024]{1,0:T(1,128)S(1)}, f32[1,1024]{1,0:T(1,128)}, u32[]{:S(2)}) copy-start(f32[1,1024]{1,0:T(1,128)} %copy-done.89) | copy-start | bytes 12292
  770.6 38.0 %copy-start.120 = (f32[128]{0:T(128)S(1)}, f32[128]{0:T(128)}, u32[]{:S(2)}) copy-start(f32[128]{0:T(128)} %copy-done.119) | copy-start | bytes 1540
  770.6 235.0 %reduce-scatter.17.cloned.1.call-start = ((), (), s32[]{:S(2)}) async-start(), calls=%async_computation.18 | async-start | bytes 4718592 | tf_op jit(solution)/shard_map/reduce_scatter | solution.py:463
  812.0 230.9 %reduce-scatter.31.cloned.1.call-start = ((), (), s32[]{:S(2)}) async-start(), calls=%async_computation.29 | async-start | bytes 294912
  826.4 13.3 copy-start.3
  826.4 13.3 copy-start.94
  826.4 15.8 copy-start.1
  826.4 15.9 copy-start.96
  826.4 18.7 copy-start.28
  842.2 238.1 %reduce-scatter.29.cloned.1.call-start = ((), (), s32[]{:S(2)}) async-start(), calls=%async_computation.28 | async-start | bytes 294912
  844.8 1130.1 %all-reduce.9.cloned.1.call-start = ((), (), s32[]{:S(2)}) async-start(), calls=%async_computation.30 | async-start | bytes 53477376 | tf_op jit(solution)/shard_map/psum | solution.py:479
  1005.7 75.4 %copy-start.79 = (bf16[128,512]{0,1:T(8,128)(2,1)S(1)}, bf16[128,512]{0,1:T(8,128)(2,1)}, u32[]{:S(2)}) copy-start(bf16[128,512]{0,1:T(8,128)(2,1)} %copy-done.78) | copy-start | bytes 393220
  1081.1 42.4 %copy-start.39 = (f32[128,1024]{1,0:T(8,128)S(1)}, f32[128,1024]{1,0:T(8,128)}, u32[]{:S(2)}) copy-start(f32[128,1024]{1,0:T(8,128)} %copy-done.37) | copy-start | bytes 1572868
  2001.9 49.0 %copy-start.81 = (bf16[1,128,2048]{2,1,0:T(8,128)(2,1)S(1)}, bf16[1,128,2048]{2,1,0:T(8,128)(2,1)}, u32[]{:S(2)}) copy-start(bf16[1,128,2048]{2,1,0:T(8,128)(2,1)} %get-tuple-element.751) | copy-start | bytes 1572868
  2001.9 49.0 %copy-start.82 = (bf16[1,128,2048]{2,1,0:T(8,128)(2,1)S(1)}, bf16[1,128,2048]{2,1,0:T(8,128)(2,1)}, u32[]{:S(2)}) copy-start(bf16[1,128,2048]{2,1,0:T(8,128)(2,1)} %get-tuple-element.752) | copy-start | bytes 1572868
  (103 other events, 400.6 us)
Sparse Core Ops, SparseCore 0:
  10.5 39.4 all-gather.20
  54.2 27.8 all-gather.16
  84.6 27.8 all-gather.22
  114.9 51.2 all-gather.24
  262.7 27.8 all-gather.18
  292.4 27.8 all-gather.26
  564.0 44.8 reduce-scatter.24
  761.7 44.9 reduce-scatter.26
  810.0 41.1 reduce-scatter.22
  854.8 51.3 reduce-scatter.18
  909.5 41.1 reduce-scatter.20
  954.3 51.3 reduce-scatter.16
  1009.3 33.5 reduce-scatter.30
  1046.6 33.5 reduce-scatter.28
  1084.0 890.8 all-reduce.8
where the time goes:
time: 2070 us; the launch traced here: 2060 us
  waiting for transfers between devices  1300 us (63%)
  local copies, waits for them, and re-layouts  267 us (13%)
  blocking collectives  189 us (9%)
  other arithmetic  115 us (6%)
  matrix products  114 us (6%)
  loops' own time  30.1 us (1%)
  starting transfers between devices  27.9 us (1%)
    psum x1, waiting for transfers between devices, local(): lax.psum(shard_grads[1].astype(jnp.bfloat16), 'dp').astype(jnp.float32)  850 us
    unnamed x19, waiting for transfers between devices  154 us
    unnamed x297, local copies, waits for them, and re-layouts  92.8 us
    reduce_scatter x2, waiting for transfers between devices, local(): lax.psum_scatter(qkv_grad.astype(jnp.bfloat16), 'ctx', scatter_dimension=...  90.7 us
    all_to_all x2, blocking collectives, local(): lax.all_to_all(outgoing_grad, 'ctx', split_axis=0, concat_axis=1, tiled=T...  72.1 us
    another operation x8, other arithmetic, local(): jnp.stack([layer_grads[layer_idx][member] for layer_idx in range(layer_co...  57.9 us
    all_to_all x2, waiting for transfers between devices, local(): lax.all_to_all(outgoing, 'ctx', split_axis=0, concat_axis=1, tiled=True)  54.9 us
    all_to_all x2, waiting for transfers between devices, local(): lax.all_to_all(row_grad, 'ctx', split_axis=1, concat_axis=0, tiled=True)  50.8 us
  transfers between devices with their start and end apart: 21, of which 15 were waited for; matrix products, arithmetic and copies ran while one was open for 12% of the time, Pallas kernels for 0%

commit v1 on v0

v1 whole, which is shorter than its diff:
```python
import functools
import math

import jax
import jax.numpy as jnp
from jax import lax
from jax.experimental import pallas as pl
from jax.experimental.pallas import tpu as pltpu
from jax.sharding import PartitionSpec as P

HEADS = 16
KVH = 8
HD = 64
TOP = 8
FE = 512
CAP = 40
BLOCK = 128
PAIR = 2 * BLOCK
EXT = 128
ROWS = 320
F32 = jnp.float32
BF16 = jnp.bfloat16

epsilon = 1e-06


def dot_nn(left, right):
    return lax.dot_general(left, right, (((1,), (0,)), ((), ())), preferred_element_type=F32)


def dot_nt(left, right):
    return lax.dot_general(left, right, (((1,), (1,)), ((), ())), preferred_element_type=F32)


def dot_tn(left, right):
    return lax.dot_general(left, right, (((0,), (0,)), ((), ())), preferred_element_type=F32)


def chip_perm(size, mask):
    return [(i, i ^ mask) for i in range(size)]


def hierarchical(size):
    return size == 8


def gather_ctx(rows):
    size = lax.axis_size("ctx")
    if not hierarchical(size):
        whole = lax.all_gather(rows, "ctx", axis=0, tiled=True)
        return [whole], []
    near = [rows] + [lax.ppermute(rows, "ctx", chip_perm(size, 2 * k)) for k in range(1, size // 2)]
    far = [lax.ppermute(piece, "ctx", chip_perm(size, 1)) for piece in near]
    return near, far


def reduce_ctx(partial):
    size = lax.axis_size("ctx")
    if not hierarchical(size):
        return [lax.psum_scatter(partial, "ctx", scatter_dimension=0, tiled=True).astype(F32)]
    half = partial.shape[0] // 2
    theirs = lax.ppermute(partial[half:], "ctx", chip_perm(size, 1))
    both = partial[:half].astype(F32) + theirs.astype(F32)
    chips = size // 2
    rows = half // chips
    low = both.astype(BF16)
    arrived = [
        lax.ppermute(low[k * rows : (k + 1) * rows], "ctx", chip_perm(size, 2 * k))
        for k in range(1, chips)
    ]
    return [both[:rows]] + [piece.astype(F32) for piece in arrived]


def other_streams(near, far):
    streams = lax.axis_size("dp")
    size = lax.axis_size("ctx")
    mine = near[0] if len(near) == 1 else jnp.concatenate(near, axis=0)
    gathered = []
    for k in range(1, streams):
        piece = lax.ppermute(mine, "dp", [(i, (i + k) % streams) for i in range(streams)])
        if hierarchical(size):
            gathered.append([piece, lax.ppermute(piece, "ctx", chip_perm(size, 1))])
        else:
            gathered.append([piece])
    return gathered


def copy_rows(pieces, target, sems):
    copies = []
    start = 0
    for index, piece in enumerate(pieces):
        rows = piece.shape[0]
        copies.append(
            pltpu.make_async_copy(piece, target.at[pl.ds(start, rows)], sems.at[index])
        )
        start += rows
    for copy in copies:
        copy.start()
    return copies


def pick_matrix(ext, first, experts):
    width = experts * 2 * CAP
    lane = lax.broadcasted_iota(jnp.int32, (PAIR, EXT), 1)
    column = lax.broadcasted_iota(jnp.int32, (PAIR, width), 1)
    late = jnp.where(lax.broadcasted_iota(jnp.int32, (PAIR, 1), 0) >= BLOCK, CAP, 0)
    hit = None
    for e in range(experts):
        code = jnp.sum(jnp.where(lane == 64 + first + e, ext, 0.0), axis=1, keepdims=True)
        code = code.astype(jnp.int32)
        slot = jnp.where(code < 0, -1, code + late + 2 * CAP * e)
        here = column == slot
        hit = here if hit is None else hit | here
    return jnp.where(hit, 1.0, 0.0).astype(BF16)


def gate_lanes(first_expert, rows):
    lane = lax.broadcasted_iota(jnp.int32, (rows, EXT), 1)
    return (lane == first_expert) | (lane == 32 + first_expert)


def moe_fwd_kernel(experts, n_pieces, first_ref, *refs):
    pieces = refs[:n_pieces]
    w_ref = refs[n_pieces]
    y_ref, x_ref, gate_ref, gu_ref, pick_ref = refs[n_pieces + 1 : n_pieces + 6]
    tokens, rows, gates, outs, hid, sems = refs[n_pieces + 6 :]
    e = pl.program_id(0)
    first = first_ref[0]
    pairs = tokens.shape[0] // PAIR
    width = y_ref.shape[1]
    slots = 2 * CAP

    @pl.when(e == 0)
    def _():
        for copy in copy_rows(pieces, tokens, sems):
            copy.wait()

        def gather(p, carry):
            base = pl.multiple_of(p * PAIR, PAIR)
            block = tokens[pl.ds(base, PAIR), :]
            pick = pick_matrix(block[:, width:].astype(F32), first, experts)
            pick_ref[pl.ds(base, PAIR), :] = pick
            found = dot_tn(pick, block)
            at = pl.multiple_of(p * slots, 16)
            for k in range(experts):
                mine = found[k * slots : (k + 1) * slots]
                rows[k, pl.ds(at, slots), :] = mine[:, :width].astype(BF16)
                gate = jnp.sum(
                    jnp.where(gate_lanes(first + k, slots), mine[:, width:], 0.0), axis=1, keepdims=True
                )
                gates[k, pl.ds(at, slots), :] = jnp.broadcast_to(gate, (slots, EXT))
            return carry

        lax.fori_loop(0, pairs, gather, 0)

    x_ref[0] = rows[e]
    gate_ref[0] = gates[e]

    def chunk(r, carry):
        at = pl.multiple_of(r * ROWS, 64)
        block = rows[e, pl.ds(at, ROWS), :]
        for n in range(2):
            gate_part = dot_nn(block, w_ref[0, 0, :, 256 * n : 256 * n + 256])
            up_part = dot_nn(block, w_ref[0, 0, :, FE + 256 * n : FE + 256 * n + 256])
            gu_ref[0, pl.ds(at, ROWS), 256 * n : 256 * n + 256] = gate_part
            gu_ref[0, pl.ds(at, ROWS), FE + 256 * n : FE + 256 * n + 256] = up_part
            hid[:, 256 * n : 256 * n + 256] = (
                gate_part / (1.0 + jnp.exp(-gate_part)) * up_part
            ).astype(BF16)
        gate = gates[e, pl.ds(at, ROWS), 0:1]
        for n in range(width // 256):
            part = dot_nt(hid[...], w_ref[0, 0, 256 * n : 256 * n + 256, 2 * FE :]) * gate
            for q in range(ROWS // slots):
                outs[
                    r * (ROWS // slots) + q,
                    pl.ds(pl.multiple_of(e * slots, 16), slots),
                    256 * n : 256 * n + 256,
                ] = part[q * slots : (q + 1) * slots].astype(BF16)
        return carry

    lax.fori_loop(0, rows.shape[1] // ROWS, chunk, 0)

    @pl.when(e == experts - 1)
    def _():
        def scatter(p, carry):
            base = pl.multiple_of(p * PAIR, PAIR)
            y_ref[pl.ds(base, PAIR), :] = dot_nn(pick_ref[pl.ds(base, PAIR), :], outs[p]).astype(BF16)
            return carry

        lax.fori_loop(0, pairs, scatter, 0)


def moe_bwd_kernel(experts, n_pieces, first_ref, *refs):
    pieces = refs[:n_pieces]
    w_ref, gate_ref, gu_ref, pick_ref = refs[n_pieces : n_pieces + 4]
    d_ref, dy_ref, hid_ref, dgu_ref = refs[n_pieces + 4 : n_pieces + 8]
    tokens, rows, outs, dots, sems = refs[n_pieces + 8 :]
    e = pl.program_id(0)
    first = first_ref[0]
    pairs = tokens.shape[0] // PAIR
    width = tokens.shape[1]
    slots = 2 * CAP

    @pl.when(e == 0)
    def _():
        for copy in copy_rows(pieces, tokens, sems):
            copy.wait()

        def gather(p, carry):
            base = pl.multiple_of(p * PAIR, PAIR)
            found = dot_tn(pick_ref[pl.ds(base, PAIR), :], tokens[pl.ds(base, PAIR), :])
            at = pl.multiple_of(p * slots, 16)
            for k in range(experts):
                rows[k, pl.ds(at, slots), :] = found[k * slots : (k + 1) * slots].astype(BF16)
            return carry

        lax.fori_loop(0, pairs, gather, 0)

    def chunk(r, carry):
        at = pl.multiple_of(r * ROWS, 64)
        block = rows[e, pl.ds(at, ROWS), :]
        gate = gate_ref[0, pl.ds(at, ROWS), 0:1]
        dy_ref[0, pl.ds(at, ROWS), :] = (block.astype(F32) * gate).astype(BF16)
        total = jnp.zeros((ROWS, 1), F32)
        for n in range(2):
            lanes = slice(256 * n, 256 * n + 256)
            uplanes = slice(FE + 256 * n, FE + 256 * n + 256)
            raw = dot_nn(block, w_ref[0, 0, :, 2 * FE + 256 * n : 2 * FE + 256 * n + 256])
            gate_part = gu_ref[0, pl.ds(at, ROWS), lanes]
            up_part = gu_ref[0, pl.ds(at, ROWS), uplanes]
            sig = 1.0 / (1.0 + jnp.exp(-gate_part))
            silu = gate_part * sig
            hidden = (silu * up_part).astype(BF16)
            hid_ref[0, pl.ds(at, ROWS), lanes] = hidden
            total = total + jnp.sum(raw * hidden.astype(F32), axis=1, keepdims=True)
            dh = raw * gate
            slope = sig * (1.0 + gate_part * (1.0 - sig))
            dgu_ref[0, pl.ds(at, ROWS), lanes] = (dh * up_part * slope).astype(BF16)
            dgu_ref[0, pl.ds(at, ROWS), uplanes] = (dh * silu).astype(BF16)
        high = total.astype(BF16).astype(F32)
        lane = lax.broadcasted_iota(jnp.int32, (ROWS, EXT), 1)
        spread = jnp.where(
            lane == first + e, high, jnp.where(lane == 32 + first + e, total - high, 0.0)
        ).astype(BF16)
        for q in range(ROWS // slots):
            dots[r * (ROWS // slots) + q, pl.ds(pl.multiple_of(e * slots, 16), slots), :] = spread[
                q * slots : (q + 1) * slots
            ]
        for n in range(width // 256):
            part = dot_nt(
                dgu_ref[0, pl.ds(at, ROWS), :], w_ref[0, 0, 256 * n : 256 * n + 256, : 2 * FE]
            )
            for q in range(ROWS // slots):
                outs[
                    r * (ROWS // slots) + q,
                    pl.ds(pl.multiple_of(e * slots, 16), slots),
                    256 * n : 256 * n + 256,
                ] = part[q * slots : (q + 1) * slots].astype(BF16)
        return carry

    lax.fori_loop(0, rows.shape[1] // ROWS, chunk, 0)

    @pl.when(e == experts - 1)
    def _():
        def scatter(p, carry):
            base = pl.multiple_of(p * PAIR, PAIR)
            pick = pick_ref[pl.ds(base, PAIR), :]
            d_ref[pl.ds(base, PAIR), :width] = dot_nn(pick, outs[p]).astype(BF16)
            d_ref[pl.ds(base, PAIR), width:] = dot_nn(pick, dots[p]).astype(BF16)
            return carry

        lax.fori_loop(0, pairs, scatter, 0)


def pick_kernel(experts, n_pieces, first_ref, *refs):
    token_pieces = refs[:n_pieces]
    grad_pieces = refs[n_pieces : 2 * n_pieces]
    x_ref, dy_ref = refs[2 * n_pieces : 2 * n_pieces + 2]
    tokens, grads, sems, grad_sems = refs[2 * n_pieces + 2 :]
    first = first_ref[0]
    pairs = tokens.shape[0] // PAIR
    width = grads.shape[1]
    slots = 2 * CAP
    for copy in copy_rows(token_pieces, tokens, sems) + copy_rows(grad_pieces, grads, grad_sems):
        copy.wait()

    def gather(p, carry):
        base = pl.multiple_of(p * PAIR, PAIR)
        block = tokens[pl.ds(base, PAIR), :]
        pick = pick_matrix(block[:, width:].astype(F32), first, experts)
        found = dot_tn(pick, block)
        grown = dot_tn(pick, grads[pl.ds(base, PAIR), :])
        at = pl.multiple_of(p * slots, 16)
        for k in range(experts):
            mine = found[k * slots : (k + 1) * slots]
            x_ref[k, pl.ds(at, slots), :] = mine[:, :width].astype(BF16)
            gate = jnp.sum(
                jnp.where(gate_lanes(first + k, slots), mine[:, width:], 0.0), axis=1, keepdims=True
            )
            dy_ref[k, pl.ds(at, slots), :] = (grown[k * slots : (k + 1) * slots] * gate).astype(BF16)
        return carry

    lax.fori_loop(0, pairs, gather, 0)


def expert_grad_kernel(streams, aliased, *refs):
    x_refs = refs[:streams]
    dy_refs = refs[streams : 2 * streams]
    hid_own, dgu_own, w_ref = refs[2 * streams : 2 * streams + 3]
    rest = refs[2 * streams + 3 + (1 if aliased else 0) :]
    out_ref, xs, dys, hids, dgus, sems = rest
    e = pl.program_id(0)
    experts = pl.num_programs(0)
    depth = xs.shape[0]
    rows = xs.shape[1] // streams
    width = xs.shape[2]

    def copies(expert, slot):
        made = []
        for s in range(streams):
            place = pl.ds(s * rows, rows)
            made.append(
                pltpu.make_async_copy(x_refs[s].at[expert], xs.at[slot, place], sems.at[slot, s])
            )
            made.append(
                pltpu.make_async_copy(
                    dy_refs[s].at[expert], dys.at[slot, place], sems.at[slot, streams + s]
                )
            )
        place = pl.ds(0, rows)
        made.append(
            pltpu.make_async_copy(
                hid_own.at[expert], hids.at[slot, place], sems.at[slot, 2 * streams]
            )
        )
        made.append(
            pltpu.make_async_copy(
                dgu_own.at[expert], dgus.at[slot, place], sems.at[slot, 2 * streams + 1]
            )
        )
        return made

    slot = lax.rem(e, depth)

    @pl.when(e == 0)
    def _():
        for copy in copies(0, 0):
            copy.start()

    if depth > 1:

        @pl.when(e + 1 < experts)
        def _():
            for copy in copies(e + 1, lax.rem(e + 1, depth)):
                copy.start()

    for copy in copies(e, slot):
        copy.wait()

    def chunk(r, carry):
        at = pl.multiple_of(r * ROWS, 64)
        block = xs[slot, pl.ds(at, ROWS), :]
        grown = dys[slot, pl.ds(at, ROWS), :]
        for n in range(2):
            lanes = slice(256 * n, 256 * n + 256)
            uplanes = slice(FE + 256 * n, FE + 256 * n + 256)
            gate_part = dot_nn(block, w_ref[0, 0, :, lanes])
            up_part = dot_nn(block, w_ref[0, 0, :, uplanes])
            dh = dot_nn(grown, w_ref[0, 0, :, 2 * FE + 256 * n : 2 * FE + 256 * n + 256])
            sig = 1.0 / (1.0 + jnp.exp(-gate_part))
            silu = gate_part * sig
            hids[slot, pl.ds(at, ROWS), lanes] = (silu * up_part).astype(BF16)
            slope = sig * (1.0 + gate_part * (1.0 - sig))
            dgus[slot, pl.ds(at, ROWS), lanes] = (dh * up_part * slope).astype(BF16)
            dgus[slot, pl.ds(at, ROWS), uplanes] = (dh * silu).astype(BF16)
        return carry

    lax.fori_loop(rows // ROWS, streams * rows // ROWS, chunk, 0)

    def tile(i, carry):
        at = pl.multiple_of(i * 256, 256)
        left = xs[slot, :, pl.ds(at, 256)]
        for n in range(2):
            out_ref[0, 0, pl.ds(at, 256), FE * n : FE * n + FE] = dot_tn(
                left, dgus[slot, :, FE * n : FE * n + FE]
            )
        out_ref[0, 0, pl.ds(at, 256), 2 * FE :] = dot_tn(dys[slot, :, pl.ds(at, 256)], hids[slot])
        return carry

    lax.fori_loop(0, width // 256, tile, 0)


ANY = pl.BlockSpec(memory_space=pl.ANY)
PARAMS = dict(vmem_limit_bytes=60 * 1024 * 1024)


def once(shape):
    return pl.BlockSpec(shape, lambda e, first: (0,) * len(shape), pipeline_mode=pl.Buffered(1))


def per_expert(*shape):
    return pl.BlockSpec((1, *shape), lambda e, first: (e,) + (0,) * len(shape))


def weight_spec(shape, layer_idx, prefetched):
    block = (1, 1, shape[2], shape[3])
    if prefetched:
        return pl.BlockSpec(block, lambda e, first: (layer_idx, e, 0, 0))
    return pl.BlockSpec(block, lambda e: (layer_idx, e, 0, 0))


def sizes(w_expert, pieces):
    experts = w_expert.shape[1]
    length = sum(piece.shape[0] for piece in pieces)
    return experts, length, length // BLOCK * CAP


def moe_fwd(pieces, w_expert, layer_idx, first):
    experts, length, rows = sizes(w_expert, pieces)
    width = w_expert.shape[2]
    picked = experts * 2 * CAP
    pairs = length // PAIR
    return pl.pallas_call(
        functools.partial(moe_fwd_kernel, experts, len(pieces)),
        out_shape=(
            jax.ShapeDtypeStruct((length, width), BF16),
            jax.ShapeDtypeStruct((experts, rows, width), BF16),
            jax.ShapeDtypeStruct((experts, rows, EXT), F32),
            jax.ShapeDtypeStruct((experts, rows, 2 * FE), F32),
            jax.ShapeDtypeStruct((length, picked), BF16),
        ),
        grid_spec=pltpu.PrefetchScalarGridSpec(
            num_scalar_prefetch=1,
            grid=(experts,),
            in_specs=[ANY] * len(pieces) + [weight_spec(w_expert.shape, layer_idx, True)],
            out_specs=(
                once((length, width)),
                per_expert(rows, width),
                per_expert(rows, EXT),
                per_expert(rows, 2 * FE),
                once((length, picked)),
            ),
            scratch_shapes=[
                pltpu.VMEM((length, width + EXT), BF16),
                pltpu.VMEM((experts, rows, width), BF16),
                pltpu.VMEM((experts, rows, EXT), F32),
                pltpu.VMEM((pairs, picked, width), BF16),
                pltpu.VMEM((ROWS, FE), BF16),
                pltpu.SemaphoreType.DMA((len(pieces),)),
            ],
        ),
        compiler_params=pltpu.CompilerParams(dimension_semantics=("arbitrary",), **PARAMS),
        cost_estimate=pl.CostEstimate(
            flops=2 * experts * rows * width * 3 * FE,
            bytes_accessed=experts * (width * 3 * FE * 2 + rows * width * 6) + length * width * 4,
            transcendentals=experts * rows * FE,
        ),
        name="moe_fwd",
    )(first, *pieces, w_expert)


def moe_bwd(pieces, w_expert, layer_idx, first, gates, pair_values, pick):
    experts, length, rows = sizes(w_expert, pieces)
    width = w_expert.shape[2]
    picked = experts * 2 * CAP
    pairs = length // PAIR
    return pl.pallas_call(
        functools.partial(moe_bwd_kernel, experts, len(pieces)),
        out_shape=(
            jax.ShapeDtypeStruct((length, width + EXT), BF16),
            jax.ShapeDtypeStruct((experts, rows, width), BF16),
            jax.ShapeDtypeStruct((experts, rows, FE), BF16),
            jax.ShapeDtypeStruct((experts, rows, 2 * FE), BF16),
        ),
        grid_spec=pltpu.PrefetchScalarGridSpec(
            num_scalar_prefetch=1,
            grid=(experts,),
            in_specs=[ANY] * len(pieces)
            + [
                weight_spec(w_expert.shape, layer_idx, True),
                per_expert(rows, EXT),
                per_expert(rows, 2 * FE),
                once((length, picked)),
            ],
            out_specs=(
                once((length, width + EXT)),
                per_expert(rows, width),
                per_expert(rows, FE),
                per_expert(rows, 2 * FE),
            ),
            scratch_shapes=[
                pltpu.VMEM((length, width), BF16),
                pltpu.VMEM((experts, rows, width), BF16),
                pltpu.VMEM((pairs, picked, width), BF16),
                pltpu.VMEM((pairs, picked, EXT), BF16),
                pltpu.SemaphoreType.DMA((len(pieces),)),
            ],
        ),
        compiler_params=pltpu.CompilerParams(dimension_semantics=("arbitrary",), **PARAMS),
        cost_estimate=pl.CostEstimate(
            flops=2 * experts * rows * width * 3 * FE,
            bytes_accessed=experts * (width * 3 * FE * 2 + rows * width * 9) + length * width * 4,
            transcendentals=experts * rows * FE,
        ),
        name="moe_bwd",
    )(first, *pieces, w_expert, gates, pair_values, pick)


def pick_rows(token_pieces, grad_pieces, w_expert, first):
    experts, length, rows = sizes(w_expert, grad_pieces)
    width = w_expert.shape[2]
    count = len(token_pieces)
    return pl.pallas_call(
        functools.partial(pick_kernel, experts, count),
        out_shape=(
            jax.ShapeDtypeStruct((experts, rows, width), BF16),
            jax.ShapeDtypeStruct((experts, rows, width), BF16),
        ),
        grid_spec=pltpu.PrefetchScalarGridSpec(
            num_scalar_prefetch=1,
            grid=(1,),
            in_specs=[ANY] * (2 * count),
            out_specs=(once((experts, rows, width)), once((experts, rows, width))),
            scratch_shapes=[
                pltpu.VMEM((length, width + EXT), BF16),
                pltpu.VMEM((length, width), BF16),
                pltpu.SemaphoreType.DMA((count,)),
                pltpu.SemaphoreType.DMA((count,)),
            ],
        ),
        compiler_params=pltpu.CompilerParams(dimension_semantics=("arbitrary",), **PARAMS),
        cost_estimate=pl.CostEstimate(
            flops=4 * length * experts * 2 * CAP * width,
            bytes_accessed=length * width * 4 + experts * rows * width * 4,
            transcendentals=0,
        ),
        name="pick_rows",
    )(first, *token_pieces, *grad_pieces)


def expert_grads(x_rows, dy_rows, hid_own, dgu_own, w_expert, layer_idx, before):
    streams = len(x_rows)
    experts, rows, width = x_rows[0].shape
    depth = min(2, experts)
    operands = [*x_rows, *dy_rows, hid_own, dgu_own, w_expert]
    in_specs = [ANY] * (2 * streams + 2) + [weight_spec(w_expert.shape, layer_idx, False)]
    aliases = {}
    if before is not None:
        aliases = {len(operands): 0}
        operands.append(before)
        in_specs.append(ANY)
    return pl.pallas_call(
        functools.partial(expert_grad_kernel, streams, before is not None),
        out_shape=jax.ShapeDtypeStruct(w_expert.shape, F32),
        grid=(experts,),
        in_specs=in_specs,
        out_specs=weight_spec(w_expert.shape, layer_idx, False),
        scratch_shapes=[
            pltpu.VMEM((depth, streams * rows, width), BF16),
            pltpu.VMEM((depth, streams * rows, width), BF16),
            pltpu.VMEM((depth, streams * rows, FE), BF16),
            pltpu.VMEM((depth, streams * rows, 2 * FE), BF16),
            pltpu.SemaphoreType.DMA((depth, 2 * streams + 2)),
        ],
        input_output_aliases=aliases,
        compiler_params=pltpu.CompilerParams(dimension_semantics=("arbitrary",), **PARAMS),
        cost_estimate=pl.CostEstimate(
            flops=2 * experts * rows * width * 3 * FE * (2 * streams - 1),
            bytes_accessed=experts * (width * 3 * FE * 6 + streams * rows * width * 4),
            transcendentals=experts * rows * FE * (streams - 1),
        ),
        name="expert_grads",
    )(*operands)


def norm_scale(values):
    return lax.rsqrt(jnp.mean(values * values, axis=-1, keepdims=True) + epsilon)


def angles(positions, head_width):
    frequency = 10000.0 ** (-jnp.arange(0, head_width, 2).astype(jnp.float32) / head_width)
    turned = positions[:, None] * frequency[None, :]
    return (jnp.cos(turned)[:, None, :], jnp.sin(turned)[:, None, :])


def rotate(values, cosine, sine_vals):
    half_width = values.shape[-1] // 2
    first_half = values[..., :half_width]
    second_half = values[..., half_width:]
    return jnp.concatenate(
        [
            first_half * cosine - second_half * sine_vals,
            second_half * cosine + first_half * sine_vals,
        ],
        axis=-1,
    )


def unrotate(values, cosine, sine_vals):
    return rotate(values, cosine, -sine_vals)


def doc_positions(doc_row):
    length = doc_row.shape[0]
    index_row = jnp.arange(length, dtype=jnp.int32)
    previous = jnp.concatenate([jnp.full((1,), -1, jnp.int32), doc_row[:-1]])
    starts = lax.cummax(jnp.where(doc_row != previous, index_row, 0), axis=0)
    return (index_row, (index_row - starts).astype(jnp.float32))


def slot_codes(mask):
    tokens = mask.shape[0]
    before = jnp.tril(jnp.ones((tokens, tokens), F32), -1)
    rank = jnp.dot(before, mask, preferred_element_type=F32)
    return jnp.where(mask > 0, rank, -100.0)


def local(x_in, doc_ids, routes, gain_attn, w_qkv, w_out, gain_moe, w_router, w_expert, cotangent):
    ctx_size = lax.axis_size("ctx")
    ctx_rank = lax.axis_index("ctx")
    local_tokens = x_in.shape[1]
    model_width = x_in.shape[2]
    length = local_tokens * ctx_size
    layer_count = w_qkv.shape[0]
    expert_count = w_router.shape[2]
    experts_here = w_expert.shape[1]
    query_width = HEADS * HD
    key_width = KVH * HD
    group_size = HEADS // KVH
    score_scale = 1.0 / math.sqrt(HD)
    first = (ctx_rank * experts_here).astype(jnp.int32).reshape(1)
    doc_row = doc_ids[0]
    index_row, positions = doc_positions(doc_row)
    offset = ctx_rank * local_tokens
    query_index = offset + jnp.arange(local_tokens, dtype=jnp.int32)
    query_doc = lax.dynamic_slice_in_dim(doc_row, offset, local_tokens)
    cosine, sine_vals = angles(lax.dynamic_slice_in_dim(positions, offset, local_tokens), HD)
    key_block = min(512, length)
    key_blocks = length // key_block
    block_index = index_row.reshape(key_blocks, key_block)
    block_doc = doc_row.reshape(key_blocks, key_block)

    def visible_mask(index_piece, doc_piece):
        return (
            (index_piece[None, :] <= query_index[:, None])
            & (doc_piece[None, :] == query_doc[:, None])
        )[:, None, None, :]

    def block_needed(index_piece, doc_piece):
        return (
            (index_piece[0] <= query_index[-1])
            & (doc_piece[-1] >= query_doc[0])
            & (doc_piece[0] <= query_doc[-1])
        )

    gains = lax.all_gather(
        jnp.concatenate([gain_attn, gain_moe], axis=0), "ctx", axis=1, tiled=True
    ).astype(F32)
    weights = []
    for layer_idx in range(layer_count):
        qkv_full = lax.all_gather(w_qkv[layer_idx], "ctx", axis=0, tiled=True)
        out_full = lax.all_gather(
            jnp.concatenate([w_out[layer_idx], w_router[layer_idx]], axis=1),
            "ctx",
            axis=0,
            tiled=True,
        )
        weights.append(
            (
                gains[layer_idx][None],
                qkv_full,
                out_full[:, :model_width],
                gains[layer_count + layer_idx][None],
                out_full[:, model_width:],
            )
        )

    residual = x_in[0].astype(jnp.float32)
    layer_store = []
    for layer_idx in range(layer_count):
        gain_one, qkv_weight, out_weight, gain_two, router_weight = weights[layer_idx]
        scale_one = norm_scale(residual)
        attn_in = (residual * scale_one * gain_one).astype(jnp.bfloat16)
        projected = jnp.dot(attn_in, qkv_weight, preferred_element_type=jnp.float32)
        queries = rotate(
            projected[:, :query_width].reshape(local_tokens, HEADS, HD), cosine, sine_vals
        ).astype(jnp.bfloat16)
        keys_local = rotate(
            projected[:, query_width : query_width + key_width].reshape(local_tokens, KVH, HD),
            cosine,
            sine_vals,
        ).astype(jnp.bfloat16)
        pair_local = jnp.concatenate(
            [
                keys_local.reshape(local_tokens, key_width),
                projected[:, query_width + key_width :].astype(jnp.bfloat16),
            ],
            axis=1,
        )
        pair_all = lax.all_gather(pair_local, "ctx", axis=0, tiled=True)
        query_four = queries.reshape(local_tokens, KVH, group_size, HD)

        def forward_block(state_pair, block_piece):
            pair_block, index_piece, doc_piece = block_piece

            def add_block(state_in):
                totals, denominator = state_in
                scores = (
                    jnp.einsum(
                        "tgrd,sgd->tgrs",
                        query_four,
                        pair_block[:, 0],
                        preferred_element_type=jnp.float32,
                    )
                    * score_scale
                )
                weights_exp = jnp.where(visible_mask(index_piece, doc_piece), jnp.exp(scores), 0.0)
                denominator = denominator + jnp.sum(weights_exp, axis=-1)
                totals = totals + jnp.einsum(
                    "tgrs,sgd->tgrd",
                    weights_exp.astype(jnp.bfloat16),
                    pair_block[:, 1],
                    preferred_element_type=jnp.float32,
                )
                return (totals, denominator)

            return (
                lax.cond(
                    block_needed(index_piece, doc_piece),
                    add_block,
                    lambda state_in: state_in,
                    state_pair,
                ),
                None,
            )

        init_carry = (
            jnp.zeros((local_tokens, KVH, group_size, HD), jnp.float32),
            jnp.zeros((local_tokens, KVH, group_size), jnp.float32),
        )
        (totals, denominator), unused = lax.scan(
            forward_block,
            init_carry,
            (pair_all.reshape(key_blocks, key_block, 2, KVH, HD), block_index, block_doc),
        )
        heads_out = (
            (totals / denominator[..., None])
            .astype(jnp.bfloat16)
            .reshape(local_tokens, query_width)
        )
        attn_out = jnp.dot(heads_out, out_weight, preferred_element_type=jnp.float32)
        mid_stream = residual + attn_out
        scale_two = norm_scale(mid_stream)
        moe_in = (mid_stream * scale_two * gain_two).astype(jnp.bfloat16)
        logits = jnp.dot(moe_in, router_weight, preferred_element_type=jnp.float32)
        route_rows = routes[layer_idx, 0]
        mask = jnp.sum(
            (route_rows[..., None] == jnp.arange(expert_count, dtype=jnp.int32)).astype(F32), axis=1
        )
        gate_dense = jax.nn.softmax(jnp.where(mask > 0, logits, -jnp.inf), axis=-1)
        gate_high = gate_dense.astype(BF16)
        gate_low = (gate_dense - gate_high.astype(F32)).astype(BF16)
        ext = jnp.concatenate(
            [
                gate_high,
                gate_low,
                slot_codes(mask).astype(BF16),
                jnp.zeros((local_tokens, EXT - 3 * expert_count), BF16),
            ],
            axis=1,
        )
        near, far = gather_ctx(jnp.concatenate([moe_in, ext], axis=1))
        others = other_streams(near, far)
        partial, x_rows, gate_rows, pair_values, pick = moe_fwd(
            near + far, w_expert, layer_idx, first
        )
        layer_store.append(
            (
                residual,
                scale_one,
                attn_in,
                query_four,
                pair_all,
                totals,
                denominator,
                heads_out,
                mid_stream,
                scale_two,
                moe_in,
                gate_dense,
                others,
                x_rows,
                gate_rows,
                pair_values,
                pick,
            )
        )
        residual = mid_stream + sum(reduce_ctx(partial))
    out_stream = residual.astype(jnp.bfloat16)[None]
    grad_stream = cotangent[0].astype(jnp.float32)
    grad_low = cotangent[0]
    layer_grads = []
    expert_sum = None
    for layer_idx in reversed(range(layer_count)):
        gain_one, qkv_weight, out_weight, gain_two, router_weight = weights[layer_idx]
        (
            layer_input,
            scale_one,
            attn_in,
            query_four,
            pair_all,
            totals,
            denominator,
            heads_out,
            mid_stream,
            scale_two,
            moe_in,
            gate_dense,
            others,
            x_rows,
            gate_rows,
            pair_values,
            pick,
        ) = layer_store[layer_idx]
        near, far = gather_ctx(grad_low)
        other_grads = other_streams(near, far)
        partial, dy_rows, hid_rows, dgu_rows = moe_bwd(
            near + far, w_expert, layer_idx, first, gate_rows, pair_values, pick
        )
        moved = sum(reduce_ctx(partial))
        picked = [
            pick_rows(tokens, grads, w_expert, first)
            for tokens, grads in zip(others, other_grads, strict=True)
        ]
        expert_sum = expert_grads(
            [x_rows] + [pair[0] for pair in picked],
            [dy_rows] + [pair[1] for pair in picked],
            hid_rows,
            dgu_rows,
            w_expert,
            layer_idx,
            expert_sum,
        )
        moe_grad = moved[:, :model_width]
        gate_grad = (
            moved[:, model_width : model_width + expert_count]
            + moved[:, model_width + expert_count : model_width + 2 * expert_count]
        )
        logit_grad = (
            gate_dense * (gate_grad - jnp.sum(gate_dense * gate_grad, axis=-1, keepdims=True))
        ).astype(BF16)
        router_grad = jnp.einsum(
            "td,te->de", moe_in, logit_grad, preferred_element_type=jnp.float32
        )
        moe_grad = moe_grad + jnp.einsum(
            "te,de->td", logit_grad, router_weight, preferred_element_type=jnp.float32
        )
        normed_two = mid_stream * scale_two
        scaled_two = moe_grad * gain_two
        gain_two_grad = jnp.sum(moe_grad * normed_two, axis=0)
        mid_grad = grad_stream + scale_two * (
            scaled_two - normed_two * jnp.mean(scaled_two * normed_two, axis=-1, keepdims=True)
        )
        attn_grad = mid_grad.astype(jnp.bfloat16)
        out_grad = jnp.einsum("tc,td->cd", heads_out, attn_grad, preferred_element_type=jnp.float32)
        heads_grad = jnp.einsum(
            "td,cd->tc", attn_grad, out_weight, preferred_element_type=jnp.float32
        ).reshape(local_tokens, KVH, group_size, HD)
        scaled_heads = (heads_grad / denominator[..., None]).astype(jnp.bfloat16)
        denominator_grad = -jnp.sum(heads_grad * totals, axis=-1) / (denominator * denominator)

        def backward_block(query_grad, block_piece):
            pair_block, index_piece, doc_piece = block_piece

            def grad_block(query_in):
                scores = (
                    jnp.einsum(
                        "tgrd,sgd->tgrs",
                        query_four,
                        pair_block[:, 0],
                        preferred_element_type=jnp.float32,
                    )
                    * score_scale
                )
                weights_exp = jnp.where(visible_mask(index_piece, doc_piece), jnp.exp(scores), 0.0)
                prob_grad = jnp.einsum(
                    "tgrd,sgd->tgrs",
                    scaled_heads,
                    pair_block[:, 1],
                    preferred_element_type=jnp.float32,
                )
                score_grad = (weights_exp * (prob_grad + denominator_grad[..., None])).astype(
                    jnp.bfloat16
                )
                query_out = (
                    query_in
                    + jnp.einsum(
                        "tgrs,sgd->tgrd",
                        score_grad,
                        pair_block[:, 0],
                        preferred_element_type=jnp.float32,
                    )
                    * score_scale
                )
                key_grad = (
                    jnp.einsum(
                        "tgrs,tgrd->sgd", score_grad, query_four, preferred_element_type=jnp.float32
                    )
                    * score_scale
                )
                value_grad = jnp.einsum(
                    "tgrs,tgrd->sgd",
                    weights_exp.astype(jnp.bfloat16),
                    scaled_heads,
                    preferred_element_type=jnp.float32,
                )
                return (query_out, jnp.stack([key_grad, value_grad], axis=1))

            def skip_block(query_in):
                return (query_in, jnp.zeros((key_block, 2, KVH, HD), jnp.float32))

            return lax.cond(
                block_needed(index_piece, doc_piece), grad_block, skip_block, query_grad
            )

        query_grad, key_pairs = lax.scan(
            backward_block,
            jnp.zeros((local_tokens, KVH, group_size, HD), jnp.float32),
            (pair_all.reshape(key_blocks, key_block, 2, KVH, HD), block_index, block_doc),
        )
        pair_grad_local = lax.psum_scatter(
            key_pairs.reshape(length, 2 * key_width).astype(jnp.bfloat16),
            "ctx",
            scatter_dimension=0,
            tiled=True,
        ).astype(jnp.float32)
        query_lin = unrotate(query_grad.reshape(local_tokens, HEADS, HD), cosine, sine_vals)
        key_lin = unrotate(
            pair_grad_local[:, :key_width].reshape(local_tokens, KVH, HD), cosine, sine_vals
        )
        projected_grad = jnp.concatenate(
            [
                query_lin.reshape(local_tokens, query_width),
                key_lin.reshape(local_tokens, key_width),
                pair_grad_local[:, key_width:],
            ],
            axis=1,
        ).astype(jnp.bfloat16)
        qkv_grad = jnp.einsum(
            "tc,tf->cf", attn_in, projected_grad, preferred_element_type=jnp.float32
        )
        attn_in_grad = jnp.einsum(
            "tf,cf->tc", projected_grad, qkv_weight, preferred_element_type=jnp.float32
        )
        normed_one = layer_input * scale_one
        scaled_one = attn_in_grad * gain_one
        gain_one_grad = jnp.sum(attn_in_grad * normed_one, axis=0)
        grad_stream = mid_grad + scale_one * (
            scaled_one - normed_one * jnp.mean(scaled_one * normed_one, axis=-1, keepdims=True)
        )
        grad_low = grad_stream.astype(BF16)
        early = jnp.concatenate([out_grad, router_grad, gain_two_grad[:, None]], axis=1)
        late = jnp.concatenate([qkv_grad, gain_one_grad[:, None]], axis=1)
        summed = []
        for part in (early, late):
            spare = -part.shape[1] % 128
            part = jnp.pad(part.astype(BF16), ((0, 0), (0, spare)))
            shard = lax.psum_scatter(part, "ctx", scatter_dimension=0, tiled=True)
            summed.append(lax.psum(shard, "dp").astype(F32))
        layer_grads.append(
            (
                summed[1][:, 2 * model_width],
                summed[1][:, : 2 * model_width],
                summed[0][:, :model_width],
                summed[0][:, model_width + expert_count],
                summed[0][:, model_width : model_width + expert_count],
            )
        )
    layer_grads = layer_grads[::-1]
    stacked = [
        jnp.stack([layer_grads[layer_idx][member] for layer_idx in range(layer_count)], axis=0)
        for member in range(5)
    ]
    return (out_stream, grad_stream[None], *stacked, expert_sum)


def solution(mesh):
    placed = (
        P("dp", "ctx", None),
        P("dp", None),
        P(None, "dp", "ctx", None),
        P(None, "ctx"),
        P(None, "ctx", None),
        P(None, "ctx", None),
        P(None, "ctx"),
        P(None, "ctx", None),
        P(None, "ctx", None, None),
        P("dp", "ctx", None),
    )
    return jax.shard_map(
        local,
        mesh=mesh,
        in_specs=placed,
        out_specs=(
            P("dp", "ctx", None),
            P("dp", "ctx", None),
            P(None, "ctx"),
            P(None, "ctx", None),
            P(None, "ctx", None),
            P(None, "ctx"),
            P(None, "ctx", None),
            P(None, "ctx", None, None),
        ),
        check_vma=False,
    )
```

time: 2070 us -> 1160 us (0.56)
  waiting for transfers between devices: 1300 us -> 544 us
  Pallas kernels: 0 us -> 206 us
  blocking collectives: 189 us -> 10.3 us
  local copies, waits for them, and re-layouts: 267 us -> 131 us
  starting transfers between devices: 27.9 us -> 127 us
  other arithmetic: 115 us -> 44.6 us
  matrix products: 114 us -> 47.5 us
    psum x1, waiting for transfers between devices: 850 us -> 35.2 us  [local(): summed.append(lax.psum(shard, 'dp').astype(F32))]
    ppermute x0 -> x68, waiting for transfers between devices: none -> 382 us  [the longest x12 270 us: other_streams(): lax.ppermute(mine, 'dp', [(i, (i + k) % streams) for i in range(streams)])]
    pallas_call x0 -> x12, Pallas kernels: none -> 206 us  [the longest x2 84.4 us: expert_grads(): pl.pallas_call(functools.partial(expert_grad_kernel, streams, before is n...]
    reduce_scatter x4 -> x2, waiting for transfers between devices: 135 us -> 0.01 us  [local(): shard = lax.psum_scatter(part, 'ctx', scatter_dimension=0, tiled=True)]
    all_to_all x6 -> x0, waiting for transfers between devices: 127 us -> none  [the longest x2 54.9 us: local(): lax.all_to_all(outgoing, 'ctx', split_axis=0, concat_axis=1, tiled=True)]
    ppermute x0 -> x68, starting transfers between devices: none -> 126 us  [the longest x12 88.7 us: other_streams(): lax.ppermute(mine, 'dp', [(i, (i + k) % streams) for i in range(streams)])]
    unnamed x19 -> x17, waiting for transfers between devices: 154 us -> 50.4 us
    all_to_all x2 -> x0, blocking collectives: 72.1 us -> none  [local(): lax.all_to_all(outgoing_grad, 'ctx', split_axis=0, concat_axis=1, tiled=T...]
  transfers between devices with their start and end apart: 21 -> 81, of which waited for: 15 -> 39; matrix products, arithmetic and copies ran while one was open for 12% -> 9% of each run, Pallas kernels for 0% -> 15%
where the time goes in v1:
time: 1160 us
  waiting for transfers between devices  544 us (47%)
  Pallas kernels  206 us (18%)
  local copies, waits for them, and re-layouts  131 us (11%)
  starting transfers between devices  127 us (11%)
  matrix products  47.5 us (4%)
  other arithmetic  44.6 us (4%)
  loops' own time  31.6 us (3%)
  between operations  16.2 us (1%)
    ppermute x12, waiting for transfers between devices, other_streams(): lax.ppermute(mine, 'dp', [(i, (i + k) % streams) for i in range(streams)])  270 us
    ppermute x12, starting transfers between devices, other_streams(): lax.ppermute(mine, 'dp', [(i, (i + k) % streams) for i in range(streams)])  88.7 us
    pallas_call x2, Pallas kernels, expert_grads(): pl.pallas_call(functools.partial(expert_grad_kernel, streams, before is n...  84.4 us
    ppermute x12, waiting for transfers between devices, gather_ctx(): lax.ppermute(rows, 'ctx', chip_perm(size, 2 * k))  55.9 us
    unnamed x264, local copies, waits for them, and re-layouts  51.2 us
    unnamed x17, waiting for transfers between devices  50.4 us
    pallas_call x6, Pallas kernels, pick_rows(): pl.pallas_call(functools.partial(pick_kernel, experts, count), out_shape=...  47.6 us
    ppermute x12, waiting for transfers between devices, reduce_ctx(): lax.ppermute(low[k * rows:(k + 1) * rows], 'ctx', chip_perm(size, 2 * k))  46.4 us
  transfers between devices with their start and end apart: 81, of which 39 were waited for; matrix products, arithmetic and copies ran while one was open for 9% of the time, Pallas kernels for 15%

profile of v1, /device:TPU:0, one launch (start us, length us, event | category | flops | bytes accessed | tf_op | source)
XLA Modules:
  0.0 1157.9 jit_solution(9633120067611391729)
XLA Ops:
  10.4 10.3 all_gather.21
  22.3 27.7 %all-gather.17.cloned.1.call-done = bf16[1,1024,2048]{2,1,0:T(8,128)(2,1)} async-done(((bf16[1,128,2048]{2,1,0:T(8,128)(2,1)}), bf16[1,1024,2048]{2,1,0:T(8,128)(2,1)}) %all-gather.17.cloned.1.call-update) | async-done | bytes 4194320 | tf_op jit(solution)/shard_map/all_gather | solution.py:661
  50.0 3.0 fusion.80
  60.4 21.8 %all-gather.9.cloned.1.call-done = bf16[1024,1024]{1,0:T(8,128)(2,1)} async-done(((bf16[128,1024]{1,0:T(8,128)(2,1)}), bf16[1024,1024]{1,0:T(8,128)(2,1)}) %all-gather.9.cloned.1.call-update) | async-done | bytes 2097168 | tf_op jit(solution)/shard_map/all_gather | solution.py:700
  82.2 6.3 reshape.559
  88.5 4.5 copy.134
  93.1 13.7 %while.54 = (s32[]{:T(128)}, f32[128,8,2,64]{0,3,2,1:T(8,128)S(1)}, f32[128,8,2]{0,2,1:T(2,128)S(1)}, s32[2,512]{1,0:T(2,128)S(1)}, s32[128]{0:T(128)S(1)}, /*in...) while((s32[]{:T(128)}, f32[128,8,2,64]{0,3,2,1:T(8,128)S(1)}, ...), condition=%wide.region_7.8_spmd, body=%wide.region_3.0_spmd.sunk | while | flops 275054592 | bytes 13088095 | solution.py:741
  106.9 6.8 all-gather.11.cloned.1.call-done
  122.2 9.5 collective-permute-done.2.refs_3_
  131.7 9.1 collective-permute-done.1.refs_2_
  143.2 18.7 %moe_fwd.2 = (bf16[1024,1024]{1,0:T(8,128)(2,1)}, bf16[4,320,1024]{2,1,0:T(8,128)(2,1)}, f32[4,320,128]{2,1,0:T(8,128)}, f32[4,320,1024]{2,1,0:T(8,128)}, bf16[1024,320]{1,0:T(8,128)(2,1)}) custom-call(s32[1]{0:T(128)} %bitcast.105.first_ref, bf16[128,1152]{1,0:T(8,128)(2,1)} %copy-done.30, bf16[128,1152]{1,0:T(8,128)(2,1)} %collective-permute-done.refs_1_, ...), custom_call_target="tpu_custom_call" | custom-call | flops 4026531840 | bytes 24641536 | tf_op jit(solution)/shard_map/moe_fwd/pallas_call | solution.py:423
  170.2 5.7 collective-permute-done.8
  175.8 5.6 collective-permute-done.10
  183.7 3.0 fusion.76
  205.4 18.2 %all-gather.13.cloned.1.call-done = bf16[1024,1024]{1,0:T(8,128)(2,1)} async-done(((bf16[128,1024]{1,0:T(8,128)(2,1)}), bf16[1024,1024]{1,0:T(8,128)(2,1)}) %all-gather.13.cloned.1.call-update) | async-done | bytes 2097168 | tf_op jit(solution)/shard_map/all_gather | solution.py:700
  223.6 6.4 reshape.560
  230.0 5.5 copy.143
  235.5 16.2 %while.55 = (s32[]{:T(128)}, f32[128,8,2,64]{0,3,2,1:T(8,128)S(1)}, f32[128,8,2]{0,2,1:T(2,128)S(1)}, s32[2,512]{1,0:T(2,128)S(1)}, s32[128]{0:T(128)S(1)}, /*in...) while((s32[]{:T(128)}, f32[128,8,2,64]{0,3,2,1:T(8,128)S(1)}, ...), condition=%wide.region_17.18_spmd, body=%wide.region_13.17_spmd.sunk | while | flops 275054592 | bytes 13088095 | solution.py:741
  241.4 4.5 conditional.9
  262.3 2.6 collective-permute-start.12
  268.4 14.6 %collective-permute-done.24.refs_3_ = bf16[128,1024]{1,0:T(8,128)(2,1)S(1)} collective-permute-done((bf16[128,1024]{1,0:T(8,128)(2,1)}, bf16[128,1024]{1,0:T(8,128)(2,1)S(1)}, u32[]{:S(2)}, u32[]{:S(2)}) %collective-permute-start.24) | collective-permute-done | bytes 262176 | tf_op jit(solution)/shard_map/ppermute | solution.py:52
  284.1 4.5 collective-permute-done.23.refs_2_
  290.1 7.1 collective-permute-done.22.refs_1_
  298.5 18.0 %moe_fwd.3 = (bf16[1024,1024]{1,0:T(8,128)(2,1)}, bf16[4,320,1024]{2,1,0:T(8,128)(2,1)}, f32[4,320,128]{2,1,0:T(8,128)}, f32[4,320,1024]{2,1,0:T(8,128)}, bf16[1024,320]{1,0:T(8,128)(2,1)}) custom-call(s32[1]{0:T(128)} %bitcast.105.first_ref, bf16[128,1152]{1,0:T(8,128)(2,1)} %copy-done.32, bf16[128,1152]{1,0:T(8,128)(2,1)} %copy-done.52, ...), custom_call_target="tpu_custom_call" | custom-call | flops 4026531840 | bytes 24641536 | tf_op jit(solution)/shard_map/moe_fwd/pallas_call | solution.py:423
  316.6 18.7 %moe_bwd.2 = (bf16[1024,1152]{1,0:T(8,128)(2,1)}, bf16[4,320,1024]{2,1,0:T(8,128)(2,1)}, bf16[4,320,512]{2,1,0:T(8,128)(2,1)}, bf16[4,320,1024]{2,1,0:T(8,128)(2,1)}) custom-call(s32[1]{0:T(128)} %bitcast.105.first_ref, bf16[128,1024]{1,0:T(8,128)(2,1)} %bitcast.404, bf16[128,1024]{1,0:T(8,128)(2,1)} %collective-permute-done.22.refs_1_, ...), custom_call_target="tpu_custom_call" | custom-call | flops 4026531840 | bytes 28573696 | tf_op jit(solution)/shard_map/moe_bwd/pallas_call | solution.py:467
  350.3 2.8 collective-permute-done.30
  354.4 5.8 collective-permute-done.32
  365.1 6.0 collective-permute-done.21
  377.3 22.1 %while.56 = (s32[]{:T(128)}, f32[128,8,2,64]{0,3,2,1:T(8,128)}, bf16[2,512,2,8,64]{1,4,3,2,0:T(8,128)(2,1)}, s32[2,512]{1,0:T(2,128)S(1)}, s32[128]{0:T(128)S(1)...) while((s32[]{:T(128)}, f32[128,8,2,64]{0,3,2,1:T(8,128)}, ...), condition=%wide.region_28.29_spmd, body=%wide.region_25.28_spmd.sunk | while | flops 680984576 | bytes 35346352 | solution.py:926
  383.2 8.0 conditional.10
  399.5 6.2 copy.195
  405.6 6.5 reshape.551
  413.3 49.6 %reduce-scatter.19.cloned.1.call-done = bf16[128,1024]{1,0:T(8,128)(2,1)} async-done(((bf16[1024,1024]{1,0:T(8,128)(2,1)}), bf16[128,1024]{1,0:T(8,128)(2,1)}) %reduce-scatter.19.cloned.1.call-update) | async-done | bytes 262160
  466.4 4.5 multiply_reduce_fusion.2
  474.7 6.6 collective-permute-done.35.refs_3_
  481.4 4.4 collective-permute-done.34.refs_2_
  488.4 18.6 %moe_bwd.3 = (bf16[1024,1152]{1,0:T(8,128)(2,1)}, bf16[4,320,1024]{2,1,0:T(8,128)(2,1)}, bf16[4,320,512]{2,1,0:T(8,128)(2,1)}, bf16[4,320,1024]{2,1,0:T(8,128)(2,1)}) custom-call(s32[1]{0:T(128)} %bitcast.105.first_ref, bf16[128,1024]{1,0:T(8,128)(2,1)} %copy-done.36, bf16[128,1024]{1,0:T(8,128)(2,1)} %copy-done.60, bf16[128,1024]{1,0:T(8,128)(2,1)} %copy-done.58, ...), custom_call_target="tpu_custom_call" | custom-call | flops 4026531840 | bytes 28573696 | tf_op jit(solution)/shard_map/moe_bwd/pallas_call | solution.py:467
  508.7 2.7 collective-permute-done.40
  517.6 6.7 collective-permute-done.41
  524.2 6.5 collective-permute-done.43
  538.7 18.6 %while.57 = (s32[]{:T(128)}, f32[128,8,2,64]{0,3,2,1:T(8,128)}, bf16[2,512,2,8,64]{1,4,3,2,0:T(8,128)(2,1)}, s32[2,512]{1,0:T(2,128)S(1)}, s32[128]{0:T(128)S(1)...) while((s32[]{:T(128)}, f32[128,8,2,64]{0,3,2,1:T(8,128)}, ...), condition=%wide.region_37.38_spmd, body=%wide.region_34.37_spmd.sunk | while | flops 680984576 | bytes 35346352 | solution.py:926
  544.5 4.8 conditional.11
  557.3 6.2 copy.196
  563.5 6.5 reshape.553
  573.5 2.9 copy.204
  581.5 3.0 copy.203
  593.2 3.4 collective-permute-start.66
  597.7 22.5 %collective-permute-done.66.refs_2_ = bf16[512,1024]{1,0:T(8,128)(2,1)} collective-permute-done((bf16[512,1024]{1,0:T(8,128)(2,1)S(1)}, bf16[512,1024]{1,0:T(8,128)(2,1)}, u32[]{:S(2)}, u32[]{:S(2)}) %collective-permute-start.66) | collective-permute-done | bytes 1048608 | tf_op jit(solution)/shard_map/ppermute | solution.py:80
  620.2 64.4 %collective-permute-done.62.refs_2_ = bf16[512,1024]{1,0:T(8,128)(2,1)} collective-permute-done((bf16[512,1024]{1,0:T(8,128)(2,1)S(1)}, bf16[512,1024]{1,0:T(8,128)(2,1)}, u32[]{:S(2)}, u32[]{:S(2)}) %collective-permute-start.62) | collective-permute-done | bytes 1048608 | tf_op jit(solution)/shard_map/ppermute | solution.py:80
  686.6 4.9 fusion.112
  705.1 20.8 %collective-permute-done.64.refs_0_ = bf16[512,1152]{1,0:T(8,128)(2,1)S(1)} collective-permute-done((bf16[512,1152]{1,0:T(8,128)(2,1)S(1)}, bf16[512,1152]{1,0:T(8,128)(2,1)S(1)}, u32[]{:S(2)}, u32[]{:S(2)}) %collective-permute-start.64) | collective-permute-done | bytes 1179680 | tf_op jit(solution)/shard_map/ppermute | solution.py:80
  725.9 75.8 %collective-permute-done.60.refs_0_ = bf16[512,1152]{1,0:T(8,128)(2,1)S(1)} collective-permute-done((bf16[512,1152]{1,0:T(8,128)(2,1)S(1)}, bf16[512,1152]{1,0:T(8,128)(2,1)S(1)}, u32[]{:S(2)}, u32[]{:S(2)}) %collective-permute-start.60) | collective-permute-done | bytes 1179680 | tf_op jit(solution)/shard_map/ppermute | solution.py:80
  802.2 76.0 %collective-permute-start.44 = (bf16[512,1152]{1,0:T(8,128)(2,1)}, bf16[512,1152]{1,0:T(8,128)(2,1)}, u32[]{:S(2)}, u32[]{:S(2)}) collective-permute-start(bf16[512,1152]{1,0:T(8,128)(2,1)} %pad_maximum_fusion.3), channel_id=1, source_target_pairs={{0,8},{8,16},{16,24},{24,0},{1,9},{9,17},{17,25},{25,1},{2,10},{10... | collective-permute-start | bytes 3538952 | tf_op jit(solution)/shard_map/ppermute | solution.py:80
  878.2 24.4 %collective-permute-done.48.refs_0_ = bf16[512,1152]{1,0:T(8,128)(2,1)S(1)} collective-permute-done((bf16[512,1152]{1,0:T(8,128)(2,1)}, bf16[512,1152]{1,0:T(8,128)(2,1)S(1)}, u32[]{:S(2)}, u32[]{:S(2)}) %collective-permute-start.48) | collective-permute-done | bytes 1179680 | tf_op jit(solution)/shard_map/ppermute | solution.py:80
  908.2 7.9 pick_rows.11
  916.1 7.9 pick_rows.10
  924.0 8.0 pick_rows.9
  932.7 62.0 %collective-permute-done.50.refs_2_ = bf16[512,1024]{1,0:T(8,128)(2,1)} collective-permute-done((bf16[512,1024]{1,0:T(8,128)(2,1)S(1)}, bf16[512,1024]{1,0:T(8,128)(2,1)}, u32[]{:S(2)}, u32[]{:S(2)}) %collective-permute-start.50) | collective-permute-done | bytes 1048608 | tf_op jit(solution)/shard_map/ppermute | solution.py:80
  995.3 42.2 %expert_grads.2.refs_11_ = f32[2,4,1024,1536]{3,2,1,0:T(8,128)} custom-call(bf16[4,320,1024]{2,1,0:T(8,128)(2,1)} %get-tuple-element.508.refs_0_, bf16[4,320,1024]{2,1,0:T(8,128)(2,1)} %get-tuple-element.509.refs_1_, bf16[4,320,1024]{2,1,0:T(8,128)(2,1)} %get-tuple-element.510.refs_2_, bf16[4,320,1024]{2,1,0:T(8,128)(2,1)} %get-tuple-element.511.refs_3_, ...), custom_call_target="tpu_custom_call" | custom-call | flops 28185722880 | bytes 58720256 | tf_op jit(solution)/shard_map/expert_grads/pallas_call | solution.py:552
  1039.4 7.9 pick_rows.8
  1047.3 7.9 pick_rows.7
  1055.2 8.0 pick_rows.6
  1065.1 42.2 %expert_grads.3 = f32[2,4,1024,1536]{3,2,1,0:T(8,128)} custom-call(bf16[4,320,1024]{2,1,0:T(8,128)(2,1)} %get-tuple-element.498.refs_0_, bf16[4,320,1024]{2,1,0:T(8,128)(2,1)} %get-tuple-element.499.refs_1_, bf16[4,320,1024]{2,1,0:T(8,128)(2,1)} %get-tuple-element.500.refs_2_, ...), custom_call_target="tpu_custom_call", output_to_operand_aliasing={{}: (11, {})} | custom-call | flops 28185722880 | bytes 58720256 | tf_op jit(solution)/shard_map/expert_grads/pallas_call | solution.py:552
  1108.4 35.2 %all-reduce.7.cloned.1.call-done = (bf16[128,2176]{1,0:T(8,128)(2,1)}, bf16[128,2176]{1,0:T(8,128)(2,1)}, bf16[128,1152]{0,1:T(8,128)(2,1)}, bf16[128,1152]{0,1:T(8,128)(2,1)}) async-done(((bf16[128,2176]{1,0:T(8,128)(2,1)}, bf16[128,2176]{1,0:T(8,128)(2,1)}, bf16[128,1152]{0,1:T(8,128)(2,1)}, bf16[128,1152]{0,1:T(8,128)(2,1)}), (bf16[128,2176]{1,0:T(8,128)(2,1)}, bf16[128,2176]{1,0:T(8,128)(2,1)}, ...) | async-done | bytes 1703952 | tf_op jit(solution)/shard_map/psum | solution.py:969
  (650 shorter events, 218.2 us)
Async XLA Ops:
  7.2 42.7 %all-gather.17.cloned.1.call-start = ((), (), s32[]{:S(2)}) async-start(), calls=%async_computation.12 | async-start | bytes 4718592 | tf_op jit(solution)/shard_map/all_gather | solution.py:661
  9.6 72.6 %all-gather.9.cloned.1.call-start = ((), (), s32[]{:S(2)}) async-start(), calls=%async_computation.6 | async-start | bytes 2359296 | tf_op jit(solution)/shard_map/all_gather | solution.py:700
  54.1 59.6 %all-gather.11.cloned.1.call-start = ((), (), s32[]{:S(2)}) async-start(), calls=%async_computation.7 | async-start | bytes 2654208 | tf_op jit(solution)/shard_map/all_gather | solution.py:662
  56.4 126.7 %all-gather.19.cloned.1.call-start = ((), (), s32[]{:S(2)}) async-start(), calls=%async_computation.13 | async-start | bytes 4718592 | tf_op jit(solution)/shard_map/all_gather | solution.py:661
  57.0 166.6 %all-gather.13.cloned.1.call-start = ((), (), s32[]{:S(2)}) async-start(), calls=%async_computation.8 | async-start | bytes 2359296 | tf_op jit(solution)/shard_map/all_gather | solution.py:700
  118.6 13.0 %collective-permute-start.2 = (bf16[128,1152]{1,0:T(8,128)(2,1)S(1)}, bf16[128,1152]{1,0:T(8,128)(2,1)S(1)}, u32[]{:S(2)}, u32[]{:S(2)}) collective-permute-start(bf16[128,1152]{1,0:T(8,128)(2,1)S(1)} %concatenate.113.refs_0_), channel_id=1, source_target_pairs={{0,6},{1,7},{2,4},{3,5},{4,2},{5,3},{6,0},{7,1},{8,14},{9,15},{10,... | collective-permute-start | bytes 884744 | tf_op jit(solution)/shard_map/ppermute | solution.py:52
  120.1 20.7 %collective-permute-start.1 = (bf16[128,1152]{1,0:T(8,128)(2,1)S(1)}, bf16[128,1152]{1,0:T(8,128)(2,1)}, u32[]{:S(2)}, u32[]{:S(2)}) collective-permute-start(bf16[128,1152]{1,0:T(8,128)(2,1)S(1)} %concatenate.113.refs_0_), channel_id=1, source_target_pairs={{0,4},{1,5},{2,6},{3,7},{4,0},{5,1},{6,2},{7,3},{8,12},{9,13},{10,... | collective-permute-start | bytes 884744 | tf_op jit(solution)/shard_map/ppermute | solution.py:52
  121.6 19.2 %collective-permute-start = (bf16[128,1152]{1,0:T(8,128)(2,1)S(1)}, bf16[128,1152]{1,0:T(8,128)(2,1)}, u32[]{:S(2)}, u32[]{:S(2)}) collective-permute-start(bf16[128,1152]{1,0:T(8,128)(2,1)S(1)} %concatenate.113.refs_0_), channel_id=1, source_target_pairs={{0,2},{1,3},{2,0},{3,1},{4,6},{5,7},{6,4},{7,5},{8,10},{9,11},{10,... | collective-permute-start | bytes 884744 | tf_op jit(solution)/shard_map/ppermute | solution.py:52
  122.2 19.1 %collective-permute-start.3 = (bf16[128,1152]{1,0:T(8,128)(2,1)S(1)}, bf16[128,1152]{1,0:T(8,128)(2,1)}, u32[]{:S(2)}, u32[]{:S(2)}) collective-permute-start(bf16[128,1152]{1,0:T(8,128)(2,1)S(1)} %concatenate.113.refs_0_), channel_id=1, source_target_pairs={{0,1},{1,0},{2,3},{3,2},{4,5},{5,4},{6,7},{7,6},{8,9},{9,8},{10,11... | collective-permute-start | bytes 884744 | tf_op jit(solution)/shard_map/ppermute | solution.py:53
  168.1 13.3 %collective-permute-start.10 = (bf16[128,1024]{1,0:T(8,128)(2,1)S(1)}, bf16[128,1024]{1,0:T(8,128)(2,1)S(1)}, u32[]{:S(2)}, u32[]{:S(2)}) collective-permute-start(bf16[128,1024]{1,0:T(8,128)(2,1)S(1)} %get-tuple-element.858), channel_id=1, source_target_pairs={{0,6},{1,7},{2,4},{3,5},{4,2},{5,3},{6,0},{7,1},{8,14},{9,15},{10,... | collective-permute-start | bytes 786440 | tf_op jit(solution)/shard_map/ppermute | solution.py:68
  169.4 13.4 %collective-permute-start.9 = (bf16[128,1024]{1,0:T(8,128)(2,1)S(1)}, bf16[128,1024]{1,0:T(8,128)(2,1)S(1)}, u32[]{:S(2)}, u32[]{:S(2)}) collective-permute-start(bf16[128,1024]{1,0:T(8,128)(2,1)S(1)} %get-tuple-element.859), channel_id=1, source_target_pairs={{0,4},{1,5},{2,6},{3,7},{4,0},{5,1},{6,2},{7,3},{8,12},{9,13},{10,... | collective-permute-start | bytes 786440 | tf_op jit(solution)/shard_map/ppermute | solution.py:68
  195.3 59.0 %all-gather.15.cloned.1.call-start = ((), (), s32[]{:S(2)}) async-start(), calls=%async_computation.9 | async-start | bytes 2654208 | tf_op jit(solution)/shard_map/all_gather | solution.py:662
  197.8 265.0 %reduce-scatter.19.cloned.1.call-start = ((), (), s32[]{:S(2)}) async-start(), calls=%async_computation.14 | async-start | bytes 2359296
  260.8 22.2 %collective-permute-start.13 = (bf16[128,1152]{1,0:T(8,128)(2,1)S(1)}, bf16[128,1152]{1,0:T(8,128)(2,1)S(1)}, u32[]{:S(2)}, u32[]{:S(2)}) collective-permute-start(bf16[128,1152]{1,0:T(8,128)(2,1)S(1)} %concatenate.120.refs_0_), channel_id=1, source_target_pairs={{0,6},{1,7},{2,4},{3,5},{4,2},{5,3},{6,0},{7,1},{8,14},{9,15},{10,... | collective-permute-start | bytes 884744 | tf_op jit(solution)/shard_map/ppermute | solution.py:52
  262.3 21.2 %collective-permute-start.12 = (bf16[128,1152]{1,0:T(8,128)(2,1)S(1)}, bf16[128,1152]{1,0:T(8,128)(2,1)S(1)}, u32[]{:S(2)}, u32[]{:S(2)}) collective-permute-start(bf16[128,1152]{1,0:T(8,128)(2,1)S(1)} %concatenate.120.refs_0_), channel_id=1, source_target_pairs={{0,4},{1,5},{2,6},{3,7},{4,0},{5,1},{6,2},{7,3},{8,12},{9,13},{10,... | collective-permute-start | bytes 884744 | tf_op jit(solution)/shard_map/ppermute | solution.py:52
  265.0 18.7 %collective-permute-start.11 = (bf16[128,1152]{1,0:T(8,128)(2,1)S(1)}, bf16[128,1152]{1,0:T(8,128)(2,1)S(1)}, u32[]{:S(2)}, u32[]{:S(2)}) collective-permute-start(bf16[128,1152]{1,0:T(8,128)(2,1)S(1)} %concatenate.120.refs_0_), channel_id=1, source_target_pairs={{0,2},{1,3},{2,0},{3,1},{4,6},{5,7},{6,4},{7,5},{8,10},{9,11},{10,... | collective-permute-start | bytes 884744 | tf_op jit(solution)/shard_map/ppermute | solution.py:52
  266.3 16.7 %collective-permute-start.24 = (bf16[128,1024]{1,0:T(8,128)(2,1)}, bf16[128,1024]{1,0:T(8,128)(2,1)S(1)}, u32[]{:S(2)}, u32[]{:S(2)}) collective-permute-start(bf16[128,1024]{1,0:T(8,128)(2,1)} %bitcast.400), channel_id=1, source_target_pairs={{0,6},{1,7},{2,4},{3,5},{4,2},{5,3},{6,0},{7,1},{8,14},{9,15},{10,... | collective-permute-start | bytes 786440 | tf_op jit(solution)/shard_map/ppermute | solution.py:52
  267.8 20.8 %collective-permute-start.23 = (bf16[128,1024]{1,0:T(8,128)(2,1)}, bf16[128,1024]{1,0:T(8,128)(2,1)}, u32[]{:S(2)}, u32[]{:S(2)}) collective-permute-start(bf16[128,1024]{1,0:T(8,128)(2,1)} %bitcast.401), channel_id=1, source_target_pairs={{0,4},{1,5},{2,6},{3,7},{4,0},{5,1},{6,2},{7,3},{8,12},{9,13},{10,... | collective-permute-start | bytes 786440 | tf_op jit(solution)/shard_map/ppermute | solution.py:52
  283.0 14.1 %collective-permute-start.14 = (bf16[128,1152]{1,0:T(8,128)(2,1)S(1)}, bf16[128,1152]{1,0:T(8,128)(2,1)S(1)}, u32[]{:S(2)}, u32[]{:S(2)}) collective-permute-start(bf16[128,1152]{1,0:T(8,128)(2,1)S(1)} %concatenate.120.refs_0_), channel_id=1, source_target_pairs={{0,1},{1,0},{2,3},{3,2},{4,5},{5,4},{6,7},{7,6},{8,9},{9,8},{10,11... | collective-permute-start | bytes 884744 | tf_op jit(solution)/shard_map/ppermute | solution.py:53
  283.0 14.6 %collective-permute-start.17 = (bf16[128,1152]{1,0:T(8,128)(2,1)S(1)}, bf16[128,1152]{1,0:T(8,128)(2,1)S(1)}, u32[]{:S(2)}, u32[]{:S(2)}) collective-permute-start(bf16[128,1152]{1,0:T(8,128)(2,1)S(1)} %collective-permute-done.13.refs_3_), channel_id=1, source_target_pairs={{0,1},{1,0},{2,3},{3,2},{4,5},{5,4},{6,7},{7,6},{8,9},{9,8},{10,11... | collective-permute-start | bytes 884744 | tf_op jit(solution)/shard_map/ppermute | solution.py:53
  283.6 14.3 %collective-permute-start.16 = (bf16[128,1152]{1,0:T(8,128)(2,1)S(1)}, bf16[128,1152]{1,0:T(8,128)(2,1)S(1)}, u32[]{:S(2)}, u32[]{:S(2)}) collective-permute-start(bf16[128,1152]{1,0:T(8,128)(2,1)S(1)} %collective-permute-done.12.refs_2_), channel_id=1, source_target_pairs={{0,1},{1,0},{2,3},{3,2},{4,5},{5,4},{6,7},{7,6},{8,9},{9,8},{10,11... | collective-permute-start | bytes 884744 | tf_op jit(solution)/shard_map/ppermute | solution.py:53
  283.6 14.9 %collective-permute-start.15 = (bf16[128,1152]{1,0:T(8,128)(2,1)S(1)}, bf16[128,1152]{1,0:T(8,128)(2,1)}, u32[]{:S(2)}, u32[]{:S(2)}) collective-permute-start(bf16[128,1152]{1,0:T(8,128)(2,1)S(1)} %collective-permute-done.11.refs_1_), channel_id=1, source_target_pairs={{0,1},{1,0},{2,3},{3,2},{4,5},{5,4},{6,7},{7,6},{8,9},{9,8},{10,11... | collective-permute-start | bytes 884744 | tf_op jit(solution)/shard_map/ppermute | solution.py:53
  297.1 19.4 %collective-permute-start.25 = (bf16[128,1024]{1,0:T(8,128)(2,1)}, bf16[128,1024]{1,0:T(8,128)(2,1)}, u32[]{:S(2)}, u32[]{:S(2)}) collective-permute-start(bf16[128,1024]{1,0:T(8,128)(2,1)} %bitcast.403), channel_id=1, source_target_pairs={{0,1},{1,0},{2,3},{3,2},{4,5},{5,4},{6,7},{7,6},{8,9},{9,8},{10,11... | collective-permute-start | bytes 786440 | tf_op jit(solution)/shard_map/ppermute | solution.py:53
  297.2 19.4 %collective-permute-start.28 = (bf16[128,1024]{1,0:T(8,128)(2,1)S(1)}, bf16[128,1024]{1,0:T(8,128)(2,1)}, u32[]{:S(2)}, u32[]{:S(2)}) collective-permute-start(bf16[128,1024]{1,0:T(8,128)(2,1)S(1)} %collective-permute-done.24.refs_3_), channel_id=1, source_target_pairs={{0,1},{1,0},{2,3},{3,2},{4,5},{5,4},{6,7},{7,6},{8,9},{9,8},{10,11... | collective-permute-start | bytes 786440 | tf_op jit(solution)/shard_map/ppermute | solution.py:53
  297.7 18.9 %collective-permute-start.27 = (bf16[128,1024]{1,0:T(8,128)(2,1)}, bf16[128,1024]{1,0:T(8,128)(2,1)}, u32[]{:S(2)}, u32[]{:S(2)}) collective-permute-start(bf16[128,1024]{1,0:T(8,128)(2,1)} %collective-permute-done.23.refs_2_), channel_id=1, source_target_pairs={{0,1},{1,0},{2,3},{3,2},{4,5},{5,4},{6,7},{7,6},{8,9},{9,8},{10,11... | collective-permute-start | bytes 786440 | tf_op jit(solution)/shard_map/ppermute | solution.py:53
  297.8 18.8 %collective-permute-start.26 = (bf16[128,1024]{1,0:T(8,128)(2,1)}, bf16[128,1024]{1,0:T(8,128)(2,1)}, u32[]{:S(2)}, u32[]{:S(2)}) collective-permute-start(bf16[128,1024]{1,0:T(8,128)(2,1)} %collective-permute-done.22.refs_1_), channel_id=1, source_target_pairs={{0,1},{1,0},{2,3},{3,2},{4,5},{5,4},{6,7},{7,6},{8,9},{9,8},{10,11... | collective-permute-start | bytes 786440 | tf_op jit(solution)/shard_map/ppermute | solution.py:53
  344.7 15.5 %collective-permute-start.32 = (bf16[128,1152]{1,0:T(8,128)(2,1)S(1)}, bf16[128,1152]{1,0:T(8,128)(2,1)S(1)}, u32[]{:S(2)}, u32[]{:S(2)}) collective-permute-start(bf16[128,1152]{1,0:T(8,128)(2,1)S(1)} %get-tuple-element.850), channel_id=1, source_target_pairs={{0,6},{1,7},{2,4},{3,5},{4,2},{5,3},{6,0},{7,1},{8,14},{9,15},{10,... | collective-permute-start | bytes 884744 | tf_op jit(solution)/shard_map/ppermute | solution.py:68
  346.1 16.2 %collective-permute-start.31 = (bf16[128,1152]{1,0:T(8,128)(2,1)S(1)}, bf16[128,1152]{1,0:T(8,128)(2,1)S(1)}, u32[]{:S(2)}, u32[]{:S(2)}) collective-permute-start(bf16[128,1152]{1,0:T(8,128)(2,1)S(1)} %get-tuple-element.851), channel_id=1, source_target_pairs={{0,4},{1,5},{2,6},{3,7},{4,0},{5,1},{6,2},{7,3},{8,12},{9,13},{10,... | collective-permute-start | bytes 884744 | tf_op jit(solution)/shard_map/ppermute | solution.py:68
  347.4 17.7 %collective-permute-start.19 = (bf16[128,1024]{1,0:T(8,128)(2,1)S(1)}, bf16[128,1024]{1,0:T(8,128)(2,1)S(1)}, u32[]{:S(2)}, u32[]{:S(2)}) collective-permute-start(bf16[128,1024]{1,0:T(8,128)(2,1)S(1)} %get-tuple-element.852), channel_id=1, source_target_pairs={{0,2},{1,3},{2,0},{3,1},{4,6},{5,7},{6,4},{7,5},{8,10},{9,11},{10,... | collective-permute-start | bytes 786440 | tf_op jit(solution)/shard_map/ppermute | solution.py:68
  348.9 22.1 %collective-permute-start.21 = (bf16[128,1024]{1,0:T(8,128)(2,1)S(1)}, bf16[128,1024]{1,0:T(8,128)(2,1)S(1)}, u32[]{:S(2)}, u32[]{:S(2)}) collective-permute-start(bf16[128,1024]{1,0:T(8,128)(2,1)S(1)} %get-tuple-element.853), channel_id=1, source_target_pairs={{0,6},{1,7},{2,4},{3,5},{4,2},{5,3},{6,0},{7,1},{8,14},{9,15},{10,... | collective-permute-start | bytes 786440 | tf_op jit(solution)/shard_map/ppermute | solution.py:68
  353.1 19.3 %collective-permute-start.20 = (bf16[128,1024]{1,0:T(8,128)(2,1)S(1)}, bf16[128,1024]{1,0:T(8,128)(2,1)S(1)}, u32[]{:S(2)}, u32[]{:S(2)}) collective-permute-start(bf16[128,1024]{1,0:T(8,128)(2,1)S(1)} %get-tuple-element.854), channel_id=1, source_target_pairs={{0,4},{1,5},{2,6},{3,7},{4,0},{5,1},{6,2},{7,3},{8,12},{9,13},{10,... | collective-permute-start | bytes 786440 | tf_op jit(solution)/shard_map/ppermute | solution.py:68
  412.2 273.1 %reduce-scatter.21.cloned.1.call-start = ((), (), s32[]{:S(2)}) async-start(), calls=%async_computation.15 | async-start | bytes 2359296
  472.7 13.1 %collective-permute-start.34 = (bf16[128,1024]{1,0:T(8,128)(2,1)S(1)}, bf16[128,1024]{1,0:T(8,128)(2,1)S(1)}, u32[]{:S(2)}, u32[]{:S(2)}) collective-permute-start(bf16[128,1024]{1,0:T(8,128)(2,1)S(1)} %get-tuple-element.802.refs_0_), channel_id=1, source_target_pairs={{0,4},{1,5},{2,6},{3,7},{4,0},{5,1},{6,2},{7,3},{8,12},{9,13},{10,... | collective-permute-start | bytes 786440 | tf_op jit(solution)/shard_map/ppermute | solution.py:52
  515.5 15.2 %collective-permute-start.43 = (bf16[128,1152]{1,0:T(8,128)(2,1)}, bf16[128,1152]{1,0:T(8,128)(2,1)}, u32[]{:S(2)}, u32[]{:S(2)}) collective-permute-start(bf16[128,1152]{1,0:T(8,128)(2,1)} %get-tuple-element.847), channel_id=1, source_target_pairs={{0,6},{1,7},{2,4},{3,5},{4,2},{5,3},{6,0},{7,1},{8,14},{9,15},{10,... | collective-permute-start | bytes 884744 | tf_op jit(solution)/shard_map/ppermute | solution.py:68
  516.9 15.1 %collective-permute-start.42 = (bf16[128,1152]{1,0:T(8,128)(2,1)}, bf16[128,1152]{1,0:T(8,128)(2,1)}, u32[]{:S(2)}, u32[]{:S(2)}) collective-permute-start(bf16[128,1152]{1,0:T(8,128)(2,1)} %get-tuple-element.848), channel_id=1, source_target_pairs={{0,4},{1,5},{2,6},{3,7},{4,0},{5,1},{6,2},{7,3},{8,12},{9,13},{10,... | collective-permute-start | bytes 884744 | tf_op jit(solution)/shard_map/ppermute | solution.py:68
  570.1 467.4 %reduce-scatter.25.cloned.1.call-start = ((), (), s32[]{:S(2)}) async-start(), calls=%async_computation.17 | async-start | bytes 2654208
  578.0 485.2 %reduce-scatter.23.cloned.1.call-start = ((), (), s32[]{:S(2)}) async-start(), calls=%async_computation.16 | async-start | bytes 2654208
  586.2 478.9 %reduce-scatter.17.cloned.1.call-start = ((), (), s32[]{:S(2)}) async-start(), calls=%async_computation.11 | async-start | bytes 5013504 | tf_op jit(solution)/shard_map/reduce_scatter | solution.py:968
  591.1 474.0 %reduce-scatter.15.cloned.1.call-start = ((), (), s32[]{:S(2)}) async-start(), calls=%async_computation.10 | async-start | bytes 5013504 | tf_op jit(solution)/shard_map/reduce_scatter | solution.py:968
  593.2 27.0 %collective-permute-start.66 = (bf16[512,1024]{1,0:T(8,128)(2,1)S(1)}, bf16[512,1024]{1,0:T(8,128)(2,1)}, u32[]{:S(2)}, u32[]{:S(2)}) collective-permute-start(bf16[512,1024]{1,0:T(8,128)(2,1)S(1)} %pad_maximum_fusion.7), channel_id=1, source_target_pairs={{0,24},{8,0},{16,8},{24,16},{1,25},{9,1},{17,9},{25,17},{2,26},{10... | collective-permute-start | bytes 3145736 | tf_op jit(solution)/shard_map/ppermute | solution.py:80
  596.6 88.0 %collective-permute-start.62 = (bf16[512,1024]{1,0:T(8,128)(2,1)S(1)}, bf16[512,1024]{1,0:T(8,128)(2,1)}, u32[]{:S(2)}, u32[]{:S(2)}) collective-permute-start(bf16[512,1024]{1,0:T(8,128)(2,1)S(1)} %pad_maximum_fusion.7), channel_id=1, source_target_pairs={{0,16},{8,24},{16,0},{24,8},{1,17},{9,25},{17,1},{25,9},{2,18},{10... | collective-permute-start | bytes 3145736 | tf_op jit(solution)/shard_map/ppermute | solution.py:80
  596.6 88.0 %collective-permute-start.58 = (bf16[512,1024]{1,0:T(8,128)(2,1)S(1)}, bf16[512,1024]{1,0:T(8,128)(2,1)}, u32[]{:S(2)}, u32[]{:S(2)}) collective-permute-start(bf16[512,1024]{1,0:T(8,128)(2,1)S(1)} %pad_maximum_fusion.7), channel_id=1, source_target_pairs={{0,8},{8,16},{16,24},{24,0},{1,9},{9,17},{17,25},{25,1},{2,10},{10... | collective-permute-start | bytes 3145736 | tf_op jit(solution)/shard_map/ppermute | solution.py:80
  620.2 78.9 %collective-permute-start.67 = (bf16[512,1024]{1,0:T(8,128)(2,1)}, bf16[512,1024]{1,0:T(8,128)(2,1)}, u32[]{:S(2)}, u32[]{:S(2)}) collective-permute-start(bf16[512,1024]{1,0:T(8,128)(2,1)} %collective-permute-done.66.refs_2_), channel_id=1, source_target_pairs={{0,1},{1,0},{2,3},{3,2},{4,5},{5,4},{6,7},{7,6},{8,9},{9,8},{10,11... | collective-permute-start | bytes 3145736 | tf_op jit(solution)/shard_map/ppermute | solution.py:82
  684.6 18.6 %collective-permute-start.63 = (bf16[512,1024]{1,0:T(8,128)(2,1)}, bf16[512,1024]{1,0:T(8,128)(2,1)}, u32[]{:S(2)}, u32[]{:S(2)}) collective-permute-start(bf16[512,1024]{1,0:T(8,128)(2,1)} %collective-permute-done.62.refs_2_), channel_id=1, source_target_pairs={{0,1},{1,0},{2,3},{3,2},{4,5},{5,4},{6,7},{7,6},{8,9},{9,8},{10,11... | collective-permute-start | bytes 3145736 | tf_op jit(solution)/shard_map/ppermute | solution.py:82
  684.6 20.5 %collective-permute-start.59 = (bf16[512,1024]{1,0:T(8,128)(2,1)}, bf16[512,1024]{1,0:T(8,128)(2,1)}, u32[]{:S(2)}, u32[]{:S(2)}) collective-permute-start(bf16[512,1024]{1,0:T(8,128)(2,1)} %collective-permute-done.58.refs_2_), channel_id=1, source_target_pairs={{0,1},{1,0},{2,3},{3,2},{4,5},{5,4},{6,7},{7,6},{8,9},{9,8},{10,11... | collective-permute-start | bytes 3145736 | tf_op jit(solution)/shard_map/ppermute | solution.py:82
  695.5 448.1 %all-reduce.7.cloned.1.call-start = ((), (), s32[]{:S(2)}) async-start(), calls=%async_computation.18 | async-start | bytes 3407872 | tf_op jit(solution)/shard_map/psum | solution.py:969
  696.8 29.1 %collective-permute-start.64 = (bf16[512,1152]{1,0:T(8,128)(2,1)S(1)}, bf16[512,1152]{1,0:T(8,128)(2,1)S(1)}, u32[]{:S(2)}, u32[]{:S(2)}) collective-permute-start(bf16[512,1152]{1,0:T(8,128)(2,1)S(1)} %pad_maximum_fusion.4), channel_id=1, source_target_pairs={{0,24},{8,0},{16,8},{24,16},{1,25},{9,1},{17,9},{25,17},{2,26},{10... | collective-permute-start | bytes 3538952 | tf_op jit(solution)/shard_map/ppermute | solution.py:80
  696.8 104.8 %collective-permute-start.60 = (bf16[512,1152]{1,0:T(8,128)(2,1)S(1)}, bf16[512,1152]{1,0:T(8,128)(2,1)S(1)}, u32[]{:S(2)}, u32[]{:S(2)}) collective-permute-start(bf16[512,1152]{1,0:T(8,128)(2,1)S(1)} %pad_maximum_fusion.4), channel_id=1, source_target_pairs={{0,16},{8,24},{16,0},{24,8},{1,17},{9,25},{17,1},{25,9},{2,18},{10... | collective-permute-start | bytes 3538952 | tf_op jit(solution)/shard_map/ppermute | solution.py:80
  699.1 102.6 %collective-permute-start.56 = (bf16[512,1152]{1,0:T(8,128)(2,1)S(1)}, bf16[512,1152]{1,0:T(8,128)(2,1)S(1)}, u32[]{:S(2)}, u32[]{:S(2)}) collective-permute-start(bf16[512,1152]{1,0:T(8,128)(2,1)S(1)} %pad_maximum_fusion.4), channel_id=1, source_target_pairs={{0,8},{8,16},{16,24},{24,0},{1,9},{9,17},{17,25},{25,1},{2,10},{10... | collective-permute-start | bytes 3538952 | tf_op jit(solution)/shard_map/ppermute | solution.py:80
  703.2 99.0 %collective-permute-start.52 = (bf16[512,1152]{1,0:T(8,128)(2,1)}, bf16[512,1152]{1,0:T(8,128)(2,1)}, u32[]{:S(2)}, u32[]{:S(2)}) collective-permute-start(bf16[512,1152]{1,0:T(8,128)(2,1)} %pad_maximum_fusion.3), channel_id=1, source_target_pairs={{0,24},{8,0},{16,8},{24,16},{1,25},{9,1},{17,9},{25,17},{2,26},{10... | collective-permute-start | bytes 3538952 | tf_op jit(solution)/shard_map/ppermute | solution.py:80
  705.1 197.5 %collective-permute-start.48 = (bf16[512,1152]{1,0:T(8,128)(2,1)}, bf16[512,1152]{1,0:T(8,128)(2,1)S(1)}, u32[]{:S(2)}, u32[]{:S(2)}) collective-permute-start(bf16[512,1152]{1,0:T(8,128)(2,1)} %pad_maximum_fusion.3), channel_id=1, source_target_pairs={{0,16},{8,24},{16,0},{24,8},{1,17},{9,25},{17,1},{25,9},{2,18},{10... | collective-permute-start | bytes 3538952 | tf_op jit(solution)/shard_map/ppermute | solution.py:80
  725.9 177.9 %collective-permute-start.65 = (bf16[512,1152]{1,0:T(8,128)(2,1)S(1)}, bf16[512,1152]{1,0:T(8,128)(2,1)S(1)}, u32[]{:S(2)}, u32[]{:S(2)}) collective-permute-start(bf16[512,1152]{1,0:T(8,128)(2,1)S(1)} %collective-permute-done.64.refs_0_), channel_id=1, source_target_pairs={{0,1},{1,0},{2,3},{3,2},{4,5},{5,4},{6,7},{7,6},{8,9},{9,8},{10,11... | collective-permute-start | bytes 3538952 | tf_op jit(solution)/shard_map/ppermute | solution.py:82
  801.6 102.2 %collective-permute-start.61 = (bf16[512,1152]{1,0:T(8,128)(2,1)S(1)}, bf16[512,1152]{1,0:T(8,128)(2,1)S(1)}, u32[]{:S(2)}, u32[]{:S(2)}) collective-permute-start(bf16[512,1152]{1,0:T(8,128)(2,1)S(1)} %collective-permute-done.60.refs_0_), channel_id=1, source_target_pairs={{0,1},{1,0},{2,3},{3,2},{4,5},{5,4},{6,7},{7,6},{8,9},{9,8},{10,11... | collective-permute-start | bytes 3538952 | tf_op jit(solution)/shard_map/ppermute | solution.py:82
  801.7 102.2 %collective-permute-start.57 = (bf16[512,1152]{1,0:T(8,128)(2,1)S(1)}, bf16[512,1152]{1,0:T(8,128)(2,1)S(1)}, u32[]{:S(2)}, u32[]{:S(2)}) collective-permute-start(bf16[512,1152]{1,0:T(8,128)(2,1)S(1)} %collective-permute-done.56.refs_0_), channel_id=1, source_target_pairs={{0,1},{1,0},{2,3},{3,2},{4,5},{5,4},{6,7},{7,6},{8,9},{9,8},{10,11... | collective-permute-start | bytes 3538952 | tf_op jit(solution)/shard_map/ppermute | solution.py:82
  802.2 129.9 %collective-permute-start.44 = (bf16[512,1152]{1,0:T(8,128)(2,1)}, bf16[512,1152]{1,0:T(8,128)(2,1)}, u32[]{:S(2)}, u32[]{:S(2)}) collective-permute-start(bf16[512,1152]{1,0:T(8,128)(2,1)} %pad_maximum_fusion.3), channel_id=1, source_target_pairs={{0,8},{8,16},{16,24},{24,0},{1,9},{9,17},{17,25},{25,1},{2,10},{10... | collective-permute-start | bytes 3538952 | tf_op jit(solution)/shard_map/ppermute | solution.py:80
  903.6 28.5 %collective-permute-start.53 = (bf16[512,1152]{1,0:T(8,128)(2,1)}, bf16[512,1152]{1,0:T(8,128)(2,1)}, u32[]{:S(2)}, u32[]{:S(2)}) collective-permute-start(bf16[512,1152]{1,0:T(8,128)(2,1)} %collective-permute-done.52.refs_0_), channel_id=1, source_target_pairs={{0,1},{1,0},{2,3},{3,2},{4,5},{5,4},{6,7},{7,6},{8,9},{9,8},{10,11... | collective-permute-start | bytes 3538952 | tf_op jit(solution)/shard_map/ppermute | solution.py:82
  903.7 28.9 %collective-permute-start.54 = (bf16[512,1024]{1,0:T(8,128)(2,1)S(1)}, bf16[512,1024]{1,0:T(8,128)(2,1)}, u32[]{:S(2)}, u32[]{:S(2)}) collective-permute-start(bf16[512,1024]{1,0:T(8,128)(2,1)S(1)} %pad_maximum_fusion.6), channel_id=1, source_target_pairs={{0,24},{8,0},{16,8},{24,16},{1,25},{9,1},{17,9},{25,17},{2,26},{10... | collective-permute-start | bytes 3145736 | tf_op jit(solution)/shard_map/ppermute | solution.py:80
  903.8 90.9 %collective-permute-start.50 = (bf16[512,1024]{1,0:T(8,128)(2,1)S(1)}, bf16[512,1024]{1,0:T(8,128)(2,1)}, u32[]{:S(2)}, u32[]{:S(2)}) collective-permute-start(bf16[512,1024]{1,0:T(8,128)(2,1)S(1)} %pad_maximum_fusion.6), channel_id=1, source_target_pairs={{0,16},{8,24},{16,0},{24,8},{1,17},{9,25},{17,1},{25,9},{2,18},{10... | collective-permute-start | bytes 3145736 | tf_op jit(solution)/shard_map/ppermute | solution.py:80
  906.3 88.5 %collective-permute-start.46 = (bf16[512,1024]{1,0:T(8,128)(2,1)S(1)}, bf16[512,1024]{1,0:T(8,128)(2,1)}, u32[]{:S(2)}, u32[]{:S(2)}) collective-permute-start(bf16[512,1024]{1,0:T(8,128)(2,1)S(1)} %pad_maximum_fusion.6), channel_id=1, source_target_pairs={{0,8},{8,16},{16,24},{24,0},{1,9},{9,17},{17,25},{25,1},{2,10},{10... | collective-permute-start | bytes 3145736 | tf_op jit(solution)/shard_map/ppermute | solution.py:80
  932.1 115.2 %collective-permute-start.49 = (bf16[512,1152]{1,0:T(8,128)(2,1)S(1)}, bf16[512,1152]{1,0:T(8,128)(2,1)}, u32[]{:S(2)}, u32[]{:S(2)}) collective-permute-start(bf16[512,1152]{1,0:T(8,128)(2,1)S(1)} %copy-done.123), channel_id=1, source_target_pairs={{0,1},{1,0},{2,3},{3,2},{4,5},{5,4},{6,7},{7,6},{8,9},{9,8},{10,11... | collective-permute-start | bytes 3538952 | tf_op jit(solution)/shard_map/ppermute | solution.py:82
  932.2 123.0 %collective-permute-start.45 = (bf16[512,1152]{1,0:T(8,128)(2,1)}, bf16[512,1152]{1,0:T(8,128)(2,1)}, u32[]{:S(2)}, u32[]{:S(2)}) collective-permute-start(bf16[512,1152]{1,0:T(8,128)(2,1)} %collective-permute-done.44.refs_0_), channel_id=1, source_target_pairs={{0,1},{1,0},{2,3},{3,2},{4,5},{5,4},{6,7},{7,6},{8,9},{9,8},{10,11... | collective-permute-start | bytes 3538952 | tf_op jit(solution)/shard_map/ppermute | solution.py:82
  932.6 106.7 %collective-permute-start.55 = (bf16[512,1024]{1,0:T(8,128)(2,1)}, bf16[512,1024]{1,0:T(8,128)(2,1)}, u32[]{:S(2)}, u32[]{:S(2)}) collective-permute-start(bf16[512,1024]{1,0:T(8,128)(2,1)} %collective-permute-done.54.refs_2_), channel_id=1, source_target_pairs={{0,1},{1,0},{2,3},{3,2},{4,5},{5,4},{6,7},{7,6},{8,9},{9,8},{10,11... | collective-permute-start | bytes 3145736 | tf_op jit(solution)/shard_map/ppermute | solution.py:82
  994.8 52.5 %collective-permute-start.51 = (bf16[512,1024]{1,0:T(8,128)(2,1)}, bf16[512,1024]{1,0:T(8,128)(2,1)}, u32[]{:S(2)}, u32[]{:S(2)}) collective-permute-start(bf16[512,1024]{1,0:T(8,128)(2,1)} %collective-permute-done.50.refs_2_), channel_id=1, source_target_pairs={{0,1},{1,0},{2,3},{3,2},{4,5},{5,4},{6,7},{7,6},{8,9},{9,8},{10,11... | collective-permute-start | bytes 3145736 | tf_op jit(solution)/shard_map/ppermute | solution.py:82
  994.8 60.4 %collective-permute-start.47 = (bf16[512,1024]{1,0:T(8,128)(2,1)}, bf16[512,1024]{1,0:T(8,128)(2,1)}, u32[]{:S(2)}, u32[]{:S(2)}) collective-permute-start(bf16[512,1024]{1,0:T(8,128)(2,1)} %collective-permute-done.46.refs_2_), channel_id=1, source_target_pairs={{0,1},{1,0},{2,3},{3,2},{4,5},{5,4},{6,7},{7,6},{8,9},{9,8},{10,11... | collective-permute-start | bytes 3145736 | tf_op jit(solution)/shard_map/ppermute | solution.py:82
  (149 other events, 3084.1 us)
Sparse Core Ops, SparseCore 0:
  10.5 39.4 all-gather.16
  54.2 27.8 all-gather.8
  84.6 29.0 all-gather.10
  116.0 44.6 all-gather.18
  195.4 28.0 all-gather.12
  225.3 29.0 all-gather.14
  412.3 50.5 reduce-scatter.18
  570.2 45.9 reduce-scatter.20
  619.6 43.2 reduce-scatter.24
  666.5 42.4 reduce-scatter.22
  712.4 53.0 reduce-scatter.16
  769.2 55.4 reduce-scatter.14
  1065.2 78.3 all-reduce.6

commit v2 on v1

v2 whole, which is shorter than its diff:
```python
import functools
import math

import jax
import jax.numpy as jnp
from jax import lax
from jax.experimental import pallas as pl
from jax.experimental.pallas import tpu as pltpu
from jax.sharding import PartitionSpec as P

HEADS = 16
KVH = 8
HD = 64
TOP = 8
FE = 512
CAP = 40
BLOCK = 128
PAIR = 2 * BLOCK
EXT = 128
ROWS = 320
F32 = jnp.float32
BF16 = jnp.bfloat16

epsilon = 1e-06


def dot_nn(left, right):
    return lax.dot_general(left, right, (((1,), (0,)), ((), ())), preferred_element_type=F32)


def dot_nt(left, right):
    return lax.dot_general(left, right, (((1,), (1,)), ((), ())), preferred_element_type=F32)


def dot_tn(left, right):
    return lax.dot_general(left, right, (((0,), (0,)), ((), ())), preferred_element_type=F32)


def chip_perm(size, mask):
    return [(i, i ^ mask) for i in range(size)]


def hierarchical(size):
    return size == 8


def swap_cores(rows):
    return lax.ppermute(rows, "ctx", chip_perm(lax.axis_size("ctx"), 1))


def gather_chips(rows):
    size = lax.axis_size("ctx")
    if not hierarchical(size):
        return lax.all_gather(rows, "ctx", axis=0, tiled=True)
    pieces = [rows] + [
        lax.ppermute(rows, "ctx", chip_perm(size, 2 * k)) for k in range(1, size // 2)
    ]
    return jnp.concatenate(pieces, axis=0)


def both_cores(near):
    if not hierarchical(lax.axis_size("ctx")):
        return [near]
    return [near, swap_cores(near)]


def gather_ctx(rows):
    return both_cores(gather_chips(rows))


def fold_kernel(near_ref, far_ref, own_ref, *sent):
    rows = own_ref.shape[0]
    own_ref[...] = near_ref[:rows].astype(F32) + far_ref[:rows].astype(F32)
    for k, out_ref in enumerate(sent):
        at = (k + 1) * rows
        total = near_ref[at : at + rows].astype(F32) + far_ref[at : at + rows].astype(F32)
        out_ref[...] = total.astype(BF16)


def reduce_start(halves):
    if len(halves) == 1:
        return halves[0], []
    near, far = halves
    far = swap_cores(far)
    chips = lax.axis_size("ctx") // 2
    rows, width = near.shape[0] // chips, near.shape[1]
    own, *sent = pl.pallas_call(
        fold_kernel,
        out_shape=[jax.ShapeDtypeStruct((rows, width), F32)]
        + [jax.ShapeDtypeStruct((rows, width), BF16)] * (chips - 1),
        compiler_params=pltpu.CompilerParams(**PARAMS),
        cost_estimate=pl.CostEstimate(
            flops=near.size, bytes_accessed=6 * near.size, transcendentals=0
        ),
        name="fold",
    )(near, far)
    return own, sent


def reduce_finish(own, sent):
    if not sent:
        return [lax.psum_scatter(own, "ctx", scatter_dimension=0, tiled=True).astype(F32)]
    size = lax.axis_size("ctx")
    return [own] + [
        lax.ppermute(piece, "ctx", chip_perm(size, 2 * (k + 1))) for k, piece in enumerate(sent)
    ]


def reduce_ctx(halves):
    return reduce_finish(*reduce_start(halves))


def all_streams(rows):
    return lax.all_gather(rows, "dp", axis=0, tiled=True)


def add_across(values, mask):
    streams = lax.axis_size("dp")
    return values.astype(F32) + lax.ppermute(values, "dp", chip_perm(streams, mask)).astype(F32)


def tie(main, *sides):
    out = lax.optimization_barrier((main, *sides))
    return out[0], out[1:]


def total_of(pieces):
    total = pieces[0]
    for piece in pieces[1:]:
        total = total + piece.astype(F32)
    return total


def copy_rows(pieces, target, sems):
    copies = []
    start = 0
    for index, piece in enumerate(pieces):
        rows = piece.shape[0]
        copies.append(
            pltpu.make_async_copy(piece, target.at[pl.ds(start, rows)], sems.at[index])
        )
        start += rows
    for copy in copies:
        copy.start()
    return copies


def copy_blocks(pieces, order_ref, columns, target, sems):
    copies = []
    rows = target.shape[0] // order_ref.shape[0]
    for piece in pieces:
        if columns is not None:
            piece = piece.at[:, pl.ds(columns, target.shape[1])]
        if len(pieces) == 1:
            copies.append(pltpu.make_async_copy(piece, target, sems.at[0]))
            continue
        for start in range(0, piece.shape[0], rows):
            index = len(copies)
            place = pl.multiple_of(order_ref[index] * rows, rows)
            copies.append(
                pltpu.make_async_copy(
                    piece.at[pl.ds(start, rows), :],
                    target.at[pl.ds(place, rows), :],
                    sems.at[index],
                )
            )
    for copy in copies:
        copy.start()
    return copies


def copy_count(pieces, order):
    return 1 if len(pieces) == 1 else order.shape[0]


def pick_matrix(ext, first, experts):
    width = experts * 2 * CAP
    lane = lax.broadcasted_iota(jnp.int32, (PAIR, EXT), 1)
    column = lax.broadcasted_iota(jnp.int32, (PAIR, width), 1)
    late = jnp.where(lax.broadcasted_iota(jnp.int32, (PAIR, 1), 0) >= BLOCK, CAP, 0)
    hit = None
    for e in range(experts):
        code = jnp.sum(jnp.where(lane == 64 + first + e, ext, 0.0), axis=1, keepdims=True)
        code = code.astype(jnp.int32)
        slot = jnp.where(code < 0, -1, code + late + 2 * CAP * e)
        here = column == slot
        hit = here if hit is None else hit | here
    return jnp.where(hit, 1.0, 0.0).astype(BF16)


def gate_lanes(first_expert, rows):
    lane = lax.broadcasted_iota(jnp.int32, (rows, EXT), 1)
    return (lane == first_expert) | (lane == 32 + first_expert)


def moe_fwd_kernel(experts, n_pieces, n_halves, first_ref, *refs):
    pieces = refs[:n_pieces]
    w_ref = refs[n_pieces]
    y_refs = refs[n_pieces + 1 : n_pieces + 1 + n_halves]
    x_ref, gate_ref, gu_ref, pick_ref = refs[n_pieces + 1 + n_halves : n_pieces + 5 + n_halves]
    tokens, rows, gates, outs, hid, sems = refs[n_pieces + 5 + n_halves :]
    e = pl.program_id(0)
    first = first_ref[0]
    pairs = tokens.shape[0] // PAIR
    width = x_ref.shape[2]
    slots = 2 * CAP

    @pl.when(e == 0)
    def _():
        for copy in copy_rows(pieces, tokens, sems):
            copy.wait()

        def gather(p, carry):
            base = pl.multiple_of(p * PAIR, PAIR)
            block = tokens[pl.ds(base, PAIR), :]
            pick = pick_matrix(block[:, width:].astype(F32), first, experts)
            pick_ref[pl.ds(base, PAIR), :] = pick
            found = dot_tn(pick, block)
            at = pl.multiple_of(p * slots, 16)
            for k in range(experts):
                mine = found[k * slots : (k + 1) * slots]
                rows[k, pl.ds(at, slots), :] = mine[:, :width].astype(BF16)
                gate = jnp.sum(
                    jnp.where(gate_lanes(first + k, slots), mine[:, width:], 0.0), axis=1, keepdims=True
                )
                gates[k, pl.ds(at, slots), :] = jnp.broadcast_to(gate, (slots, EXT))
            return carry

        lax.fori_loop(0, pairs, gather, 0)

    x_ref[0] = rows[e]
    gate_ref[0] = gates[e]

    def chunk(r, carry):
        at = pl.multiple_of(r * ROWS, 64)
        block = rows[e, pl.ds(at, ROWS), :]
        for n in range(2):
            gate_part = dot_nn(block, w_ref[0, 0, :, 256 * n : 256 * n + 256])
            up_part = dot_nn(block, w_ref[0, 0, :, FE + 256 * n : FE + 256 * n + 256])
            gu_ref[0, pl.ds(at, ROWS), 256 * n : 256 * n + 256] = gate_part
            gu_ref[0, pl.ds(at, ROWS), FE + 256 * n : FE + 256 * n + 256] = up_part
            hid[:, 256 * n : 256 * n + 256] = (
                gate_part / (1.0 + jnp.exp(-gate_part)) * up_part
            ).astype(BF16)
        gate = gates[e, pl.ds(at, ROWS), 0:1]
        for n in range(width // 256):
            part = dot_nt(hid[...], w_ref[0, 0, 256 * n : 256 * n + 256, 2 * FE :]) * gate
            for q in range(ROWS // slots):
                outs[
                    r * (ROWS // slots) + q,
                    pl.ds(pl.multiple_of(e * slots, 16), slots),
                    256 * n : 256 * n + 256,
                ] = part[q * slots : (q + 1) * slots].astype(BF16)
        return carry

    lax.fori_loop(0, rows.shape[1] // ROWS, chunk, 0)

    @pl.when(e == experts - 1)
    def _():
        for k, y_ref in enumerate(y_refs):
            skip = k * (pairs // n_halves)

            def scatter(p, carry):
                base = pl.multiple_of(p * PAIR, PAIR)
                pick = pick_ref[pl.ds(base + skip * PAIR, PAIR), :]
                y_ref[pl.ds(base, PAIR), :] = dot_nn(pick, outs[p + skip]).astype(BF16)
                return carry

            lax.fori_loop(0, pairs // n_halves, scatter, 0)


def moe_bwd_kernel(experts, n_pieces, n_halves, first_ref, *refs):
    pieces = refs[:n_pieces]
    w_ref, gate_ref, gu_ref, pick_ref = refs[n_pieces : n_pieces + 4]
    d_refs = refs[n_pieces + 4 : n_pieces + 4 + n_halves]
    dy_ref, hid_ref, dgu_ref = refs[n_pieces + 4 + n_halves : n_pieces + 7 + n_halves]
    tokens, rows, outs, dots, sems = refs[n_pieces + 7 + n_halves :]
    e = pl.program_id(0)
    first = first_ref[0]
    pairs = tokens.shape[0] // PAIR
    width = tokens.shape[1]
    slots = 2 * CAP

    @pl.when(e == 0)
    def _():
        for copy in copy_rows(pieces, tokens, sems):
            copy.wait()

        def gather(p, carry):
            base = pl.multiple_of(p * PAIR, PAIR)
            found = dot_tn(pick_ref[pl.ds(base, PAIR), :], tokens[pl.ds(base, PAIR), :])
            at = pl.multiple_of(p * slots, 16)
            for k in range(experts):
                rows[k, pl.ds(at, slots), :] = found[k * slots : (k + 1) * slots].astype(BF16)
            return carry

        lax.fori_loop(0, pairs, gather, 0)

    def chunk(r, carry):
        at = pl.multiple_of(r * ROWS, 64)
        block = rows[e, pl.ds(at, ROWS), :]
        gate = gate_ref[0, pl.ds(at, ROWS), 0:1]
        dy_ref[0, pl.ds(at, ROWS), :] = (block.astype(F32) * gate).astype(BF16)
        total = jnp.zeros((ROWS, 1), F32)
        for n in range(2):
            lanes = slice(256 * n, 256 * n + 256)
            uplanes = slice(FE + 256 * n, FE + 256 * n + 256)
            raw = dot_nn(block, w_ref[0, 0, :, 2 * FE + 256 * n : 2 * FE + 256 * n + 256])
            gate_part = gu_ref[0, pl.ds(at, ROWS), lanes]
            up_part = gu_ref[0, pl.ds(at, ROWS), uplanes]
            sig = 1.0 / (1.0 + jnp.exp(-gate_part))
            silu = gate_part * sig
            hidden = (silu * up_part).astype(BF16)
            hid_ref[0, pl.ds(at, ROWS), lanes] = hidden
            total = total + jnp.sum(raw * hidden.astype(F32), axis=1, keepdims=True)
            dh = raw * gate
            slope = sig * (1.0 + gate_part * (1.0 - sig))
            dgu_ref[0, pl.ds(at, ROWS), lanes] = (dh * up_part * slope).astype(BF16)
            dgu_ref[0, pl.ds(at, ROWS), uplanes] = (dh * silu).astype(BF16)
        high = total.astype(BF16).astype(F32)
        lane = lax.broadcasted_iota(jnp.int32, (ROWS, EXT), 1)
        spread = jnp.where(
            lane == first + e, high, jnp.where(lane == 32 + first + e, total - high, 0.0)
        ).astype(BF16)
        for q in range(ROWS // slots):
            dots[r * (ROWS // slots) + q, pl.ds(pl.multiple_of(e * slots, 16), slots), :] = spread[
                q * slots : (q + 1) * slots
            ]
        for n in range(width // 256):
            part = dot_nt(
                dgu_ref[0, pl.ds(at, ROWS), :], w_ref[0, 0, 256 * n : 256 * n + 256, : 2 * FE]
            )
            for q in range(ROWS // slots):
                outs[
                    r * (ROWS // slots) + q,
                    pl.ds(pl.multiple_of(e * slots, 16), slots),
                    256 * n : 256 * n + 256,
                ] = part[q * slots : (q + 1) * slots].astype(BF16)
        return carry

    lax.fori_loop(0, rows.shape[1] // ROWS, chunk, 0)

    @pl.when(e == experts - 1)
    def _():
        for k, d_ref in enumerate(d_refs):
            skip = k * (pairs // n_halves)

            def scatter(p, carry):
                base = pl.multiple_of(p * PAIR, PAIR)
                pick = pick_ref[pl.ds(base + skip * PAIR, PAIR), :]
                d_ref[pl.ds(base, PAIR), :width] = dot_nn(pick, outs[p + skip]).astype(BF16)
                d_ref[pl.ds(base, PAIR), width:] = dot_nn(pick, dots[p + skip]).astype(BF16)
                return carry

            lax.fori_loop(0, pairs // n_halves, scatter, 0)


def pick_kernel(experts, token_rows, grad_rows, first_ref, stream_ref, *refs):
    counts = (len(token_rows), len(grad_rows))
    token_pieces = refs[: counts[0]]
    grad_pieces = refs[counts[0] : counts[0] + counts[1]]
    x_ref, dy_ref = refs[sum(counts) : sum(counts) + 2]
    tokens, grads, sems, grad_sems = refs[sum(counts) + 2 :]
    first = first_ref[0]
    p = pl.program_id(0)
    width = grads.shape[1]
    slots = 2 * CAP

    stream = stream_ref[0]
    copies = []
    for pieces, heights, target, sem in (
        (token_pieces, token_rows, tokens, sems),
        (grad_pieces, grad_rows, grads, grad_sems),
    ):
        start = 0
        for index, (piece, rows) in enumerate(zip(pieces, heights, strict=True)):
            source = piece.at[pl.ds(pl.multiple_of(stream * rows, PAIR), rows)]
            copies.append(
                (start, pltpu.make_async_copy(source, target.at[pl.ds(start, rows)], sem.at[index]))
            )
            start += rows

    @pl.when(p == 0)
    def _():
        for start, copy in copies:
            copy.start()

    for start, copy in copies:

        @pl.when(p == start // PAIR)
        def _():
            copy.wait()

    base = pl.multiple_of(p * PAIR, PAIR)
    block = tokens[pl.ds(base, PAIR), :]
    pick = pick_matrix(block[:, width:].astype(F32), first, experts)
    found = dot_tn(pick, block)
    grown = dot_tn(pick, grads[pl.ds(base, PAIR), :])
    for k in range(experts):
        mine = found[k * slots : (k + 1) * slots]
        x_ref[k] = mine[:, :width].astype(BF16)
        gate = jnp.sum(
            jnp.where(gate_lanes(first + k, slots), mine[:, width:], 0.0), axis=1, keepdims=True
        )
        dy_ref[k] = (grown[k * slots : (k + 1) * slots] * gate).astype(BF16)


def expert_grad_kernel(streams, aliased, start, *refs):
    x_refs = refs[:streams]
    dy_refs = refs[streams : 2 * streams]
    hid_own, dgu_own, w_ref = refs[2 * streams : 2 * streams + 3]
    rest = refs[2 * streams + 3 + (1 if aliased else 0) :]
    out_ref, xs, dys, hids, dgus, sems = rest
    e = pl.program_id(0)
    experts = pl.num_programs(0)
    depth = xs.shape[0]
    rows = xs.shape[1] // streams
    width = xs.shape[2]

    def copies(expert, slot):
        made = []
        for s in range(streams):
            place = pl.ds(s * rows, rows)
            made.append(
                pltpu.make_async_copy(
                    x_refs[s].at[start + expert], xs.at[slot, place], sems.at[slot, s]
                )
            )
            made.append(
                pltpu.make_async_copy(
                    dy_refs[s].at[start + expert], dys.at[slot, place], sems.at[slot, streams + s]
                )
            )
        place = pl.ds(0, rows)
        made.append(
            pltpu.make_async_copy(
                hid_own.at[start + expert], hids.at[slot, place], sems.at[slot, 2 * streams]
            )
        )
        made.append(
            pltpu.make_async_copy(
                dgu_own.at[start + expert], dgus.at[slot, place], sems.at[slot, 2 * streams + 1]
            )
        )
        return made

    slot = lax.rem(e, depth)

    @pl.when(e == 0)
    def _():
        for copy in copies(0, 0):
            copy.start()

    if depth > 1:

        @pl.when(e + 1 < experts)
        def _():
            for copy in copies(e + 1, lax.rem(e + 1, depth)):
                copy.start()

    for copy in copies(e, slot):
        copy.wait()

    def chunk(r, carry):
        at = pl.multiple_of(r * ROWS, 64)
        block = xs[slot, pl.ds(at, ROWS), :]
        grown = dys[slot, pl.ds(at, ROWS), :]
        for n in range(2):
            lanes = slice(256 * n, 256 * n + 256)
            uplanes = slice(FE + 256 * n, FE + 256 * n + 256)
            gate_part = dot_nn(block, w_ref[0, 0, :, lanes])
            up_part = dot_nn(block, w_ref[0, 0, :, uplanes])
            dh = dot_nn(grown, w_ref[0, 0, :, 2 * FE + 256 * n : 2 * FE + 256 * n + 256])
            sig = 1.0 / (1.0 + jnp.exp(-gate_part))
            silu = gate_part * sig
            hids[slot, pl.ds(at, ROWS), lanes] = (silu * up_part).astype(BF16)
            slope = sig * (1.0 + gate_part * (1.0 - sig))
            dgus[slot, pl.ds(at, ROWS), lanes] = (dh * up_part * slope).astype(BF16)
            dgus[slot, pl.ds(at, ROWS), uplanes] = (dh * silu).astype(BF16)
        return carry

    lax.fori_loop(rows // ROWS, streams * rows // ROWS, chunk, 0)

    def tile(i, carry):
        at = pl.multiple_of(i * 256, 256)
        left = xs[slot, :, pl.ds(at, 256)]
        for n in range(2):
            out_ref[0, 0, pl.ds(at, 256), FE * n : FE * n + FE] = dot_tn(
                left, dgus[slot, :, FE * n : FE * n + FE]
            )
        out_ref[0, 0, pl.ds(at, 256), 2 * FE :] = dot_tn(dys[slot, :, pl.ds(at, 256)], hids[slot])
        return carry

    lax.fori_loop(0, width // 256, tile, 0)


ANY = pl.BlockSpec(memory_space=pl.ANY)
PARAMS = dict(vmem_limit_bytes=60 * 1024 * 1024)


def once(shape):
    return pl.BlockSpec(shape, lambda e, first: (0,) * len(shape), pipeline_mode=pl.Buffered(1))


def per_expert(*shape):
    return pl.BlockSpec((1, *shape), lambda e, first: (e,) + (0,) * len(shape))


def weight_spec(shape, layer_idx, prefetched, start=0):
    block = (1, 1, shape[2], shape[3])
    if prefetched:
        return pl.BlockSpec(block, lambda e, first: (layer_idx, e, 0, 0))
    return pl.BlockSpec(block, lambda e: (layer_idx, start + e, 0, 0))


def halves_of(pieces):
    return 2 if hierarchical(lax.axis_size("ctx")) else 1


def sizes(w_expert, pieces):
    experts = w_expert.shape[1]
    length = sum(piece.shape[0] for piece in pieces)
    return experts, length, length // BLOCK * CAP


def moe_fwd(pieces, w_expert, layer_idx, first):
    experts, length, rows = sizes(w_expert, pieces)
    width = w_expert.shape[2]
    picked = experts * 2 * CAP
    pairs = length // PAIR
    halves = halves_of(pieces)
    *partial, x_rows, gates, pair_values, pick = pl.pallas_call(
        functools.partial(moe_fwd_kernel, experts, len(pieces), halves),
        out_shape=(
            *[jax.ShapeDtypeStruct((length // halves, width), BF16)] * halves,
            jax.ShapeDtypeStruct((experts, rows, width), BF16),
            jax.ShapeDtypeStruct((experts, rows, EXT), F32),
            jax.ShapeDtypeStruct((experts, rows, 2 * FE), F32),
            jax.ShapeDtypeStruct((length, picked), BF16),
        ),
        grid_spec=pltpu.PrefetchScalarGridSpec(
            num_scalar_prefetch=1,
            grid=(experts,),
            in_specs=[ANY] * len(pieces) + [weight_spec(w_expert.shape, layer_idx, True)],
            out_specs=(
                *[once((length // halves, width))] * halves,
                per_expert(rows, width),
                per_expert(rows, EXT),
                per_expert(rows, 2 * FE),
                once((length, picked)),
            ),
            scratch_shapes=[
                pltpu.VMEM((length, width + EXT), BF16),
                pltpu.VMEM((experts, rows, width), BF16),
                pltpu.VMEM((experts, rows, EXT), F32),
                pltpu.VMEM((pairs, picked, width), BF16),
                pltpu.VMEM((ROWS, FE), BF16),
                pltpu.SemaphoreType.DMA((len(pieces),)),
            ],
        ),
        compiler_params=pltpu.CompilerParams(dimension_semantics=("arbitrary",), **PARAMS),
        cost_estimate=pl.CostEstimate(
            flops=2 * experts * rows * width * 3 * FE,
            bytes_accessed=experts * (width * 3 * FE * 2 + rows * width * 6) + length * width * 4,
            transcendentals=experts * rows * FE,
        ),
        name="moe_fwd",
    )(first, *pieces, w_expert)
    return partial, x_rows, gates, pair_values, pick


def moe_bwd(pieces, w_expert, layer_idx, first, gates, pair_values, pick):
    experts, length, rows = sizes(w_expert, pieces)
    width = w_expert.shape[2]
    picked = experts * 2 * CAP
    pairs = length // PAIR
    halves = halves_of(pieces)
    *partial, dy_rows, hid_rows, dgu_rows = pl.pallas_call(
        functools.partial(moe_bwd_kernel, experts, len(pieces), halves),
        out_shape=(
            *[jax.ShapeDtypeStruct((length // halves, width + EXT), BF16)] * halves,
            jax.ShapeDtypeStruct((experts, rows, width), BF16),
            jax.ShapeDtypeStruct((experts, rows, FE), BF16),
            jax.ShapeDtypeStruct((experts, rows, 2 * FE), BF16),
        ),
        grid_spec=pltpu.PrefetchScalarGridSpec(
            num_scalar_prefetch=1,
            grid=(experts,),
            in_specs=[ANY] * len(pieces)
            + [
                weight_spec(w_expert.shape, layer_idx, True),
                per_expert(rows, EXT),
                per_expert(rows, 2 * FE),
                once((length, picked)),
            ],
            out_specs=(
                *[once((length // halves, width + EXT))] * halves,
                per_expert(rows, width),
                per_expert(rows, FE),
                per_expert(rows, 2 * FE),
            ),
            scratch_shapes=[
                pltpu.VMEM((length, width), BF16),
                pltpu.VMEM((experts, rows, width), BF16),
                pltpu.VMEM((pairs, picked, width), BF16),
                pltpu.VMEM((pairs, picked, EXT), BF16),
                pltpu.SemaphoreType.DMA((len(pieces),)),
            ],
        ),
        compiler_params=pltpu.CompilerParams(dimension_semantics=("arbitrary",), **PARAMS),
        cost_estimate=pl.CostEstimate(
            flops=2 * experts * rows * width * 3 * FE,
            bytes_accessed=experts * (width * 3 * FE * 2 + rows * width * 9) + length * width * 4,
            transcendentals=experts * rows * FE,
        ),
        name="moe_bwd",
    )(first, *pieces, w_expert, gates, pair_values, pick)
    return partial, dy_rows, hid_rows, dgu_rows


def pick_rows(token_pieces, grad_pieces, w_expert, first, stream):
    streams = lax.axis_size("dp")
    heights = [
        tuple(piece.shape[0] // streams for piece in pieces) for pieces in (token_pieces, grad_pieces)
    ]
    experts, width = w_expert.shape[1:3]
    length = sum(heights[0])
    rows = length // BLOCK * CAP
    counts = (len(token_pieces), len(grad_pieces))
    slab = pl.BlockSpec((experts, 2 * CAP, width), lambda p, *scalars: (0, p, 0))
    return pl.pallas_call(
        functools.partial(pick_kernel, experts, *heights),
        out_shape=(
            jax.ShapeDtypeStruct((experts, rows, width), BF16),
            jax.ShapeDtypeStruct((experts, rows, width), BF16),
        ),
        grid_spec=pltpu.PrefetchScalarGridSpec(
            num_scalar_prefetch=2,
            grid=(length // PAIR,),
            in_specs=[ANY] * sum(counts),
            out_specs=(slab, slab),
            scratch_shapes=[
                pltpu.VMEM((length, width + EXT), BF16),
                pltpu.VMEM((length, width), BF16),
                pltpu.SemaphoreType.DMA((counts[0],)),
                pltpu.SemaphoreType.DMA((counts[1],)),
            ],
        ),
        compiler_params=pltpu.CompilerParams(dimension_semantics=("arbitrary",), **PARAMS),
        cost_estimate=pl.CostEstimate(
            flops=4 * length * experts * 2 * CAP * width,
            bytes_accessed=length * width * 4 + experts * rows * width * 4,
            transcendentals=0,
        ),
        name="pick_rows",
    )(first, stream, *token_pieces, *grad_pieces)


def expert_grads(x_rows, dy_rows, hid_own, dgu_own, w_expert, layer_idx, start, experts, before):
    streams = len(x_rows)
    unused, rows, width = x_rows[0].shape
    depth = min(2, experts)
    operands = [*x_rows, *dy_rows, hid_own, dgu_own, w_expert]
    in_specs = [ANY] * (2 * streams + 2) + [weight_spec(w_expert.shape, layer_idx, False, start)]
    aliases = {}
    if before is not None:
        aliases = {len(operands): 0}
        operands.append(before)
        in_specs.append(ANY)
    return pl.pallas_call(
        functools.partial(expert_grad_kernel, streams, before is not None, start),
        out_shape=jax.ShapeDtypeStruct(w_expert.shape, F32),
        grid=(experts,),
        in_specs=in_specs,
        out_specs=weight_spec(w_expert.shape, layer_idx, False, start),
        scratch_shapes=[
            pltpu.VMEM((depth, streams * rows, width), BF16),
            pltpu.VMEM((depth, streams * rows, width), BF16),
            pltpu.VMEM((depth, streams * rows, FE), BF16),
            pltpu.VMEM((depth, streams * rows, 2 * FE), BF16),
            pltpu.SemaphoreType.DMA((depth, 2 * streams + 2)),
        ],
        input_output_aliases=aliases,
        compiler_params=pltpu.CompilerParams(dimension_semantics=("arbitrary",), **PARAMS),
        cost_estimate=pl.CostEstimate(
            flops=2 * experts * rows * width * 3 * FE * (2 * streams - 1),
            bytes_accessed=experts * (width * 3 * FE * 6 + streams * rows * width * 4),
            transcendentals=experts * rows * FE * (streams - 1),
        ),
        name="expert_grads",
    )(*operands)


def whole(*shape):
    return pl.BlockSpec(shape, lambda i, *scalars: (0,) * len(shape), pipeline_mode=pl.Buffered(1))


def swap_halves(values):
    width = values.shape[1]
    lane = lax.broadcasted_iota(jnp.int32, values.shape, 1)
    up = pltpu.roll(values, width - HD // 2, axis=1)
    down = pltpu.roll(values, HD // 2, axis=1)
    return jnp.where(lane % HD < HD // 2, up, down)


def turn(values, cosine, sine):
    times = values.shape[1] // cosine.shape[1]
    cosine = jnp.concatenate([cosine] * times, axis=1)
    sine = jnp.concatenate([sine] * times, axis=1)
    return values * cosine + swap_halves(values) * sine


def row_scale(values):
    return lax.rsqrt(jnp.mean(values * values, axis=1, keepdims=True) + epsilon)


def reorder(source_ref, target_ref, order_ref, reordered):
    if not reordered:
        target_ref[...] = source_ref[...]
        return
    for j in range(source_ref.shape[1] // BLOCK):
        target_ref[:, j * BLOCK : (j + 1) * BLOCK] = source_ref[
            :, pl.ds(pl.multiple_of(order_ref[j] * BLOCK, BLOCK), BLOCK)
        ]


def project_kernel(n_pieces, reordered, columns, turned, scale, order_ref, *refs):
    pieces = refs[:n_pieces]
    x_ref, gain_ref, cos_ref, sin_ref, out_ref, a_ref, turned_ref, weight, sems = refs[n_pieces:]
    copies = copy_blocks(pieces, order_ref, columns, weight, sems)
    x = x_ref[...].astype(F32)
    a_ref[...] = (x * row_scale(x) * gain_ref[...]).astype(BF16)
    reorder(a_ref, turned_ref, order_ref, reordered)
    for copy in copies:
        copy.wait()
    block = 512
    for at in range(0, weight.shape[1], block):
        made = dot_nn(a_ref[...], weight[:, at : at + block])
        if at < turned:
            made = turn(made, cos_ref[...], sin_ref[...])
        out_ref[:, at : at + block] = (made * scale).astype(BF16)


def project(x, gain, pieces, order, columns, turned, scale, cosine, sine):
    tokens, width = x.shape
    wide = HEADS * HD
    return pl.pallas_call(
        functools.partial(
            project_kernel, len(pieces), hierarchical(order.shape[0]), columns, turned, scale
        ),
        out_shape=(
            jax.ShapeDtypeStruct((tokens, wide), BF16),
            jax.ShapeDtypeStruct((tokens, width), BF16),
            jax.ShapeDtypeStruct((tokens, width), BF16),
        ),
        grid_spec=pltpu.PrefetchScalarGridSpec(
            num_scalar_prefetch=1,
            grid=(1,),
            in_specs=[ANY] * len(pieces)
            + [whole(tokens, width), whole(1, width), whole(tokens, 128), whole(tokens, 128)],
            out_specs=(whole(tokens, wide), whole(tokens, width), whole(tokens, width)),
            scratch_shapes=[
                pltpu.VMEM((width, wide), BF16),
                pltpu.SemaphoreType.DMA((copy_count(pieces, order),)),
            ],
        ),
        compiler_params=pltpu.CompilerParams(dimension_semantics=("arbitrary",), **PARAMS),
        cost_estimate=pl.CostEstimate(
            flops=2 * tokens * width * wide, bytes_accessed=2 * width * wide, transcendentals=0
        ),
        name="project",
    )(order, *pieces, x, gain, cosine, sine)


def low_lanes(rows):
    return lax.broadcasted_iota(jnp.int32, (rows, 128), 1) < HD


def spread_heads(left, right):
    low = low_lanes(left.shape[0])
    return jnp.concatenate(
        [
            jnp.where(low, left, 0.0),
            jnp.where(low, pltpu.roll(left, HD, axis=1), 0.0),
            jnp.where(low, 0.0, pltpu.roll(right, HD, axis=1)),
            jnp.where(low, 0.0, right),
        ],
        axis=0,
    )


def join_heads(stacked):
    tokens = stacked.shape[0] // 4
    low = low_lanes(tokens)
    a, b, c, d = (stacked[k * tokens : (k + 1) * tokens] for k in range(4))
    return (
        jnp.where(low, a, pltpu.roll(b, HD, axis=1)),
        jnp.where(low, pltpu.roll(c, HD, axis=1), d),
    )


def seen(key_ref, query_ref, j):
    keys = key_ref[pl.ds(j, 1), :]
    query = query_ref[...]
    mask = (keys <= query[:, 0:1]) & (keys >= query[:, 1:2])
    return jnp.concatenate([mask] * 4, axis=0)


GROUPS = KVH // 2


def attend_kernel(n_pieces, n_weights, reordered, need_ref, order_ref, *refs):
    pieces = refs[:n_pieces]
    w_pieces = refs[n_pieces : n_pieces + n_weights]
    refs = refs[n_pieces + n_weights :]
    q_ref, key_ref, query_ref, x_ref, gain_ref, table_ref = refs[:6]
    o_ref, o_order_ref, den_ref, un_ref, h_ref, pay_ref, gates_ref = refs[6:13]
    kv, w_ref, spread, sems, w_sems = refs[13:]
    tokens = q_ref.shape[0]
    width = x_ref.shape[1]
    keys = KVH * HD
    copies = copy_rows(pieces, kv, sems)
    w_copies = copy_blocks(w_pieces, order_ref, None, w_ref, w_sems)
    for i in range(GROUPS):
        spread[i] = spread_heads(
            q_ref[:, 256 * i : 256 * i + 128].astype(F32),
            q_ref[:, 256 * i + 128 : 256 * i + 256].astype(F32),
        ).astype(BF16)
        den_ref[i] = jnp.zeros((4 * tokens, 128), F32)
        un_ref[i] = jnp.zeros((4 * tokens, 128), F32)
    for copy in copies:
        copy.wait()

    def block(j, carry):
        @pl.when(need_ref[j] > 0)
        def _():
            at = pl.multiple_of(j * BLOCK, BLOCK)
            mask = seen(key_ref, query_ref, j)
            for i in range(GROUPS):
                scores = dot_nt(spread[i], kv[pl.ds(at, BLOCK), 128 * i : 128 * i + 128])
                weights = jnp.where(mask, jnp.exp(scores), 0.0)
                den_ref[i] += weights
                un_ref[i] += dot_nn(
                    weights.astype(BF16), kv[pl.ds(at, BLOCK), keys + 128 * i : keys + 128 * i + 128]
                )

        return carry

    lax.fori_loop(0, kv.shape[0] // BLOCK, block, 0)
    for i in range(GROUPS):
        den = jnp.sum(den_ref[i], axis=1, keepdims=True)
        den_ref[i] = jnp.broadcast_to(den, (4 * tokens, 128))
        left, right = join_heads(un_ref[i] / den)
        o_ref[:, 256 * i : 256 * i + 128] = left.astype(BF16)
        o_ref[:, 256 * i + 128 : 256 * i + 256] = right.astype(BF16)
    reorder(o_ref, o_order_ref, order_ref, reordered)
    for copy in w_copies:
        copy.wait()
    h = x_ref[...].astype(F32) + dot_nn(o_ref[...], w_ref[:, :width])
    h_ref[...] = h
    normed = (h * row_scale(h) * gain_ref[...]).astype(BF16)
    pay_ref[:, :width] = normed
    lane = lax.broadcasted_iota(jnp.int32, (tokens, EXT), 1)
    table = table_ref[...]
    logits = dot_nn(normed, w_ref[:, width:])
    logits = jnp.where((lane < 64) & (table > 0.0), logits, -1e30)
    powers = jnp.exp(logits - jnp.max(logits, axis=1, keepdims=True))
    powers = jnp.where((lane < 64) & (table > 0.0), powers, 0.0)
    gates = powers / (0.5 * jnp.sum(powers, axis=1, keepdims=True))
    gates_ref[...] = gates
    high = gates.astype(BF16).astype(F32)
    pay_ref[:, width:] = jnp.where(
        lane < 32, high, jnp.where(lane < 64, gates - high, table)
    ).astype(BF16)


def attend(pieces, w_pieces, need, order, q, keys, queries, x, gain, table):
    tokens, width = x.shape
    length = sum(piece.shape[0] for piece in pieces)
    stack = (GROUPS, 4 * tokens, 128)
    return pl.pallas_call(
        functools.partial(
            attend_kernel, len(pieces), len(w_pieces), hierarchical(order.shape[0])
        ),
        out_shape=(
            jax.ShapeDtypeStruct((tokens, width), BF16),
            jax.ShapeDtypeStruct((tokens, width), BF16),
            jax.ShapeDtypeStruct(stack, F32),
            jax.ShapeDtypeStruct(stack, F32),
            jax.ShapeDtypeStruct((tokens, width), F32),
            jax.ShapeDtypeStruct((tokens, width + EXT), BF16),
            jax.ShapeDtypeStruct((tokens, EXT), F32),
        ),
        grid_spec=pltpu.PrefetchScalarGridSpec(
            num_scalar_prefetch=2,
            grid=(1,),
            in_specs=[ANY] * (len(pieces) + len(w_pieces))
            + [
                whole(tokens, width),
                whole(*keys.shape),
                whole(*queries.shape),
                whole(tokens, width),
                whole(1, width),
                whole(tokens, EXT),
            ],
            out_specs=(
                whole(tokens, width),
                whole(tokens, width),
                whole(*stack),
                whole(*stack),
                whole(tokens, width),
                whole(tokens, width + EXT),
                whole(tokens, EXT),
            ),
            scratch_shapes=[
                pltpu.VMEM((length, 2 * KVH * HD), BF16),
                pltpu.VMEM((width, w_pieces[0].shape[1]), BF16),
                pltpu.VMEM(stack, BF16),
                pltpu.SemaphoreType.DMA((len(pieces),)),
                pltpu.SemaphoreType.DMA((copy_count(w_pieces, order),)),
            ],
        ),
        compiler_params=pltpu.CompilerParams(dimension_semantics=("arbitrary",), **PARAMS),
        cost_estimate=pl.CostEstimate(
            flops=4 * tokens * (length // 2) * width + 2 * tokens * width * width,
            bytes_accessed=length * width * 2 + width * width * 2 + tokens * width * 20,
            transcendentals=tokens * HEADS * (length // 2),
        ),
        name="attend",
    )(need, order, *pieces, *w_pieces, q, keys, queries, x, gain, table)


def attend_back_kernel(n_pieces, n_weights, n_sums, n_halves, need_ref, order_ref, *refs):
    pieces = refs[:n_pieces]
    w_pieces = refs[n_pieces : n_pieces + n_weights]
    refs = refs[n_pieces + n_weights :]
    sums = refs[:n_sums]
    (
        q_ref,
        key_ref,
        query_ref,
        h_ref,
        gain_ref,
        gates_ref,
        den_ref,
        un_ref,
        gx_ref,
        cos_ref,
        sin_ref,
    ) = refs[n_sums : n_sums + 11]
    dh_ref, dattn_ref, dlog_ref, dgain_ref, dq_ref = refs[n_sums + 11 : n_sums + 16]
    dkv_refs = refs[n_sums + 16 : n_sums + 16 + n_halves]
    kv, w_ref, spread, grown, dden, dq_acc, sems, w_sems = refs[n_sums + 16 + n_halves :]
    tokens, width = h_ref.shape
    keys = KVH * HD
    w_copies = copy_blocks(w_pieces, order_ref, None, w_ref, w_sems)
    copies = copy_rows(pieces, kv, sems)
    moved = sums[0][...]
    for piece in sums[1:]:
        moved = moved + piece[...].astype(F32)
    lane = lax.broadcasted_iota(jnp.int32, (tokens, EXT), 1)
    ext = moved[:, width:]
    dgate = jnp.where(lane < 32, ext + pltpu.roll(ext, EXT - 32, axis=1), 0.0)
    gates = jnp.where(lane < 32, gates_ref[...], 0.0)
    dlog = (gates * (dgate - jnp.sum(gates * dgate, axis=1, keepdims=True))).astype(BF16)
    dlog_ref[...] = dlog
    for copy in w_copies:
        copy.wait()
    db = moved[:, :width] + dot_nt(dlog, w_ref[:, width:])
    h = h_ref[...]
    scale = row_scale(h)
    normed = h * scale
    dn = db * gain_ref[...]
    dgain_ref[...] = jnp.sum(db * normed, axis=0, keepdims=True)
    dh = gx_ref[...].astype(F32) + scale * (dn - normed * jnp.mean(dn * normed, axis=1, keepdims=True))
    dh_ref[...] = dh
    dattn = dh.astype(BF16)
    dattn_ref[...] = dattn
    do = dot_nt(dattn, w_ref[:, :width])
    for i in range(GROUPS):
        spread[i] = spread_heads(
            q_ref[:, 256 * i : 256 * i + 128].astype(F32),
            q_ref[:, 256 * i + 128 : 256 * i + 256].astype(F32),
        ).astype(BF16)
        stacked = spread_heads(
            do[:, 256 * i : 256 * i + 128], do[:, 256 * i + 128 : 256 * i + 256]
        )
        den = den_ref[i]
        grown[i] = (stacked / den).astype(BF16)
        dden[i] = jnp.broadcast_to(
            -jnp.sum(stacked * un_ref[i], axis=1, keepdims=True), den.shape
        ) / (den * den)
        dq_acc[i] = jnp.zeros((4 * tokens, 128), F32)
    for copy in copies:
        copy.wait()

    def block(dkv_ref, skip, i, carry):
        at = pl.multiple_of(i * BLOCK, BLOCK)
        j = i + skip
        here = pl.multiple_of(j * BLOCK, BLOCK)

        @pl.when(need_ref[j] > 0)
        def _():
            mask = seen(key_ref, query_ref, j)
            for i in range(GROUPS):
                key = kv[pl.ds(here, BLOCK), 128 * i : 128 * i + 128]
                value = kv[pl.ds(here, BLOCK), keys + 128 * i : keys + 128 * i + 128]
                weights = jnp.where(mask, jnp.exp(dot_nt(spread[i], key)), 0.0)
                prob = dot_nt(grown[i], value)
                ds = (weights * (prob + dden[i])).astype(BF16)
                dq_acc[i] += dot_nn(ds, key)
                dkv_ref[pl.ds(at, BLOCK), 128 * i : 128 * i + 128] = dot_tn(ds, spread[i]).astype(BF16)
                dkv_ref[pl.ds(at, BLOCK), keys + 128 * i : keys + 128 * i + 128] = dot_tn(
                    weights.astype(BF16), grown[i]
                ).astype(BF16)

        @pl.when(need_ref[j] == 0)
        def _():
            dkv_ref[pl.ds(at, BLOCK), :] = jnp.zeros((BLOCK, 2 * keys), BF16)

        return carry

    count = kv.shape[0] // BLOCK // n_halves
    for k, dkv_ref in enumerate(dkv_refs):
        lax.fori_loop(0, count, functools.partial(block, dkv_ref, k * count), 0)
    for i in range(GROUPS):
        for k, part in enumerate(join_heads(dq_acc[i])):
            at = 256 * i + 128 * k
            dq_ref[:, at : at + 128] = (
                turn(part, cos_ref[...], -sin_ref[...]) * (1.0 / math.sqrt(HD))
            ).astype(BF16)


def attend_back(
    pieces, w_pieces, sums, need, order, q, keys, queries, h, gain, gates, den, un, gx, cosine, sine
):
    tokens, width = h.shape
    length = sum(piece.shape[0] for piece in pieces)
    stack = (GROUPS, 4 * tokens, 128)
    blocks = [q, keys, queries, h, gain, gates, den, un, gx, cosine, sine]
    halves = halves_of(pieces)
    made = pl.pallas_call(
        functools.partial(attend_back_kernel, len(pieces), len(w_pieces), len(sums), halves),
        out_shape=(
            jax.ShapeDtypeStruct((tokens, width), F32),
            jax.ShapeDtypeStruct((tokens, width), BF16),
            jax.ShapeDtypeStruct((tokens, EXT), BF16),
            jax.ShapeDtypeStruct((1, width), F32),
            jax.ShapeDtypeStruct((tokens, HEADS * HD), BF16),
            *[jax.ShapeDtypeStruct((length // halves, 2 * KVH * HD), BF16)] * halves,
        ),
        grid_spec=pltpu.PrefetchScalarGridSpec(
            num_scalar_prefetch=2,
            grid=(1,),
            in_specs=[ANY] * (len(pieces) + len(w_pieces))
            + [whole(*value.shape) for value in [*sums, *blocks]],
            out_specs=(
                whole(tokens, width),
                whole(tokens, width),
                whole(tokens, EXT),
                whole(1, width),
                whole(tokens, HEADS * HD),
                *[whole(length // halves, 2 * KVH * HD)] * halves,
            ),
            scratch_shapes=[
                pltpu.VMEM((length, 2 * KVH * HD), BF16),
                pltpu.VMEM((width, w_pieces[0].shape[1]), BF16),
                pltpu.VMEM(stack, BF16),
                pltpu.VMEM(stack, BF16),
                pltpu.VMEM(stack, F32),
                pltpu.VMEM(stack, F32),
                pltpu.SemaphoreType.DMA((len(pieces),)),
                pltpu.SemaphoreType.DMA((copy_count(w_pieces, order),)),
            ],
        ),
        compiler_params=pltpu.CompilerParams(dimension_semantics=("arbitrary",), **PARAMS),
        cost_estimate=pl.CostEstimate(
            flops=10 * tokens * (length // 2) * width + 2 * tokens * width * width,
            bytes_accessed=length * width * 4 + width * width * 2 + tokens * width * 30,
            transcendentals=tokens * HEADS * (length // 2),
        ),
        name="attend_back",
    )(need, order, *pieces, *w_pieces, *sums, *blocks)
    return (*made[:5], made[5:])


def project_back_kernel(n_weights, n_groups, n_sums, order_ref, *refs):
    groups = [refs[k * n_weights : (k + 1) * n_weights] for k in range(n_groups)]
    refs = refs[n_groups * n_weights :]
    sums = refs[:n_sums]
    dq_ref, x_ref, gain_ref, dh_ref, cos_ref, sin_ref = refs[n_sums : n_sums + 6]
    gx_ref, low_ref, dp_ref, dgain_ref, weight, sems = refs[n_sums + 6 :]
    keys = KVH * HD
    query_width = HEADS * HD
    copies = []
    for k, pieces in enumerate(groups):
        columns = weight.shape[1] // n_groups
        copies += copy_blocks(
            pieces, order_ref, None, weight.at[:, pl.ds(k * columns, columns)], sems.at[k]
        )
    dkv = sums[0][...]
    for piece in sums[1:]:
        dkv = dkv + piece[...].astype(F32)
    dp_ref[:, :query_width] = dq_ref[...]
    dp_ref[:, query_width : query_width + keys] = turn(
        dkv[:, :keys], cos_ref[...], -sin_ref[...]
    ).astype(BF16)
    dp_ref[:, query_width + keys : query_width + 2 * keys] = dkv[:, keys:].astype(BF16)
    dp_ref[:, query_width + 2 * keys :] = jnp.zeros((dp_ref.shape[0], EXT), BF16)
    for copy in copies:
        copy.wait()
    da = dot_nt(dp_ref[:, : query_width + 2 * keys], weight[...])
    x = x_ref[...].astype(F32)
    scale = row_scale(x)
    normed = x * scale
    dn = da * gain_ref[...]
    dgain_ref[...] = jnp.sum(da * normed, axis=0, keepdims=True)
    gx = dh_ref[...] + scale * (dn - normed * jnp.mean(dn * normed, axis=1, keepdims=True))
    gx_ref[...] = gx
    low_ref[...] = gx.astype(BF16)


def project_back(groups, sums, order, dq, x, gain, dh, cosine, sine):
    tokens, width = x.shape
    wide = sum(pieces[0].shape[1] for pieces in groups)
    operands = [*sums, dq, x, gain, dh, cosine, sine]
    weights = [piece for pieces in groups for piece in pieces]
    return pl.pallas_call(
        functools.partial(project_back_kernel, len(groups[0]), len(groups), len(sums)),
        out_shape=(
            jax.ShapeDtypeStruct((tokens, width), F32),
            jax.ShapeDtypeStruct((tokens, width), BF16),
            jax.ShapeDtypeStruct((tokens, wide + EXT), BF16),
            jax.ShapeDtypeStruct((1, width), F32),
        ),
        grid_spec=pltpu.PrefetchScalarGridSpec(
            num_scalar_prefetch=1,
            grid=(1,),
            in_specs=[ANY] * len(weights) + [whole(*value.shape) for value in operands],
            out_specs=(
                whole(tokens, width),
                whole(tokens, width),
                whole(tokens, wide + EXT),
                whole(1, width),
            ),
            scratch_shapes=[
                pltpu.VMEM((width, wide), BF16),
                pltpu.SemaphoreType.DMA((len(groups), copy_count(groups[0], order))),
            ],
        ),
        compiler_params=pltpu.CompilerParams(dimension_semantics=("arbitrary",), **PARAMS),
        cost_estimate=pl.CostEstimate(
            flops=2 * tokens * width * wide,
            bytes_accessed=2 * width * wide + tokens * width * 24,
            transcendentals=0,
        ),
        name="project_back",
    )(order, *weights, *operands)


def slot_tables(mask):
    tokens, experts = mask.shape
    before = jnp.tril(jnp.ones((tokens, tokens), F32), -1)
    rank = jnp.dot(before, mask, preferred_element_type=F32)
    codes = jnp.where(mask > 0, rank, -100.0)
    return jnp.concatenate(
        [mask, mask, codes, jnp.zeros((tokens, EXT - 3 * experts), F32)], axis=1
    )


def block_order(rank, size):
    if not hierarchical(size):
        return jnp.arange(size, dtype=jnp.int32)
    masks = list(range(0, size, 2)) + list(range(1, size, 2))
    return rank ^ jnp.asarray(masks, jnp.int32)


def local(x_in, doc_ids, routes, gain_attn, w_qkv, w_out, gain_moe, w_router, w_expert, cotangent):
    ctx_size = lax.axis_size("ctx")
    ctx_rank = lax.axis_index("ctx")
    tokens = x_in.shape[1]
    width = x_in.shape[2]
    length = tokens * ctx_size
    layers = w_qkv.shape[0]
    expert_count = w_router.shape[2]
    experts_here = w_expert.shape[1]
    query_width = HEADS * HD
    first = (ctx_rank * experts_here).astype(jnp.int32).reshape(1)

    doc_row = doc_ids[0]
    index_row = jnp.arange(length, dtype=jnp.int32)
    offset = ctx_rank * tokens
    query_index = offset + jnp.arange(tokens, dtype=jnp.int32)
    query_doc = lax.dynamic_slice_in_dim(doc_row, offset, tokens)
    starts = jnp.sum((doc_row[None, :] < query_doc[:, None]).astype(jnp.int32), axis=1)
    lane = jnp.arange(128) % HD
    frequency = 10000.0 ** (-((lane % (HD // 2)) * 2).astype(F32) / HD)
    angle = (query_index - starts).astype(F32)[:, None] * frequency[None, :]
    cosine = jnp.cos(angle)
    sine = jnp.where(lane[None, :] < HD // 2, -jnp.sin(angle), jnp.sin(angle))
    order = block_order(ctx_rank, ctx_size)
    keys = order[:, None] * BLOCK + jnp.arange(BLOCK, dtype=jnp.int32)[None, :]
    queries = jnp.stack([query_index, starts], axis=1)
    need = ((order <= ctx_rank) & (order * BLOCK + BLOCK > starts[0])).astype(jnp.int32)

    tables = []
    for layer_idx in range(layers):
        hits = routes[layer_idx, 0][..., None] == jnp.arange(expert_count, dtype=jnp.int32)
        tables.append(slot_tables(jnp.sum(hits.astype(F32), axis=1)))

    def pieces_of(weight):
        return gather_ctx(weight)

    def with_router(layer_idx):
        router = w_router[layer_idx]
        blank = jnp.zeros((router.shape[0], EXT - 2 * expert_count), BF16)
        return jnp.concatenate([w_out[layer_idx], router, router, blank], axis=1)

    gain_pieces = gather_ctx(
        jnp.concatenate([gain_attn, gain_moe, jnp.zeros((8 - 2 * layers, gain_attn.shape[1]), BF16)])
    )
    kv_weight = pieces_of(w_qkv[0, :, query_width:])
    q_weight, kv_weight = tie(w_qkv[0, :, :query_width], *kv_weight)
    q_weight, kv_weight = pieces_of(q_weight), list(kv_weight)
    gain_blocks = jnp.concatenate(gain_pieces, axis=0).reshape(ctx_size, 8, -1)
    if hierarchical(ctx_size):
        gain_blocks = jnp.take(gain_blocks, jnp.argsort(order), axis=0)
    gains = jnp.transpose(gain_blocks, (1, 0, 2)).reshape(8, width).astype(F32)
    out_weight = with_router(0)
    out_weight, q_weight = tie(out_weight, *q_weight)
    weights = [
        (gains[0][None], [list(q_weight), kv_weight], gains[layers][None], pieces_of(out_weight))
    ]
    for layer_idx in range(1, layers):
        next_out, (weights[0],) = tie(with_router(layer_idx), weights[0])
        weights.append((gains[layer_idx][None], None, gains[layers + layer_idx][None], pieces_of(next_out)))
    gx, (weights[0],) = tie(cotangent[0], weights[0])
    grad_near = gather_chips(gx)
    grad_side = all_streams(grad_near)

    x = x_in[0]
    store = []
    sides = {}
    for layer_idx in range(layers):
        gain_one, qkv_weight, gain_two, out_weight = weights[layer_idx]
        columns = 0 if len(qkv_weight) > 1 else query_width
        kv, a, unused = project(
            x, gain_one, qkv_weight[-1], order, columns, KVH * HD, 1.0, cosine, sine
        )
        kv_pieces = gather_ctx(kv)
        q, unused, a_order = project(
            x, gain_one, qkv_weight[0], order, 0, query_width, 1.0 / math.sqrt(HD), cosine, sine
        )
        *o, den, un, h, pay, gates = attend(
            kv_pieces, out_weight, need, order, q, keys, queries, x, gain_two, tables[layer_idx]
        )
        near = gather_chips(pay)
        if layer_idx + 1 < layers:
            next_qkv, (near,) = tie(w_qkv[layer_idx + 1], near)
            next_qkv = pieces_of(next_qkv)
        else:
            near, (sides[0],) = tie(near, sides[0])
        sides[layer_idx] = all_streams(near)
        partial, x_rows, gate_rows, pair_values, pick = moe_fwd(
            both_cores(near), w_expert, layer_idx, first
        )
        store.append(
            [x, (a, a_order), q, kv_pieces, o, den, un, h, pay, gates, x_rows, gate_rows, pair_values, pick]
        )
        own, sent = reduce_start(partial)
        if layer_idx + 1 < layers:
            x = total_of([h, *reduce_finish(own, sent)])
            x, (next_qkv, grad_side) = tie(x, next_qkv, grad_side)
            upper_gain, unused, moe_gain, upper_out = weights[layer_idx + 1]
            weights[layer_idx + 1] = (upper_gain, [next_qkv], moe_gain, upper_out)
    last_h, last_own, last_sent = h, own, sent

    streams = lax.axis_size("dp")

    def pick_others(tokens_of, grads_of):
        tokens_of, grads_of = both_cores(tokens_of), both_cores(grads_of)
        return [
            pick_rows(
                tokens_of,
                grads_of,
                w_expert,
                first,
                ((lax.axis_index("dp") + k) % streams).astype(jnp.int32).reshape(1),
            )
            for k in range(1, streams)
        ]

    expert_sum = None
    early, late, routed = {}, {}, {}
    split = (experts_here + 1) // 2
    for layer_idx in reversed(range(layers)):
        gain_one, qkv_weight, gain_two, out_weight = weights[layer_idx]
        x, a, q, kv_pieces, o, den, un, h, pay, gates, x_rows, gate_rows, pair_values, pick = store[
            layer_idx
        ]
        top = layer_idx == layers - 1
        if not top:
            grad_side = all_streams(grad_near)
        partial, dy_rows, hid_rows, dgu_rows = moe_bwd(
            both_cores(grad_near), w_expert, layer_idx, first, gate_rows, pair_values, pick
        )
        own, sent = reduce_start(partial)
        sums = reduce_finish(own, sent)
        if not top:
            y_out = total_of([last_h, *reduce_finish(last_own, last_sent)]).astype(BF16)[None]
            sums[0], (picked, early[1], late[1], y_out) = tie(
                sums[0], picked, early[1], late[1], y_out
            )
            late[1] = lax.psum_scatter(late[1], "ctx", scatter_dimension=0, tiled=True)
        dh, dattn, dlog, dgain_two, dq, dkv = attend_back(
            kv_pieces,
            out_weight,
            sums,
            need,
            order,
            q,
            keys,
            queries,
            h,
            gain_two,
            gates,
            den,
            un,
            gx,
            cosine,
            sine,
        )
        count = halves_of(sums)
        half = width // count
        if top:
            early[1] = dot_tn(o[0], dattn).astype(BF16)
        else:
            early[0] = [
                dot_tn(o[1][:, at : at + half], dattn).astype(BF16) for at in range(0, width, half)
            ]
        routed[layer_idx] = dot_tn(pay[:, :width], dlog[:, :expert_count])
        sums = reduce_ctx(dkv)
        if top:
            sums[0], (early[1],) = tie(sums[0], early[1])
        else:
            upper_sum = functools.partial(
                expert_grads,
                [upper[0]] + [pair[0] for pair in picked],
                [upper[1]] + [pair[1] for pair in picked],
                upper[2],
                upper[3],
                w_expert,
                layer_idx + 1,
            )
            expert_sum = upper_sum(0, split, None)
            early[0] = reduce_start(early[0])
            sums[0], (expert_sum, early[0]) = tie(sums[0], expert_sum, early[0])
        if top:
            early[1] = lax.psum_scatter(early[1], "ctx", scatter_dimension=0, tiled=True)
        gx, grad_low, dprojected, dgain_one = project_back(
            qkv_weight, sums, order, dq, x, gain_one, dh, cosine, sine
        )
        routed[layer_idx] = jnp.concatenate(
            [routed[layer_idx], dgain_one.T, dgain_two.T], axis=1
        )
        if top:
            late[1] = dot_tn(a[0], dprojected[:, : 2 * width]).astype(BF16)
            upper = (x_rows, dy_rows, hid_rows, dgu_rows)
            grad_near = gather_chips(grad_low)
            grad_near, (last_own, last_sent) = tie(grad_near, last_own, last_sent)
            (side, grad_side), (grad_near,) = tie((sides[layer_idx], grad_side), grad_near)
            picked = pick_others(side, grad_side)
        else:
            spare = EXT - layers * (expert_count + 2)
            small = jnp.pad(
                jnp.concatenate([routed[k] for k in range(layers)], axis=1), ((0, 0), (0, spare))
            )
            if hierarchical(ctx_size):
                small = jnp.take(small.reshape(ctx_size, -1, EXT), order, axis=0).reshape(-1, EXT)
            small = jnp.pad(small, ((0, 0), (2 * width, 0)))
            early[0] = reduce_finish(*early[0])
            own, sent = reduce_start(
                [
                    (dot_tn(a[1][:, at : at + half], dprojected) + small[at : at + half]).astype(BF16)
                    for at in range(0, width, half)
                ]
            )
            if split < experts_here:
                expert_sum, (own, sent, early[0]) = tie(expert_sum, own, sent, early[0])
                expert_sum = upper_sum(split, experts_here - split, expert_sum)
            arrived = reduce_finish(own, sent)
            expert_sum, (arrived,) = tie(expert_sum, arrived)
            below = jnp.concatenate([total_of(arrived), total_of(early[0])], axis=1).astype(BF16)
            below = add_across(below, 1).astype(BF16)
            (side, grad_side), (expert_sum,) = tie((sides[layer_idx], grad_side), expert_sum)
            picked = pick_others(side, grad_side)
            picked[0], (below, expert_sum) = tie(picked[0], below, expert_sum)
            upper_grads, (picked,) = tie(jnp.concatenate([early[1], late[1]], axis=1), picked)
            expert_sum = expert_grads(
                [x_rows] + [pair[0] for pair in picked],
                [dy_rows] + [pair[1] for pair in picked],
                hid_rows,
                dgu_rows,
                w_expert,
                layer_idx,
                0,
                experts_here,
                expert_sum,
            )
    low_sum = add_across(below, 2)
    upper_grads, (expert_sum, low_sum) = tie(lax.psum(upper_grads, "dp"), expert_sum, low_sum)
    upper_grads = upper_grads.astype(F32)
    spread = low_sum[:, 2 * width : 2 * width + EXT]
    each = [spread[:, k * (expert_count + 2) :] for k in range(layers)]
    stacked = [
        jnp.stack([value[:, expert_count] for value in each]),
        jnp.stack([low_sum[:, : 2 * width], upper_grads[:, width:]]),
        jnp.stack([low_sum[:, 2 * width + EXT :], upper_grads[:, :width]]),
        jnp.stack([value[:, expert_count + 1] for value in each]),
        jnp.stack([value[:, :expert_count] for value in each]),
    ]
    return (y_out, gx[None], *stacked, expert_sum)


def solution(mesh):
    placed = (
        P("dp", "ctx", None),
        P("dp", None),
        P(None, "dp", "ctx", None),
        P(None, "ctx"),
        P(None, "ctx", None),
        P(None, "ctx", None),
        P(None, "ctx"),
        P(None, "ctx", None),
        P(None, "ctx", None, None),
        P("dp", "ctx", None),
    )
    return jax.shard_map(
        local,
        mesh=mesh,
        in_specs=placed,
        out_specs=(
            P("dp", "ctx", None),
            P("dp", "ctx", None),
            P(None, "ctx"),
            P(None, "ctx", None),
            P(None, "ctx", None),
            P(None, "ctx"),
            P(None, "ctx", None),
            P(None, "ctx", None, None),
        ),
        check_vma=False,
    )
```

time: 1160 us -> 736 us (0.63)
  waiting for transfers between devices: 544 us -> 242 us
  Pallas kernels: 206 us -> 299 us
  local copies, waits for them, and re-layouts: 131 us -> 39.5 us
  matrix products: 47.5 us -> 15.6 us
  loops' own time: 31.6 us -> 0 us
  starting transfers between devices: 127 us -> 96.3 us
  other arithmetic: 44.6 us -> 21.5 us
    ppermute x68 -> x86, waiting for transfers between devices: 382 us -> 234 us  [the longest x36 119 us: gather_chips(): lax.ppermute(rows, 'ctx', chip_perm(size, 2 * k))]
    pallas_call x10 -> x28, Pallas kernels: 122 us -> 206 us  [the longest x6 39.1 us: pick_rows(): pl.pallas_call(functools.partial(pick_kernel, experts, *heights), out_sha...]
    all_gather x6 -> x4, waiting for transfers between devices: 76.3 us -> 0.03 us  [all_streams(): return lax.all_gather(rows, 'dp', axis=0, tiled=True)]
    unnamed x17 -> x7, waiting for transfers between devices: 50.4 us -> 0.12 us
    dot_general x34 -> x10, matrix products: 47.5 us -> 15.6 us  [the longest x8 15.2 us: dot_tn(): lax.dot_general(left, right, (((0,), (0,)), ((), ())), preferred_element_...]
    slice x50 -> x3, local copies, waits for them, and re-layouts: 32.6 us -> 0.87 us  [the longest x1 0.62 us: local(): gains[layers + layer_idx][None]]
    another operation x12 -> x0, loops' own time: 31.6 us -> none  [the longest x2 15.8 us: local(): lax.scan(forward_block, init_carry, (pair_all.reshape(key_blocks, key_blo...]
    ppermute x68 -> x86, starting transfers between devices: 126 us -> 95.4 us  [the longest x36 52.9 us: gather_chips(): lax.ppermute(rows, 'ctx', chip_perm(size, 2 * k))]
  transfers between devices with their start and end apart: 81 -> 93, of which waited for: 39 -> 48; matrix products, arithmetic and copies ran while one was open for 9% -> 7% of each run, Pallas kernels for 15% -> 38%
where the time goes in v2:
time: 736 us; the launch traced here: 730 us
  Pallas kernels  299 us (41%)
  waiting for transfers between devices  242 us (33%)
  starting transfers between devices  96.3 us (13%)
  local copies, waits for them, and re-layouts  39.5 us (5%)
  other arithmetic  21.5 us (3%)
  between operations  16 us (2%)
  matrix products  15.6 us (2%)
    ppermute x36, waiting for transfers between devices, gather_chips(): lax.ppermute(rows, 'ctx', chip_perm(size, 2 * k))  119 us
    pallas_call x3, Pallas kernels, expert_grads(): pl.pallas_call(functools.partial(expert_grad_kernel, streams, before is n...  93 us
    ppermute x24, waiting for transfers between devices, reduce_finish(): lax.ppermute(piece, 'ctx', chip_perm(size, 2 * (k + 1)))  62.1 us
    ppermute x36, starting transfers between devices, gather_chips(): lax.ppermute(rows, 'ctx', chip_perm(size, 2 * k))  52.9 us
    pallas_call x6, Pallas kernels, pick_rows(): pl.pallas_call(functools.partial(pick_kernel, experts, *heights), out_sha...  39.1 us
    pallas_call x2, Pallas kernels, moe_bwd(): pl.pallas_call(functools.partial(moe_bwd_kernel, experts, len(pieces), ha...  37.2 us
    pallas_call x2, Pallas kernels, moe_fwd(): pl.pallas_call(functools.partial(moe_fwd_kernel, experts, len(pieces), ha...  37.1 us
    ppermute x24, starting transfers between devices, reduce_finish(): lax.ppermute(piece, 'ctx', chip_perm(size, 2 * (k + 1)))  36.9 us
  transfers between devices with their start and end apart: 93, of which 48 were waited for; matrix products, arithmetic and copies ran while one was open for 7% of the time, Pallas kernels for 38%

profile of v2, /device:TPU:0, one launch (start us, length us, event | category | flops | bytes accessed | tf_op | source)
XLA Modules:
  0.0 729.9 jit_solution(8914010636166377082)
XLA Ops:
  8.3 4.0 collective-permute-start.6
  12.9 6.5 collective-permute-done.6
  19.4 4.7 collective-permute-done.5
  30.8 5.6 collective-permute-done.8
  36.5 6.0 collective-permute-done.9
  51.5 3.8 collective-permute-done.12
  57.7 5.8 collective-permute-done.13
  73.6 4.9 collective-permute-done.32
  78.5 6.0 collective-permute-done.33
  86.9 4.4 project.4
  95.9 4.9 collective-permute-done.16
  100.8 3.9 collective-permute-done.17
  108.5 4.6 project.5
  114.1 7.3 attend.2
  128.2 4.4 collective-permute-done.22
  132.5 6.2 collective-permute-done.21
  144.9 11.2 %collective-permute-done.28 = bf16[128,2048]{1,0:T(8,128)(2,1)S(1)} collective-permute-done((bf16[128,2048]{1,0:T(8,128)(2,1)S(1)}, bf16[128,2048]{1,0:T(8,128)(2,1)S(1)}, u32[]{:S(2)}, u32[]{:S(2)}) %collective-permute-start.28) | collective-permute-done | bytes 524320 | tf_op jit(solution)/shard_map/ppermute | solution.py:56
  156.2 12.6 %collective-permute-done.29 = bf16[128,2048]{1,0:T(8,128)(2,1)} collective-permute-done((bf16[128,2048]{1,0:T(8,128)(2,1)S(1)}, bf16[128,2048]{1,0:T(8,128)(2,1)}, u32[]{:S(2)}, u32[]{:S(2)}) %collective-permute-start.29) | collective-permute-done | bytes 524320 | tf_op jit(solution)/shard_map/ppermute | solution.py:56
  170.1 19.0 %moe_fwd.2 = (bf16[512,1024]{1,0:T(8,128)(2,1)}, bf16[512,1024]{1,0:T(8,128)(2,1)}, bf16[4,320,1024]{2,1,0:T(8,128)(2,1)}, f32[4,320,128]{2,1,0:T(8,128)}, f32[4...) custom-call(s32[1]{0:T(128)} %bitcast.first_ref, bf16[512,1152]{1,0:T(8,128)(2,1)} %pad_maximum_fusion.1.refs_0_, ...), custom_call_target="tpu_custom_call" | custom-call | flops 4026531840 | bytes 24641536 | tf_op jit(solution)/shard_map/moe_fwd/pallas_call | solution.py:532
  204.8 6.4 collective-permute-done.27
  213.3 4.5 project.6
  218.5 7.5 %collective-permute-start.35 = (bf16[128,1024]{1,0:T(8,128)(2,1)}, bf16[128,1024]{1,0:T(8,128)(2,1)S(1)}, u32[]{:S(2)}, u32[]{:S(2)}) collective-permute-start(bf16[128,1024]{1,0:T(8,128)(2,1)} %get-tuple-element.242), channel_id=1, source_target_pairs={{0,2},{1,3},{2,0},{3,1},{4,6},{5,7},{6,4},{7,5},{8,10},{9,11},{10,... | collective-permute-start | bytes 786440 | tf_op jit(solution)/shard_map/ppermute | solution.py:56
  228.4 4.8 collective-permute-done.35
  233.3 4.0 collective-permute-done.37
  237.4 4.6 project.7
  243.1 7.4 %attend.3 = (bf16[128,1024]{1,0:T(8,128)(2,1)}, bf16[128,1024]{1,0:T(8,128)(2,1)}, f32[4,512,128]{2,1,0:T(8,128)}, f32[4,512,128]{2,1,0:T(8,128)}, f32[128,1024]...) custom-call(s32[8]{0:T(128)} %get-tuple-element.438.need_ref, s32[8]{0:T(128)} %copy-done.56, ...), custom_call_target="tpu_custom_call" | custom-call | flops 536870912 | bytes 6815744 | tf_op jit(solution)/shard_map/attend/pallas_call | solution.py:881
  250.5 3.6 collective-permute-start.45
  256.3 5.8 collective-permute-done.45
  262.1 6.1 collective-permute-done.44
  271.6 3.3 collective-permute-done.47.refs_1_
  276.0 18.2 %moe_fwd.3 = (bf16[512,1024]{1,0:T(8,128)(2,1)}, bf16[512,1024]{1,0:T(8,128)(2,1)}, bf16[4,320,1024]{2,1,0:T(8,128)(2,1)}, f32[4,320,128]{2,1,0:T(8,128)}, f32[4...) custom-call(s32[1]{0:T(128)} %bitcast.first_ref, bf16[512,1152]{1,0:T(8,128)(2,1)} %pad_maximum_fusion.2.refs_0_, ...), custom_call_target="tpu_custom_call" | custom-call | flops 4026531840 | bytes 24641536 | tf_op jit(solution)/shard_map/moe_fwd/pallas_call | solution.py:532
  295.2 18.4 %moe_bwd.2 = (bf16[512,1152]{1,0:T(8,128)(2,1)}, bf16[512,1152]{1,0:T(8,128)(2,1)}, bf16[4,320,1024]{2,1,0:T(8,128)(2,1)}, bf16[4,320,512]{2,1,0:T(8,128)(2,1)}, bf16[4,320,1024]{2,1,0:T(8,128)(2,1)}) custom-call(s32[1]{0:T(128)} %bitcast.first_ref, bf16[512,1024]{1,0:T(8,128)(2,1)} %copy-done.5, bf16[512,1024]{1,0:T(8,128)(2,1)} %copy-done.24, ...), custom_call_target="tpu_custom_call" | custom-call | flops 4026531840 | bytes 28573696 | tf_op jit(solution)/shard_map/moe_bwd/pallas_call | solution.py:578
  324.1 6.6 collective-permute-done.49.refs_5_
  330.6 7.0 collective-permute-done.50.refs_6_
  338.5 10.5 %attend_back.2 = (f32[128,1024]{1,0:T(8,128)}, bf16[128,1024]{1,0:T(8,128)(2,1)}, bf16[128,128]{1,0:T(8,128)(2,1)}, f32[1,1024]{1,0:T(1,128)}, bf16[128,1024]{1,...) custom-call(s32[8]{0:T(128)} %get-tuple-element.438.need_ref, s32[8]{0:T(128)} %copy-done.56, ...), custom_call_target="tpu_custom_call" | custom-call | flops 939524096 | bytes 10223616 | tf_op jit(solution)/shard_map/attend_back/pallas_call | solution.py:1042
  356.3 3.3 collective-permute-start.53
  366.9 7.1 collective-permute-done.54.refs_4_
  376.6 7.3 %project_back.2 = (f32[128,1024]{1,0:T(8,128)}, bf16[128,1024]{1,0:T(8,128)(2,1)}, bf16[128,2176]{1,0:T(8,128)(2,1)}, f32[1,1024]{1,0:T(1,128)}) custom-call(s32[8]{0:T(128)} %copy-done.56, bf16[512,2048]{1,0:T(8,128)(2,1)} %copy-done, bf16[512,2048]{1,0:T(8,128)(2,1)} %collective-permute-done.31.refs_1_, f32[128,1024]{1,0:T(8,128)} %get-tuple-element.266.refs_2_, ...), custom_call_target="tpu_custom_call" | custom-call | flops 536870912 | bytes 7340032 | tf_op jit(solution)/shard_map/project_back/pallas_call | solution.py:1128
  391.2 3.2 collective-permute-done.58
  394.4 3.8 collective-permute-done.57
  399.4 8.9 %collective-permute-done.60.refs_1_ = bf16[512,1024]{1,0:T(8,128)(2,1)S(1)} collective-permute-done((bf16[512,1024]{1,0:T(8,128)(2,1)S(1)}, bf16[512,1024]{1,0:T(8,128)(2,1)S(1)}, u32[]{:S(2)}, u32[]{:S(2)}) %collective-permute-start.60) | collective-permute-done | bytes 1048608 | tf_op jit(solution)/shard_map/ppermute | solution.py:48
  409.3 18.8 %moe_bwd.3 = (bf16[512,1152]{1,0:T(8,128)(2,1)}, bf16[512,1152]{1,0:T(8,128)(2,1)}, bf16[4,320,1024]{2,1,0:T(8,128)(2,1)}, bf16[4,320,512]{2,1,0:T(8,128)(2,1)}, bf16[4,320,1024]{2,1,0:T(8,128)(2,1)}) custom-call(s32[1]{0:T(128)} %bitcast.first_ref, bf16[512,1024]{1,0:T(8,128)(2,1)} %copy-done.1, bf16[512,1024]{1,0:T(8,128)(2,1)} %copy-done.25, ...), custom_call_target="tpu_custom_call" | custom-call | flops 4026531840 | bytes 28573696 | tf_op jit(solution)/shard_map/moe_bwd/pallas_call | solution.py:578
  431.9 7.2 collective-permute-done.64
  440.6 4.5 convolution_convert_fusion
  445.1 6.1 collective-permute-done.66
  460.4 6.7 pick_rows.8
  467.2 6.4 pick_rows.7
  473.6 6.5 pick_rows.6
  481.1 10.7 %attend_back.3 = (f32[128,1024]{1,0:T(8,128)}, bf16[128,1024]{1,0:T(8,128)(2,1)}, bf16[128,128]{1,0:T(8,128)(2,1)}, f32[1,1024]{1,0:T(1,128)}, bf16[128,1024]{1,...) custom-call(s32[8]{0:T(128)} %get-tuple-element.438.need_ref, s32[8]{0:T(128)} %copy-done.56, ...), custom_call_target="tpu_custom_call" | custom-call | flops 939524096 | bytes 10223616 | tf_op jit(solution)/shard_map/attend_back/pallas_call | solution.py:1042
  493.7 25.0 %expert_grads.3.refs_11_ = f32[2,4,1024,1536]{3,2,1,0:T(8,128)} custom-call(bf16[4,320,1024]{2,1,0:T(8,128)(2,1)} %get-tuple-element.314.refs_0_, bf16[4,320,1024]{2,1,0:T(8,128)(2,1)} %get-tuple-element.315.refs_1_, bf16[4,320,1024]{2,1,0:T(8,128)(2,1)} %get-tuple-element.316.refs_2_, bf16[4,320,1024]{2,1,0:T(8,128)(2,1)} %get-tuple-element.317.refs_3_, ...), custom_call_target="tpu_custom_call" | custom-call | flops 14092861440 | bytes 29360128 | tf_op jit(solution)/shard_map/expert_grads/pallas_call | solution.py:670
  525.1 4.2 collective-permute-start.73
  536.1 4.9 collective-permute-done.73.refs_6_
  543.5 7.4 %project_back.3 = (f32[128,1024]{1,0:T(8,128)}, bf16[128,1024]{1,0:T(8,128)(2,1)}, bf16[128,2176]{1,0:T(8,128)(2,1)}, f32[1,1024]{1,0:T(1,128)}) custom-call(s32[8]{0:T(128)} %copy-done.56, bf16[512,1024]{1,0:T(8,128)(2,1)} %copy-done.8, bf16[512,1024]{1,0:T(8,128)(2,1)} %copy-done.14, bf16[512,1024]{1,0:T(8,128)(2,1)} %copy-done.2, ...), custom_call_target="tpu_custom_call" | custom-call | flops 536870912 | bytes 7340032 | tf_op jit(solution)/shard_map/project_back/pallas_call | solution.py:1128
  558.9 3.2 fusion.near_ref
  563.5 4.4 fold.15
  574.6 25.7 %expert_grads.4.refs_11_ = f32[2,4,1024,1536]{3,2,1,0:T(8,128)} custom-call(bf16[4,320,1024]{2,1,0:T(8,128)(2,1)} %get-tuple-element.314.refs_0_, bf16[4,320,1024]{2,1,0:T(8,128)(2,1)} %get-tuple-element.315.refs_1_, bf16[4,320,1024]{2,1,0:T(8,128)(2,1)} %get-tuple-element.316.refs_2_, ...), custom_call_target="tpu_custom_call", output_to_operand_aliasing={{}: (11, {})} | custom-call | flops 14092861440 | bytes 29360128 | tf_op jit(solution)/shard_map/expert_grads/pallas_call | solution.py:670
  600.3 9.0 %collective-permute-done.81 = bf16[128,2176]{1,0:T(8,128)(2,1)S(1)} collective-permute-done((bf16[128,2176]{1,0:T(8,128)(2,1)}, bf16[128,2176]{1,0:T(8,128)(2,1)S(1)}, u32[]{:S(2)}, u32[]{:S(2)}) %collective-permute-start.81) | collective-permute-done | bytes 557088 | tf_op jit(solution)/shard_map/ppermute | solution.py:105
  611.5 20.1 %collective-permute-done.84 = bf16[128,3200]{1,0:T(8,128)(2,1)S(1)} collective-permute-done((bf16[128,3200]{1,0:T(8,128)(2,1)S(1)}, bf16[128,3200]{1,0:T(8,128)(2,1)S(1)}, u32[]{:S(2)}, u32[]{:S(2)}) %collective-permute-start.84) | collective-permute-done | bytes 819232 | tf_op jit(solution)/shard_map/ppermute | solution.py:119
  633.8 6.5 pick_rows.9
  640.3 6.5 pick_rows.11
  646.8 6.5 pick_rows.10
  654.5 42.4 %expert_grads.5 = f32[2,4,1024,1536]{3,2,1,0:T(8,128)} custom-call(bf16[4,320,1024]{2,1,0:T(8,128)(2,1)} %get-tuple-element.383.refs_0_, bf16[4,320,1024]{2,1,0:T(8,128)(2,1)} %get-tuple-element.384.refs_1_, bf16[4,320,1024]{2,1,0:T(8,128)(2,1)} %get-tuple-element.385.refs_2_, ...), custom_call_target="tpu_custom_call", output_to_operand_aliasing={{}: (11, {})} | custom-call | flops 28185722880 | bytes 58720256 | tf_op jit(solution)/shard_map/expert_grads/pallas_call | solution.py:670
  696.9 11.1 %collective-permute-done.85 = bf16[128,3200]{1,0:T(8,128)(2,1)S(1)} collective-permute-done((bf16[128,3200]{1,0:T(8,128)(2,1)S(1)}, bf16[128,3200]{1,0:T(8,128)(2,1)S(1)}, u32[]{:S(2)}, u32[]{:S(2)}) %collective-permute-start.85) | collective-permute-done | bytes 819232 | tf_op jit(solution)/shard_map/ppermute | solution.py:119
  708.1 8.7 %all-reduce.4.cloned.1.call-done = bf16[128,3072]{1,0:T(8,128)(2,1)} async-done(((bf16[128,3072]{1,0:T(8,128)(2,1)}), bf16[128,3072]{1,0:T(8,128)(2,1)}) %all-reduce.4.cloned.1.call-update) | async-done | bytes 786448 | tf_op jit(solution)/shard_map/psum | solution.py:1411
  (417 shorter events, 183.3 us)
Async XLA Ops:
  7.2 206.1 %all-gather.5.cloned.1.call-start = ((), (), s32[]{:S(2)}) async-start(), calls=%async_computation.2 | async-start | bytes 5242880 | tf_op jit(solution)/shard_map/all_gather | solution.py:114
  12.3 11.9 %collective-permute-start.5 = (bf16[128,1024]{1,0:T(8,128)(2,1)S(1)}, bf16[128,1024]{1,0:T(8,128)(2,1)S(1)}, u32[]{:S(2)}, u32[]{:S(2)}) collective-permute-start(bf16[128,1024]{1,0:T(8,128)(2,1)S(1)} %get-tuple-element.422), channel_id=1, source_target_pairs={{0,4},{1,5},{2,6},{3,7},{4,0},{5,1},{6,2},{7,3},{8,12},{9,13},{10,... | collective-permute-start | bytes 786440 | tf_op jit(solution)/shard_map/ppermute | solution.py:56
  12.8 11.7 %collective-permute-start.4 = (bf16[128,1024]{1,0:T(8,128)(2,1)S(1)}, bf16[128,1024]{1,0:T(8,128)(2,1)S(1)}, u32[]{:S(2)}, u32[]{:S(2)}) collective-permute-start(bf16[128,1024]{1,0:T(8,128)(2,1)S(1)} %get-tuple-element.422), channel_id=1, source_target_pairs={{0,2},{1,3},{2,0},{3,1},{4,6},{5,7},{6,4},{7,5},{8,10},{9,11},{10,... | collective-permute-start | bytes 786440 | tf_op jit(solution)/shard_map/ppermute | solution.py:56
  28.8 13.7 %collective-permute-start.9 = (bf16[128,1024]{1,0:T(8,128)(2,1)S(1)}, bf16[128,1024]{1,0:T(8,128)(2,1)S(1)}, u32[]{:S(2)}, u32[]{:S(2)}) collective-permute-start(bf16[128,1024]{1,0:T(8,128)(2,1)S(1)} %get-tuple-element.204), channel_id=1, source_target_pairs={{0,4},{1,5},{2,6},{3,7},{4,0},{5,1},{6,2},{7,3},{8,12},{9,13},{10,... | collective-permute-start | bytes 786440 | tf_op jit(solution)/shard_map/ppermute | solution.py:56
  29.4 13.1 %collective-permute-start.10 = (bf16[128,1024]{1,0:T(8,128)(2,1)S(1)}, bf16[128,1024]{1,0:T(8,128)(2,1)S(1)}, u32[]{:S(2)}, u32[]{:S(2)}) collective-permute-start(bf16[128,1024]{1,0:T(8,128)(2,1)S(1)} %get-tuple-element.204), channel_id=1, source_target_pairs={{0,6},{1,7},{2,4},{3,5},{4,2},{5,3},{6,0},{7,1},{8,14},{9,15},{10,... | collective-permute-start | bytes 786440 | tf_op jit(solution)/shard_map/ppermute | solution.py:56
  46.5 19.3 %collective-permute-start.2 = (bf16[8,128]{1,0:T(8,128)(2,1)S(1)}, bf16[8,128]{1,0:T(8,128)(2,1)S(1)}, u32[]{:S(2)}, u32[]{:S(2)}) collective-permute-start(bf16[8,128]{1,0:T(8,128)(2,1)S(1)} %pad_maximum_fusion.11), channel_id=1, source_target_pairs={{0,6},{1,7},{2,4},{3,5},{4,2},{5,3},{6,0},{7,1},{8,14},{9,15},{10,... | collective-permute-start | bytes 6152 | tf_op jit(solution)/shard_map/ppermute | solution.py:56
  48.1 17.7 %collective-permute-start.1 = (bf16[8,128]{1,0:T(8,128)(2,1)S(1)}, bf16[8,128]{1,0:T(8,128)(2,1)S(1)}, u32[]{:S(2)}, u32[]{:S(2)}) collective-permute-start(bf16[8,128]{1,0:T(8,128)(2,1)S(1)} %pad_maximum_fusion.11), channel_id=1, source_target_pairs={{0,4},{1,5},{2,6},{3,7},{4,0},{5,1},{6,2},{7,3},{8,12},{9,13},{10,... | collective-permute-start | bytes 6152 | tf_op jit(solution)/shard_map/ppermute | solution.py:56
  49.5 16.3 %collective-permute-start = (bf16[8,128]{1,0:T(8,128)(2,1)S(1)}, bf16[8,128]{1,0:T(8,128)(2,1)S(1)}, u32[]{:S(2)}, u32[]{:S(2)}) collective-permute-start(bf16[8,128]{1,0:T(8,128)(2,1)S(1)} %pad_maximum_fusion.11), channel_id=1, source_target_pairs={{0,2},{1,3},{2,0},{3,1},{4,6},{5,7},{6,4},{7,5},{8,10},{9,11},{10,... | collective-permute-start | bytes 6152 | tf_op jit(solution)/shard_map/ppermute | solution.py:56
  50.1 13.4 %collective-permute-start.13 = (bf16[128,1152]{1,0:T(8,128)(2,1)S(1)}, bf16[128,1152]{1,0:T(8,128)(2,1)S(1)}, u32[]{:S(2)}, u32[]{:S(2)}) collective-permute-start(bf16[128,1152]{1,0:T(8,128)(2,1)S(1)} %concatenate.83), channel_id=1, source_target_pairs={{0,4},{1,5},{2,6},{3,7},{4,0},{5,1},{6,2},{7,3},{8,12},{9,13},{10,... | collective-permute-start | bytes 884744 | tf_op jit(solution)/shard_map/ppermute | solution.py:56
  70.5 13.9 %collective-permute-start.33 = (bf16[128,1024]{1,0:T(8,128)(2,1)}, bf16[128,1024]{1,0:T(8,128)(2,1)S(1)}, u32[]{:S(2)}, u32[]{:S(2)}) collective-permute-start(bf16[128,1024]{1,0:T(8,128)(2,1)} %bitcast.4.refs_16_), channel_id=1, source_target_pairs={{0,4},{1,5},{2,6},{3,7},{4,0},{5,1},{6,2},{7,3},{8,12},{9,13},{10,... | collective-permute-start | bytes 786440 | tf_op jit(solution)/shard_map/ppermute | solution.py:56
  71.1 13.4 %collective-permute-start.34 = (bf16[128,1024]{1,0:T(8,128)(2,1)}, bf16[128,1024]{1,0:T(8,128)(2,1)S(1)}, u32[]{:S(2)}, u32[]{:S(2)}) collective-permute-start(bf16[128,1024]{1,0:T(8,128)(2,1)} %bitcast.4.refs_16_), channel_id=1, source_target_pairs={{0,6},{1,7},{2,4},{3,5},{4,2},{5,3},{6,0},{7,1},{8,14},{9,15},{10,... | collective-permute-start | bytes 786440 | tf_op jit(solution)/shard_map/ppermute | solution.py:56
  85.5 185.1 %all-gather.7.cloned.1.call-start = ((), (), s32[]{:S(2)}) async-start(), calls=%async_computation.3 | async-start | bytes 5898240 | tf_op jit(solution)/shard_map/all_gather | solution.py:114
  91.9 12.8 %collective-permute-start.17 = (bf16[128,1024]{1,0:T(8,128)(2,1)}, bf16[128,1024]{1,0:T(8,128)(2,1)S(1)}, u32[]{:S(2)}, u32[]{:S(2)}) collective-permute-start(bf16[128,1024]{1,0:T(8,128)(2,1)} %get-tuple-element.221), channel_id=1, source_target_pairs={{0,4},{1,5},{2,6},{3,7},{4,0},{5,1},{6,2},{7,3},{8,12},{9,13},{10,... | collective-permute-start | bytes 786440 | tf_op jit(solution)/shard_map/ppermute | solution.py:56
  123.6 15.1 %collective-permute-start.21 = (bf16[128,1152]{1,0:T(8,128)(2,1)}, bf16[128,1152]{1,0:T(8,128)(2,1)S(1)}, u32[]{:S(2)}, u32[]{:S(2)}) collective-permute-start(bf16[128,1152]{1,0:T(8,128)(2,1)} %get-tuple-element.229), channel_id=1, source_target_pairs={{0,4},{1,5},{2,6},{3,7},{4,0},{5,1},{6,2},{7,3},{8,12},{9,13},{10,... | collective-permute-start | bytes 884744 | tf_op jit(solution)/shard_map/ppermute | solution.py:56
  125.7 13.2 %collective-permute-start.20 = (bf16[128,1152]{1,0:T(8,128)(2,1)}, bf16[128,1152]{1,0:T(8,128)(2,1)S(1)}, u32[]{:S(2)}, u32[]{:S(2)}) collective-permute-start(bf16[128,1152]{1,0:T(8,128)(2,1)} %get-tuple-element.229), channel_id=1, source_target_pairs={{0,2},{1,3},{2,0},{3,1},{4,6},{5,7},{6,4},{7,5},{8,10},{9,11},{10,... | collective-permute-start | bytes 884744 | tf_op jit(solution)/shard_map/ppermute | solution.py:56
  141.0 257.3 %all-gather.9.cloned.1.call-start = ((), (), s32[]{:S(2)}) async-start(), calls=%async_computation.4 | async-start | bytes 5898240 | tf_op jit(solution)/shard_map/all_gather | solution.py:114
  141.3 14.8 %collective-permute-start.28 = (bf16[128,2048]{1,0:T(8,128)(2,1)S(1)}, bf16[128,2048]{1,0:T(8,128)(2,1)S(1)}, u32[]{:S(2)}, u32[]{:S(2)}) collective-permute-start(bf16[128,2048]{1,0:T(8,128)(2,1)S(1)} %slice_bitcast_fusion.4), channel_id=1, source_target_pairs={{0,2},{1,3},{2,0},{3,1},{4,6},{5,7},{6,4},{7,5},{8,10},{9,11},{10,... | collective-permute-start | bytes 1572872 | tf_op jit(solution)/shard_map/ppermute | solution.py:56
  143.1 26.9 %collective-permute-start.23 = (bf16[512,1152]{1,0:T(8,128)(2,1)}, bf16[512,1152]{1,0:T(8,128)(2,1)}, u32[]{:S(2)}, u32[]{:S(2)}) collective-permute-start(bf16[512,1152]{1,0:T(8,128)(2,1)} %pad_maximum_fusion.1.refs_0_), channel_id=1, source_target_pairs={{0,1},{1,0},{2,3},{3,2},{4,5},{5,4},{6,7},{7,6},{8,9},{9,8},{10,11... | collective-permute-start | bytes 3538952 | tf_op jit(solution)/shard_map/ppermute | solution.py:48
  143.1 25.7 %collective-permute-start.29 = (bf16[128,2048]{1,0:T(8,128)(2,1)S(1)}, bf16[128,2048]{1,0:T(8,128)(2,1)}, u32[]{:S(2)}, u32[]{:S(2)}) collective-permute-start(bf16[128,2048]{1,0:T(8,128)(2,1)S(1)} %slice_bitcast_fusion.4), channel_id=1, source_target_pairs={{0,4},{1,5},{2,6},{3,7},{4,0},{5,1},{6,2},{7,3},{8,12},{9,13},{10,... | collective-permute-start | bytes 1572872 | tf_op jit(solution)/shard_map/ppermute | solution.py:56
  144.6 25.3 %collective-permute-start.30 = (bf16[128,2048]{1,0:T(8,128)(2,1)S(1)}, bf16[128,2048]{1,0:T(8,128)(2,1)S(1)}, u32[]{:S(2)}, u32[]{:S(2)}) collective-permute-start(bf16[128,2048]{1,0:T(8,128)(2,1)S(1)} %slice_bitcast_fusion.4), channel_id=1, source_target_pairs={{0,6},{1,7},{2,4},{3,5},{4,2},{5,3},{6,0},{7,1},{8,14},{9,15},{10,... | collective-permute-start | bytes 1572872 | tf_op jit(solution)/shard_map/ppermute | solution.py:56
  170.0 43.3 %collective-permute-start.31 = (bf16[512,2048]{1,0:T(8,128)(2,1)S(1)}, bf16[512,2048]{1,0:T(8,128)(2,1)}, u32[]{:S(2)}, u32[]{:S(2)}) collective-permute-start(bf16[512,2048]{1,0:T(8,128)(2,1)S(1)} %constant_dynamic-update-slice_fusion.12.refs_0_), channel_id=1, source_target_pairs={{0,1},{1,0},{2,3},{3,2},{4,5},{5,4},{6,7},{7,6},{8,9},{9,8},{10,11... | collective-permute-start | bytes 6291464 | tf_op jit(solution)/shard_map/ppermute | solution.py:48
  189.2 12.0 %collective-permute-start.40 = (bf16[128,1152]{1,0:T(8,128)(2,1)}, bf16[128,1152]{1,0:T(8,128)(2,1)}, u32[]{:S(2)}, u32[]{:S(2)}) collective-permute-start(bf16[128,1152]{1,0:T(8,128)(2,1)} %concatenate.79), channel_id=1, source_target_pairs={{0,4},{1,5},{2,6},{3,7},{4,0},{5,1},{6,2},{7,3},{8,12},{9,13},{10,... | collective-permute-start | bytes 884744 | tf_op jit(solution)/shard_map/ppermute | solution.py:56
  199.3 11.9 %collective-permute-start.27 = (bf16[128,1024]{1,0:T(8,128)(2,1)}, bf16[128,1024]{1,0:T(8,128)(2,1)S(1)}, u32[]{:S(2)}, u32[]{:S(2)}) collective-permute-start(bf16[128,1024]{1,0:T(8,128)(2,1)} %get-tuple-element.236), channel_id=1, source_target_pairs={{0,6},{1,7},{2,4},{3,5},{4,2},{5,3},{6,0},{7,1},{8,14},{9,15},{10,... | collective-permute-start | bytes 786440 | tf_op jit(solution)/shard_map/ppermute | solution.py:105
  201.2 24.8 %collective-permute-start.41 = (bf16[128,1152]{1,0:T(8,128)(2,1)}, bf16[128,1152]{1,0:T(8,128)(2,1)}, u32[]{:S(2)}, u32[]{:S(2)}) collective-permute-start(bf16[128,1152]{1,0:T(8,128)(2,1)} %concatenate.79), channel_id=1, source_target_pairs={{0,6},{1,7},{2,4},{3,5},{4,2},{5,3},{6,0},{7,1},{8,14},{9,15},{10,... | collective-permute-start | bytes 884744 | tf_op jit(solution)/shard_map/ppermute | solution.py:56
  217.8 15.4 %collective-permute-start.36 = (bf16[128,1024]{1,0:T(8,128)(2,1)}, bf16[128,1024]{1,0:T(8,128)(2,1)S(1)}, u32[]{:S(2)}, u32[]{:S(2)}) collective-permute-start(bf16[128,1024]{1,0:T(8,128)(2,1)} %get-tuple-element.242), channel_id=1, source_target_pairs={{0,4},{1,5},{2,6},{3,7},{4,0},{5,1},{6,2},{7,3},{8,12},{9,13},{10,... | collective-permute-start | bytes 786440 | tf_op jit(solution)/shard_map/ppermute | solution.py:56
  218.5 14.7 %collective-permute-start.35 = (bf16[128,1024]{1,0:T(8,128)(2,1)}, bf16[128,1024]{1,0:T(8,128)(2,1)S(1)}, u32[]{:S(2)}, u32[]{:S(2)}) collective-permute-start(bf16[128,1024]{1,0:T(8,128)(2,1)} %get-tuple-element.242), channel_id=1, source_target_pairs={{0,2},{1,3},{2,0},{3,1},{4,6},{5,7},{6,4},{7,5},{8,10},{9,11},{10,... | collective-permute-start | bytes 786440 | tf_op jit(solution)/shard_map/ppermute | solution.py:56
  227.0 15.0 %collective-permute-start.42 = (bf16[512,1152]{1,0:T(8,128)(2,1)S(1)}, bf16[512,1152]{1,0:T(8,128)(2,1)S(1)}, u32[]{:S(2)}, u32[]{:S(2)}) collective-permute-start(bf16[512,1152]{1,0:T(8,128)(2,1)S(1)} %constant_dynamic-update-slice_fusion.24.refs_2_), channel_id=1, source_target_pairs={{0,1},{1,0},{2,3},{3,2},{4,5},{5,4},{6,7},{7,6},{8,9},{9,8},{10,11... | collective-permute-start | bytes 3538952 | tf_op jit(solution)/shard_map/ppermute | solution.py:48
  254.0 14.2 %collective-permute-start.44 = (bf16[128,1152]{1,0:T(8,128)(2,1)}, bf16[128,1152]{1,0:T(8,128)(2,1)S(1)}, u32[]{:S(2)}, u32[]{:S(2)}) collective-permute-start(bf16[128,1152]{1,0:T(8,128)(2,1)} %get-tuple-element.245), channel_id=1, source_target_pairs={{0,4},{1,5},{2,6},{3,7},{4,0},{5,1},{6,2},{7,3},{8,12},{9,13},{10,... | collective-permute-start | bytes 884744 | tf_op jit(solution)/shard_map/ppermute | solution.py:56
  255.1 13.4 %collective-permute-start.43 = (bf16[128,1152]{1,0:T(8,128)(2,1)}, bf16[128,1152]{1,0:T(8,128)(2,1)S(1)}, u32[]{:S(2)}, u32[]{:S(2)}) collective-permute-start(bf16[128,1152]{1,0:T(8,128)(2,1)} %get-tuple-element.245), channel_id=1, source_target_pairs={{0,2},{1,3},{2,0},{3,1},{4,6},{5,7},{6,4},{7,5},{8,10},{9,11},{10,... | collective-permute-start | bytes 884744 | tf_op jit(solution)/shard_map/ppermute | solution.py:56
  270.6 209.5 %reduce-scatter.3.cloned.1.call-start = ((), (), s32[]{:S(2)}) async-start(), calls=%async_computation.5 | async-start | bytes 2359296 | tf_op jit(solution)/shard_map/reduce_scatter | solution.py:1359
  271.2 23.0 %collective-permute-start.46 = (bf16[512,1024]{1,0:T(8,128)(2,1)S(1)}, bf16[512,1024]{1,0:T(8,128)(2,1)S(1)}, u32[]{:S(2)}, u32[]{:S(2)}) collective-permute-start(bf16[512,1024]{1,0:T(8,128)(2,1)S(1)} %copy-done.6), channel_id=1, source_target_pairs={{0,1},{1,0},{2,3},{3,2},{4,5},{5,4},{6,7},{7,6},{8,9},{9,8},{10,11... | collective-permute-start | bytes 3145736 | tf_op jit(solution)/shard_map/ppermute | solution.py:48
  322.4 15.3 %collective-permute-start.50 = (bf16[128,1152]{1,0:T(8,128)(2,1)}, bf16[128,1152]{1,0:T(8,128)(2,1)S(1)}, u32[]{:S(2)}, u32[]{:S(2)}) collective-permute-start(bf16[128,1152]{1,0:T(8,128)(2,1)} %get-tuple-element.255), channel_id=1, source_target_pairs={{0,4},{1,5},{2,6},{3,7},{4,0},{5,1},{6,2},{7,3},{8,12},{9,13},{10,... | collective-permute-start | bytes 884744 | tf_op jit(solution)/shard_map/ppermute | solution.py:105
  322.9 14.8 %collective-permute-start.51 = (bf16[128,1152]{1,0:T(8,128)(2,1)}, bf16[128,1152]{1,0:T(8,128)(2,1)S(1)}, u32[]{:S(2)}, u32[]{:S(2)}) collective-permute-start(bf16[128,1152]{1,0:T(8,128)(2,1)} %get-tuple-element.256), channel_id=1, source_target_pairs={{0,6},{1,7},{2,4},{3,5},{4,2},{5,3},{6,0},{7,1},{8,14},{9,15},{10,... | collective-permute-start | bytes 884744 | tf_op jit(solution)/shard_map/ppermute | solution.py:105
  349.1 38.4 %collective-permute-start.59 = (bf16[512,1024]{1,0:T(8,128)(2,1)S(1)}, bf16[512,1024]{1,0:T(8,128)(2,1)S(1)}, u32[]{:S(2)}, u32[]{:S(2)}) collective-permute-start(bf16[512,1024]{1,0:T(8,128)(2,1)S(1)} %copy-done.69), channel_id=1, source_target_pairs={{0,1},{1,0},{2,3},{3,2},{4,5},{5,4},{6,7},{7,6},{8,9},{9,8},{10,11... | collective-permute-start | bytes 3145736 | tf_op jit(solution)/shard_map/ppermute | solution.py:48
  359.6 14.4 %collective-permute-start.54 = (bf16[128,1024]{1,0:T(8,128)(2,1)}, bf16[128,1024]{1,0:T(8,128)(2,1)S(1)}, u32[]{:S(2)}, u32[]{:S(2)}) collective-permute-start(bf16[128,1024]{1,0:T(8,128)(2,1)} %get-tuple-element.268), channel_id=1, source_target_pairs={{0,4},{1,5},{2,6},{3,7},{4,0},{5,1},{6,2},{7,3},{8,12},{9,13},{10,... | collective-permute-start | bytes 786440 | tf_op jit(solution)/shard_map/ppermute | solution.py:105
  362.2 13.6 %collective-permute-start.55 = (bf16[128,1024]{1,0:T(8,128)(2,1)}, bf16[128,1024]{1,0:T(8,128)(2,1)S(1)}, u32[]{:S(2)}, u32[]{:S(2)}) collective-permute-start(bf16[128,1024]{1,0:T(8,128)(2,1)} %get-tuple-element.269), channel_id=1, source_target_pairs={{0,6},{1,7},{2,4},{3,5},{4,2},{5,3},{6,0},{7,1},{8,14},{9,15},{10,... | collective-permute-start | bytes 786440 | tf_op jit(solution)/shard_map/ppermute | solution.py:105
  385.8 12.4 %collective-permute-start.57 = (bf16[128,1024]{1,0:T(8,128)(2,1)}, bf16[128,1024]{1,0:T(8,128)(2,1)S(1)}, u32[]{:S(2)}, u32[]{:S(2)}) collective-permute-start(bf16[128,1024]{1,0:T(8,128)(2,1)} %get-tuple-element.272), channel_id=1, source_target_pairs={{0,4},{1,5},{2,6},{3,7},{4,0},{5,1},{6,2},{7,3},{8,12},{9,13},{10,... | collective-permute-start | bytes 786440 | tf_op jit(solution)/shard_map/ppermute | solution.py:56
  386.1 12.1 %collective-permute-start.56 = (bf16[128,1024]{1,0:T(8,128)(2,1)}, bf16[128,1024]{1,0:T(8,128)(2,1)S(1)}, u32[]{:S(2)}, u32[]{:S(2)}) collective-permute-start(bf16[128,1024]{1,0:T(8,128)(2,1)} %get-tuple-element.272), channel_id=1, source_target_pairs={{0,2},{1,3},{2,0},{3,1},{4,6},{5,7},{6,4},{7,5},{8,10},{9,11},{10,... | collective-permute-start | bytes 786440 | tf_op jit(solution)/shard_map/ppermute | solution.py:56
  391.2 218.1 %all-gather.11.cloned.1.call-start = ((), (), s32[]{:S(2)}) async-start(), calls=%async_computation.7 | async-start | bytes 5242880 | tf_op jit(solution)/shard_map/all_gather | solution.py:114
  398.3 62.1 %collective-permute-start.62 = (bf16[2048,1152]{1,0:T(8,128)(2,1)}, bf16[2048,1152]{1,0:T(8,128)(2,1)}, u32[]{:S(2)}, u32[]{:S(2)}) collective-permute-start(bf16[2048,1152]{1,0:T(8,128)(2,1)} %all-gather.9.cloned.1.call-done.refs_0_), channel_id=1, source_target_pairs={{0,1},{1,0},{2,3},{3,2},{4,5},{5,4},{6,7},{7,6},{8,9},{9,8},{10,11... | collective-permute-start | bytes 14155784 | tf_op jit(solution)/shard_map/ppermute | solution.py:48
  398.4 62.0 %collective-permute-start.63 = (bf16[2048,1024]{1,0:T(8,128)(2,1)}, bf16[2048,1024]{1,0:T(8,128)(2,1)}, u32[]{:S(2)}, u32[]{:S(2)}) collective-permute-start(bf16[2048,1024]{1,0:T(8,128)(2,1)} %all-gather.5.cloned.1.call-done.refs_2_), channel_id=1, source_target_pairs={{0,1},{1,0},{2,3},{3,2},{4,5},{5,4},{6,7},{7,6},{8,9},{9,8},{10,11... | collective-permute-start | bytes 12582920 | tf_op jit(solution)/shard_map/ppermute | solution.py:48
  399.3 232.5 %reduce-scatter.5.cloned.1.call-start = ((), (), s32[]{:S(2)}) async-start(), calls=%async_computation.6 | async-start | bytes 4718592 | tf_op jit(solution)/shard_map/reduce_scatter | solution.py:1314
  428.1 25.0 %collective-permute-start.61 = (bf16[512,1152]{1,0:T(8,128)(2,1)}, bf16[512,1152]{1,0:T(8,128)(2,1)S(1)}, u32[]{:S(2)}, u32[]{:S(2)}) collective-permute-start(bf16[512,1152]{1,0:T(8,128)(2,1)} %get-tuple-element.285), channel_id=1, source_target_pairs={{0,1},{1,0},{2,3},{3,2},{4,5},{5,4},{6,7},{7,6},{8,9},{9,8},{10,11... | collective-permute-start | bytes 3538952 | tf_op jit(solution)/shard_map/ppermute | solution.py:48
  430.6 14.5 %collective-permute-start.65 = (bf16[128,1024]{1,0:T(8,128)(2,1)}, bf16[128,1024]{1,0:T(8,128)(2,1)S(1)}, u32[]{:S(2)}, u32[]{:S(2)}) collective-permute-start(bf16[128,1024]{1,0:T(8,128)(2,1)} %get-tuple-element.300), channel_id=1, source_target_pairs={{0,4},{1,5},{2,6},{3,7},{4,0},{5,1},{6,2},{7,3},{8,12},{9,13},{10,... | collective-permute-start | bytes 786440 | tf_op jit(solution)/shard_map/ppermute | solution.py:105
  439.1 12.1 %collective-permute-start.66 = (bf16[128,1024]{1,0:T(8,128)(2,1)}, bf16[128,1024]{1,0:T(8,128)(2,1)}, u32[]{:S(2)}, u32[]{:S(2)}) collective-permute-start(bf16[128,1024]{1,0:T(8,128)(2,1)} %get-tuple-element.301), channel_id=1, source_target_pairs={{0,6},{1,7},{2,4},{3,5},{4,2},{5,3},{6,0},{7,1},{8,14},{9,15},{10,... | collective-permute-start | bytes 786440 | tf_op jit(solution)/shard_map/ppermute | solution.py:105
  456.9 23.2 %collective-permute-start.67 = (bf16[128,1152]{1,0:T(8,128)(2,1)}, bf16[128,1152]{1,0:T(8,128)(2,1)S(1)}, u32[]{:S(2)}, u32[]{:S(2)}) collective-permute-start(bf16[128,1152]{1,0:T(8,128)(2,1)} %get-tuple-element.304), channel_id=1, source_target_pairs={{0,2},{1,3},{2,0},{3,1},{4,6},{5,7},{6,4},{7,5},{8,10},{9,11},{10,... | collective-permute-start | bytes 884744 | tf_op jit(solution)/shard_map/ppermute | solution.py:105
  457.0 23.2 %collective-permute-start.68 = (bf16[128,1152]{1,0:T(8,128)(2,1)}, bf16[128,1152]{1,0:T(8,128)(2,1)S(1)}, u32[]{:S(2)}, u32[]{:S(2)}) collective-permute-start(bf16[128,1152]{1,0:T(8,128)(2,1)} %get-tuple-element.305), channel_id=1, source_target_pairs={{0,4},{1,5},{2,6},{3,7},{4,0},{5,1},{6,2},{7,3},{8,12},{9,13},{10,... | collective-permute-start | bytes 884744 | tf_op jit(solution)/shard_map/ppermute | solution.py:105
  459.0 21.2 %collective-permute-start.69 = (bf16[128,1152]{1,0:T(8,128)(2,1)}, bf16[128,1152]{1,0:T(8,128)(2,1)S(1)}, u32[]{:S(2)}, u32[]{:S(2)}) collective-permute-start(bf16[128,1152]{1,0:T(8,128)(2,1)} %get-tuple-element.306), channel_id=1, source_target_pairs={{0,6},{1,7},{2,4},{3,5},{4,2},{5,3},{6,0},{7,1},{8,14},{9,15},{10,... | collective-permute-start | bytes 884744 | tf_op jit(solution)/shard_map/ppermute | solution.py:105
  493.2 39.3 %collective-permute-start.71 = (bf16[512,1024]{1,0:T(8,128)(2,1)S(1)}, bf16[512,1024]{1,0:T(8,128)(2,1)S(1)}, u32[]{:S(2)}, u32[]{:S(2)}) collective-permute-start(bf16[512,1024]{1,0:T(8,128)(2,1)S(1)} %convolution_convert_fusion.2), channel_id=1, source_target_pairs={{0,1},{1,0},{2,3},{3,2},{4,5},{5,4},{6,7},{7,6},{8,9},{9,8},{10,11... | collective-permute-start | bytes 3145736 | tf_op jit(solution)/shard_map/ppermute | solution.py:48
  493.2 25.5 %collective-permute-start.70 = (bf16[512,1024]{1,0:T(8,128)(2,1)}, bf16[512,1024]{1,0:T(8,128)(2,1)S(1)}, u32[]{:S(2)}, u32[]{:S(2)}) collective-permute-start(bf16[512,1024]{1,0:T(8,128)(2,1)} %get-tuple-element.312), channel_id=1, source_target_pairs={{0,1},{1,0},{2,3},{3,2},{4,5},{5,4},{6,7},{7,6},{8,9},{9,8},{10,11... | collective-permute-start | bytes 3145736 | tf_op jit(solution)/shard_map/ppermute | solution.py:48
  522.4 13.7 %collective-permute-start.72 = (bf16[128,1024]{1,0:T(8,128)(2,1)}, bf16[128,1024]{1,0:T(8,128)(2,1)S(1)}, u32[]{:S(2)}, u32[]{:S(2)}) collective-permute-start(bf16[128,1024]{1,0:T(8,128)(2,1)} %get-tuple-element.331), channel_id=1, source_target_pairs={{0,2},{1,3},{2,0},{3,1},{4,6},{5,7},{6,4},{7,5},{8,10},{9,11},{10,... | collective-permute-start | bytes 786440 | tf_op jit(solution)/shard_map/ppermute | solution.py:105
  525.1 15.9 %collective-permute-start.73 = (bf16[128,1024]{1,0:T(8,128)(2,1)}, bf16[128,1024]{1,0:T(8,128)(2,1)S(1)}, u32[]{:S(2)}, u32[]{:S(2)}) collective-permute-start(bf16[128,1024]{1,0:T(8,128)(2,1)} %get-tuple-element.332), channel_id=1, source_target_pairs={{0,4},{1,5},{2,6},{3,7},{4,0},{5,1},{6,2},{7,3},{8,12},{9,13},{10,... | collective-permute-start | bytes 786440 | tf_op jit(solution)/shard_map/ppermute | solution.py:105
  529.3 13.5 %collective-permute-start.74 = (bf16[128,1024]{1,0:T(8,128)(2,1)}, bf16[128,1024]{1,0:T(8,128)(2,1)S(1)}, u32[]{:S(2)}, u32[]{:S(2)}) collective-permute-start(bf16[128,1024]{1,0:T(8,128)(2,1)} %get-tuple-element.333), channel_id=1, source_target_pairs={{0,6},{1,7},{2,4},{3,5},{4,2},{5,3},{6,0},{7,1},{8,14},{9,15},{10,... | collective-permute-start | bytes 786440 | tf_op jit(solution)/shard_map/ppermute | solution.py:105
  555.3 161.6 %all-reduce.4.cloned.1.call-start = ((), (), s32[]{:S(2)}) async-start(), calls=%async_computation.8 | async-start | bytes 1572864 | tf_op jit(solution)/shard_map/psum | solution.py:1411
  555.3 12.6 %collective-permute-start.76 = (bf16[128,1024]{1,0:T(8,128)(2,1)}, bf16[128,1024]{1,0:T(8,128)(2,1)S(1)}, u32[]{:S(2)}, u32[]{:S(2)}) collective-permute-start(bf16[128,1024]{1,0:T(8,128)(2,1)} %get-tuple-element.354), channel_id=1, source_target_pairs={{0,2},{1,3},{2,0},{3,1},{4,6},{5,7},{6,4},{7,5},{8,10},{9,11},{10,... | collective-permute-start | bytes 786440 | tf_op jit(solution)/shard_map/ppermute | solution.py:105
  556.1 14.3 %collective-permute-start.77 = (bf16[128,1024]{1,0:T(8,128)(2,1)}, bf16[128,1024]{1,0:T(8,128)(2,1)S(1)}, u32[]{:S(2)}, u32[]{:S(2)}) collective-permute-start(bf16[128,1024]{1,0:T(8,128)(2,1)} %get-tuple-element.355), channel_id=1, source_target_pairs={{0,4},{1,5},{2,6},{3,7},{4,0},{5,1},{6,2},{7,3},{8,12},{9,13},{10,... | collective-permute-start | bytes 786440 | tf_op jit(solution)/shard_map/ppermute | solution.py:105
  557.8 12.5 %collective-permute-start.78 = (bf16[128,1024]{1,0:T(8,128)(2,1)}, bf16[128,1024]{1,0:T(8,128)(2,1)S(1)}, u32[]{:S(2)}, u32[]{:S(2)}) collective-permute-start(bf16[128,1024]{1,0:T(8,128)(2,1)} %get-tuple-element.356), channel_id=1, source_target_pairs={{0,6},{1,7},{2,4},{3,5},{4,2},{5,3},{6,0},{7,1},{8,14},{9,15},{10,... | collective-permute-start | bytes 786440 | tf_op jit(solution)/shard_map/ppermute | solution.py:105
  571.1 29.2 %collective-permute-start.79 = (bf16[128,2176]{1,0:T(8,128)(2,1)}, bf16[128,2176]{1,0:T(8,128)(2,1)S(1)}, u32[]{:S(2)}, u32[]{:S(2)}) collective-permute-start(bf16[128,2176]{1,0:T(8,128)(2,1)} %get-tuple-element.359), channel_id=1, source_target_pairs={{0,2},{1,3},{2,0},{3,1},{4,6},{5,7},{6,4},{7,5},{8,10},{9,11},{10,... | collective-permute-start | bytes 1671176 | tf_op jit(solution)/shard_map/ppermute | solution.py:105
  572.5 27.8 %collective-permute-start.80 = (bf16[128,2176]{1,0:T(8,128)(2,1)}, bf16[128,2176]{1,0:T(8,128)(2,1)S(1)}, u32[]{:S(2)}, u32[]{:S(2)}) collective-permute-start(bf16[128,2176]{1,0:T(8,128)(2,1)} %get-tuple-element.360), channel_id=1, source_target_pairs={{0,4},{1,5},{2,6},{3,7},{4,0},{5,1},{6,2},{7,3},{8,12},{9,13},{10,... | collective-permute-start | bytes 1671176 | tf_op jit(solution)/shard_map/ppermute | solution.py:105
  573.2 36.1 %collective-permute-start.81 = (bf16[128,2176]{1,0:T(8,128)(2,1)}, bf16[128,2176]{1,0:T(8,128)(2,1)S(1)}, u32[]{:S(2)}, u32[]{:S(2)}) collective-permute-start(bf16[128,2176]{1,0:T(8,128)(2,1)} %get-tuple-element.361), channel_id=1, source_target_pairs={{0,6},{1,7},{2,4},{3,5},{4,2},{5,3},{6,0},{7,1},{8,14},{9,15},{10,... | collective-permute-start | bytes 1671176 | tf_op jit(solution)/shard_map/ppermute | solution.py:105
  609.3 24.5 %collective-permute-start.82 = (bf16[2048,1152]{1,0:T(8,128)(2,1)}, bf16[2048,1152]{1,0:T(8,128)(2,1)}, u32[]{:S(2)}, u32[]{:S(2)}) collective-permute-start(bf16[2048,1152]{1,0:T(8,128)(2,1)} %all-gather.7.cloned.1.call-done.refs_0_), channel_id=1, source_target_pairs={{0,1},{1,0},{2,3},{3,2},{4,5},{5,4},{6,7},{7,6},{8,9},{9,8},{10,11... | collective-permute-start | bytes 14155784 | tf_op jit(solution)/shard_map/ppermute | solution.py:48
  609.3 24.5 %collective-permute-start.83 = (bf16[2048,1024]{1,0:T(8,128)(2,1)}, bf16[2048,1024]{1,0:T(8,128)(2,1)}, u32[]{:S(2)}, u32[]{:S(2)}) collective-permute-start(bf16[2048,1024]{1,0:T(8,128)(2,1)} %all-gather.11.cloned.1.call-done.refs_2_), channel_id=1, source_target_pairs={{0,1},{1,0},{2,3},{3,2},{4,5},{5,4},{6,7},{7,6},{8,9},{9,8},{10,11... | collective-permute-start | bytes 12582920 | tf_op jit(solution)/shard_map/ppermute | solution.py:48
  611.4 20.2 %collective-permute-start.84 = (bf16[128,3200]{1,0:T(8,128)(2,1)S(1)}, bf16[128,3200]{1,0:T(8,128)(2,1)S(1)}, u32[]{:S(2)}, u32[]{:S(2)}) collective-permute-start(bf16[128,3200]{1,0:T(8,128)(2,1)S(1)} %pad_maximum_fusion.6), channel_id=1, source_target_pairs={{0,8},{8,0},{16,24},{24,16},{1,9},{9,1},{17,25},{25,17},{2,10},{10... | collective-permute-start | bytes 2457608 | tf_op jit(solution)/shard_map/ppermute | solution.py:119
  653.3 54.6 %collective-permute-start.85 = (bf16[128,3200]{1,0:T(8,128)(2,1)S(1)}, bf16[128,3200]{1,0:T(8,128)(2,1)S(1)}, u32[]{:S(2)}, u32[]{:S(2)}) collective-permute-start(bf16[128,3200]{1,0:T(8,128)(2,1)S(1)} %add_convert_fusion), channel_id=1, source_target_pairs={{0,16},{8,24},{16,0},{24,8},{1,17},{9,25},{17,1},{25,9},{2,18},{10... | collective-permute-start | bytes 2457608 | tf_op jit(solution)/shard_map/ppermute | solution.py:119
  (102 other events, 1009.4 us)
Sparse Core Ops, SparseCore 0:
  85.6 80.9 all-gather.4
  168.2 87.9 all-gather.6
  270.7 91.2 all-gather.8
  391.3 60.8 reduce-scatter.2
  453.7 80.3 all-gather.10
  555.4 67.8 reduce-scatter.4
  653.5 63.3 all-reduce.3

commit v3 on v2

--- a/solution.py
+++ b/solution.py
@@ -48,13 +48,15 @@
     return lax.ppermute(rows, "ctx", chip_perm(lax.axis_size("ctx"), 1))
 
 
-def gather_chips(rows):
+def gather_chips(rows, after=None):
     size = lax.axis_size("ctx")
     if not hierarchical(size):
         return lax.all_gather(rows, "ctx", axis=0, tiled=True)
     pieces = [rows] + [
         lax.ppermute(rows, "ctx", chip_perm(size, 2 * k)) for k in range(1, size // 2)
     ]
+    if after is not None:
+        pieces, after = tie(pieces, after)
     return jnp.concatenate(pieces, axis=0)
 
 
@@ -114,9 +116,10 @@
     return lax.all_gather(rows, "dp", axis=0, tiled=True)
 
 
-def add_across(values, mask):
+def add_across(values, mask, after):
     streams = lax.axis_size("dp")
-    return values.astype(F32) + lax.ppermute(values, "dp", chip_perm(streams, mask)).astype(F32)
+    moved, after = tie(lax.ppermute(values, "dp", chip_perm(streams, mask)), after)
+    return values.astype(F32) + moved.astype(F32)
 
 
 def tie(main, *sides):
@@ -145,32 +148,34 @@
     return copies
 
 
-def copy_blocks(pieces, order_ref, columns, target, sems):
+def copy_blocks(pieces, parts, order_ref, columns, target, sems):
+    if columns is not None:
+        pieces = [piece.at[:, pl.ds(columns, target.shape[1])] for piece in pieces]
     copies = []
-    rows = target.shape[0] // order_ref.shape[0]
-    for piece in pieces:
-        if columns is not None:
-            piece = piece.at[:, pl.ds(columns, target.shape[1])]
-        if len(pieces) == 1:
-            copies.append(pltpu.make_async_copy(piece, target, sems.at[0]))
-            continue
-        for start in range(0, piece.shape[0], rows):
-            index = len(copies)
-            place = pl.multiple_of(order_ref[index] * rows, rows)
-            copies.append(
-                pltpu.make_async_copy(
-                    piece.at[pl.ds(start, rows), :],
-                    target.at[pl.ds(place, rows), :],
-                    sems.at[index],
-                )
-            )
+    if len(pieces) == 1:
+        copies.append(pltpu.make_async_copy(pieces[0], target, sems.at[0]))
+    else:
+        blocks = order_ref.shape[0] // len(pieces)
+        whole_rows = target.shape[0] // order_ref.shape[0]
+        rows = whole_rows // parts
+        for index, piece in enumerate(pieces):
+            for part in range(parts):
+                for block in range(blocks):
+                    place = order_ref[index * blocks + block] * whole_rows + part * rows
+                    copies.append(
+                        pltpu.make_async_copy(
+                            piece.at[pl.ds((part * blocks + block) * rows, rows), :],
+                            target.at[pl.ds(pl.multiple_of(place, rows), rows), :],
+                            sems.at[len(copies)],
+                        )
+                    )
     for copy in copies:
         copy.start()
     return copies
 
 
-def copy_count(pieces, order):
-    return 1 if len(pieces) == 1 else order.shape[0]
+def copy_count(pieces, order, parts):
+    return 1 if len(pieces) == 1 else order.shape[0] * parts
 
 
 def pick_matrix(ext, first, experts):
@@ -461,10 +466,12 @@
     for copy in copies(e, slot):
         copy.wait()
 
+    span = (streams - 1) * ROWS
+
     def chunk(r, carry):
-        at = pl.multiple_of(r * ROWS, 64)
-        block = xs[slot, pl.ds(at, ROWS), :]
-        grown = dys[slot, pl.ds(at, ROWS), :]
+        at = pl.multiple_of(rows + r * span, 64)
+        block = xs[slot, pl.ds(at, span), :]
+        grown = dys[slot, pl.ds(at, span), :]
         for n in range(2):
             lanes = slice(256 * n, 256 * n + 256)
             uplanes = slice(FE + 256 * n, FE + 256 * n + 256)
@@ -473,25 +480,22 @@
             dh = dot_nn(grown, w_ref[0, 0, :, 2 * FE + 256 * n : 2 * FE + 256 * n + 256])
             sig = 1.0 / (1.0 + jnp.exp(-gate_part))
             silu = gate_part * sig
-            hids[slot, pl.ds(at, ROWS), lanes] = (silu * up_part).astype(BF16)
+            hids[slot, pl.ds(at, span), lanes] = (silu * up_part).astype(BF16)
             slope = sig * (1.0 + gate_part * (1.0 - sig))
-            dgus[slot, pl.ds(at, ROWS), lanes] = (dh * up_part * slope).astype(BF16)
-            dgus[slot, pl.ds(at, ROWS), uplanes] = (dh * silu).astype(BF16)
+            dgus[slot, pl.ds(at, span), lanes] = (dh * up_part * slope).astype(BF16)
+            dgus[slot, pl.ds(at, span), uplanes] = (dh * silu).astype(BF16)
         return carry
 
-    lax.fori_loop(rows // ROWS, streams * rows // ROWS, chunk, 0)
-
-    def tile(i, carry):
-        at = pl.multiple_of(i * 256, 256)
-        left = xs[slot, :, pl.ds(at, 256)]
-        for n in range(2):
-            out_ref[0, 0, pl.ds(at, 256), FE * n : FE * n + FE] = dot_tn(
-                left, dgus[slot, :, FE * n : FE * n + FE]
-            )
-        out_ref[0, 0, pl.ds(at, 256), 2 * FE :] = dot_tn(dys[slot, :, pl.ds(at, 256)], hids[slot])
-        return carry
-
-    lax.fori_loop(0, width // 256, tile, 0)
+    lax.fori_loop(0, (streams - 1) * rows // span, chunk, 0)
+
+    for n in range(4):
+        out_ref[0, 0, :, 256 * n : 256 * n + 256] = dot_tn(
+            xs[slot], dgus[slot, :, 256 * n : 256 * n + 256]
+        )
+    for n in range(2):
+        out_ref[0, 0, :, 2 * FE + 256 * n : 2 * FE + 256 * n + 256] = dot_tn(
+            dys[slot], hids[slot, :, 256 * n : 256 * n + 256]
+        )
 
 
 ANY = pl.BlockSpec(memory_space=pl.ANY)
@@ -724,10 +728,10 @@
         ]
 
 
-def project_kernel(n_pieces, reordered, columns, turned, scale, order_ref, *refs):
+def project_kernel(n_pieces, parts, reordered, columns, turned, scale, order_ref, *refs):
     pieces = refs[:n_pieces]
     x_ref, gain_ref, cos_ref, sin_ref, out_ref, a_ref, turned_ref, weight, sems = refs[n_pieces:]
-    copies = copy_blocks(pieces, order_ref, columns, weight, sems)
+    copies = copy_blocks(pieces, parts, order_ref, columns, weight, sems)
     x = x_ref[...].astype(F32)
     a_ref[...] = (x * row_scale(x) * gain_ref[...]).astype(BF16)
     reorder(a_ref, turned_ref, order_ref, reordered)
@@ -741,12 +745,12 @@
         out_ref[:, at : at + block] = (made * scale).astype(BF16)
 
 
-def project(x, gain, pieces, order, columns, turned, scale, cosine, sine):
+def project(x, gain, pieces, parts, order, columns, turned, scale, cosine, sine):
     tokens, width = x.shape
     wide = HEADS * HD
     return pl.pallas_call(
         functools.partial(
-            project_kernel, len(pieces), hierarchical(order.shape[0]), columns, turned, scale
+            project_kernel, len(pieces), parts, hierarchical(order.shape[0]), columns, turned, scale
         ),
         out_shape=(
             jax.ShapeDtypeStruct((tokens, wide), BF16),
@@ -761,7 +765,7 @@
             out_specs=(whole(tokens, wide), whole(tokens, width), whole(tokens, width)),
             scratch_shapes=[
                 pltpu.VMEM((width, wide), BF16),
-                pltpu.SemaphoreType.DMA((copy_count(pieces, order),)),
+                pltpu.SemaphoreType.DMA((copy_count(pieces, order, parts),)),
             ],
         ),
         compiler_params=pltpu.CompilerParams(dimension_semantics=("arbitrary",), **PARAMS),
@@ -809,7 +813,7 @@
 GROUPS = KVH // 2
 
 
-def attend_kernel(n_pieces, n_weights, reordered, need_ref, order_ref, *refs):
+def attend_kernel(n_pieces, n_weights, parts, columns, reordered, need_ref, order_ref, *refs):
     pieces = refs[:n_pieces]
     w_pieces = refs[n_pieces : n_pieces + n_weights]
     refs = refs[n_pieces + n_weights :]
@@ -820,7 +824,7 @@
     width = x_ref.shape[1]
     keys = KVH * HD
     copies = copy_rows(pieces, kv, sems)
-    w_copies = copy_blocks(w_pieces, order_ref, None, w_ref, w_sems)
+    w_copies = copy_blocks(w_pieces, parts, order_ref, columns, w_ref, w_sems)
     for i in range(GROUPS):
         spread[i] = spread_heads(
             q_ref[:, 256 * i : 256 * i + 128].astype(F32),
@@ -874,13 +878,13 @@
     ).astype(BF16)
 
 
-def attend(pieces, w_pieces, need, order, q, keys, queries, x, gain, table):
+def attend(pieces, w_pieces, parts, columns, need, order, q, keys, queries, x, gain, table):
     tokens, width = x.shape
     length = sum(piece.shape[0] for piece in pieces)
     stack = (GROUPS, 4 * tokens, 128)
     return pl.pallas_call(
         functools.partial(
-            attend_kernel, len(pieces), len(w_pieces), hierarchical(order.shape[0])
+            attend_kernel, len(pieces), len(w_pieces), parts, columns, hierarchical(order.shape[0])
         ),
         out_shape=(
             jax.ShapeDtypeStruct((tokens, width), BF16),
@@ -914,10 +918,10 @@
             ),
             scratch_shapes=[
                 pltpu.VMEM((length, 2 * KVH * HD), BF16),
-                pltpu.VMEM((width, w_pieces[0].shape[1]), BF16),
+                pltpu.VMEM((width, width + EXT), BF16),
                 pltpu.VMEM(stack, BF16),
                 pltpu.SemaphoreType.DMA((len(pieces),)),
-                pltpu.SemaphoreType.DMA((copy_count(w_pieces, order),)),
+                pltpu.SemaphoreType.DMA((copy_count(w_pieces, order, parts),)),
             ],
         ),
         compiler_params=pltpu.CompilerParams(dimension_semantics=("arbitrary",), **PARAMS),
@@ -930,7 +934,9 @@
     )(need, order, *pieces, *w_pieces, q, keys, queries, x, gain, table)
 
 
-def attend_back_kernel(n_pieces, n_weights, n_sums, n_halves, need_ref, order_ref, *refs):
+def attend_back_kernel(
+    n_pieces, n_weights, parts, columns, n_sums, n_halves, need_ref, order_ref, *refs
+):
     pieces = refs[:n_pieces]
     w_pieces = refs[n_pieces : n_pieces + n_weights]
     refs = refs[n_pieces + n_weights :]
@@ -953,7 +959,7 @@
     kv, w_ref, spread, grown, dden, dq_acc, sems, w_sems = refs[n_sums + 16 + n_halves :]
     tokens, width = h_ref.shape
     keys = KVH * HD
-    w_copies = copy_blocks(w_pieces, order_ref, None, w_ref, w_sems)
+    w_copies = copy_blocks(w_pieces, parts, order_ref, columns, w_ref, w_sems)
     copies = copy_rows(pieces, kv, sems)
     moved = sums[0][...]
     for piece in sums[1:]:
@@ -1032,7 +1038,7 @@
 
 
 def attend_back(
-    pieces, w_pieces, sums, need, order, q, keys, queries, h, gain, gates, den, un, gx, cosine, sine
+    pieces, w_pieces, parts, columns, sums, need, order, q, keys, queries, h, gain, gates, den, un, gx, cosine, sine
 ):
     tokens, width = h.shape
     length = sum(piece.shape[0] for piece in pieces)
@@ -1040,7 +1046,9 @@
     blocks = [q, keys, queries, h, gain, gates, den, un, gx, cosine, sine]
     halves = halves_of(pieces)
     made = pl.pallas_call(
-        functools.partial(attend_back_kernel, len(pieces), len(w_pieces), len(sums), halves),
+        functools.partial(
+            attend_back_kernel, len(pieces), len(w_pieces), parts, columns, len(sums), halves
+        ),
         out_shape=(
             jax.ShapeDtypeStruct((tokens, width), F32),
             jax.ShapeDtypeStruct((tokens, width), BF16),
@@ -1064,13 +1072,13 @@
             ),
             scratch_shapes=[
                 pltpu.VMEM((length, 2 * KVH * HD), BF16),
-                pltpu.VMEM((width, w_pieces[0].shape[1]), BF16),
+                pltpu.VMEM((width, width + EXT), BF16),
                 pltpu.VMEM(stack, BF16),
                 pltpu.VMEM(stack, BF16),
                 pltpu.VMEM(stack, F32),
                 pltpu.VMEM(stack, F32),
                 pltpu.SemaphoreType.DMA((len(pieces),)),
-                pltpu.SemaphoreType.DMA((copy_count(w_pieces, order),)),
+                pltpu.SemaphoreType.DMA((copy_count(w_pieces, order, parts),)),
             ],
         ),
         compiler_params=pltpu.CompilerParams(dimension_semantics=("arbitrary",), **PARAMS),
@@ -1084,7 +1092,7 @@
     return (*made[:5], made[5:])
 
 
-def project_back_kernel(n_weights, n_groups, n_sums, order_ref, *refs):
+def project_back_kernel(n_weights, parts, n_groups, n_sums, order_ref, *refs):
     groups = [refs[k * n_weights : (k + 1) * n_weights] for k in range(n_groups)]
     refs = refs[n_groups * n_weights :]
     sums = refs[:n_sums]
@@ -1096,7 +1104,7 @@
     for k, pieces in enumerate(groups):
         columns = weight.shape[1] // n_groups
         copies += copy_blocks(
-            pieces, order_ref, None, weight.at[:, pl.ds(k * columns, columns)], sems.at[k]
+            pieces, parts, order_ref, 0, weight.at[:, pl.ds(k * columns, columns)], sems.at[k]
         )
     dkv = sums[0][...]
     for piece in sums[1:]:
@@ -1120,13 +1128,13 @@
     low_ref[...] = gx.astype(BF16)
 
 
-def project_back(groups, sums, order, dq, x, gain, dh, cosine, sine):
+def project_back(groups, parts, sums, order, dq, x, gain, dh, cosine, sine):
     tokens, width = x.shape
-    wide = sum(pieces[0].shape[1] for pieces in groups)
+    wide = HEADS * HD + 2 * KVH * HD
     operands = [*sums, dq, x, gain, dh, cosine, sine]
     weights = [piece for pieces in groups for piece in pieces]
     return pl.pallas_call(
-        functools.partial(project_back_kernel, len(groups[0]), len(groups), len(sums)),
+        functools.partial(project_back_kernel, len(groups[0]), parts, len(groups), len(sums)),
         out_shape=(
             jax.ShapeDtypeStruct((tokens, width), F32),
             jax.ShapeDtypeStruct((tokens, width), BF16),
@@ -1145,7 +1153,7 @@
             ),
             scratch_shapes=[
                 pltpu.VMEM((width, wide), BF16),
-                pltpu.SemaphoreType.DMA((len(groups), copy_count(groups[0], order))),
+                pltpu.SemaphoreType.DMA((len(groups), copy_count(groups[0], order, parts))),
             ],
         ),
         compiler_params=pltpu.CompilerParams(dimension_semantics=("arbitrary",), **PARAMS),
@@ -1220,65 +1228,99 @@
         jnp.concatenate([gain_attn, gain_moe, jnp.zeros((8 - 2 * layers, gain_attn.shape[1]), BF16)])
     )
     kv_weight = pieces_of(w_qkv[0, :, query_width:])
-    q_weight, kv_weight = tie(w_qkv[0, :, :query_width], *kv_weight)
-    q_weight, kv_weight = pieces_of(q_weight), list(kv_weight)
     gain_blocks = jnp.concatenate(gain_pieces, axis=0).reshape(ctx_size, 8, -1)
     if hierarchical(ctx_size):
         gain_blocks = jnp.take(gain_blocks, jnp.argsort(order), axis=0)
     gains = jnp.transpose(gain_blocks, (1, 0, 2)).reshape(8, width).astype(F32)
-    out_weight = with_router(0)
-    out_weight, q_weight = tie(out_weight, *q_weight)
-    weights = [
-        (gains[0][None], [list(q_weight), kv_weight], gains[layers][None], pieces_of(out_weight))
-    ]
-    for layer_idx in range(1, layers):
-        next_out, (weights[0],) = tie(with_router(layer_idx), weights[0])
-        weights.append((gains[layer_idx][None], None, gains[layers + layer_idx][None], pieces_of(next_out)))
-    gx, (weights[0],) = tie(cotangent[0], weights[0])
-    grad_near = gather_chips(gx)
-    grad_side = all_streams(grad_near)
 
     x = x_in[0]
     store = []
     sides = {}
+    qkv_weight = [None, kv_weight]
+    out_weight = None
+    parts, out_columns = 1, 0
+    streams = lax.axis_size("dp")
     for layer_idx in range(layers):
-        gain_one, qkv_weight, gain_two, out_weight = weights[layer_idx]
-        columns = 0 if len(qkv_weight) > 1 else query_width
+        gain_one, gain_two = gains[layer_idx][None], gains[layers + layer_idx][None]
+        columns = 0 if layer_idx == 0 else query_width
         kv, a, unused = project(
-            x, gain_one, qkv_weight[-1], order, columns, KVH * HD, 1.0, cosine, sine
+            x, gain_one, qkv_weight[-1], parts, order, columns, KVH * HD, 1.0, cosine, sine
         )
         kv_pieces = gather_ctx(kv)
+        if layer_idx == 0:
+            (q_weight, out_weight), (kv,) = tie((w_qkv[0, :, :query_width], with_router(0)), kv)
+            qkv_weight[0] = pieces_of(q_weight)
+            out_weight, (qkv_weight[0],) = tie(out_weight, qkv_weight[0])
+            gain_one, (tables, keys, queries, need) = tie(gain_one, tables, keys, queries, need)
         q, unused, a_order = project(
-            x, gain_one, qkv_weight[0], order, 0, query_width, 1.0 / math.sqrt(HD), cosine, sine
-        )
+            x,
+            gain_one,
+            qkv_weight[0],
+            parts,
+            order,
+            0,
+            query_width,
+            1.0 / math.sqrt(HD),
+            cosine,
+            sine,
+        )
+        if layer_idx == 0:
+            out_weight = both_cores(gather_chips(out_weight, q))
+        if layer_idx + 1 < layers:
+            next_qkv = w_qkv[layer_idx + 1]
+            if hierarchical(ctx_size):
+                share = next_qkv.shape[0] // streams
+                next_qkv = lax.dynamic_slice_in_dim(
+                    next_qkv, lax.axis_index("dp") * share, share, axis=0
+                )
+            next_qkv, (q, out_weight) = tie(next_qkv, q, out_weight)
         *o, den, un, h, pay, gates = attend(
-            kv_pieces, out_weight, need, order, q, keys, queries, x, gain_two, tables[layer_idx]
+            kv_pieces,
+            out_weight,
+            1,
+            out_columns,
+            need,
+            order,
+            q,
+            keys,
+            queries,
+            x,
+            gain_two,
+            tables[layer_idx],
         )
         near = gather_chips(pay)
         if layer_idx + 1 < layers:
-            next_qkv, (near,) = tie(w_qkv[layer_idx + 1], near)
-            next_qkv = pieces_of(next_qkv)
+            next_qkv = gather_chips(next_qkv, pay)
+            if hierarchical(ctx_size):
+                next_qkv = all_streams(next_qkv)
+            next_out, unused = tie(with_router(layer_idx + 1), near)
         else:
-            near, (sides[0],) = tie(near, sides[0])
+            gx, (near,) = tie(cotangent[0], near)
         sides[layer_idx] = all_streams(near)
         partial, x_rows, gate_rows, pair_values, pick = moe_fwd(
             both_cores(near), w_expert, layer_idx, first
         )
         store.append(
             [x, (a, a_order), q, kv_pieces, o, den, un, h, pay, gates, x_rows, gate_rows, pair_values, pick]
-        )
+            + [gain_one, qkv_weight, gain_two, out_weight, parts, out_columns]
+        )
+        if layer_idx + 1 < layers:
+            next_out = both_cores(gather_chips(next_out, partial))
         own, sent = reduce_start(partial)
         if layer_idx + 1 < layers:
+            next_qkv, unused = tie(next_qkv, sent)
+            next_qkv = both_cores(next_qkv)
             x = total_of([h, *reduce_finish(own, sent)])
-            x, (next_qkv, grad_side) = tie(x, next_qkv, grad_side)
-            upper_gain, unused, moe_gain, upper_out = weights[layer_idx + 1]
-            weights[layer_idx + 1] = (upper_gain, [next_qkv], moe_gain, upper_out)
+            x, (next_qkv,) = tie(x, next_qkv)
+            qkv_weight, out_weight = [next_qkv], next_out
+            parts = streams if hierarchical(ctx_size) else 1
+        else:
+            grad_near = gather_chips(gx, sent)
+            grad_near, (own, sent) = tie(grad_near, own, sent)
+            grad_side = all_streams(grad_near)
     last_h, last_own, last_sent = h, own, sent
 
-    streams = lax.axis_size("dp")
-
-    def pick_others(tokens_of, grads_of):
-        tokens_of, grads_of = both_cores(tokens_of), both_cores(grads_of)
+    def pick_others(tokens_of, grads_of, which):
         return [
             pick_rows(
                 tokens_of,
@@ -1287,34 +1329,42 @@
                 first,
                 ((lax.axis_index("dp") + k) % streams).astype(jnp.int32).reshape(1),
             )
-            for k in range(1, streams)
+            for k in which
         ]
 
     expert_sum = None
     early, late, routed = {}, {}, {}
-    split = (experts_here + 1) // 2
+    split = 1
     for layer_idx in reversed(range(layers)):
-        gain_one, qkv_weight, gain_two, out_weight = weights[layer_idx]
-        x, a, q, kv_pieces, o, den, un, h, pay, gates, x_rows, gate_rows, pair_values, pick = store[
+        (x, a, q, kv_pieces, o, den, un, h, pay, gates, x_rows, gate_rows, pair_values, pick) = store[
             layer_idx
-        ]
+        ][:14]
+        gain_one, qkv_weight, gain_two, out_weight, parts, out_columns = store[layer_idx][14:]
         top = layer_idx == layers - 1
         if not top:
-            grad_side = all_streams(grad_near)
+            new_side = all_streams(grad_near)
         partial, dy_rows, hid_rows, dgu_rows = moe_bwd(
             both_cores(grad_near), w_expert, layer_idx, first, gate_rows, pair_values, pick
         )
+        waiting = reduce_finish(last_own, last_sent) if top else reduce_finish(*late[1])
+        partial, (waiting, sides[0]) = tie(partial, waiting, sides[0])
         own, sent = reduce_start(partial)
         sums = reduce_finish(own, sent)
-        if not top:
-            y_out = total_of([last_h, *reduce_finish(last_own, last_sent)]).astype(BF16)[None]
-            sums[0], (picked, early[1], late[1], y_out) = tie(
-                sums[0], picked, early[1], late[1], y_out
-            )
-            late[1] = lax.psum_scatter(late[1], "ctx", scatter_dimension=0, tiled=True)
+        if top:
+            y_out = total_of([last_h, *waiting]).astype(BF16)[None]
+        else:
+            (side, grad_side), (partial,) = tie((side, grad_side), partial)
+            side, grad_side = both_cores(side), both_cores(grad_side)
+            (side, grad_side), (sent,) = tie((side, grad_side), sent)
+            picked = pick_others(side, grad_side, range(1, streams))
+            late[1] = total_of(waiting).astype(BF16)
+            sums[0], (picked, late[1]) = tie(sums[0], picked, late[1])
+            (upper_own, upper_sent), (sums[0],) = tie(early[1], sums[0])
         dh, dattn, dlog, dgain_two, dq, dkv = attend_back(
             kv_pieces,
             out_weight,
+            1,
+            out_columns,
             sums,
             need,
             order,
@@ -1332,17 +1382,21 @@
         )
         count = halves_of(sums)
         half = width // count
+        early[layer_idx] = [
+            dot_tn(o[1][:, at : at + half], dattn).astype(BF16) for at in range(0, width, half)
+        ]
+        routed[layer_idx] = dot_tn(pay[:, :width], dlog[:, :expert_count])
+        if not top:
+            arrived, (dkv,) = tie(reduce_finish(upper_own, upper_sent), dkv)
+            upper_grads = jnp.concatenate([total_of(arrived).astype(BF16), late[1]], axis=1)
+            upper_grads = lax.psum(upper_grads, "dp")
+        own, sent = reduce_start(dkv)
+        sums = reduce_finish(own, sent)
         if top:
-            early[1] = dot_tn(o[0], dattn).astype(BF16)
-        else:
-            early[0] = [
-                dot_tn(o[1][:, at : at + half], dattn).astype(BF16) for at in range(0, width, half)
-            ]
-        routed[layer_idx] = dot_tn(pay[:, :width], dlog[:, :expert_count])
-        sums = reduce_ctx(dkv)
-        if top:
+            early[1] = reduce_start(early[1])
             sums[0], (early[1],) = tie(sums[0], early[1])
         else:
+            picked, (sent,) = tie(picked, sent)
             upper_sum = functools.partial(
                 expert_grads,
                 [upper[0]] + [pair[0] for pair in picked],
@@ -1353,23 +1407,25 @@
                 layer_idx + 1,
             )
             expert_sum = upper_sum(0, split, None)
+            sums[0], (expert_sum, new_side) = tie(sums[0], expert_sum, new_side)
             early[0] = reduce_start(early[0])
-            sums[0], (expert_sum, early[0]) = tie(sums[0], expert_sum, early[0])
-        if top:
-            early[1] = lax.psum_scatter(early[1], "ctx", scatter_dimension=0, tiled=True)
         gx, grad_low, dprojected, dgain_one = project_back(
-            qkv_weight, sums, order, dq, x, gain_one, dh, cosine, sine
+            qkv_weight, parts, sums, order, dq, x, gain_one, dh, cosine, sine
         )
         routed[layer_idx] = jnp.concatenate(
             [routed[layer_idx], dgain_one.T, dgain_two.T], axis=1
         )
         if top:
-            late[1] = dot_tn(a[0], dprojected[:, : 2 * width]).astype(BF16)
+            late[1] = reduce_start(
+                [
+                    dot_tn(a[1][:, at : at + half], dprojected[:, : 2 * width]).astype(BF16)
+                    for at in range(0, width, half)
+                ]
+            )
             upper = (x_rows, dy_rows, hid_rows, dgu_rows)
             grad_near = gather_chips(grad_low)
-            grad_near, (last_own, last_sent) = tie(grad_near, last_own, last_sent)
-            (side, grad_side), (grad_near,) = tie((sides[layer_idx], grad_side), grad_near)
-            picked = pick_others(side, grad_side)
+            grad_near, (late[1],) = tie(grad_near, late[1])
+            side = sides[layer_idx]
         else:
             spare = EXT - layers * (expert_count + 2)
             small = jnp.pad(
@@ -1388,14 +1444,13 @@
             if split < experts_here:
                 expert_sum, (own, sent, early[0]) = tie(expert_sum, own, sent, early[0])
                 expert_sum = upper_sum(split, experts_here - split, expert_sum)
-            arrived = reduce_finish(own, sent)
-            expert_sum, (arrived,) = tie(expert_sum, arrived)
+            arrived, (expert_sum,) = tie(reduce_finish(own, sent), expert_sum)
             below = jnp.concatenate([total_of(arrived), total_of(early[0])], axis=1).astype(BF16)
-            below = add_across(below, 1).astype(BF16)
-            (side, grad_side), (expert_sum,) = tie((sides[layer_idx], grad_side), expert_sum)
-            picked = pick_others(side, grad_side)
-            picked[0], (below, expert_sum) = tie(picked[0], below, expert_sum)
-            upper_grads, (picked,) = tie(jnp.concatenate([early[1], late[1]], axis=1), picked)
+            (side, new_side), (expert_sum, upper_grads) = tie(
+                (sides[layer_idx], new_side), expert_sum, upper_grads
+            )
+            picked = pick_others(both_cores(side), both_cores(new_side), range(1, streams))
+            below = add_across(below, 1, picked[1]).astype(BF16)
             expert_sum = expert_grads(
                 [x_rows] + [pair[0] for pair in picked],
                 [dy_rows] + [pair[1] for pair in picked],
@@ -1407,8 +1462,8 @@
                 experts_here,
                 expert_sum,
             )
-    low_sum = add_across(below, 2)
-    upper_grads, (expert_sum, low_sum) = tie(lax.psum(upper_grads, "dp"), expert_sum, low_sum)
+    low_sum = add_across(below, 2, expert_sum)
+    upper_grads, (expert_sum, low_sum) = tie(upper_grads, expert_sum, low_sum)
     upper_grads = upper_grads.astype(F32)
     spread = low_sum[:, 2 * width : 2 * width + EXT]
     each = [spread[:, k * (expert_count + 2) :] for k in range(layers)]

time: 736 us -> 674 us (0.916)
  waiting for transfers between devices: 242 us -> 172 us
    ppermute x2, waiting for transfers between devices: 31.2 us -> 2.75 us  [add_across(): lax.ppermute(values, 'dp', chip_perm(streams, mask))]
    ppermute x24 -> x30, waiting for transfers between devices: 62.1 us -> 38.3 us  [reduce_finish(): lax.ppermute(piece, 'ctx', chip_perm(size, 2 * (k + 1)))]
    ppermute x36, waiting for transfers between devices: 119 us -> 98.5 us  [gather_chips(): lax.ppermute(rows, 'ctx', chip_perm(size, 2 * k))]
    ppermute x24 -> x26, waiting for transfers between devices: 21.6 us -> 32.1 us  [swap_cores(): return lax.ppermute(rows, 'ctx', chip_perm(lax.axis_size('ctx'), 1))]
    pallas_call x3, Pallas kernels: 93 us -> 83.9 us  [expert_grads(): pl.pallas_call(functools.partial(expert_grad_kernel, streams, before is n...]
    psum x1, waiting for transfers between devices: 8.74 us -> 0.02 us  [local(): upper_grads = lax.psum(upper_grads, 'dp')]
    ppermute x36, starting transfers between devices: 52.9 us -> 45.3 us  [gather_chips(): lax.ppermute(rows, 'ctx', chip_perm(size, 2 * k))]
    pallas_call x8 -> x10, Pallas kernels: 23.5 us -> 29.6 us  [reduce_start(): pl.pallas_call(fold_kernel, out_shape=[jax.ShapeDtypeStruct((rows, width)...]
  transfers between devices with their start and end apart: 93 -> 100, of which waited for: 48 -> 44; matrix products, arithmetic and copies ran while one was open for 7% -> 8% of each run, Pallas kernels for 38% -> 43%
where the time goes in v3:
time: 674 us; the launch traced here: 666 us
  Pallas kernels  296 us (44%)
  waiting for transfers between devices  172 us (26%)
  starting transfers between devices  96.3 us (14%)
  local copies, waits for them, and re-layouts  44.4 us (7%)
  other arithmetic  23.8 us (4%)
  matrix products  17.8 us (3%)
  between operations  15.9 us (2%)
    ppermute x36, waiting for transfers between devices, gather_chips(): lax.ppermute(rows, 'ctx', chip_perm(size, 2 * k))  98.5 us
    pallas_call x3, Pallas kernels, expert_grads(): pl.pallas_call(functools.partial(expert_grad_kernel, streams, before is n...  83.9 us
    ppermute x36, starting transfers between devices, gather_chips(): lax.ppermute(rows, 'ctx', chip_perm(size, 2 * k))  45.3 us
    ppermute x30, starting transfers between devices, reduce_finish(): lax.ppermute(piece, 'ctx', chip_perm(size, 2 * (k + 1)))  41.2 us
    pallas_call x6, Pallas kernels, pick_rows(): pl.pallas_call(functools.partial(pick_kernel, experts, *heights), out_sha...  38.8 us
    ppermute x30, waiting for transfers between devices, reduce_finish(): lax.ppermute(piece, 'ctx', chip_perm(size, 2 * (k + 1)))  38.3 us
    pallas_call x2, Pallas kernels, moe_bwd(): pl.pallas_call(functools.partial(moe_bwd_kernel, experts, len(pieces), ha...  36.9 us
    pallas_call x2, Pallas kernels, moe_fwd(): pl.pallas_call(functools.partial(moe_fwd_kernel, experts, len(pieces), ha...  36.8 us
  transfers between devices with their start and end apart: 100, of which 44 were waited for; matrix products, arithmetic and copies ran while one was open for 8% of the time, Pallas kernels for 43%

profile of v3, /device:TPU:0, one launch (start us, length us, event | category | flops | bytes accessed | tf_op | source)
XLA Modules:
  0.0 666.1 jit_solution(16199194610210775920)
XLA Ops:
  8.0 4.0 collective-permute-start.2
  23.9 3.7 collective-permute-done.5
  33.2 4.4 project.4
  41.1 6.2 collective-permute-done.12
  47.5 5.4 collective-permute-done.14
  61.7 2.7 collective-permute-done.8
  65.0 4.5 project.5
  70.8 2.9 collective-permute-done.17
  73.7 3.5 collective-permute-done.16
  80.3 3.6 collective-permute-done.9
  92.4 7.3 %attend.2 = (bf16[128,1024]{1,0:T(8,128)(2,1)}, bf16[128,1024]{1,0:T(8,128)(2,1)}, f32[4,512,128]{2,1,0:T(8,128)}, f32[4,512,128]{2,1,0:T(8,128)}, f32[128,1024]...) custom-call(s32[8]{0:T(128)} %get-tuple-element.247.need_ref, s32[8]{0:T(128)} %copy-done.75, ...), custom_call_target="tpu_custom_call" | custom-call | flops 536870912 | bytes 6815744 | tf_op jit(solution)/shard_map/attend/pallas_call | solution.py:885
  103.8 2.9 collective-permute-start.22
  107.7 4.1 collective-permute-done.20
  111.8 9.7 %collective-permute-done.21 = bf16[128,1152]{1,0:T(8,128)(2,1)S(1)} collective-permute-done((bf16[128,1152]{1,0:T(8,128)(2,1)}, bf16[128,1152]{1,0:T(8,128)(2,1)S(1)}, u32[]{:S(2)}, u32[]{:S(2)}) %collective-permute-start.21) | collective-permute-done | bytes 294944 | tf_op jit(solution)/shard_map/ppermute | solution.py:56
  125.6 18.1 %moe_fwd.2 = (bf16[512,1024]{1,0:T(8,128)(2,1)}, bf16[512,1024]{1,0:T(8,128)(2,1)}, bf16[4,320,1024]{2,1,0:T(8,128)(2,1)}, f32[4,320,128]{2,1,0:T(8,128)}, f32[4...) custom-call(s32[1]{0:T(128)} %bitcast.16.first_ref, bf16[512,1152]{1,0:T(8,128)(2,1)} %copy-done.4, ...), custom_call_target="tpu_custom_call" | custom-call | flops 4026531840 | bytes 24641536 | tf_op jit(solution)/shard_map/moe_fwd/pallas_call | solution.py:536
  143.9 2.8 collective-permute-done.24.far_ref
  154.2 7.3 %collective-permute-done.38 = bf16[128,1152]{1,0:T(8,128)(2,1)S(1)} collective-permute-done((bf16[128,1152]{1,0:T(8,128)(2,1)S(1)}, bf16[128,1152]{1,0:T(8,128)(2,1)S(1)}, u32[]{:S(2)}, u32[]{:S(2)}) %collective-permute-start.38) | collective-permute-done | bytes 294944 | tf_op jit(solution)/shard_map/ppermute | solution.py:56
  161.5 5.7 collective-permute-done.37
  171.9 5.8 collective-permute-done.25
  177.7 5.4 collective-permute-done.26
  186.4 4.8 project.6
  195.9 6.2 collective-permute-done.32
  202.2 3.4 collective-permute-done.34
  205.7 5.0 project.7
  211.7 7.4 %attend.3 = (bf16[128,1024]{1,0:T(8,128)(2,1)}, bf16[128,1024]{1,0:T(8,128)(2,1)}, f32[4,512,128]{2,1,0:T(8,128)}, f32[4,512,128]{2,1,0:T(8,128)}, f32[128,1024]...) custom-call(s32[8]{0:T(128)} %get-tuple-element.247.need_ref, s32[8]{0:T(128)} %copy-done.75, ...), custom_call_target="tpu_custom_call" | custom-call | flops 536870912 | bytes 6815744 | tf_op jit(solution)/shard_map/attend/pallas_call | solution.py:885
  223.8 6.2 collective-permute-done.42
  230.0 6.6 collective-permute-done.41
  244.6 18.7 %moe_fwd.3 = (bf16[512,1024]{1,0:T(8,128)(2,1)}, bf16[512,1024]{1,0:T(8,128)(2,1)}, bf16[4,320,1024]{2,1,0:T(8,128)(2,1)}, f32[4,320,128]{2,1,0:T(8,128)}, f32[4...) custom-call(s32[1]{0:T(128)} %bitcast.16.first_ref, bf16[512,1152]{1,0:T(8,128)(2,1)} %pad_maximum_fusion.1.refs_0_, ...), custom_call_target="tpu_custom_call" | custom-call | flops 4026531840 | bytes 24641536 | tf_op jit(solution)/shard_map/moe_fwd/pallas_call | solution.py:536
  271.0 2.9 collective-permute-done.45
  273.9 3.9 collective-permute-done.44
  282.6 18.4 %moe_bwd.2 = (bf16[512,1152]{1,0:T(8,128)(2,1)}, bf16[512,1152]{1,0:T(8,128)(2,1)}, bf16[4,320,1024]{2,1,0:T(8,128)(2,1)}, bf16[4,320,512]{2,1,0:T(8,128)(2,1)}, bf16[4,320,1024]{2,1,0:T(8,128)(2,1)}) custom-call(s32[1]{0:T(128)} %bitcast.16.first_ref, bf16[512,1024]{1,0:T(8,128)(2,1)} %copy-done.2, bf16[512,1024]{1,0:T(8,128)(2,1)} %copy-done.27, ...), custom_call_target="tpu_custom_call" | custom-call | flops 4026531840 | bytes 28573696 | tf_op jit(solution)/shard_map/moe_bwd/pallas_call | solution.py:582
  302.0 3.0 collective-permute-done.52.far_ref
  306.1 2.8 fold.12
  312.4 6.6 collective-permute-done.53.refs_5_
  319.1 6.2 collective-permute-done.55.refs_7_
  326.0 10.9 %attend_back.2 = (f32[128,1024]{1,0:T(8,128)}, bf16[128,1024]{1,0:T(8,128)(2,1)}, bf16[128,128]{1,0:T(8,128)(2,1)}, f32[1,1024]{1,0:T(1,128)}, bf16[128,1024]{1,...) custom-call(s32[8]{0:T(128)} %get-tuple-element.247.need_ref, s32[8]{0:T(128)} %copy-done.75, ...), custom_call_target="tpu_custom_call" | custom-call | flops 939524096 | bytes 10223616 | tf_op jit(solution)/shard_map/attend_back/pallas_call | solution.py:1048
  346.0 2.7 collective-permute-start.59
  352.6 2.8 fold.14
  355.4 5.3 collective-permute-done.59.refs_4_
  363.2 7.8 %project_back.2 = (f32[128,1024]{1,0:T(8,128)}, bf16[128,1024]{1,0:T(8,128)(2,1)}, bf16[128,2176]{1,0:T(8,128)(2,1)}, f32[1,1024]{1,0:T(1,128)}) custom-call(s32[8]{0:T(128)} %copy-done.75, bf16[512,2048]{1,0:T(8,128)(2,1)} %all-gather.6.cloned.1.call-done.refs_0_, bf16[512,2048]{1,0:T(8,128)(2,1)} %copy-done, f32[128,1024]{1,0:T(8,128)} %get-tuple-element.341.refs_2_, ...), custom_call_target="tpu_custom_call" | custom-call | flops 536870912 | bytes 7340032 | tf_op jit(solution)/shard_map/project_back/pallas_call | solution.py:1136
  371.0 3.1 convolution_convert_fusion
  379.8 4.5 collective-permute-done.63
  384.2 5.2 collective-permute-done.62
  390.9 3.8 fold.15
  399.3 18.5 %moe_bwd.3 = (bf16[512,1152]{1,0:T(8,128)(2,1)}, bf16[512,1152]{1,0:T(8,128)(2,1)}, bf16[4,320,1024]{2,1,0:T(8,128)(2,1)}, bf16[4,320,512]{2,1,0:T(8,128)(2,1)}, bf16[4,320,1024]{2,1,0:T(8,128)(2,1)}) custom-call(s32[1]{0:T(128)} %bitcast.16.first_ref, bf16[512,1024]{1,0:T(8,128)(2,1)} %copy-done.1, bf16[512,1024]{1,0:T(8,128)(2,1)} %copy-done.28, ...), custom_call_target="tpu_custom_call" | custom-call | flops 4026531840 | bytes 28573696 | tf_op jit(solution)/shard_map/moe_bwd/pallas_call | solution.py:582
  417.8 3.5 collective-permute-done.67
  423.9 8.9 %collective-permute-done.69.far_ref = bf16[512,1152]{1,0:T(8,128)(2,1)S(1)} collective-permute-done((bf16[512,1152]{1,0:T(8,128)(2,1)}, bf16[512,1152]{1,0:T(8,128)(2,1)S(1)}, u32[]{:S(2)}, u32[]{:S(2)}) %collective-permute-start.69) | collective-permute-done | bytes 1179680 | tf_op jit(solution)/shard_map/ppermute | solution.py:48
  433.9 2.8 fold.16
  440.2 6.4 pick_rows.8
  446.6 6.4 pick_rows.7
  453.1 6.5 pick_rows.6
  464.1 10.6 %attend_back.3 = (f32[128,1024]{1,0:T(8,128)}, bf16[128,1024]{1,0:T(8,128)(2,1)}, bf16[128,128]{1,0:T(8,128)(2,1)}, f32[1,1024]{1,0:T(1,128)}, bf16[128,1024]{1,...) custom-call(s32[8]{0:T(128)} %get-tuple-element.247.need_ref, s32[8]{0:T(128)} %copy-done.75, ...), custom_call_target="tpu_custom_call" | custom-call | flops 939524096 | bytes 10223616 | tf_op jit(solution)/shard_map/attend_back/pallas_call | solution.py:1048
  483.8 3.0 collective-permute-start.80
  488.3 15.0 %expert_grads.3.refs_11_ = f32[2,4,1024,1536]{3,2,1,0:T(8,128)} custom-call(bf16[4,320,1024]{2,1,0:T(8,128)(2,1)} %get-tuple-element.402.refs_0_, bf16[4,320,1024]{2,1,0:T(8,128)(2,1)} %get-tuple-element.412.refs_1_, bf16[4,320,1024]{2,1,0:T(8,128)(2,1)} %get-tuple-element.413.refs_2_, bf16[4,320,1024]{2,1,0:T(8,128)(2,1)} %get-tuple-element.414.refs_3_, ...), custom_call_target="tpu_custom_call" | custom-call | flops 7046430720 | bytes 14680064 | tf_op jit(solution)/shard_map/expert_grads/pallas_call | solution.py:674
  504.2 7.4 %project_back.3 = (f32[128,1024]{1,0:T(8,128)}, bf16[128,1024]{1,0:T(8,128)(2,1)}, bf16[128,2176]{1,0:T(8,128)(2,1)}, f32[1,1024]{1,0:T(1,128)}) custom-call(s32[8]{0:T(128)} %copy-done.75, bf16[512,1024]{1,0:T(8,128)(2,1)} %copy-done.8, bf16[512,1024]{1,0:T(8,128)(2,1)} %copy-done.12, bf16[512,1024]{1,0:T(8,128)(2,1)} %copy-done.3, ...), custom_call_target="tpu_custom_call" | custom-call | flops 536870912 | bytes 7340032 | tf_op jit(solution)/shard_map/project_back/pallas_call | solution.py:1136
  528.6 3.2 fusion.near_ref
  533.1 4.0 fold.18
  544.9 30.8 %expert_grads.4.refs_11_ = f32[2,4,1024,1536]{3,2,1,0:T(8,128)} custom-call(bf16[4,320,1024]{2,1,0:T(8,128)(2,1)} %get-tuple-element.402.refs_0_, bf16[4,320,1024]{2,1,0:T(8,128)(2,1)} %get-tuple-element.412.refs_1_, bf16[4,320,1024]{2,1,0:T(8,128)(2,1)} %get-tuple-element.413.refs_2_, ...), custom_call_target="tpu_custom_call", output_to_operand_aliasing={{}: (11, {})} | custom-call | flops 21139292160 | bytes 44040192 | tf_op jit(solution)/shard_map/expert_grads/pallas_call | solution.py:674
  581.2 8.9 %collective-permute-done.91.refs_3_ = bf16[2048,1024]{1,0:T(8,128)(2,1)} collective-permute-done((bf16[2048,1024]{1,0:T(8,128)(2,1)}, bf16[2048,1024]{1,0:T(8,128)(2,1)}, u32[]{:S(2)}, u32[]{:S(2)}) %collective-permute-start.91) | collective-permute-done | bytes 4194336 | tf_op jit(solution)/shard_map/ppermute | solution.py:48
  590.1 6.5 pick_rows.10
  596.5 2.7 collective-permute-done.92
  602.0 6.4 pick_rows.11
  608.5 6.5 pick_rows.9
  615.0 38.1 %expert_grads.5 = f32[2,4,1024,1536]{3,2,1,0:T(8,128)} custom-call(bf16[4,320,1024]{2,1,0:T(8,128)(2,1)} %get-tuple-element.458.refs_0_, bf16[4,320,1024]{2,1,0:T(8,128)(2,1)} %get-tuple-element.461.refs_1_, bf16[4,320,1024]{2,1,0:T(8,128)(2,1)} %get-tuple-element.462.refs_2_, ...), custom_call_target="tpu_custom_call", output_to_operand_aliasing={{}: (11, {})} | custom-call | flops 28185722880 | bytes 58720256 | tf_op jit(solution)/shard_map/expert_grads/pallas_call | solution.py:674
  (473 shorter events, 195.6 us)
Async XLA Ops:
  7.2 143.1 %all-gather.6.cloned.1.call-start = ((), (), s32[]{:S(2)}) async-start(), calls=%async_computation | async-start | bytes 2621440 | tf_op jit(solution)/shard_map/all_gather | solution.py:116
  8.0 21.3 %collective-permute-start.2 = (bf16[8,128]{1,0:T(8,128)(2,1)S(1)}, bf16[8,128]{1,0:T(8,128)(2,1)S(1)}, u32[]{:S(2)}, u32[]{:S(2)}) collective-permute-start(bf16[8,128]{1,0:T(8,128)(2,1)S(1)} %pad_maximum_fusion.12), channel_id=1, source_target_pairs={{0,6},{1,7},{2,4},{3,5},{4,2},{5,3},{6,0},{7,1},{8,14},{9,15},{10,... | collective-permute-start | bytes 6152 | tf_op jit(solution)/shard_map/ppermute | solution.py:56
  12.0 17.4 %collective-permute-start.1 = (bf16[8,128]{1,0:T(8,128)(2,1)S(1)}, bf16[8,128]{1,0:T(8,128)(2,1)S(1)}, u32[]{:S(2)}, u32[]{:S(2)}) collective-permute-start(bf16[8,128]{1,0:T(8,128)(2,1)S(1)} %pad_maximum_fusion.12), channel_id=1, source_target_pairs={{0,4},{1,5},{2,6},{3,7},{4,0},{5,1},{6,2},{7,3},{8,12},{9,13},{10,... | collective-permute-start | bytes 6152 | tf_op jit(solution)/shard_map/ppermute | solution.py:56
  15.1 12.5 %collective-permute-start.5 = (bf16[128,1024]{1,0:T(8,128)(2,1)S(1)}, bf16[128,1024]{1,0:T(8,128)(2,1)S(1)}, u32[]{:S(2)}, u32[]{:S(2)}) collective-permute-start(bf16[128,1024]{1,0:T(8,128)(2,1)S(1)} %get-tuple-element.509), channel_id=1, source_target_pairs={{0,4},{1,5},{2,6},{3,7},{4,0},{5,1},{6,2},{7,3},{8,12},{9,13},{10,... | collective-permute-start | bytes 786440 | tf_op jit(solution)/shard_map/ppermute | solution.py:56
  15.2 12.5 %collective-permute-start.4 = (bf16[128,1024]{1,0:T(8,128)(2,1)S(1)}, bf16[128,1024]{1,0:T(8,128)(2,1)S(1)}, u32[]{:S(2)}, u32[]{:S(2)}) collective-permute-start(bf16[128,1024]{1,0:T(8,128)(2,1)S(1)} %get-tuple-element.509), channel_id=1, source_target_pairs={{0,2},{1,3},{2,0},{3,1},{4,6},{5,7},{6,4},{7,5},{8,10},{9,11},{10,... | collective-permute-start | bytes 786440 | tf_op jit(solution)/shard_map/ppermute | solution.py:56
  39.6 13.3 %collective-permute-start.14 = (bf16[128,1024]{1,0:T(8,128)(2,1)S(1)}, bf16[128,1024]{1,0:T(8,128)(2,1)S(1)}, u32[]{:S(2)}, u32[]{:S(2)}) collective-permute-start(bf16[128,1024]{1,0:T(8,128)(2,1)S(1)} %get-tuple-element.250), channel_id=1, source_target_pairs={{0,6},{1,7},{2,4},{3,5},{4,2},{5,3},{6,0},{7,1},{8,14},{9,15},{10,... | collective-permute-start | bytes 786440 | tf_op jit(solution)/shard_map/ppermute | solution.py:56
  55.6 15.2 %collective-permute-start.18 = (bf16[128,1152]{1,0:T(8,128)(2,1)}, bf16[128,1152]{1,0:T(8,128)(2,1)S(1)}, u32[]{:S(2)}, u32[]{:S(2)}) collective-permute-start(bf16[128,1152]{1,0:T(8,128)(2,1)} %concatenate.86), channel_id=1, source_target_pairs={{0,6},{1,7},{2,4},{3,5},{4,2},{5,3},{6,0},{7,1},{8,14},{9,15},{10,... | collective-permute-start | bytes 884744 | tf_op jit(solution)/shard_map/ppermute | solution.py:56
  57.2 16.5 %collective-permute-start.17 = (bf16[128,1152]{1,0:T(8,128)(2,1)}, bf16[128,1152]{1,0:T(8,128)(2,1)}, u32[]{:S(2)}, u32[]{:S(2)}) collective-permute-start(bf16[128,1152]{1,0:T(8,128)(2,1)} %concatenate.86), channel_id=1, source_target_pairs={{0,4},{1,5},{2,6},{3,7},{4,0},{5,1},{6,2},{7,3},{8,12},{9,13},{10,... | collective-permute-start | bytes 884744 | tf_op jit(solution)/shard_map/ppermute | solution.py:56
  58.7 18.5 %collective-permute-start.16 = (bf16[128,1152]{1,0:T(8,128)(2,1)}, bf16[128,1152]{1,0:T(8,128)(2,1)}, u32[]{:S(2)}, u32[]{:S(2)}) collective-permute-start(bf16[128,1152]{1,0:T(8,128)(2,1)} %concatenate.86), channel_id=1, source_target_pairs={{0,2},{1,3},{2,0},{3,1},{4,6},{5,7},{6,4},{7,5},{8,10},{9,11},{10,... | collective-permute-start | bytes 884744 | tf_op jit(solution)/shard_map/ppermute | solution.py:56
  59.2 25.7 %collective-permute-start.10 = (bf16[128,1024]{1,0:T(8,128)(2,1)}, bf16[128,1024]{1,0:T(8,128)(2,1)S(1)}, u32[]{:S(2)}, u32[]{:S(2)}) collective-permute-start(bf16[128,1024]{1,0:T(8,128)(2,1)} %get-tuple-element.248), channel_id=1, source_target_pairs={{0,6},{1,7},{2,4},{3,5},{4,2},{5,3},{6,0},{7,1},{8,14},{9,15},{10,... | collective-permute-start | bytes 786440 | tf_op jit(solution)/shard_map/ppermute | solution.py:56
  64.4 19.5 %collective-permute-start.9 = (bf16[128,1024]{1,0:T(8,128)(2,1)}, bf16[128,1024]{1,0:T(8,128)(2,1)}, u32[]{:S(2)}, u32[]{:S(2)}) collective-permute-start(bf16[128,1024]{1,0:T(8,128)(2,1)} %get-tuple-element.248), channel_id=1, source_target_pairs={{0,4},{1,5},{2,6},{3,7},{4,0},{5,1},{6,2},{7,3},{8,12},{9,13},{10,... | collective-permute-start | bytes 786440 | tf_op jit(solution)/shard_map/ppermute | solution.py:56
  101.6 199.5 %all-gather.8.cloned.1.call-start = ((), (), s32[]{:S(2)}) async-start(), calls=%async_computation.1 | async-start | bytes 5898240 | tf_op jit(solution)/shard_map/all_gather | solution.py:116
  103.8 17.8 %collective-permute-start.22 = (bf16[128,1152]{1,0:T(8,128)(2,1)}, bf16[128,1152]{1,0:T(8,128)(2,1)S(1)}, u32[]{:S(2)}, u32[]{:S(2)}) collective-permute-start(bf16[128,1152]{1,0:T(8,128)(2,1)} %get-tuple-element.267), channel_id=1, source_target_pairs={{0,6},{1,7},{2,4},{3,5},{4,2},{5,3},{6,0},{7,1},{8,14},{9,15},{10,... | collective-permute-start | bytes 884744 | tf_op jit(solution)/shard_map/ppermute | solution.py:56
  106.7 14.9 %collective-permute-start.21 = (bf16[128,1152]{1,0:T(8,128)(2,1)}, bf16[128,1152]{1,0:T(8,128)(2,1)S(1)}, u32[]{:S(2)}, u32[]{:S(2)}) collective-permute-start(bf16[128,1152]{1,0:T(8,128)(2,1)} %get-tuple-element.267), channel_id=1, source_target_pairs={{0,4},{1,5},{2,6},{3,7},{4,0},{5,1},{6,2},{7,3},{8,12},{9,13},{10,... | collective-permute-start | bytes 884744 | tf_op jit(solution)/shard_map/ppermute | solution.py:56
  122.7 298.6 %all-gather.10.cloned.1.call-start = ((), (), s32[]{:S(2)}) async-start(), calls=%async_computation.2 | async-start | bytes 5898240 | tf_op jit(solution)/shard_map/all_gather | solution.py:116
  150.2 34.8 %collective-permute-start.31 = (bf16[512,2048]{1,0:T(8,128)(2,1)}, bf16[512,2048]{1,0:T(8,128)(2,1)S(1)}, u32[]{:S(2)}, u32[]{:S(2)}) collective-permute-start(bf16[512,2048]{1,0:T(8,128)(2,1)} %all-gather.6.cloned.1.call-done.refs_0_), channel_id=1, source_target_pairs={{0,1},{1,0},{2,3},{3,2},{4,5},{5,4},{6,7},{7,6},{8,9},{9,8},{10,11... | collective-permute-start | bytes 6291464 | tf_op jit(solution)/shard_map/ppermute | solution.py:48
  152.3 14.9 %collective-permute-start.37 = (bf16[128,1152]{1,0:T(8,128)(2,1)S(1)}, bf16[128,1152]{1,0:T(8,128)(2,1)S(1)}, u32[]{:S(2)}, u32[]{:S(2)}) collective-permute-start(bf16[128,1152]{1,0:T(8,128)(2,1)S(1)} %concatenate.92), channel_id=1, source_target_pairs={{0,4},{1,5},{2,6},{3,7},{4,0},{5,1},{6,2},{7,3},{8,12},{9,13},{10,... | collective-permute-start | bytes 884744 | tf_op jit(solution)/shard_map/ppermute | solution.py:56
  152.9 14.4 %collective-permute-start.36 = (bf16[128,1152]{1,0:T(8,128)(2,1)S(1)}, bf16[128,1152]{1,0:T(8,128)(2,1)S(1)}, u32[]{:S(2)}, u32[]{:S(2)}) collective-permute-start(bf16[128,1152]{1,0:T(8,128)(2,1)S(1)} %concatenate.92), channel_id=1, source_target_pairs={{0,2},{1,3},{2,0},{3,1},{4,6},{5,7},{6,4},{7,5},{8,10},{9,11},{10,... | collective-permute-start | bytes 884744 | tf_op jit(solution)/shard_map/ppermute | solution.py:56
  169.1 13.9 %collective-permute-start.26 = (bf16[128,1024]{1,0:T(8,128)(2,1)}, bf16[128,1024]{1,0:T(8,128)(2,1)S(1)}, u32[]{:S(2)}, u32[]{:S(2)}) collective-permute-start(bf16[128,1024]{1,0:T(8,128)(2,1)} %get-tuple-element.272), channel_id=1, source_target_pairs={{0,4},{1,5},{2,6},{3,7},{4,0},{5,1},{6,2},{7,3},{8,12},{9,13},{10,... | collective-permute-start | bytes 786440 | tf_op jit(solution)/shard_map/ppermute | solution.py:107
  170.6 12.5 %collective-permute-start.27 = (bf16[128,1024]{1,0:T(8,128)(2,1)}, bf16[128,1024]{1,0:T(8,128)(2,1)S(1)}, u32[]{:S(2)}, u32[]{:S(2)}) collective-permute-start(bf16[128,1024]{1,0:T(8,128)(2,1)} %get-tuple-element.273), channel_id=1, source_target_pairs={{0,6},{1,7},{2,4},{3,5},{4,2},{5,3},{6,0},{7,1},{8,14},{9,15},{10,... | collective-permute-start | bytes 786440 | tf_op jit(solution)/shard_map/ppermute | solution.py:107
  193.3 17.4 %collective-permute-start.39 = (bf16[512,1152]{1,0:T(8,128)(2,1)S(1)}, bf16[512,1152]{1,0:T(8,128)(2,1)}, u32[]{:S(2)}, u32[]{:S(2)}) collective-permute-start(bf16[512,1152]{1,0:T(8,128)(2,1)S(1)} %constant_dynamic-update-slice_fusion.20.refs_2_), channel_id=1, source_target_pairs={{0,1},{1,0},{2,3},{3,2},{4,5},{5,4},{6,7},{7,6},{8,9},{9,8},{10,11... | collective-permute-start | bytes 3538952 | tf_op jit(solution)/shard_map/ppermute | solution.py:48
  193.4 12.3 %collective-permute-start.34 = (bf16[128,1024]{1,0:T(8,128)(2,1)}, bf16[128,1024]{1,0:T(8,128)(2,1)S(1)}, u32[]{:S(2)}, u32[]{:S(2)}) collective-permute-start(bf16[128,1024]{1,0:T(8,128)(2,1)} %get-tuple-element.283), channel_id=1, source_target_pairs={{0,6},{1,7},{2,4},{3,5},{4,2},{5,3},{6,0},{7,1},{8,14},{9,15},{10,... | collective-permute-start | bytes 786440 | tf_op jit(solution)/shard_map/ppermute | solution.py:56
  221.2 15.4 %collective-permute-start.41 = (bf16[128,1152]{1,0:T(8,128)(2,1)}, bf16[128,1152]{1,0:T(8,128)(2,1)S(1)}, u32[]{:S(2)}, u32[]{:S(2)}) collective-permute-start(bf16[128,1152]{1,0:T(8,128)(2,1)} %get-tuple-element.292), channel_id=1, source_target_pairs={{0,4},{1,5},{2,6},{3,7},{4,0},{5,1},{6,2},{7,3},{8,12},{9,13},{10,... | collective-permute-start | bytes 884744 | tf_op jit(solution)/shard_map/ppermute | solution.py:56
  222.6 15.3 %collective-permute-start.40 = (bf16[128,1152]{1,0:T(8,128)(2,1)}, bf16[128,1152]{1,0:T(8,128)(2,1)S(1)}, u32[]{:S(2)}, u32[]{:S(2)}) collective-permute-start(bf16[128,1152]{1,0:T(8,128)(2,1)} %get-tuple-element.292), channel_id=1, source_target_pairs={{0,2},{1,3},{2,0},{3,1},{4,6},{5,7},{6,4},{7,5},{8,10},{9,11},{10,... | collective-permute-start | bytes 884744 | tf_op jit(solution)/shard_map/ppermute | solution.py:56
  240.1 181.3 %all-gather.12.cloned.1.call-start = ((), (), s32[]{:S(2)}) async-start(), calls=%async_computation.3 | async-start | bytes 5242880 | tf_op jit(solution)/shard_map/all_gather | solution.py:116
  263.8 14.0 %collective-permute-start.44 = (bf16[128,1024]{1,0:T(8,128)(2,1)S(1)}, bf16[128,1024]{1,0:T(8,128)(2,1)S(1)}, u32[]{:S(2)}, u32[]{:S(2)}) collective-permute-start(bf16[128,1024]{1,0:T(8,128)(2,1)S(1)} %bitcast.95), channel_id=1, source_target_pairs={{0,4},{1,5},{2,6},{3,7},{4,0},{5,1},{6,2},{7,3},{8,12},{9,13},{10,... | collective-permute-start | bytes 786440 | tf_op jit(solution)/shard_map/ppermute | solution.py:56
  265.1 12.8 %collective-permute-start.43 = (bf16[128,1024]{1,0:T(8,128)(2,1)S(1)}, bf16[128,1024]{1,0:T(8,128)(2,1)S(1)}, u32[]{:S(2)}, u32[]{:S(2)}) collective-permute-start(bf16[128,1024]{1,0:T(8,128)(2,1)S(1)} %bitcast.96), channel_id=1, source_target_pairs={{0,2},{1,3},{2,0},{3,1},{4,6},{5,7},{6,4},{7,5},{8,10},{9,11},{10,... | collective-permute-start | bytes 786440 | tf_op jit(solution)/shard_map/ppermute | solution.py:56
  278.1 23.0 %collective-permute-start.49 = (bf16[128,1024]{1,0:T(8,128)(2,1)S(1)}, bf16[128,1024]{1,0:T(8,128)(2,1)S(1)}, u32[]{:S(2)}, u32[]{:S(2)}) collective-permute-start(bf16[128,1024]{1,0:T(8,128)(2,1)S(1)} %copy-done.92), channel_id=1, source_target_pairs={{0,2},{1,3},{2,0},{3,1},{4,6},{5,7},{6,4},{7,5},{8,10},{9,11},{10,... | collective-permute-start | bytes 786440 | tf_op jit(solution)/shard_map/ppermute | solution.py:107
  278.9 22.2 %collective-permute-start.50 = (bf16[128,1024]{1,0:T(8,128)(2,1)S(1)}, bf16[128,1024]{1,0:T(8,128)(2,1)S(1)}, u32[]{:S(2)}, u32[]{:S(2)}) collective-permute-start(bf16[128,1024]{1,0:T(8,128)(2,1)S(1)} %copy-done.91), channel_id=1, source_target_pairs={{0,4},{1,5},{2,6},{3,7},{4,0},{5,1},{6,2},{7,3},{8,12},{9,13},{10,... | collective-permute-start | bytes 786440 | tf_op jit(solution)/shard_map/ppermute | solution.py:107
  279.8 21.3 %collective-permute-start.51 = (bf16[128,1024]{1,0:T(8,128)(2,1)S(1)}, bf16[128,1024]{1,0:T(8,128)(2,1)S(1)}, u32[]{:S(2)}, u32[]{:S(2)}) collective-permute-start(bf16[128,1024]{1,0:T(8,128)(2,1)S(1)} %copy-done.90), channel_id=1, source_target_pairs={{0,6},{1,7},{2,4},{3,5},{4,2},{5,3},{6,0},{7,1},{8,14},{9,15},{10,... | collective-permute-start | bytes 786440 | tf_op jit(solution)/shard_map/ppermute | solution.py:107
  302.0 201.3 %all-gather.14.cloned.1.call-start = ((), (), s32[]{:S(2)}) async-start(), calls=%async_computation.4 | async-start | bytes 5242880 | tf_op jit(solution)/shard_map/all_gather | solution.py:116
  310.5 14.8 %collective-permute-start.55 = (bf16[128,1152]{1,0:T(8,128)(2,1)}, bf16[128,1152]{1,0:T(8,128)(2,1)S(1)}, u32[]{:S(2)}, u32[]{:S(2)}) collective-permute-start(bf16[128,1152]{1,0:T(8,128)(2,1)} %get-tuple-element.324), channel_id=1, source_target_pairs={{0,6},{1,7},{2,4},{3,5},{4,2},{5,3},{6,0},{7,1},{8,14},{9,15},{10,... | collective-permute-start | bytes 884744 | tf_op jit(solution)/shard_map/ppermute | solution.py:107
  339.2 12.4 %collective-permute-start.57 = (bf16[512,1024]{1,0:T(8,128)(2,1)S(1)}, bf16[512,1024]{1,0:T(8,128)(2,1)S(1)}, u32[]{:S(2)}, u32[]{:S(2)}) collective-permute-start(bf16[512,1024]{1,0:T(8,128)(2,1)S(1)} %convolution_convert_fusion.4), channel_id=1, source_target_pairs={{0,1},{1,0},{2,3},{3,2},{4,5},{5,4},{6,7},{7,6},{8,9},{9,8},{10,11... | collective-permute-start | bytes 3145736 | tf_op jit(solution)/shard_map/ppermute | solution.py:48
  346.0 14.7 %collective-permute-start.59 = (bf16[128,1024]{1,0:T(8,128)(2,1)}, bf16[128,1024]{1,0:T(8,128)(2,1)S(1)}, u32[]{:S(2)}, u32[]{:S(2)}) collective-permute-start(bf16[128,1024]{1,0:T(8,128)(2,1)} %get-tuple-element.343), channel_id=1, source_target_pairs={{0,4},{1,5},{2,6},{3,7},{4,0},{5,1},{6,2},{7,3},{8,12},{9,13},{10,... | collective-permute-start | bytes 786440 | tf_op jit(solution)/shard_map/ppermute | solution.py:107
  348.7 13.8 %collective-permute-start.60 = (bf16[128,1024]{1,0:T(8,128)(2,1)}, bf16[128,1024]{1,0:T(8,128)(2,1)S(1)}, u32[]{:S(2)}, u32[]{:S(2)}) collective-permute-start(bf16[128,1024]{1,0:T(8,128)(2,1)} %get-tuple-element.344), channel_id=1, source_target_pairs={{0,6},{1,7},{2,4},{3,5},{4,2},{5,3},{6,0},{7,1},{8,14},{9,15},{10,... | collective-permute-start | bytes 786440 | tf_op jit(solution)/shard_map/ppermute | solution.py:107
  374.2 15.3 %collective-permute-start.64 = (bf16[512,2048]{1,0:T(8,128)(2,1)}, bf16[512,2048]{1,0:T(8,128)(2,1)S(1)}, u32[]{:S(2)}, u32[]{:S(2)}) collective-permute-start(bf16[512,2048]{1,0:T(8,128)(2,1)} %convolution_convert_fusion), channel_id=1, source_target_pairs={{0,1},{1,0},{2,3},{3,2},{4,5},{5,4},{6,7},{7,6},{8,9},{9,8},{10,11... | collective-permute-start | bytes 6291464 | tf_op jit(solution)/shard_map/ppermute | solution.py:48
  376.1 13.4 %collective-permute-start.62 = (bf16[128,1024]{1,0:T(8,128)(2,1)S(1)}, bf16[128,1024]{1,0:T(8,128)(2,1)S(1)}, u32[]{:S(2)}, u32[]{:S(2)}) collective-permute-start(bf16[128,1024]{1,0:T(8,128)(2,1)S(1)} %copy-done.73), channel_id=1, source_target_pairs={{0,4},{1,5},{2,6},{3,7},{4,0},{5,1},{6,2},{7,3},{8,12},{9,13},{10,... | collective-permute-start | bytes 786440 | tf_op jit(solution)/shard_map/ppermute | solution.py:56
  376.3 13.1 %collective-permute-start.61 = (bf16[128,1024]{1,0:T(8,128)(2,1)S(1)}, bf16[128,1024]{1,0:T(8,128)(2,1)S(1)}, u32[]{:S(2)}, u32[]{:S(2)}) collective-permute-start(bf16[128,1024]{1,0:T(8,128)(2,1)S(1)} %copy-done.73), channel_id=1, source_target_pairs={{0,2},{1,3},{2,0},{3,1},{4,6},{5,7},{6,4},{7,5},{8,10},{9,11},{10,... | collective-permute-start | bytes 786440 | tf_op jit(solution)/shard_map/ppermute | solution.py:56
  394.8 23.0 %collective-permute-start.66 = (bf16[128,2048]{1,0:T(8,128)(2,1)}, bf16[128,2048]{1,0:T(8,128)(2,1)}, u32[]{:S(2)}, u32[]{:S(2)}) collective-permute-start(bf16[128,2048]{1,0:T(8,128)(2,1)} %get-tuple-element.361), channel_id=1, source_target_pairs={{0,2},{1,3},{2,0},{3,1},{4,6},{5,7},{6,4},{7,5},{8,10},{9,11},{10,... | collective-permute-start | bytes 1572872 | tf_op jit(solution)/shard_map/ppermute | solution.py:107
  395.8 25.5 %collective-permute-start.67 = (bf16[128,2048]{1,0:T(8,128)(2,1)}, bf16[128,2048]{1,0:T(8,128)(2,1)}, u32[]{:S(2)}, u32[]{:S(2)}) collective-permute-start(bf16[128,2048]{1,0:T(8,128)(2,1)} %get-tuple-element.362), channel_id=1, source_target_pairs={{0,4},{1,5},{2,6},{3,7},{4,0},{5,1},{6,2},{7,3},{8,12},{9,13},{10,... | collective-permute-start | bytes 1572872 | tf_op jit(solution)/shard_map/ppermute | solution.py:107
  397.1 24.2 %collective-permute-start.68 = (bf16[128,2048]{1,0:T(8,128)(2,1)}, bf16[128,2048]{1,0:T(8,128)(2,1)}, u32[]{:S(2)}, u32[]{:S(2)}) collective-permute-start(bf16[128,2048]{1,0:T(8,128)(2,1)} %get-tuple-element.363), channel_id=1, source_target_pairs={{0,6},{1,7},{2,4},{3,5},{4,2},{5,3},{6,0},{7,1},{8,14},{9,15},{10,... | collective-permute-start | bytes 1572872 | tf_op jit(solution)/shard_map/ppermute | solution.py:107
  421.3 18.9 %collective-permute-start.70 = (bf16[2048,1152]{1,0:T(8,128)(2,1)}, bf16[2048,1152]{1,0:T(8,128)(2,1)}, u32[]{:S(2)}, u32[]{:S(2)}) collective-permute-start(bf16[2048,1152]{1,0:T(8,128)(2,1)} %all-gather.10.cloned.1.call-done.refs_0_), channel_id=1, source_target_pairs={{0,1},{1,0},{2,3},{3,2},{4,5},{5,4},{6,7},{7,6},{8,9},{9,8},{10,11... | collective-permute-start | bytes 14155784 | tf_op jit(solution)/shard_map/ppermute | solution.py:48
  421.4 18.8 %collective-permute-start.71 = (bf16[2048,1024]{1,0:T(8,128)(2,1)}, bf16[2048,1024]{1,0:T(8,128)(2,1)}, u32[]{:S(2)}, u32[]{:S(2)}) collective-permute-start(bf16[2048,1024]{1,0:T(8,128)(2,1)} %all-gather.12.cloned.1.call-done.refs_2_), channel_id=1, source_target_pairs={{0,1},{1,0},{2,3},{3,2},{4,5},{5,4},{6,7},{7,6},{8,9},{9,8},{10,11... | collective-permute-start | bytes 12582920 | tf_op jit(solution)/shard_map/ppermute | solution.py:48
  421.9 153.8 %all-reduce.4.cloned.1.call-start = ((), (), s32[]{:S(2)}) async-start(), calls=%async_computation.5 | async-start | bytes 1572864 | tf_op jit(solution)/shard_map/psum | solution.py:1392
  436.7 24.7 %collective-permute-start.75 = (bf16[128,1152]{1,0:T(8,128)(2,1)}, bf16[128,1152]{1,0:T(8,128)(2,1)S(1)}, u32[]{:S(2)}, u32[]{:S(2)}) collective-permute-start(bf16[128,1152]{1,0:T(8,128)(2,1)} %get-tuple-element.370), channel_id=1, source_target_pairs={{0,2},{1,3},{2,0},{3,1},{4,6},{5,7},{6,4},{7,5},{8,10},{9,11},{10,... | collective-permute-start | bytes 884744 | tf_op jit(solution)/shard_map/ppermute | solution.py:107
  437.7 25.6 %collective-permute-start.76 = (bf16[128,1152]{1,0:T(8,128)(2,1)}, bf16[128,1152]{1,0:T(8,128)(2,1)S(1)}, u32[]{:S(2)}, u32[]{:S(2)}) collective-permute-start(bf16[128,1152]{1,0:T(8,128)(2,1)} %get-tuple-element.371), channel_id=1, source_target_pairs={{0,4},{1,5},{2,6},{3,7},{4,0},{5,1},{6,2},{7,3},{8,12},{9,13},{10,... | collective-permute-start | bytes 884744 | tf_op jit(solution)/shard_map/ppermute | solution.py:107
  438.4 24.9 %collective-permute-start.77 = (bf16[128,1152]{1,0:T(8,128)(2,1)}, bf16[128,1152]{1,0:T(8,128)(2,1)S(1)}, u32[]{:S(2)}, u32[]{:S(2)}) collective-permute-start(bf16[128,1152]{1,0:T(8,128)(2,1)} %get-tuple-element.372), channel_id=1, source_target_pairs={{0,6},{1,7},{2,4},{3,5},{4,2},{5,3},{6,0},{7,1},{8,14},{9,15},{10,... | collective-permute-start | bytes 884744 | tf_op jit(solution)/shard_map/ppermute | solution.py:107
  459.7 15.1 %collective-permute-start.72 = (bf16[128,1024]{1,0:T(8,128)(2,1)S(1)}, bf16[128,1024]{1,0:T(8,128)(2,1)S(1)}, u32[]{:S(2)}, u32[]{:S(2)}) collective-permute-start(bf16[128,1024]{1,0:T(8,128)(2,1)S(1)} %copy-done.89), channel_id=1, source_target_pairs={{0,2},{1,3},{2,0},{3,1},{4,6},{5,7},{6,4},{7,5},{8,10},{9,11},{10,... | collective-permute-start | bytes 786440 | tf_op jit(solution)/shard_map/ppermute | solution.py:107
  460.7 14.1 %collective-permute-start.73 = (bf16[128,1024]{1,0:T(8,128)(2,1)S(1)}, bf16[128,1024]{1,0:T(8,128)(2,1)S(1)}, u32[]{:S(2)}, u32[]{:S(2)}) collective-permute-start(bf16[128,1024]{1,0:T(8,128)(2,1)S(1)} %copy-done.88), channel_id=1, source_target_pairs={{0,4},{1,5},{2,6},{3,7},{4,0},{5,1},{6,2},{7,3},{8,12},{9,13},{10,... | collective-permute-start | bytes 786440 | tf_op jit(solution)/shard_map/ppermute | solution.py:107
  461.4 13.4 %collective-permute-start.74 = (bf16[128,1024]{1,0:T(8,128)(2,1)S(1)}, bf16[128,1024]{1,0:T(8,128)(2,1)S(1)}, u32[]{:S(2)}, u32[]{:S(2)}) collective-permute-start(bf16[128,1024]{1,0:T(8,128)(2,1)S(1)} %copy-done.87), channel_id=1, source_target_pairs={{0,6},{1,7},{2,4},{3,5},{4,2},{5,3},{6,0},{7,1},{8,14},{9,15},{10,... | collective-permute-start | bytes 786440 | tf_op jit(solution)/shard_map/ppermute | solution.py:107
  481.4 21.9 %collective-permute-start.79 = (bf16[128,1024]{1,0:T(8,128)(2,1)}, bf16[128,1024]{1,0:T(8,128)(2,1)S(1)}, u32[]{:S(2)}, u32[]{:S(2)}) collective-permute-start(bf16[128,1024]{1,0:T(8,128)(2,1)} %get-tuple-element.409), channel_id=1, source_target_pairs={{0,2},{1,3},{2,0},{3,1},{4,6},{5,7},{6,4},{7,5},{8,10},{9,11},{10,... | collective-permute-start | bytes 786440 | tf_op jit(solution)/shard_map/ppermute | solution.py:107
  483.8 19.5 %collective-permute-start.80 = (bf16[128,1024]{1,0:T(8,128)(2,1)}, bf16[128,1024]{1,0:T(8,128)(2,1)S(1)}, u32[]{:S(2)}, u32[]{:S(2)}) collective-permute-start(bf16[128,1024]{1,0:T(8,128)(2,1)} %get-tuple-element.410), channel_id=1, source_target_pairs={{0,4},{1,5},{2,6},{3,7},{4,0},{5,1},{6,2},{7,3},{8,12},{9,13},{10,... | collective-permute-start | bytes 786440 | tf_op jit(solution)/shard_map/ppermute | solution.py:107
  486.8 16.5 %collective-permute-start.81 = (bf16[128,1024]{1,0:T(8,128)(2,1)}, bf16[128,1024]{1,0:T(8,128)(2,1)S(1)}, u32[]{:S(2)}, u32[]{:S(2)}) collective-permute-start(bf16[128,1024]{1,0:T(8,128)(2,1)} %get-tuple-element.411), channel_id=1, source_target_pairs={{0,6},{1,7},{2,4},{3,5},{4,2},{5,3},{6,0},{7,1},{8,14},{9,15},{10,... | collective-permute-start | bytes 786440 | tf_op jit(solution)/shard_map/ppermute | solution.py:107
  516.2 15.5 %collective-permute-start.82 = (bf16[512,2176]{1,0:T(8,128)(2,1)}, bf16[512,2176]{1,0:T(8,128)(2,1)S(1)}, u32[]{:S(2)}, u32[]{:S(2)}) collective-permute-start(bf16[512,2176]{1,0:T(8,128)(2,1)} %fusion.1), channel_id=1, source_target_pairs={{0,1},{1,0},{2,3},{3,2},{4,5},{5,4},{6,7},{7,6},{8,9},{9,8},{10,11... | collective-permute-start | bytes 6684680 | tf_op jit(solution)/shard_map/ppermute | solution.py:48
  525.1 12.1 %collective-permute-start.84 = (bf16[128,1024]{1,0:T(8,128)(2,1)}, bf16[128,1024]{1,0:T(8,128)(2,1)S(1)}, u32[]{:S(2)}, u32[]{:S(2)}) collective-permute-start(bf16[128,1024]{1,0:T(8,128)(2,1)} %get-tuple-element.443), channel_id=1, source_target_pairs={{0,2},{1,3},{2,0},{3,1},{4,6},{5,7},{6,4},{7,5},{8,10},{9,11},{10,... | collective-permute-start | bytes 786440 | tf_op jit(solution)/shard_map/ppermute | solution.py:107
  525.6 13.3 %collective-permute-start.85 = (bf16[128,1024]{1,0:T(8,128)(2,1)}, bf16[128,1024]{1,0:T(8,128)(2,1)S(1)}, u32[]{:S(2)}, u32[]{:S(2)}) collective-permute-start(bf16[128,1024]{1,0:T(8,128)(2,1)} %get-tuple-element.444), channel_id=1, source_target_pairs={{0,4},{1,5},{2,6},{3,7},{4,0},{5,1},{6,2},{7,3},{8,12},{9,13},{10,... | collective-permute-start | bytes 786440 | tf_op jit(solution)/shard_map/ppermute | solution.py:107
  527.1 13.6 %collective-permute-start.86 = (bf16[128,1024]{1,0:T(8,128)(2,1)}, bf16[128,1024]{1,0:T(8,128)(2,1)S(1)}, u32[]{:S(2)}, u32[]{:S(2)}) collective-permute-start(bf16[128,1024]{1,0:T(8,128)(2,1)} %get-tuple-element.445), channel_id=1, source_target_pairs={{0,6},{1,7},{2,4},{3,5},{4,2},{5,3},{6,0},{7,1},{8,14},{9,15},{10,... | collective-permute-start | bytes 786440 | tf_op jit(solution)/shard_map/ppermute | solution.py:107
  541.4 34.3 %collective-permute-start.87 = (bf16[128,2176]{1,0:T(8,128)(2,1)}, bf16[128,2176]{1,0:T(8,128)(2,1)S(1)}, u32[]{:S(2)}, u32[]{:S(2)}) collective-permute-start(bf16[128,2176]{1,0:T(8,128)(2,1)} %get-tuple-element.447), channel_id=1, source_target_pairs={{0,2},{1,3},{2,0},{3,1},{4,6},{5,7},{6,4},{7,5},{8,10},{9,11},{10,... | collective-permute-start | bytes 1671176 | tf_op jit(solution)/shard_map/ppermute | solution.py:107
  542.1 33.6 %collective-permute-start.88 = (bf16[128,2176]{1,0:T(8,128)(2,1)}, bf16[128,2176]{1,0:T(8,128)(2,1)S(1)}, u32[]{:S(2)}, u32[]{:S(2)}) collective-permute-start(bf16[128,2176]{1,0:T(8,128)(2,1)} %get-tuple-element.448), channel_id=1, source_target_pairs={{0,4},{1,5},{2,6},{3,7},{4,0},{5,1},{6,2},{7,3},{8,12},{9,13},{10,... | collective-permute-start | bytes 1671176 | tf_op jit(solution)/shard_map/ppermute | solution.py:107
  543.8 31.9 %collective-permute-start.89 = (bf16[128,2176]{1,0:T(8,128)(2,1)}, bf16[128,2176]{1,0:T(8,128)(2,1)}, u32[]{:S(2)}, u32[]{:S(2)}) collective-permute-start(bf16[128,2176]{1,0:T(8,128)(2,1)} %get-tuple-element.449), channel_id=1, source_target_pairs={{0,6},{1,7},{2,4},{3,5},{4,2},{5,3},{6,0},{7,1},{8,14},{9,15},{10,... | collective-permute-start | bytes 1671176 | tf_op jit(solution)/shard_map/ppermute | solution.py:107
  575.7 14.3 %collective-permute-start.90 = (bf16[2048,1152]{1,0:T(8,128)(2,1)}, bf16[2048,1152]{1,0:T(8,128)(2,1)}, u32[]{:S(2)}, u32[]{:S(2)}) collective-permute-start(bf16[2048,1152]{1,0:T(8,128)(2,1)} %all-gather.8.cloned.1.call-done.refs_0_), channel_id=1, source_target_pairs={{0,1},{1,0},{2,3},{3,2},{4,5},{5,4},{6,7},{7,6},{8,9},{9,8},{10,11... | collective-permute-start | bytes 14155784 | tf_op jit(solution)/shard_map/ppermute | solution.py:48
  575.8 14.2 %collective-permute-start.91 = (bf16[2048,1024]{1,0:T(8,128)(2,1)}, bf16[2048,1024]{1,0:T(8,128)(2,1)}, u32[]{:S(2)}, u32[]{:S(2)}) collective-permute-start(bf16[2048,1024]{1,0:T(8,128)(2,1)} %all-gather.14.cloned.1.call-done.refs_2_), channel_id=1, source_target_pairs={{0,1},{1,0},{2,3},{3,2},{4,5},{5,4},{6,7},{7,6},{8,9},{9,8},{10,11... | collective-permute-start | bytes 12582920 | tf_op jit(solution)/shard_map/ppermute | solution.py:48
  579.0 20.3 %collective-permute-start.92 = (bf16[128,3200]{1,0:T(8,128)(2,1)S(1)}, bf16[128,3200]{1,0:T(8,128)(2,1)S(1)}, u32[]{:S(2)}, u32[]{:S(2)}) collective-permute-start(bf16[128,3200]{1,0:T(8,128)(2,1)S(1)} %pad_maximum_fusion.6), channel_id=1, source_target_pairs={{0,8},{8,0},{16,24},{24,16},{1,9},{9,1},{17,25},{25,17},{2,10},{10... | collective-permute-start | bytes 2457608 | tf_op jit(solution)/shard_map/ppermute | solution.py:121
  599.5 53.7 %collective-permute-start.93 = (bf16[128,3200]{1,0:T(8,128)(2,1)S(1)}, bf16[128,3200]{1,0:T(8,128)(2,1)S(1)}, u32[]{:S(2)}, u32[]{:S(2)}) collective-permute-start(bf16[128,3200]{1,0:T(8,128)(2,1)S(1)} %add_convert_fusion), channel_id=1, source_target_pairs={{0,16},{8,24},{16,0},{24,8},{1,17},{9,25},{17,1},{25,9},{2,18},{10... | collective-permute-start | bytes 2457608 | tf_op jit(solution)/shard_map/ppermute | solution.py:121
  (129 other events, 979.4 us)
Sparse Core Ops, SparseCore 0:
  101.8 47.7 all-gather.5
  151.2 88.1 all-gather.7
  240.9 87.8 all-gather.9
  330.2 79.2 all-gather.11
  422.0 79.2 all-gather.13
  520.9 44.2 all-reduce.3

commit v4 on v3

--- a/solution.py
+++ b/solution.py
@@ -367,54 +367,63 @@
     x_ref, dy_ref = refs[sum(counts) : sum(counts) + 2]
     tokens, grads, sems, grad_sems = refs[sum(counts) + 2 :]
     first = first_ref[0]
-    p = pl.program_id(0)
-    width = grads.shape[1]
+    s = pl.program_id(0)
+    p = pl.program_id(1)
+    width = grads.shape[2]
     slots = 2 * CAP
 
-    stream = stream_ref[0]
-    copies = []
-    for pieces, heights, target, sem in (
-        (token_pieces, token_rows, tokens, sems),
-        (grad_pieces, grad_rows, grads, grad_sems),
-    ):
-        start = 0
-        for index, (piece, rows) in enumerate(zip(pieces, heights, strict=True)):
-            source = piece.at[pl.ds(pl.multiple_of(stream * rows, PAIR), rows)]
-            copies.append(
-                (start, pltpu.make_async_copy(source, target.at[pl.ds(start, rows)], sem.at[index]))
-            )
-            start += rows
-
-    @pl.when(p == 0)
+    def copies(index, slot):
+        stream = stream_ref[index]
+        made = []
+        for pieces, heights, target, sem in (
+            (token_pieces, token_rows, tokens, sems),
+            (grad_pieces, grad_rows, grads, grad_sems),
+        ):
+            start = 0
+            for k, (piece, rows) in enumerate(zip(pieces, heights, strict=True)):
+                source = piece.at[pl.ds(pl.multiple_of(stream * rows, PAIR), rows)]
+                place = target.at[slot, pl.ds(start, rows)]
+                made.append((start, pltpu.make_async_copy(source, place, sem.at[slot, k])))
+                start += rows
+        return made
+
+    slot = lax.rem(s, 2)
+
+    @pl.when((p == 0) & (s == 0))
     def _():
-        for start, copy in copies:
+        for start, copy in copies(0, 0):
             copy.start()
 
-    for start, copy in copies:
+    @pl.when((p == 0) & (s + 1 < pl.num_programs(0)))
+    def _():
+        for start, copy in copies(s + 1, lax.rem(s + 1, 2)):
+            copy.start()
+
+    for start, copy in copies(s, slot):
 
         @pl.when(p == start // PAIR)
         def _():
             copy.wait()
 
     base = pl.multiple_of(p * PAIR, PAIR)
-    block = tokens[pl.ds(base, PAIR), :]
+    block = tokens[slot, pl.ds(base, PAIR), :]
     pick = pick_matrix(block[:, width:].astype(F32), first, experts)
     found = dot_tn(pick, block)
-    grown = dot_tn(pick, grads[pl.ds(base, PAIR), :])
+    grown = dot_tn(pick, grads[slot, pl.ds(base, PAIR), :])
     for k in range(experts):
         mine = found[k * slots : (k + 1) * slots]
-        x_ref[k] = mine[:, :width].astype(BF16)
+        x_ref[0, k] = mine[:, :width].astype(BF16)
         gate = jnp.sum(
             jnp.where(gate_lanes(first + k, slots), mine[:, width:], 0.0), axis=1, keepdims=True
         )
-        dy_ref[k] = (grown[k * slots : (k + 1) * slots] * gate).astype(BF16)
+        dy_ref[0, k] = (grown[k * slots : (k + 1) * slots] * gate).astype(BF16)
 
 
 def expert_grad_kernel(streams, aliased, start, *refs):
-    x_refs = refs[:streams]
-    dy_refs = refs[streams : 2 * streams]
-    hid_own, dgu_own, w_ref = refs[2 * streams : 2 * streams + 3]
-    rest = refs[2 * streams + 3 + (1 if aliased else 0) :]
+    x_own, x_others, dy_own, dy_others, hid_own, dgu_own, w_ref = refs[:7]
+    x_refs = [x_own] + [x_others.at[k] for k in range(streams - 1)]
+    dy_refs = [dy_own] + [dy_others.at[k] for k in range(streams - 1)]
+    rest = refs[7 + (1 if aliased else 0) :]
     out_ref, xs, dys, hids, dgus, sems = rest
     e = pl.program_id(0)
     experts = pl.num_programs(0)
@@ -622,8 +631,9 @@
     return partial, dy_rows, hid_rows, dgu_rows
 
 
-def pick_rows(token_pieces, grad_pieces, w_expert, first, stream):
+def pick_rows(token_pieces, grad_pieces, w_expert, first):
     streams = lax.axis_size("dp")
+    order = (lax.axis_index("dp") + jnp.arange(1, streams, dtype=jnp.int32)) % streams
     heights = [
         tuple(piece.shape[0] // streams for piece in pieces) for pieces in (token_pieces, grad_pieces)
     ]
@@ -631,41 +641,41 @@
     length = sum(heights[0])
     rows = length // BLOCK * CAP
     counts = (len(token_pieces), len(grad_pieces))
-    slab = pl.BlockSpec((experts, 2 * CAP, width), lambda p, *scalars: (0, p, 0))
+    slab = pl.BlockSpec((1, experts, 2 * CAP, width), lambda s, p, *scalars: (s, 0, p, 0))
     return pl.pallas_call(
         functools.partial(pick_kernel, experts, *heights),
         out_shape=(
-            jax.ShapeDtypeStruct((experts, rows, width), BF16),
-            jax.ShapeDtypeStruct((experts, rows, width), BF16),
+            jax.ShapeDtypeStruct((streams - 1, experts, rows, width), BF16),
+            jax.ShapeDtypeStruct((streams - 1, experts, rows, width), BF16),
         ),
         grid_spec=pltpu.PrefetchScalarGridSpec(
             num_scalar_prefetch=2,
-            grid=(length // PAIR,),
+            grid=(streams - 1, length // PAIR),
             in_specs=[ANY] * sum(counts),
             out_specs=(slab, slab),
             scratch_shapes=[
-                pltpu.VMEM((length, width + EXT), BF16),
-                pltpu.VMEM((length, width), BF16),
-                pltpu.SemaphoreType.DMA((counts[0],)),
-                pltpu.SemaphoreType.DMA((counts[1],)),
+                pltpu.VMEM((2, length, width + EXT), BF16),
+                pltpu.VMEM((2, length, width), BF16),
+                pltpu.SemaphoreType.DMA((2, counts[0])),
+                pltpu.SemaphoreType.DMA((2, counts[1])),
             ],
         ),
-        compiler_params=pltpu.CompilerParams(dimension_semantics=("arbitrary",), **PARAMS),
+        compiler_params=pltpu.CompilerParams(dimension_semantics=("arbitrary", "arbitrary"), **PARAMS),
         cost_estimate=pl.CostEstimate(
-            flops=4 * length * experts * 2 * CAP * width,
-            bytes_accessed=length * width * 4 + experts * rows * width * 4,
+            flops=4 * (streams - 1) * length * experts * 2 * CAP * width,
+            bytes_accessed=(streams - 1) * (length * width * 4 + experts * rows * width * 4),
             transcendentals=0,
         ),
         name="pick_rows",
-    )(first, stream, *token_pieces, *grad_pieces)
+    )(first, order, *token_pieces, *grad_pieces)
 
 
 def expert_grads(x_rows, dy_rows, hid_own, dgu_own, w_expert, layer_idx, start, experts, before):
-    streams = len(x_rows)
+    streams = x_rows[1].shape[0] + 1
     unused, rows, width = x_rows[0].shape
     depth = min(2, experts)
     operands = [*x_rows, *dy_rows, hid_own, dgu_own, w_expert]
-    in_specs = [ANY] * (2 * streams + 2) + [weight_spec(w_expert.shape, layer_idx, False, start)]
+    in_specs = [ANY] * 6 + [weight_spec(w_expert.shape, layer_idx, False, start)]
     aliases = {}
     if before is not None:
         aliases = {len(operands): 0}
@@ -1304,13 +1314,12 @@
             [x, (a, a_order), q, kv_pieces, o, den, un, h, pay, gates, x_rows, gate_rows, pair_values, pick]
             + [gain_one, qkv_weight, gain_two, out_weight, parts, out_columns]
         )
-        if layer_idx + 1 < layers:
-            next_out = both_cores(gather_chips(next_out, partial))
         own, sent = reduce_start(partial)
         if layer_idx + 1 < layers:
             next_qkv, unused = tie(next_qkv, sent)
             next_qkv = both_cores(next_qkv)
             x = total_of([h, *reduce_finish(own, sent)])
+            next_out = both_cores(gather_chips(next_out, x))
             x, (next_qkv,) = tie(x, next_qkv)
             qkv_weight, out_weight = [next_qkv], next_out
             parts = streams if hierarchical(ctx_size) else 1
@@ -1319,18 +1328,6 @@
             grad_near, (own, sent) = tie(grad_near, own, sent)
             grad_side = all_streams(grad_near)
     last_h, last_own, last_sent = h, own, sent
-
-    def pick_others(tokens_of, grads_of, which):
-        return [
-            pick_rows(
-                tokens_of,
-                grads_of,
-                w_expert,
-                first,
-                ((lax.axis_index("dp") + k) % streams).astype(jnp.int32).reshape(1),
-            )
-            for k in which
-        ]
 
     expert_sum = None
     early, late, routed = {}, {}, {}
@@ -1356,7 +1353,7 @@
             (side, grad_side), (partial,) = tie((side, grad_side), partial)
             side, grad_side = both_cores(side), both_cores(grad_side)
             (side, grad_side), (sent,) = tie((side, grad_side), sent)
-            picked = pick_others(side, grad_side, range(1, streams))
+            picked = pick_rows(side, grad_side, w_expert, first)
             late[1] = total_of(waiting).astype(BF16)
             sums[0], (picked, late[1]) = tie(sums[0], picked, late[1])
             (upper_own, upper_sent), (sums[0],) = tie(early[1], sums[0])
@@ -1399,8 +1396,8 @@
             picked, (sent,) = tie(picked, sent)
             upper_sum = functools.partial(
                 expert_grads,
-                [upper[0]] + [pair[0] for pair in picked],
-                [upper[1]] + [pair[1] for pair in picked],
+                [upper[0], picked[0]],
+                [upper[1], picked[1]],
                 upper[2],
                 upper[3],
                 w_expert,
@@ -1449,11 +1446,11 @@
             (side, new_side), (expert_sum, upper_grads) = tie(
                 (sides[layer_idx], new_side), expert_sum, upper_grads
             )
-            picked = pick_others(both_cores(side), both_cores(new_side), range(1, streams))
+            picked = pick_rows(both_cores(side), both_cores(new_side), w_expert, first)
             below = add_across(below, 1, picked[1]).astype(BF16)
             expert_sum = expert_grads(
-                [x_rows] + [pair[0] for pair in picked],
-                [dy_rows] + [pair[1] for pair in picked],
+                [x_rows, picked[0]],
+                [dy_rows, picked[1]],
                 hid_rows,
                 dgu_rows,
                 w_expert,

time: 674 us -> 659 us (0.978)
  Pallas kernels: 296 us -> 287 us
  starting transfers between devices: 96.3 us -> 88.6 us
    all_gather x5, waiting for transfers between devices: 0.05 us -> 8.79 us  [all_streams(): return lax.all_gather(rows, 'dp', axis=0, tiled=True)]
    pallas_call x6 -> x2, Pallas kernels: 38.8 us -> 30.1 us  [pick_rows(): pl.pallas_call(functools.partial(pick_kernel, experts, *heights), out_sha...]
    ppermute x36, waiting for transfers between devices: 98.5 us -> 91.1 us  [gather_chips(): lax.ppermute(rows, 'ctx', chip_perm(size, 2 * k))]
    unnamed x206 -> x198, local copies, waits for them, and re-layouts: 31.9 us -> 32.9 us
  transfers between devices with their start and end apart: 100 -> 100, of which waited for: 44 -> 44; matrix products, arithmetic and copies ran while one was open for 8% -> 7% of each run, Pallas kernels for 43% -> 42%
where the time goes in v4:
time: 659 us; the launch traced here: 653 us
  Pallas kernels  287 us (44%)
  waiting for transfers between devices  175 us (27%)
  starting transfers between devices  88.6 us (13%)
  local copies, waits for them, and re-layouts  44.5 us (7%)
  other arithmetic  23.5 us (4%)
  matrix products  17.9 us (3%)
  between operations  16 us (2%)
    ppermute x36, waiting for transfers between devices, gather_chips(): lax.ppermute(rows, 'ctx', chip_perm(size, 2 * k))  91.1 us
    pallas_call x3, Pallas kernels, expert_grads(): pl.pallas_call(functools.partial(expert_grad_kernel, streams, before is n...  84 us
    ppermute x36, starting transfers between devices, gather_chips(): lax.ppermute(rows, 'ctx', chip_perm(size, 2 * k))  43.9 us
    ppermute x30, waiting for transfers between devices, reduce_finish(): lax.ppermute(piece, 'ctx', chip_perm(size, 2 * (k + 1)))  42.3 us
    ppermute x30, starting transfers between devices, reduce_finish(): lax.ppermute(piece, 'ctx', chip_perm(size, 2 * (k + 1)))  38.1 us
    pallas_call x2, Pallas kernels, moe_bwd(): pl.pallas_call(functools.partial(moe_bwd_kernel, experts, len(pieces), ha...  36.9 us
    pallas_call x2, Pallas kernels, moe_fwd(): pl.pallas_call(functools.partial(moe_fwd_kernel, experts, len(pieces), ha...  36.2 us
    ppermute x26, waiting for transfers between devices, swap_cores(): return lax.ppermute(rows, 'ctx', chip_perm(lax.axis_size('ctx'), 1))  32.9 us
  transfers between devices with their start and end apart: 100, of which 44 were waited for; matrix products, arithmetic and copies ran while one was open for 7% of the time, Pallas kernels for 42%

profile of v4, /device:TPU:0, one launch (start us, length us, event | category | flops | bytes accessed | tf_op | source)
XLA Modules:
  0.0 652.5 jit_solution(6158915367231922791)
XLA Ops:
  7.9 4.0 collective-permute-start.2
  23.8 3.7 collective-permute-done.5
  32.9 4.4 project.4
  40.9 6.2 collective-permute-done.12
  47.2 5.6 collective-permute-done.14
  61.6 2.7 collective-permute-done.8
  64.9 4.5 project.5
  70.7 2.7 collective-permute-done.17
  73.4 3.7 collective-permute-done.16
  80.2 3.4 collective-permute-done.9
  93.1 7.2 %attend.2 = (bf16[128,1024]{1,0:T(8,128)(2,1)}, bf16[128,1024]{1,0:T(8,128)(2,1)}, f32[4,512,128]{2,1,0:T(8,128)}, f32[4,512,128]{2,1,0:T(8,128)}, f32[128,1024]...) custom-call(s32[8]{0:T(128)} %get-tuple-element.231.need_ref, s32[8]{0:T(128)} %copy-done.73, ...), custom_call_target="tpu_custom_call" | custom-call | flops 536870912 | bytes 6815744 | tf_op jit(solution)/shard_map/attend/pallas_call | solution.py:895
  106.1 6.5 collective-permute-done.20
  112.6 7.9 %collective-permute-done.21 = bf16[128,1152]{1,0:T(8,128)(2,1)S(1)} collective-permute-done((bf16[128,1152]{1,0:T(8,128)(2,1)}, bf16[128,1152]{1,0:T(8,128)(2,1)S(1)}, u32[]{:S(2)}, u32[]{:S(2)}) %collective-permute-start.21) | collective-permute-done | bytes 294944 | tf_op jit(solution)/shard_map/ppermute | solution.py:56
  124.5 18.0 %moe_fwd.2 = (bf16[512,1024]{1,0:T(8,128)(2,1)}, bf16[512,1024]{1,0:T(8,128)(2,1)}, bf16[4,320,1024]{2,1,0:T(8,128)(2,1)}, f32[4,320,128]{2,1,0:T(8,128)}, f32[4...) custom-call(s32[1]{0:T(128)} %bitcast.16.first_ref, bf16[512,1152]{1,0:T(8,128)(2,1)} %copy-done.4, ...), custom_call_target="tpu_custom_call" | custom-call | flops 4026531840 | bytes 24641536 | tf_op jit(solution)/shard_map/moe_fwd/pallas_call | solution.py:545
  142.7 2.8 collective-permute-done.24.far_ref
  146.5 2.7 fold.10
  157.5 3.2 collective-permute-done.25
  162.2 11.4 %collective-permute-done.26 = bf16[128,1024]{1,0:T(8,128)(2,1)} collective-permute-done((bf16[128,1024]{1,0:T(8,128)(2,1)}, bf16[128,1024]{1,0:T(8,128)(2,1)}, u32[]{:S(2)}, u32[]{:S(2)}) %collective-permute-start.26) | collective-permute-done | bytes 262176 | tf_op jit(solution)/shard_map/ppermute | solution.py:107
  175.9 3.8 collective-permute-done.37
  183.0 4.8 project.6
  187.9 2.7 collective-permute-start.33
  193.3 6.6 %collective-permute-done.32 = bf16[128,1024]{1,0:T(8,128)(2,1)S(1)} collective-permute-done((bf16[128,1024]{1,0:T(8,128)(2,1)}, bf16[128,1024]{1,0:T(8,128)(2,1)S(1)}, u32[]{:S(2)}, u32[]{:S(2)}) %collective-permute-start.32) | collective-permute-done | bytes 262176 | tf_op jit(solution)/shard_map/ppermute | solution.py:56
  202.4 5.0 project.7
  208.4 7.4 %attend.3 = (bf16[128,1024]{1,0:T(8,128)(2,1)}, bf16[128,1024]{1,0:T(8,128)(2,1)}, f32[4,512,128]{2,1,0:T(8,128)}, f32[4,512,128]{2,1,0:T(8,128)}, f32[128,1024]...) custom-call(s32[8]{0:T(128)} %get-tuple-element.231.need_ref, s32[8]{0:T(128)} %copy-done.73, ...), custom_call_target="tpu_custom_call" | custom-call | flops 536870912 | bytes 6815744 | tf_op jit(solution)/shard_map/attend/pallas_call | solution.py:895
  215.8 3.0 collective-permute-start.42
  219.5 7.1 %collective-permute-done.42 = bf16[128,1152]{1,0:T(8,128)(2,1)S(1)} collective-permute-done((bf16[128,1152]{1,0:T(8,128)(2,1)}, bf16[128,1152]{1,0:T(8,128)(2,1)S(1)}, u32[]{:S(2)}, u32[]{:S(2)}) %collective-permute-start.42) | collective-permute-done | bytes 294944 | tf_op jit(solution)/shard_map/ppermute | solution.py:56
  226.6 6.6 %collective-permute-done.41 = bf16[128,1152]{1,0:T(8,128)(2,1)S(1)} collective-permute-done((bf16[128,1152]{1,0:T(8,128)(2,1)}, bf16[128,1152]{1,0:T(8,128)(2,1)S(1)}, u32[]{:S(2)}, u32[]{:S(2)}) %collective-permute-start.41) | collective-permute-done | bytes 294944 | tf_op jit(solution)/shard_map/ppermute | solution.py:56
  236.2 2.7 collective-permute-done.46.refs_1_
  240.0 18.2 %moe_fwd.3 = (bf16[512,1024]{1,0:T(8,128)(2,1)}, bf16[512,1024]{1,0:T(8,128)(2,1)}, bf16[4,320,1024]{2,1,0:T(8,128)(2,1)}, f32[4,320,128]{2,1,0:T(8,128)}, f32[4...) custom-call(s32[1]{0:T(128)} %bitcast.16.first_ref, bf16[512,1152]{1,0:T(8,128)(2,1)} %pad_maximum_fusion.1.refs_0_, ...), custom_call_target="tpu_custom_call" | custom-call | flops 4026531840 | bytes 24641536 | tf_op jit(solution)/shard_map/moe_fwd/pallas_call | solution.py:545
  263.2 2.7 fold.11
  265.9 2.9 collective-permute-done.45
  268.8 4.8 collective-permute-done.44
  278.4 18.5 %moe_bwd.2 = (bf16[512,1152]{1,0:T(8,128)(2,1)}, bf16[512,1152]{1,0:T(8,128)(2,1)}, bf16[4,320,1024]{2,1,0:T(8,128)(2,1)}, bf16[4,320,512]{2,1,0:T(8,128)(2,1)}, bf16[4,320,1024]{2,1,0:T(8,128)(2,1)}) custom-call(s32[1]{0:T(128)} %bitcast.16.first_ref, bf16[512,1024]{1,0:T(8,128)(2,1)} %copy-done.1, bf16[512,1024]{1,0:T(8,128)(2,1)} %copy-done.30, ...), custom_call_target="tpu_custom_call" | custom-call | flops 4026531840 | bytes 28573696 | tf_op jit(solution)/shard_map/moe_bwd/pallas_call | solution.py:591
  297.2 3.0 collective-permute-done.52.far_ref
  301.2 2.9 fold.12
  307.6 6.6 %collective-permute-done.53.refs_5_ = bf16[128,1152]{1,0:T(8,128)(2,1)S(1)} collective-permute-done((bf16[128,1152]{1,0:T(8,128)(2,1)}, bf16[128,1152]{1,0:T(8,128)(2,1)S(1)}, u32[]{:S(2)}, u32[]{:S(2)}) %collective-permute-start.53) | collective-permute-done | bytes 294944 | tf_op jit(solution)/shard_map/ppermute | solution.py:107
  314.2 6.8 %collective-permute-done.54.refs_6_ = bf16[128,1152]{1,0:T(8,128)(2,1)S(1)} collective-permute-done((bf16[128,1152]{1,0:T(8,128)(2,1)}, bf16[128,1152]{1,0:T(8,128)(2,1)S(1)}, u32[]{:S(2)}, u32[]{:S(2)}) %collective-permute-start.54) | collective-permute-done | bytes 294944 | tf_op jit(solution)/shard_map/ppermute | solution.py:107
  321.8 10.7 %attend_back.2 = (f32[128,1024]{1,0:T(8,128)}, bf16[128,1024]{1,0:T(8,128)(2,1)}, bf16[128,128]{1,0:T(8,128)(2,1)}, f32[1,1024]{1,0:T(1,128)}, bf16[128,1024]{1,...) custom-call(s32[8]{0:T(128)} %get-tuple-element.231.need_ref, s32[8]{0:T(128)} %copy-done.73, ...), custom_call_target="tpu_custom_call" | custom-call | flops 939524096 | bytes 10223616 | tf_op jit(solution)/shard_map/attend_back/pallas_call | solution.py:1058
  336.5 2.9 fold.13
  341.2 2.9 collective-permute-start.59
  346.6 2.7 fold.14
  349.3 7.2 %collective-permute-done.59.refs_4_ = bf16[128,1024]{1,0:T(8,128)(2,1)S(1)} collective-permute-done((bf16[128,1024]{1,0:T(8,128)(2,1)}, bf16[128,1024]{1,0:T(8,128)(2,1)S(1)}, u32[]{:S(2)}, u32[]{:S(2)}) %collective-permute-start.59) | collective-permute-done | bytes 262176 | tf_op jit(solution)/shard_map/ppermute | solution.py:107
  357.3 7.8 %project_back.2 = (f32[128,1024]{1,0:T(8,128)}, bf16[128,1024]{1,0:T(8,128)(2,1)}, bf16[128,2176]{1,0:T(8,128)(2,1)}, f32[1,1024]{1,0:T(1,128)}) custom-call(s32[8]{0:T(128)} %copy-done.73, bf16[512,2048]{1,0:T(8,128)(2,1)} %all-gather.6.cloned.1.call-done.refs_0_, bf16[512,2048]{1,0:T(8,128)(2,1)} %copy-done, f32[128,1024]{1,0:T(8,128)} %get-tuple-element.325.refs_2_, ...), custom_call_target="tpu_custom_call" | custom-call | flops 536870912 | bytes 7340032 | tf_op jit(solution)/shard_map/project_back/pallas_call | solution.py:1146
  365.1 3.2 convolution_convert_fusion
  373.8 4.5 collective-permute-done.63
  378.3 5.2 collective-permute-done.62
  385.3 3.9 fold.15
  393.7 18.4 %moe_bwd.3 = (bf16[512,1152]{1,0:T(8,128)(2,1)}, bf16[512,1152]{1,0:T(8,128)(2,1)}, bf16[4,320,1024]{2,1,0:T(8,128)(2,1)}, bf16[4,320,512]{2,1,0:T(8,128)(2,1)}, bf16[4,320,1024]{2,1,0:T(8,128)(2,1)}) custom-call(s32[1]{0:T(128)} %bitcast.16.first_ref, bf16[512,1024]{1,0:T(8,128)(2,1)} %copy-done.2, bf16[512,1024]{1,0:T(8,128)(2,1)} %copy-done.31, ...), custom_call_target="tpu_custom_call" | custom-call | flops 4026531840 | bytes 28573696 | tf_op jit(solution)/shard_map/moe_bwd/pallas_call | solution.py:591
  412.1 3.7 collective-permute-done.68
  419.1 8.3 %collective-permute-done.69.far_ref = bf16[512,1152]{1,0:T(8,128)(2,1)S(1)} collective-permute-done((bf16[512,1152]{1,0:T(8,128)(2,1)}, bf16[512,1152]{1,0:T(8,128)(2,1)S(1)}, u32[]{:S(2)}, u32[]{:S(2)}) %collective-permute-start.69) | collective-permute-done | bytes 1179680 | tf_op jit(solution)/shard_map/ppermute | solution.py:48
  428.3 2.8 fold.16
  434.6 15.1 %pick_rows.2 = (bf16[3,4,320,1024]{3,2,1,0:T(8,128)(2,1)}, bf16[3,4,320,1024]{3,2,1,0:T(8,128)(2,1)}) custom-call(s32[1]{0:T(128)} %bitcast.16.first_ref, s32[3]{0:T(128)} %and_select_fusion.stream_ref, bf16[2048,1152]{1,0:T(8,128)(2,1)} %all-gather.10.cloned.1.call-done.refs_0_, bf16[2048,1152]{1,0:T(8,128)(2,1)} %collective-permute-done.70.refs_1_, ...), custom_call_target="tpu_custom_call" | custom-call | flops 4026531840 | bytes 28311552 | tf_op jit(solution)/shard_map/pick_rows/pallas_call | solution.py:645
  454.2 10.6 %attend_back.3 = (f32[128,1024]{1,0:T(8,128)}, bf16[128,1024]{1,0:T(8,128)(2,1)}, bf16[128,128]{1,0:T(8,128)(2,1)}, f32[1,1024]{1,0:T(1,128)}, bf16[128,1024]{1,...) custom-call(s32[8]{0:T(128)} %get-tuple-element.231.need_ref, s32[8]{0:T(128)} %copy-done.73, ...), custom_call_target="tpu_custom_call" | custom-call | flops 939524096 | bytes 10223616 | tf_op jit(solution)/shard_map/attend_back/pallas_call | solution.py:1058
  473.8 2.7 collective-permute-start.80
  476.6 15.0 %expert_grads.3.refs_7_ = f32[2,4,1024,1536]{3,2,1,0:T(8,128)} custom-call(bf16[4,320,1024]{2,1,0:T(8,128)(2,1)} %get-tuple-element.382.refs_0_, bf16[3,4,320,1024]{3,2,1,0:T(8,128)(2,1)} %get-tuple-element.388.refs_1_, bf16[4,320,1024]{2,1,0:T(8,128)(2,1)} %get-tuple-element.389.refs_2_, bf16[3,4,320,1024]{3,2,1,0:T(8,128)(2,1)} %get-tuple-element.390.refs_3_, ...), custom_call_target="tpu_custom_call" | custom-call | flops 7046430720 | bytes 14680064 | tf_op jit(solution)/shard_map/expert_grads/pallas_call | solution.py:684
  491.6 6.5 %all-gather.14.cloned.1.call-done.refs_2_ = bf16[2048,1024]{1,0:T(8,128)(2,1)} async-done(((bf16[512,1024]{1,0:T(8,128)(2,1)}), bf16[2048,1024]{1,0:T(8,128)(2,1)}) %all-gather.14.cloned.1.call-update) | async-done | bytes 4194320 | tf_op jit(solution)/shard_map/all_gather | solution.py:116
  499.0 7.4 %project_back.3 = (f32[128,1024]{1,0:T(8,128)}, bf16[128,1024]{1,0:T(8,128)(2,1)}, bf16[128,2176]{1,0:T(8,128)(2,1)}, f32[1,1024]{1,0:T(1,128)}) custom-call(s32[8]{0:T(128)} %copy-done.73, bf16[512,1024]{1,0:T(8,128)(2,1)} %copy-done.8, bf16[512,1024]{1,0:T(8,128)(2,1)} %copy-done.13, bf16[512,1024]{1,0:T(8,128)(2,1)} %copy-done.3, ...), custom_call_target="tpu_custom_call" | custom-call | flops 536870912 | bytes 7340032 | tf_op jit(solution)/shard_map/project_back/pallas_call | solution.py:1146
  523.2 3.2 fusion.near_ref
  527.8 4.0 fold.18
  531.8 3.3 collective-permute-done.85
  539.4 30.9 %expert_grads.4.refs_7_ = f32[2,4,1024,1536]{3,2,1,0:T(8,128)} custom-call(bf16[4,320,1024]{2,1,0:T(8,128)(2,1)} %get-tuple-element.382.refs_0_, bf16[3,4,320,1024]{3,2,1,0:T(8,128)(2,1)} %get-tuple-element.388.refs_1_, bf16[4,320,1024]{2,1,0:T(8,128)(2,1)} %get-tuple-element.389.refs_2_, ...), custom_call_target="tpu_custom_call", output_to_operand_aliasing={{}: (7, {})} | custom-call | flops 21139292160 | bytes 44040192 | tf_op jit(solution)/shard_map/expert_grads/pallas_call | solution.py:684
  574.8 9.9 %collective-permute-done.91.refs_3_ = bf16[2048,1024]{1,0:T(8,128)(2,1)} collective-permute-done((bf16[2048,1024]{1,0:T(8,128)(2,1)}, bf16[2048,1024]{1,0:T(8,128)(2,1)}, u32[]{:S(2)}, u32[]{:S(2)}) %collective-permute-start.91) | collective-permute-done | bytes 4194336 | tf_op jit(solution)/shard_map/ppermute | solution.py:48
  584.7 15.1 %pick_rows.3 = (bf16[3,4,320,1024]{3,2,1,0:T(8,128)(2,1)}, bf16[3,4,320,1024]{3,2,1,0:T(8,128)(2,1)}) custom-call(s32[1]{0:T(128)} %bitcast.16.first_ref, s32[3]{0:T(128)} %and_select_fusion.stream_ref, bf16[2048,1152]{1,0:T(8,128)(2,1)} %all-gather.8.cloned.1.call-done.refs_0_, bf16[2048,1152]{1,0:T(8,128)(2,1)} %collective-permute-done.90.refs_1_, ...), custom_call_target="tpu_custom_call" | custom-call | flops 4026531840 | bytes 28311552 | tf_op jit(solution)/shard_map/pick_rows/pallas_call | solution.py:645
  600.9 38.1 %expert_grads.5 = f32[2,4,1024,1536]{3,2,1,0:T(8,128)} custom-call(bf16[4,320,1024]{2,1,0:T(8,128)(2,1)} %get-tuple-element.430.refs_0_, bf16[3,4,320,1024]{3,2,1,0:T(8,128)(2,1)} %get-tuple-element.433.refs_1_, bf16[4,320,1024]{2,1,0:T(8,128)(2,1)} %get-tuple-element.434.refs_2_, ...), custom_call_target="tpu_custom_call", output_to_operand_aliasing={{}: (7, {})} | custom-call | flops 28185722880 | bytes 58720256 | tf_op jit(solution)/shard_map/expert_grads/pallas_call | solution.py:684
  (462 shorter events, 174.2 us)
Async XLA Ops:
  7.2 144.2 %all-gather.6.cloned.1.call-start = ((), (), s32[]{:S(2)}) async-start(), calls=%async_computation | async-start | bytes 2621440 | tf_op jit(solution)/shard_map/all_gather | solution.py:116
  7.9 21.3 %collective-permute-start.2 = (bf16[8,128]{1,0:T(8,128)(2,1)S(1)}, bf16[8,128]{1,0:T(8,128)(2,1)S(1)}, u32[]{:S(2)}, u32[]{:S(2)}) collective-permute-start(bf16[8,128]{1,0:T(8,128)(2,1)S(1)} %pad_maximum_fusion.12), channel_id=1, source_target_pairs={{0,6},{1,7},{2,4},{3,5},{4,2},{5,3},{6,0},{7,1},{8,14},{9,15},{10,... | collective-permute-start | bytes 6152 | tf_op jit(solution)/shard_map/ppermute | solution.py:56
  11.9 17.4 %collective-permute-start.1 = (bf16[8,128]{1,0:T(8,128)(2,1)S(1)}, bf16[8,128]{1,0:T(8,128)(2,1)S(1)}, u32[]{:S(2)}, u32[]{:S(2)}) collective-permute-start(bf16[8,128]{1,0:T(8,128)(2,1)S(1)} %pad_maximum_fusion.12), channel_id=1, source_target_pairs={{0,4},{1,5},{2,6},{3,7},{4,0},{5,1},{6,2},{7,3},{8,12},{9,13},{10,... | collective-permute-start | bytes 6152 | tf_op jit(solution)/shard_map/ppermute | solution.py:56
  15.0 12.5 %collective-permute-start.5 = (bf16[128,1024]{1,0:T(8,128)(2,1)S(1)}, bf16[128,1024]{1,0:T(8,128)(2,1)S(1)}, u32[]{:S(2)}, u32[]{:S(2)}) collective-permute-start(bf16[128,1024]{1,0:T(8,128)(2,1)S(1)} %get-tuple-element.477), channel_id=1, source_target_pairs={{0,4},{1,5},{2,6},{3,7},{4,0},{5,1},{6,2},{7,3},{8,12},{9,13},{10,... | collective-permute-start | bytes 786440 | tf_op jit(solution)/shard_map/ppermute | solution.py:56
  15.1 12.5 %collective-permute-start.4 = (bf16[128,1024]{1,0:T(8,128)(2,1)S(1)}, bf16[128,1024]{1,0:T(8,128)(2,1)S(1)}, u32[]{:S(2)}, u32[]{:S(2)}) collective-permute-start(bf16[128,1024]{1,0:T(8,128)(2,1)S(1)} %get-tuple-element.477), channel_id=1, source_target_pairs={{0,2},{1,3},{2,0},{3,1},{4,6},{5,7},{6,4},{7,5},{8,10},{9,11},{10,... | collective-permute-start | bytes 786440 | tf_op jit(solution)/shard_map/ppermute | solution.py:56
  39.3 13.4 %collective-permute-start.14 = (bf16[128,1024]{1,0:T(8,128)(2,1)S(1)}, bf16[128,1024]{1,0:T(8,128)(2,1)S(1)}, u32[]{:S(2)}, u32[]{:S(2)}) collective-permute-start(bf16[128,1024]{1,0:T(8,128)(2,1)S(1)} %get-tuple-element.234), channel_id=1, source_target_pairs={{0,6},{1,7},{2,4},{3,5},{4,2},{5,3},{6,0},{7,1},{8,14},{9,15},{10,... | collective-permute-start | bytes 786440 | tf_op jit(solution)/shard_map/ppermute | solution.py:56
  55.5 15.1 %collective-permute-start.18 = (bf16[128,1152]{1,0:T(8,128)(2,1)S(1)}, bf16[128,1152]{1,0:T(8,128)(2,1)S(1)}, u32[]{:S(2)}, u32[]{:S(2)}) collective-permute-start(bf16[128,1152]{1,0:T(8,128)(2,1)S(1)} %concatenate.86), channel_id=1, source_target_pairs={{0,6},{1,7},{2,4},{3,5},{4,2},{5,3},{6,0},{7,1},{8,14},{9,15},{10,... | collective-permute-start | bytes 884744 | tf_op jit(solution)/shard_map/ppermute | solution.py:56
  57.1 16.3 %collective-permute-start.17 = (bf16[128,1152]{1,0:T(8,128)(2,1)S(1)}, bf16[128,1152]{1,0:T(8,128)(2,1)}, u32[]{:S(2)}, u32[]{:S(2)}) collective-permute-start(bf16[128,1152]{1,0:T(8,128)(2,1)S(1)} %concatenate.86), channel_id=1, source_target_pairs={{0,4},{1,5},{2,6},{3,7},{4,0},{5,1},{6,2},{7,3},{8,12},{9,13},{10,... | collective-permute-start | bytes 884744 | tf_op jit(solution)/shard_map/ppermute | solution.py:56
  58.6 18.5 %collective-permute-start.16 = (bf16[128,1152]{1,0:T(8,128)(2,1)S(1)}, bf16[128,1152]{1,0:T(8,128)(2,1)}, u32[]{:S(2)}, u32[]{:S(2)}) collective-permute-start(bf16[128,1152]{1,0:T(8,128)(2,1)S(1)} %concatenate.86), channel_id=1, source_target_pairs={{0,2},{1,3},{2,0},{3,1},{4,6},{5,7},{6,4},{7,5},{8,10},{9,11},{10,... | collective-permute-start | bytes 884744 | tf_op jit(solution)/shard_map/ppermute | solution.py:56
  59.1 25.5 %collective-permute-start.10 = (bf16[128,1024]{1,0:T(8,128)(2,1)}, bf16[128,1024]{1,0:T(8,128)(2,1)S(1)}, u32[]{:S(2)}, u32[]{:S(2)}) collective-permute-start(bf16[128,1024]{1,0:T(8,128)(2,1)} %get-tuple-element.232), channel_id=1, source_target_pairs={{0,6},{1,7},{2,4},{3,5},{4,2},{5,3},{6,0},{7,1},{8,14},{9,15},{10,... | collective-permute-start | bytes 786440 | tf_op jit(solution)/shard_map/ppermute | solution.py:56
  64.3 19.3 %collective-permute-start.9 = (bf16[128,1024]{1,0:T(8,128)(2,1)}, bf16[128,1024]{1,0:T(8,128)(2,1)}, u32[]{:S(2)}, u32[]{:S(2)}) collective-permute-start(bf16[128,1024]{1,0:T(8,128)(2,1)} %get-tuple-element.232), channel_id=1, source_target_pairs={{0,4},{1,5},{2,6},{3,7},{4,0},{5,1},{6,2},{7,3},{8,12},{9,13},{10,... | collective-permute-start | bytes 786440 | tf_op jit(solution)/shard_map/ppermute | solution.py:56
  87.8 12.6 %collective-permute-start.30 = (bf16[32,2048]{1,0:T(8,128)(2,1)S(1)}, bf16[32,2048]{1,0:T(8,128)(2,1)}, u32[]{:S(2)}, u32[]{:S(2)}) collective-permute-start(bf16[32,2048]{1,0:T(8,128)(2,1)S(1)} %dynamic-slice_bitcast_fusion), channel_id=1, source_target_pairs={{0,6},{1,7},{2,4},{3,5},{4,2},{5,3},{6,0},{7,1},{8,14},{9,15},{10,... | collective-permute-start | bytes 393224 | tf_op jit(solution)/shard_map/ppermute | solution.py:56
  102.4 194.6 %all-gather.8.cloned.1.call-start = ((), (), s32[]{:S(2)}) async-start(), calls=%async_computation.1 | async-start | bytes 5898240 | tf_op jit(solution)/shard_map/all_gather | solution.py:116
  104.5 16.0 %collective-permute-start.22 = (bf16[128,1152]{1,0:T(8,128)(2,1)}, bf16[128,1152]{1,0:T(8,128)(2,1)S(1)}, u32[]{:S(2)}, u32[]{:S(2)}) collective-permute-start(bf16[128,1152]{1,0:T(8,128)(2,1)} %get-tuple-element.251), channel_id=1, source_target_pairs={{0,6},{1,7},{2,4},{3,5},{4,2},{5,3},{6,0},{7,1},{8,14},{9,15},{10,... | collective-permute-start | bytes 884744 | tf_op jit(solution)/shard_map/ppermute | solution.py:56
  105.4 15.1 %collective-permute-start.21 = (bf16[128,1152]{1,0:T(8,128)(2,1)}, bf16[128,1152]{1,0:T(8,128)(2,1)S(1)}, u32[]{:S(2)}, u32[]{:S(2)}) collective-permute-start(bf16[128,1152]{1,0:T(8,128)(2,1)} %get-tuple-element.251), channel_id=1, source_target_pairs={{0,4},{1,5},{2,6},{3,7},{4,0},{5,1},{6,2},{7,3},{8,12},{9,13},{10,... | collective-permute-start | bytes 884744 | tf_op jit(solution)/shard_map/ppermute | solution.py:56
  121.6 294.2 %all-gather.10.cloned.1.call-start = ((), (), s32[]{:S(2)}) async-start(), calls=%async_computation.2 | async-start | bytes 5898240 | tf_op jit(solution)/shard_map/all_gather | solution.py:116
  151.3 30.4 %collective-permute-start.31 = (bf16[512,2048]{1,0:T(8,128)(2,1)}, bf16[512,2048]{1,0:T(8,128)(2,1)S(1)}, u32[]{:S(2)}, u32[]{:S(2)}) collective-permute-start(bf16[512,2048]{1,0:T(8,128)(2,1)} %all-gather.6.cloned.1.call-done.refs_0_), channel_id=1, source_target_pairs={{0,1},{1,0},{2,3},{3,2},{4,5},{5,4},{6,7},{7,6},{8,9},{9,8},{10,11... | collective-permute-start | bytes 6291464 | tf_op jit(solution)/shard_map/ppermute | solution.py:48
  152.8 20.8 %collective-permute-start.26 = (bf16[128,1024]{1,0:T(8,128)(2,1)}, bf16[128,1024]{1,0:T(8,128)(2,1)}, u32[]{:S(2)}, u32[]{:S(2)}) collective-permute-start(bf16[128,1024]{1,0:T(8,128)(2,1)} %get-tuple-element.256), channel_id=1, source_target_pairs={{0,4},{1,5},{2,6},{3,7},{4,0},{5,1},{6,2},{7,3},{8,12},{9,13},{10,... | collective-permute-start | bytes 786440 | tf_op jit(solution)/shard_map/ppermute | solution.py:107
  154.2 19.4 %collective-permute-start.27 = (bf16[128,1024]{1,0:T(8,128)(2,1)}, bf16[128,1024]{1,0:T(8,128)(2,1)}, u32[]{:S(2)}, u32[]{:S(2)}) collective-permute-start(bf16[128,1024]{1,0:T(8,128)(2,1)} %get-tuple-element.257), channel_id=1, source_target_pairs={{0,6},{1,7},{2,4},{3,5},{4,2},{5,3},{6,0},{7,1},{8,14},{9,15},{10,... | collective-permute-start | bytes 786440 | tf_op jit(solution)/shard_map/ppermute | solution.py:107
  155.1 20.8 %collective-permute-start.38 = (bf16[128,1152]{1,0:T(8,128)(2,1)S(1)}, bf16[128,1152]{1,0:T(8,128)(2,1)S(1)}, u32[]{:S(2)}, u32[]{:S(2)}) collective-permute-start(bf16[128,1152]{1,0:T(8,128)(2,1)S(1)} %concatenate.92), channel_id=1, source_target_pairs={{0,6},{1,7},{2,4},{3,5},{4,2},{5,3},{6,0},{7,1},{8,14},{9,15},{10,... | collective-permute-start | bytes 884744 | tf_op jit(solution)/shard_map/ppermute | solution.py:56
  160.7 19.0 %collective-permute-start.37 = (bf16[128,1152]{1,0:T(8,128)(2,1)S(1)}, bf16[128,1152]{1,0:T(8,128)(2,1)S(1)}, u32[]{:S(2)}, u32[]{:S(2)}) collective-permute-start(bf16[128,1152]{1,0:T(8,128)(2,1)S(1)} %concatenate.92), channel_id=1, source_target_pairs={{0,4},{1,5},{2,6},{3,7},{4,0},{5,1},{6,2},{7,3},{8,12},{9,13},{10,... | collective-permute-start | bytes 884744 | tf_op jit(solution)/shard_map/ppermute | solution.py:56
  187.9 12.0 %collective-permute-start.33 = (bf16[128,1024]{1,0:T(8,128)(2,1)}, bf16[128,1024]{1,0:T(8,128)(2,1)S(1)}, u32[]{:S(2)}, u32[]{:S(2)}) collective-permute-start(bf16[128,1024]{1,0:T(8,128)(2,1)} %get-tuple-element.267), channel_id=1, source_target_pairs={{0,4},{1,5},{2,6},{3,7},{4,0},{5,1},{6,2},{7,3},{8,12},{9,13},{10,... | collective-permute-start | bytes 786440 | tf_op jit(solution)/shard_map/ppermute | solution.py:56
  190.9 16.5 %collective-permute-start.39 = (bf16[512,1152]{1,0:T(8,128)(2,1)S(1)}, bf16[512,1152]{1,0:T(8,128)(2,1)S(1)}, u32[]{:S(2)}, u32[]{:S(2)}) collective-permute-start(bf16[512,1152]{1,0:T(8,128)(2,1)S(1)} %constant_dynamic-update-slice_fusion.20.refs_2_), channel_id=1, source_target_pairs={{0,1},{1,0},{2,3},{3,2},{4,5},{5,4},{6,7},{7,6},{8,9},{9,8},{10,11... | collective-permute-start | bytes 3538952 | tf_op jit(solution)/shard_map/ppermute | solution.py:48
  218.8 14.4 %collective-permute-start.41 = (bf16[128,1152]{1,0:T(8,128)(2,1)}, bf16[128,1152]{1,0:T(8,128)(2,1)S(1)}, u32[]{:S(2)}, u32[]{:S(2)}) collective-permute-start(bf16[128,1152]{1,0:T(8,128)(2,1)} %get-tuple-element.276), channel_id=1, source_target_pairs={{0,4},{1,5},{2,6},{3,7},{4,0},{5,1},{6,2},{7,3},{8,12},{9,13},{10,... | collective-permute-start | bytes 884744 | tf_op jit(solution)/shard_map/ppermute | solution.py:56
  219.2 14.2 %collective-permute-start.40 = (bf16[128,1152]{1,0:T(8,128)(2,1)}, bf16[128,1152]{1,0:T(8,128)(2,1)S(1)}, u32[]{:S(2)}, u32[]{:S(2)}) collective-permute-start(bf16[128,1152]{1,0:T(8,128)(2,1)} %get-tuple-element.276), channel_id=1, source_target_pairs={{0,2},{1,3},{2,0},{3,1},{4,6},{5,7},{6,4},{7,5},{8,10},{9,11},{10,... | collective-permute-start | bytes 884744 | tf_op jit(solution)/shard_map/ppermute | solution.py:56
  235.5 180.3 %all-gather.12.cloned.1.call-start = ((), (), s32[]{:S(2)}) async-start(), calls=%async_computation.3 | async-start | bytes 5242880 | tf_op jit(solution)/shard_map/all_gather | solution.py:116
  260.4 13.2 %collective-permute-start.44 = (bf16[128,1024]{1,0:T(8,128)(2,1)S(1)}, bf16[128,1024]{1,0:T(8,128)(2,1)S(1)}, u32[]{:S(2)}, u32[]{:S(2)}) collective-permute-start(bf16[128,1024]{1,0:T(8,128)(2,1)S(1)} %bitcast.92), channel_id=1, source_target_pairs={{0,4},{1,5},{2,6},{3,7},{4,0},{5,1},{6,2},{7,3},{8,12},{9,13},{10,... | collective-permute-start | bytes 786440 | tf_op jit(solution)/shard_map/ppermute | solution.py:56
  273.9 23.1 %collective-permute-start.49 = (bf16[128,1024]{1,0:T(8,128)(2,1)}, bf16[128,1024]{1,0:T(8,128)(2,1)S(1)}, u32[]{:S(2)}, u32[]{:S(2)}) collective-permute-start(bf16[128,1024]{1,0:T(8,128)(2,1)} %get-tuple-element.296), channel_id=1, source_target_pairs={{0,2},{1,3},{2,0},{3,1},{4,6},{5,7},{6,4},{7,5},{8,10},{9,11},{10,... | collective-permute-start | bytes 786440 | tf_op jit(solution)/shard_map/ppermute | solution.py:107
  275.5 21.5 %collective-permute-start.50 = (bf16[128,1024]{1,0:T(8,128)(2,1)S(1)}, bf16[128,1024]{1,0:T(8,128)(2,1)S(1)}, u32[]{:S(2)}, u32[]{:S(2)}) collective-permute-start(bf16[128,1024]{1,0:T(8,128)(2,1)S(1)} %copy-done.88), channel_id=1, source_target_pairs={{0,4},{1,5},{2,6},{3,7},{4,0},{5,1},{6,2},{7,3},{8,12},{9,13},{10,... | collective-permute-start | bytes 786440 | tf_op jit(solution)/shard_map/ppermute | solution.py:107
  276.1 20.9 %collective-permute-start.51 = (bf16[128,1024]{1,0:T(8,128)(2,1)S(1)}, bf16[128,1024]{1,0:T(8,128)(2,1)S(1)}, u32[]{:S(2)}, u32[]{:S(2)}) collective-permute-start(bf16[128,1024]{1,0:T(8,128)(2,1)S(1)} %copy-done.87), channel_id=1, source_target_pairs={{0,6},{1,7},{2,4},{3,5},{4,2},{5,3},{6,0},{7,1},{8,14},{9,15},{10,... | collective-permute-start | bytes 786440 | tf_op jit(solution)/shard_map/ppermute | solution.py:107
  297.1 201.0 %all-gather.14.cloned.1.call-start = ((), (), s32[]{:S(2)}) async-start(), calls=%async_computation.4 | async-start | bytes 5242880 | tf_op jit(solution)/shard_map/all_gather | solution.py:116
  305.7 15.3 %collective-permute-start.54 = (bf16[128,1152]{1,0:T(8,128)(2,1)}, bf16[128,1152]{1,0:T(8,128)(2,1)S(1)}, u32[]{:S(2)}, u32[]{:S(2)}) collective-permute-start(bf16[128,1152]{1,0:T(8,128)(2,1)} %get-tuple-element.307), channel_id=1, source_target_pairs={{0,4},{1,5},{2,6},{3,7},{4,0},{5,1},{6,2},{7,3},{8,12},{9,13},{10,... | collective-permute-start | bytes 884744 | tf_op jit(solution)/shard_map/ppermute | solution.py:107
  306.3 14.7 %collective-permute-start.55 = (bf16[128,1152]{1,0:T(8,128)(2,1)}, bf16[128,1152]{1,0:T(8,128)(2,1)S(1)}, u32[]{:S(2)}, u32[]{:S(2)}) collective-permute-start(bf16[128,1152]{1,0:T(8,128)(2,1)} %get-tuple-element.308), channel_id=1, source_target_pairs={{0,6},{1,7},{2,4},{3,5},{4,2},{5,3},{6,0},{7,1},{8,14},{9,15},{10,... | collective-permute-start | bytes 884744 | tf_op jit(solution)/shard_map/ppermute | solution.py:107
  341.2 15.3 %collective-permute-start.59 = (bf16[128,1024]{1,0:T(8,128)(2,1)}, bf16[128,1024]{1,0:T(8,128)(2,1)S(1)}, u32[]{:S(2)}, u32[]{:S(2)}) collective-permute-start(bf16[128,1024]{1,0:T(8,128)(2,1)} %get-tuple-element.327), channel_id=1, source_target_pairs={{0,4},{1,5},{2,6},{3,7},{4,0},{5,1},{6,2},{7,3},{8,12},{9,13},{10,... | collective-permute-start | bytes 786440 | tf_op jit(solution)/shard_map/ppermute | solution.py:107
  344.1 12.4 %collective-permute-start.60 = (bf16[128,1024]{1,0:T(8,128)(2,1)}, bf16[128,1024]{1,0:T(8,128)(2,1)S(1)}, u32[]{:S(2)}, u32[]{:S(2)}) collective-permute-start(bf16[128,1024]{1,0:T(8,128)(2,1)} %get-tuple-element.328), channel_id=1, source_target_pairs={{0,6},{1,7},{2,4},{3,5},{4,2},{5,3},{6,0},{7,1},{8,14},{9,15},{10,... | collective-permute-start | bytes 786440 | tf_op jit(solution)/shard_map/ppermute | solution.py:107
  368.3 15.7 %collective-permute-start.64 = (bf16[512,2048]{1,0:T(8,128)(2,1)}, bf16[512,2048]{1,0:T(8,128)(2,1)S(1)}, u32[]{:S(2)}, u32[]{:S(2)}) collective-permute-start(bf16[512,2048]{1,0:T(8,128)(2,1)} %convolution_convert_fusion), channel_id=1, source_target_pairs={{0,1},{1,0},{2,3},{3,2},{4,5},{5,4},{6,7},{7,6},{8,9},{9,8},{10,11... | collective-permute-start | bytes 6291464 | tf_op jit(solution)/shard_map/ppermute | solution.py:48
  369.7 13.8 %collective-permute-start.62 = (bf16[128,1024]{1,0:T(8,128)(2,1)S(1)}, bf16[128,1024]{1,0:T(8,128)(2,1)S(1)}, u32[]{:S(2)}, u32[]{:S(2)}) collective-permute-start(bf16[128,1024]{1,0:T(8,128)(2,1)S(1)} %copy-done.71), channel_id=1, source_target_pairs={{0,4},{1,5},{2,6},{3,7},{4,0},{5,1},{6,2},{7,3},{8,12},{9,13},{10,... | collective-permute-start | bytes 786440 | tf_op jit(solution)/shard_map/ppermute | solution.py:56
  371.1 12.7 %collective-permute-start.61 = (bf16[128,1024]{1,0:T(8,128)(2,1)S(1)}, bf16[128,1024]{1,0:T(8,128)(2,1)S(1)}, u32[]{:S(2)}, u32[]{:S(2)}) collective-permute-start(bf16[128,1024]{1,0:T(8,128)(2,1)S(1)} %copy-done.71), channel_id=1, source_target_pairs={{0,2},{1,3},{2,0},{3,1},{4,6},{5,7},{6,4},{7,5},{8,10},{9,11},{10,... | collective-permute-start | bytes 786440 | tf_op jit(solution)/shard_map/ppermute | solution.py:56
  389.2 22.9 %collective-permute-start.66 = (bf16[128,2048]{1,0:T(8,128)(2,1)}, bf16[128,2048]{1,0:T(8,128)(2,1)S(1)}, u32[]{:S(2)}, u32[]{:S(2)}) collective-permute-start(bf16[128,2048]{1,0:T(8,128)(2,1)} %get-tuple-element.345), channel_id=1, source_target_pairs={{0,2},{1,3},{2,0},{3,1},{4,6},{5,7},{6,4},{7,5},{8,10},{9,11},{10,... | collective-permute-start | bytes 1572872 | tf_op jit(solution)/shard_map/ppermute | solution.py:107
  390.4 21.8 %collective-permute-start.67 = (bf16[128,2048]{1,0:T(8,128)(2,1)}, bf16[128,2048]{1,0:T(8,128)(2,1)}, u32[]{:S(2)}, u32[]{:S(2)}) collective-permute-start(bf16[128,2048]{1,0:T(8,128)(2,1)} %get-tuple-element.346), channel_id=1, source_target_pairs={{0,4},{1,5},{2,6},{3,7},{4,0},{5,1},{6,2},{7,3},{8,12},{9,13},{10,... | collective-permute-start | bytes 1572872 | tf_op jit(solution)/shard_map/ppermute | solution.py:107
  391.0 24.8 %collective-permute-start.68 = (bf16[128,2048]{1,0:T(8,128)(2,1)}, bf16[128,2048]{1,0:T(8,128)(2,1)}, u32[]{:S(2)}, u32[]{:S(2)}) collective-permute-start(bf16[128,2048]{1,0:T(8,128)(2,1)} %get-tuple-element.347), channel_id=1, source_target_pairs={{0,6},{1,7},{2,4},{3,5},{4,2},{5,3},{6,0},{7,1},{8,14},{9,15},{10,... | collective-permute-start | bytes 1572872 | tf_op jit(solution)/shard_map/ppermute | solution.py:107
  415.8 18.8 %collective-permute-start.70 = (bf16[2048,1152]{1,0:T(8,128)(2,1)}, bf16[2048,1152]{1,0:T(8,128)(2,1)}, u32[]{:S(2)}, u32[]{:S(2)}) collective-permute-start(bf16[2048,1152]{1,0:T(8,128)(2,1)} %all-gather.10.cloned.1.call-done.refs_0_), channel_id=1, source_target_pairs={{0,1},{1,0},{2,3},{3,2},{4,5},{5,4},{6,7},{7,6},{8,9},{9,8},{10,11... | collective-permute-start | bytes 14155784 | tf_op jit(solution)/shard_map/ppermute | solution.py:48
  415.8 18.8 %collective-permute-start.71 = (bf16[2048,1024]{1,0:T(8,128)(2,1)}, bf16[2048,1024]{1,0:T(8,128)(2,1)}, u32[]{:S(2)}, u32[]{:S(2)}) collective-permute-start(bf16[2048,1024]{1,0:T(8,128)(2,1)} %all-gather.12.cloned.1.call-done.refs_2_), channel_id=1, source_target_pairs={{0,1},{1,0},{2,3},{3,2},{4,5},{5,4},{6,7},{7,6},{8,9},{9,8},{10,11... | collective-permute-start | bytes 12582920 | tf_op jit(solution)/shard_map/ppermute | solution.py:48
  416.4 154.0 %all-reduce.4.cloned.1.call-start = ((), (), s32[]{:S(2)}) async-start(), calls=%async_computation.5 | async-start | bytes 1572864 | tf_op jit(solution)/shard_map/psum | solution.py:1389
  431.1 21.1 %collective-permute-start.75 = (bf16[128,1152]{1,0:T(8,128)(2,1)}, bf16[128,1152]{1,0:T(8,128)(2,1)S(1)}, u32[]{:S(2)}, u32[]{:S(2)}) collective-permute-start(bf16[128,1152]{1,0:T(8,128)(2,1)} %get-tuple-element.354), channel_id=1, source_target_pairs={{0,2},{1,3},{2,0},{3,1},{4,6},{5,7},{6,4},{7,5},{8,10},{9,11},{10,... | collective-permute-start | bytes 884744 | tf_op jit(solution)/shard_map/ppermute | solution.py:107
  432.2 21.2 %collective-permute-start.76 = (bf16[128,1152]{1,0:T(8,128)(2,1)}, bf16[128,1152]{1,0:T(8,128)(2,1)S(1)}, u32[]{:S(2)}, u32[]{:S(2)}) collective-permute-start(bf16[128,1152]{1,0:T(8,128)(2,1)} %get-tuple-element.355), channel_id=1, source_target_pairs={{0,4},{1,5},{2,6},{3,7},{4,0},{5,1},{6,2},{7,3},{8,12},{9,13},{10,... | collective-permute-start | bytes 884744 | tf_op jit(solution)/shard_map/ppermute | solution.py:107
  433.5 19.8 %collective-permute-start.77 = (bf16[128,1152]{1,0:T(8,128)(2,1)}, bf16[128,1152]{1,0:T(8,128)(2,1)S(1)}, u32[]{:S(2)}, u32[]{:S(2)}) collective-permute-start(bf16[128,1152]{1,0:T(8,128)(2,1)} %get-tuple-element.356), channel_id=1, source_target_pairs={{0,6},{1,7},{2,4},{3,5},{4,2},{5,3},{6,0},{7,1},{8,14},{9,15},{10,... | collective-permute-start | bytes 884744 | tf_op jit(solution)/shard_map/ppermute | solution.py:107
  449.7 15.0 %collective-permute-start.72 = (bf16[128,1024]{1,0:T(8,128)(2,1)S(1)}, bf16[128,1024]{1,0:T(8,128)(2,1)S(1)}, u32[]{:S(2)}, u32[]{:S(2)}) collective-permute-start(bf16[128,1024]{1,0:T(8,128)(2,1)S(1)} %copy-done.86), channel_id=1, source_target_pairs={{0,2},{1,3},{2,0},{3,1},{4,6},{5,7},{6,4},{7,5},{8,10},{9,11},{10,... | collective-permute-start | bytes 786440 | tf_op jit(solution)/shard_map/ppermute | solution.py:107
  450.8 13.9 %collective-permute-start.73 = (bf16[128,1024]{1,0:T(8,128)(2,1)S(1)}, bf16[128,1024]{1,0:T(8,128)(2,1)S(1)}, u32[]{:S(2)}, u32[]{:S(2)}) collective-permute-start(bf16[128,1024]{1,0:T(8,128)(2,1)S(1)} %copy-done.85), channel_id=1, source_target_pairs={{0,4},{1,5},{2,6},{3,7},{4,0},{5,1},{6,2},{7,3},{8,12},{9,13},{10,... | collective-permute-start | bytes 786440 | tf_op jit(solution)/shard_map/ppermute | solution.py:107
  452.2 12.6 %collective-permute-start.74 = (bf16[128,1024]{1,0:T(8,128)(2,1)S(1)}, bf16[128,1024]{1,0:T(8,128)(2,1)S(1)}, u32[]{:S(2)}, u32[]{:S(2)}) collective-permute-start(bf16[128,1024]{1,0:T(8,128)(2,1)S(1)} %copy-done.84), channel_id=1, source_target_pairs={{0,6},{1,7},{2,4},{3,5},{4,2},{5,3},{6,0},{7,1},{8,14},{9,15},{10,... | collective-permute-start | bytes 786440 | tf_op jit(solution)/shard_map/ppermute | solution.py:107
  471.4 26.7 %collective-permute-start.79 = (bf16[128,1024]{1,0:T(8,128)(2,1)}, bf16[128,1024]{1,0:T(8,128)(2,1)S(1)}, u32[]{:S(2)}, u32[]{:S(2)}) collective-permute-start(bf16[128,1024]{1,0:T(8,128)(2,1)} %get-tuple-element.385), channel_id=1, source_target_pairs={{0,2},{1,3},{2,0},{3,1},{4,6},{5,7},{6,4},{7,5},{8,10},{9,11},{10,... | collective-permute-start | bytes 786440 | tf_op jit(solution)/shard_map/ppermute | solution.py:107
  473.8 24.3 %collective-permute-start.80 = (bf16[128,1024]{1,0:T(8,128)(2,1)}, bf16[128,1024]{1,0:T(8,128)(2,1)S(1)}, u32[]{:S(2)}, u32[]{:S(2)}) collective-permute-start(bf16[128,1024]{1,0:T(8,128)(2,1)} %get-tuple-element.386), channel_id=1, source_target_pairs={{0,4},{1,5},{2,6},{3,7},{4,0},{5,1},{6,2},{7,3},{8,12},{9,13},{10,... | collective-permute-start | bytes 786440 | tf_op jit(solution)/shard_map/ppermute | solution.py:107
  476.6 21.6 %collective-permute-start.81 = (bf16[128,1024]{1,0:T(8,128)(2,1)}, bf16[128,1024]{1,0:T(8,128)(2,1)S(1)}, u32[]{:S(2)}, u32[]{:S(2)}) collective-permute-start(bf16[128,1024]{1,0:T(8,128)(2,1)} %get-tuple-element.387), channel_id=1, source_target_pairs={{0,6},{1,7},{2,4},{3,5},{4,2},{5,3},{6,0},{7,1},{8,14},{9,15},{10,... | collective-permute-start | bytes 786440 | tf_op jit(solution)/shard_map/ppermute | solution.py:107
  510.9 15.6 %collective-permute-start.82 = (bf16[512,2176]{1,0:T(8,128)(2,1)}, bf16[512,2176]{1,0:T(8,128)(2,1)S(1)}, u32[]{:S(2)}, u32[]{:S(2)}) collective-permute-start(bf16[512,2176]{1,0:T(8,128)(2,1)} %fusion.1), channel_id=1, source_target_pairs={{0,1},{1,0},{2,3},{3,2},{4,5},{5,4},{6,7},{7,6},{8,9},{9,8},{10,11... | collective-permute-start | bytes 6684680 | tf_op jit(solution)/shard_map/ppermute | solution.py:48
  519.7 12.1 %collective-permute-start.84 = (bf16[128,1024]{1,0:T(8,128)(2,1)}, bf16[128,1024]{1,0:T(8,128)(2,1)S(1)}, u32[]{:S(2)}, u32[]{:S(2)}) collective-permute-start(bf16[128,1024]{1,0:T(8,128)(2,1)} %get-tuple-element.415), channel_id=1, source_target_pairs={{0,2},{1,3},{2,0},{3,1},{4,6},{5,7},{6,4},{7,5},{8,10},{9,11},{10,... | collective-permute-start | bytes 786440 | tf_op jit(solution)/shard_map/ppermute | solution.py:107
  521.2 13.9 %collective-permute-start.85 = (bf16[128,1024]{1,0:T(8,128)(2,1)}, bf16[128,1024]{1,0:T(8,128)(2,1)S(1)}, u32[]{:S(2)}, u32[]{:S(2)}) collective-permute-start(bf16[128,1024]{1,0:T(8,128)(2,1)} %get-tuple-element.416), channel_id=1, source_target_pairs={{0,4},{1,5},{2,6},{3,7},{4,0},{5,1},{6,2},{7,3},{8,12},{9,13},{10,... | collective-permute-start | bytes 786440 | tf_op jit(solution)/shard_map/ppermute | solution.py:107
  522.7 12.4 %collective-permute-start.86 = (bf16[128,1024]{1,0:T(8,128)(2,1)}, bf16[128,1024]{1,0:T(8,128)(2,1)S(1)}, u32[]{:S(2)}, u32[]{:S(2)}) collective-permute-start(bf16[128,1024]{1,0:T(8,128)(2,1)} %get-tuple-element.417), channel_id=1, source_target_pairs={{0,6},{1,7},{2,4},{3,5},{4,2},{5,3},{6,0},{7,1},{8,14},{9,15},{10,... | collective-permute-start | bytes 786440 | tf_op jit(solution)/shard_map/ppermute | solution.py:107
  535.9 34.4 %collective-permute-start.87 = (bf16[128,2176]{1,0:T(8,128)(2,1)}, bf16[128,2176]{1,0:T(8,128)(2,1)S(1)}, u32[]{:S(2)}, u32[]{:S(2)}) collective-permute-start(bf16[128,2176]{1,0:T(8,128)(2,1)} %get-tuple-element.419), channel_id=1, source_target_pairs={{0,2},{1,3},{2,0},{3,1},{4,6},{5,7},{6,4},{7,5},{8,10},{9,11},{10,... | collective-permute-start | bytes 1671176 | tf_op jit(solution)/shard_map/ppermute | solution.py:107
  537.0 33.3 %collective-permute-start.88 = (bf16[128,2176]{1,0:T(8,128)(2,1)}, bf16[128,2176]{1,0:T(8,128)(2,1)S(1)}, u32[]{:S(2)}, u32[]{:S(2)}) collective-permute-start(bf16[128,2176]{1,0:T(8,128)(2,1)} %get-tuple-element.420), channel_id=1, source_target_pairs={{0,4},{1,5},{2,6},{3,7},{4,0},{5,1},{6,2},{7,3},{8,12},{9,13},{10,... | collective-permute-start | bytes 1671176 | tf_op jit(solution)/shard_map/ppermute | solution.py:107
  537.9 32.4 %collective-permute-start.89 = (bf16[128,2176]{1,0:T(8,128)(2,1)}, bf16[128,2176]{1,0:T(8,128)(2,1)S(1)}, u32[]{:S(2)}, u32[]{:S(2)}) collective-permute-start(bf16[128,2176]{1,0:T(8,128)(2,1)} %get-tuple-element.421), channel_id=1, source_target_pairs={{0,6},{1,7},{2,4},{3,5},{4,2},{5,3},{6,0},{7,1},{8,14},{9,15},{10,... | collective-permute-start | bytes 1671176 | tf_op jit(solution)/shard_map/ppermute | solution.py:107
  570.3 14.3 %collective-permute-start.90 = (bf16[2048,1152]{1,0:T(8,128)(2,1)}, bf16[2048,1152]{1,0:T(8,128)(2,1)}, u32[]{:S(2)}, u32[]{:S(2)}) collective-permute-start(bf16[2048,1152]{1,0:T(8,128)(2,1)} %all-gather.8.cloned.1.call-done.refs_0_), channel_id=1, source_target_pairs={{0,1},{1,0},{2,3},{3,2},{4,5},{5,4},{6,7},{7,6},{8,9},{9,8},{10,11... | collective-permute-start | bytes 14155784 | tf_op jit(solution)/shard_map/ppermute | solution.py:48
  570.4 14.2 %collective-permute-start.91 = (bf16[2048,1024]{1,0:T(8,128)(2,1)}, bf16[2048,1024]{1,0:T(8,128)(2,1)}, u32[]{:S(2)}, u32[]{:S(2)}) collective-permute-start(bf16[2048,1024]{1,0:T(8,128)(2,1)} %all-gather.14.cloned.1.call-done.refs_2_), channel_id=1, source_target_pairs={{0,1},{1,0},{2,3},{3,2},{4,5},{5,4},{6,7},{7,6},{8,9},{9,8},{10,11... | collective-permute-start | bytes 12582920 | tf_op jit(solution)/shard_map/ppermute | solution.py:48
  572.7 27.1 %collective-permute-start.92 = (bf16[128,3200]{1,0:T(8,128)(2,1)S(1)}, bf16[128,3200]{1,0:T(8,128)(2,1)S(1)}, u32[]{:S(2)}, u32[]{:S(2)}) collective-permute-start(bf16[128,3200]{1,0:T(8,128)(2,1)S(1)} %pad_maximum_fusion.6), channel_id=1, source_target_pairs={{0,8},{8,0},{16,24},{24,16},{1,9},{9,1},{17,25},{25,17},{2,10},{10... | collective-permute-start | bytes 2457608 | tf_op jit(solution)/shard_map/ppermute | solution.py:121
  599.9 39.0 %collective-permute-start.93 = (bf16[128,3200]{1,0:T(8,128)(2,1)S(1)}, bf16[128,3200]{1,0:T(8,128)(2,1)S(1)}, u32[]{:S(2)}, u32[]{:S(2)}) collective-permute-start(bf16[128,3200]{1,0:T(8,128)(2,1)S(1)} %add_convert_fusion), channel_id=1, source_target_pairs={{0,16},{8,24},{16,0},{24,8},{1,17},{9,25},{17,1},{25,9},{2,18},{10... | collective-permute-start | bytes 2457608 | tf_op jit(solution)/shard_map/ppermute | solution.py:121
  (125 other events, 832.1 us)
Sparse Core Ops, SparseCore 0:
  102.5 48.8 all-gather.5
  152.9 88.1 all-gather.7
  242.6 87.8 all-gather.9
  331.9 79.2 all-gather.11
  416.5 81.5 all-gather.13
  515.5 42.1 all-reduce.3

commit v5 on v4

--- a/solution.py
+++ b/solution.py
@@ -1284,6 +1284,8 @@
                     next_qkv, lax.axis_index("dp") * share, share, axis=0
                 )
             next_qkv, (q, out_weight) = tie(next_qkv, q, out_weight)
+        else:
+            gx, unused = tie(cotangent[0], q)
         *o, den, un, h, pay, gates = attend(
             kv_pieces,
             out_weight,
@@ -1305,7 +1307,7 @@
                 next_qkv = all_streams(next_qkv)
             next_out, unused = tie(with_router(layer_idx + 1), near)
         else:
-            gx, (near,) = tie(cotangent[0], near)
+            grad_near = gather_chips(gx, pay)
         sides[layer_idx] = all_streams(near)
         partial, x_rows, gate_rows, pair_values, pick = moe_fwd(
             both_cores(near), w_expert, layer_idx, first
@@ -1324,7 +1326,6 @@
             qkv_weight, out_weight = [next_qkv], next_out
             parts = streams if hierarchical(ctx_size) else 1
         else:
-            grad_near = gather_chips(gx, sent)
             grad_near, (own, sent) = tie(grad_near, own, sent)
             grad_side = all_streams(grad_near)
     last_h, last_own, last_sent = h, own, sent
@@ -1438,15 +1439,17 @@
                     for at in range(0, width, half)
                 ]
             )
+            (side, new_side), unused = tie((sides[layer_idx], new_side), sent)
+            side, new_side = both_cores(side), both_cores(new_side)
             if split < experts_here:
                 expert_sum, (own, sent, early[0]) = tie(expert_sum, own, sent, early[0])
                 expert_sum = upper_sum(split, experts_here - split, expert_sum)
             arrived, (expert_sum,) = tie(reduce_finish(own, sent), expert_sum)
             below = jnp.concatenate([total_of(arrived), total_of(early[0])], axis=1).astype(BF16)
             (side, new_side), (expert_sum, upper_grads) = tie(
-                (sides[layer_idx], new_side), expert_sum, upper_grads
+                (side, new_side), expert_sum, upper_grads
             )
-            picked = pick_rows(both_cores(side), both_cores(new_side), w_expert, first)
+            picked = pick_rows(side, new_side, w_expert, first)
             below = add_across(below, 1, picked[1]).astype(BF16)
             expert_sum = expert_grads(
                 [x_rows, picked[0]],

time: 659 us -> 659 us (level)
  waiting for transfers between devices: 175 us -> 168 us
    ppermute x26, waiting for transfers between devices: 32.9 us -> 21.5 us  [swap_cores(): return lax.ppermute(rows, 'ctx', chip_perm(lax.axis_size('ctx'), 1))]
    unnamed x198 -> x203, local copies, waits for them, and re-layouts: 32.9 us -> 35.4 us
where the time goes in v5:
time: 659 us; the launch traced here: 651 us
  Pallas kernels  287 us (44%)
  waiting for transfers between devices  168 us (25%)
  starting transfers between devices  91.7 us (14%)
  local copies, waits for them, and re-layouts  49 us (7%)
  other arithmetic  21.1 us (3%)
  matrix products  18.4 us (3%)
  between operations  16 us (2%)
    ppermute x36, waiting for transfers between devices, gather_chips(): lax.ppermute(rows, 'ctx', chip_perm(size, 2 * k))  95.6 us
    pallas_call x3, Pallas kernels, expert_grads(): pl.pallas_call(functools.partial(expert_grad_kernel, streams, before is n...  83.9 us
    ppermute x36, starting transfers between devices, gather_chips(): lax.ppermute(rows, 'ctx', chip_perm(size, 2 * k))  45.5 us
    ppermute x30, waiting for transfers between devices, reduce_finish(): lax.ppermute(piece, 'ctx', chip_perm(size, 2 * (k + 1)))  45 us
    ppermute x30, starting transfers between devices, reduce_finish(): lax.ppermute(piece, 'ctx', chip_perm(size, 2 * (k + 1)))  39.9 us
    pallas_call x2, Pallas kernels, moe_bwd(): pl.pallas_call(functools.partial(moe_bwd_kernel, experts, len(pieces), ha...  36.9 us
    pallas_call x2, Pallas kernels, moe_fwd(): pl.pallas_call(functools.partial(moe_fwd_kernel, experts, len(pieces), ha...  36.2 us
    unnamed x203, local copies, waits for them, and re-layouts  35.4 us
  transfers between devices with their start and end apart: 100, of which 44 were waited for; matrix products, arithmetic and copies ran while one was open for 7% of the time, Pallas kernels for 42%

profile of v5, /device:TPU:0, one launch (start us, length us, event | category | flops | bytes accessed | tf_op | source)
XLA Modules:
  0.0 650.6 jit_solution(2216501461506514157)
XLA Ops:
  7.9 3.0 collective-permute-start
  14.2 2.9 collective-permute-start.6
  22.8 4.1 collective-permute-done.5
  32.2 4.4 project.4
  40.2 5.6 collective-permute-done.12
  45.9 6.3 collective-permute-done.13
  60.7 3.0 collective-permute-done.8
  64.9 4.5 project.5
  70.1 6.5 collective-permute-done.18
  79.6 3.3 collective-permute-done.9
  92.4 7.3 %attend.2 = (bf16[128,1024]{1,0:T(8,128)(2,1)}, bf16[128,1024]{1,0:T(8,128)(2,1)}, f32[4,512,128]{2,1,0:T(8,128)}, f32[4,512,128]{2,1,0:T(8,128)}, f32[128,1024]...) custom-call(s32[8]{0:T(128)} %get-tuple-element.234.need_ref, s32[8]{0:T(128)} %copy-done.74, ...), custom_call_target="tpu_custom_call" | custom-call | flops 536870912 | bytes 6815744 | tf_op jit(solution)/shard_map/attend/pallas_call | solution.py:895
  105.8 6.0 collective-permute-done.20
  111.9 5.6 collective-permute-done.21
  123.1 18.0 %moe_fwd.2 = (bf16[512,1024]{1,0:T(8,128)(2,1)}, bf16[512,1024]{1,0:T(8,128)(2,1)}, bf16[4,320,1024]{2,1,0:T(8,128)(2,1)}, f32[4,320,128]{2,1,0:T(8,128)}, f32[4...) custom-call(s32[1]{0:T(128)} %bitcast.16.first_ref, bf16[512,1152]{1,0:T(8,128)(2,1)} %copy-done.4, ...), custom_call_target="tpu_custom_call" | custom-call | flops 4026531840 | bytes 24641536 | tf_op jit(solution)/shard_map/moe_fwd/pallas_call | solution.py:545
  141.4 2.7 collective-permute-done.24.far_ref
  145.1 2.7 fold.10
  154.3 4.1 collective-permute-done.25
  159.9 5.0 collective-permute-done.26
  170.3 7.1 %collective-permute-done.37 = bf16[128,1152]{1,0:T(8,128)(2,1)S(1)} collective-permute-done((bf16[128,1152]{1,0:T(8,128)(2,1)S(1)}, bf16[128,1152]{1,0:T(8,128)(2,1)S(1)}, u32[]{:S(2)}, u32[]{:S(2)}) %collective-permute-start.37) | collective-permute-done | bytes 294944 | tf_op jit(solution)/shard_map/ppermute | solution.py:56
  179.8 4.8 project.6
  189.4 4.7 collective-permute-done.32
  194.1 5.4 collective-permute-done.33
  199.6 5.0 project.7
  205.7 7.3 %attend.3 = (bf16[128,1024]{1,0:T(8,128)(2,1)}, bf16[128,1024]{1,0:T(8,128)(2,1)}, f32[4,512,128]{2,1,0:T(8,128)}, f32[4,512,128]{2,1,0:T(8,128)}, f32[128,1024]...) custom-call(s32[8]{0:T(128)} %get-tuple-element.234.need_ref, s32[8]{0:T(128)} %copy-done.74, ...), custom_call_target="tpu_custom_call" | custom-call | flops 536870912 | bytes 6815744 | tf_op jit(solution)/shard_map/attend/pallas_call | solution.py:895
  218.7 4.2 collective-permute-done.43
  223.0 7.1 %collective-permute-done.44 = bf16[128,1152]{1,0:T(8,128)(2,1)S(1)} collective-permute-done((bf16[128,1152]{1,0:T(8,128)(2,1)}, bf16[128,1152]{1,0:T(8,128)(2,1)S(1)}, u32[]{:S(2)}, u32[]{:S(2)}) %collective-permute-start.44) | collective-permute-done | bytes 294944 | tf_op jit(solution)/shard_map/ppermute | solution.py:56
  233.6 2.7 collective-permute-done.46.refs_1_
  237.4 18.2 %moe_fwd.3 = (bf16[512,1024]{1,0:T(8,128)(2,1)}, bf16[512,1024]{1,0:T(8,128)(2,1)}, bf16[4,320,1024]{2,1,0:T(8,128)(2,1)}, f32[4,320,128]{2,1,0:T(8,128)}, f32[4...) custom-call(s32[1]{0:T(128)} %bitcast.16.first_ref, bf16[512,1152]{1,0:T(8,128)(2,1)} %copy-done.5, ...), custom_call_target="tpu_custom_call" | custom-call | flops 4026531840 | bytes 24641536 | tf_op jit(solution)/shard_map/moe_fwd/pallas_call | solution.py:545
  259.6 5.7 collective-permute-done.40
  265.2 5.5 collective-permute-done.41
  271.9 2.7 fold.11
  279.0 18.5 %moe_bwd.2 = (bf16[512,1152]{1,0:T(8,128)(2,1)}, bf16[512,1152]{1,0:T(8,128)(2,1)}, bf16[4,320,1024]{2,1,0:T(8,128)(2,1)}, bf16[4,320,512]{2,1,0:T(8,128)(2,1)}, bf16[4,320,1024]{2,1,0:T(8,128)(2,1)}) custom-call(s32[1]{0:T(128)} %bitcast.16.first_ref, bf16[512,1024]{1,0:T(8,128)(2,1)} %copy-done.1, bf16[512,1024]{1,0:T(8,128)(2,1)} %copy-done.31, ...), custom_call_target="tpu_custom_call" | custom-call | flops 4026531840 | bytes 28573696 | tf_op jit(solution)/shard_map/moe_bwd/pallas_call | solution.py:591
  297.8 3.0 collective-permute-done.52.far_ref
  301.7 2.9 fold.12
  308.2 6.6 %collective-permute-done.53.refs_5_ = bf16[128,1152]{1,0:T(8,128)(2,1)S(1)} collective-permute-done((bf16[128,1152]{1,0:T(8,128)(2,1)}, bf16[128,1152]{1,0:T(8,128)(2,1)S(1)}, u32[]{:S(2)}, u32[]{:S(2)}) %collective-permute-start.53) | collective-permute-done | bytes 294944 | tf_op jit(solution)/shard_map/ppermute | solution.py:107
  314.7 5.0 collective-permute-done.54.refs_6_
  322.2 10.7 %attend_back.2 = (f32[128,1024]{1,0:T(8,128)}, bf16[128,1024]{1,0:T(8,128)(2,1)}, bf16[128,128]{1,0:T(8,128)(2,1)}, f32[1,1024]{1,0:T(1,128)}, bf16[128,1024]{1,...) custom-call(s32[8]{0:T(128)} %get-tuple-element.234.need_ref, s32[8]{0:T(128)} %copy-done.74, ...), custom_call_target="tpu_custom_call" | custom-call | flops 939524096 | bytes 10223616 | tf_op jit(solution)/shard_map/attend_back/pallas_call | solution.py:1058
  337.3 2.9 fold.13
  341.9 2.5 collective-permute-start.59
  348.3 2.7 fold.14
  351.0 5.3 collective-permute-done.59.refs_4_
  358.9 7.8 %project_back.2 = (f32[128,1024]{1,0:T(8,128)}, bf16[128,1024]{1,0:T(8,128)(2,1)}, bf16[128,2176]{1,0:T(8,128)(2,1)}, f32[1,1024]{1,0:T(1,128)}) custom-call(s32[8]{0:T(128)} %copy-done.74, bf16[512,2048]{1,0:T(8,128)(2,1)} %all-gather.6.cloned.1.call-done.refs_0_, bf16[512,2048]{1,0:T(8,128)(2,1)} %copy-done, f32[128,1024]{1,0:T(8,128)} %get-tuple-element.327.refs_2_, ...), custom_call_target="tpu_custom_call" | custom-call | flops 536870912 | bytes 7340032 | tf_op jit(solution)/shard_map/project_back/pallas_call | solution.py:1146
  366.7 3.2 convolution_convert_fusion
  375.5 3.5 collective-permute-done.61
  379.0 5.6 collective-permute-done.62
  386.1 3.9 fold.15
  394.6 18.4 %moe_bwd.3 = (bf16[512,1152]{1,0:T(8,128)(2,1)}, bf16[512,1152]{1,0:T(8,128)(2,1)}, bf16[4,320,1024]{2,1,0:T(8,128)(2,1)}, bf16[4,320,512]{2,1,0:T(8,128)(2,1)}, bf16[4,320,1024]{2,1,0:T(8,128)(2,1)}) custom-call(s32[1]{0:T(128)} %bitcast.16.first_ref, bf16[512,1024]{1,0:T(8,128)(2,1)} %copy-done.2, bf16[512,1024]{1,0:T(8,128)(2,1)} %copy-done.32, ...), custom_call_target="tpu_custom_call" | custom-call | flops 4026531840 | bytes 28573696 | tf_op jit(solution)/shard_map/moe_bwd/pallas_call | solution.py:591
  420.1 8.5 %collective-permute-done.69.far_ref = bf16[512,1152]{1,0:T(8,128)(2,1)S(1)} collective-permute-done((bf16[512,1152]{1,0:T(8,128)(2,1)}, bf16[512,1152]{1,0:T(8,128)(2,1)S(1)}, u32[]{:S(2)}, u32[]{:S(2)}) %collective-permute-start.69) | collective-permute-done | bytes 1179680 | tf_op jit(solution)/shard_map/ppermute | solution.py:48
  429.6 2.8 fold.16
  435.9 15.1 %pick_rows.2 = (bf16[3,4,320,1024]{3,2,1,0:T(8,128)(2,1)}, bf16[3,4,320,1024]{3,2,1,0:T(8,128)(2,1)}) custom-call(s32[1]{0:T(128)} %bitcast.16.first_ref, s32[3]{0:T(128)} %and_select_fusion.stream_ref, bf16[2048,1152]{1,0:T(8,128)(2,1)} %all-gather.10.cloned.1.call-done.refs_0_, bf16[2048,1152]{1,0:T(8,128)(2,1)} %collective-permute-done.70.refs_1_, ...), custom_call_target="tpu_custom_call" | custom-call | flops 4026531840 | bytes 28311552 | tf_op jit(solution)/shard_map/pick_rows/pallas_call | solution.py:645
  455.5 10.6 %attend_back.3 = (f32[128,1024]{1,0:T(8,128)}, bf16[128,1024]{1,0:T(8,128)(2,1)}, bf16[128,128]{1,0:T(8,128)(2,1)}, f32[1,1024]{1,0:T(1,128)}, bf16[128,1024]{1,...) custom-call(s32[8]{0:T(128)} %get-tuple-element.234.need_ref, s32[8]{0:T(128)} %copy-done.74, ...), custom_call_target="tpu_custom_call" | custom-call | flops 939524096 | bytes 10223616 | tf_op jit(solution)/shard_map/attend_back/pallas_call | solution.py:1058
  470.6 2.7 fold.17
  475.2 2.7 collective-permute-start.80
  479.3 15.0 %expert_grads.3.refs_7_ = f32[2,4,1024,1536]{3,2,1,0:T(8,128)} custom-call(bf16[4,320,1024]{2,1,0:T(8,128)(2,1)} %get-tuple-element.384.refs_0_, bf16[3,4,320,1024]{3,2,1,0:T(8,128)(2,1)} %get-tuple-element.390.refs_1_, bf16[4,320,1024]{2,1,0:T(8,128)(2,1)} %get-tuple-element.391.refs_2_, bf16[3,4,320,1024]{3,2,1,0:T(8,128)(2,1)} %get-tuple-element.392.refs_3_, ...), custom_call_target="tpu_custom_call" | custom-call | flops 7046430720 | bytes 14680064 | tf_op jit(solution)/shard_map/expert_grads/pallas_call | solution.py:684
  494.3 2.5 all-gather.14.cloned.1.call-done.refs_2_
  497.8 7.4 %project_back.3 = (f32[128,1024]{1,0:T(8,128)}, bf16[128,1024]{1,0:T(8,128)(2,1)}, bf16[128,2176]{1,0:T(8,128)(2,1)}, f32[1,1024]{1,0:T(1,128)}) custom-call(s32[8]{0:T(128)} %copy-done.74, bf16[512,1024]{1,0:T(8,128)(2,1)} %copy-done.9, bf16[512,1024]{1,0:T(8,128)(2,1)} %copy-done.14, bf16[512,1024]{1,0:T(8,128)(2,1)} %copy-done.3, ...), custom_call_target="tpu_custom_call" | custom-call | flops 536870912 | bytes 7340032 | tf_op jit(solution)/shard_map/project_back/pallas_call | solution.py:1146
  512.0 3.1 fusion.near_ref
  516.4 4.0 fold.18
  525.0 2.7 fold.19
  532.2 4.9 collective-permute-done.86
  537.0 6.4 collective-permute-done.87
  546.9 30.8 %expert_grads.4.refs_7_ = f32[2,4,1024,1536]{3,2,1,0:T(8,128)} custom-call(bf16[4,320,1024]{2,1,0:T(8,128)(2,1)} %get-tuple-element.384.refs_0_, bf16[3,4,320,1024]{3,2,1,0:T(8,128)(2,1)} %get-tuple-element.390.refs_1_, bf16[4,320,1024]{2,1,0:T(8,128)(2,1)} %get-tuple-element.391.refs_2_, ...), custom_call_target="tpu_custom_call", output_to_operand_aliasing={{}: (7, {})} | custom-call | flops 21139292160 | bytes 44040192 | tf_op jit(solution)/shard_map/expert_grads/pallas_call | solution.py:684
  581.5 15.1 %pick_rows.3 = (bf16[3,4,320,1024]{3,2,1,0:T(8,128)(2,1)}, bf16[3,4,320,1024]{3,2,1,0:T(8,128)(2,1)}) custom-call(s32[1]{0:T(128)} %bitcast.16.first_ref, s32[3]{0:T(128)} %and_select_fusion.stream_ref, bf16[2048,1152]{1,0:T(8,128)(2,1)} %all-gather.8.cloned.1.call-done.refs_0_, bf16[2048,1152]{1,0:T(8,128)(2,1)} %collective-permute-done.83.refs_1_, ...), custom_call_target="tpu_custom_call" | custom-call | flops 4026531840 | bytes 28311552 | tf_op jit(solution)/shard_map/pick_rows/pallas_call | solution.py:645
  599.3 38.1 %expert_grads.5 = f32[2,4,1024,1536]{3,2,1,0:T(8,128)} custom-call(bf16[4,320,1024]{2,1,0:T(8,128)(2,1)} %get-tuple-element.434.refs_0_, bf16[3,4,320,1024]{3,2,1,0:T(8,128)(2,1)} %get-tuple-element.439.refs_1_, bf16[4,320,1024]{2,1,0:T(8,128)(2,1)} %get-tuple-element.440.refs_2_, ...), custom_call_target="tpu_custom_call", output_to_operand_aliasing={{}: (7, {})} | custom-call | flops 28185722880 | bytes 58720256 | tf_op jit(solution)/shard_map/expert_grads/pallas_call | solution.py:684
  (467 shorter events, 184.8 us)
Async XLA Ops:
  7.2 141.9 %all-gather.6.cloned.1.call-start = ((), (), s32[]{:S(2)}) async-start(), calls=%async_computation | async-start | bytes 2621440 | tf_op jit(solution)/shard_map/all_gather | solution.py:116
  7.9 20.6 %collective-permute-start = (bf16[8,128]{1,0:T(8,128)(2,1)S(1)}, bf16[8,128]{1,0:T(8,128)(2,1)S(1)}, u32[]{:S(2)}, u32[]{:S(2)}) collective-permute-start(bf16[8,128]{1,0:T(8,128)(2,1)S(1)} %pad_maximum_fusion.11), channel_id=1, source_target_pairs={{0,2},{1,3},{2,0},{3,1},{4,6},{5,7},{6,4},{7,5},{8,10},{9,11},{10,... | collective-permute-start | bytes 6152 | tf_op jit(solution)/shard_map/ppermute | solution.py:56
  10.9 17.6 %collective-permute-start.1 = (bf16[8,128]{1,0:T(8,128)(2,1)S(1)}, bf16[8,128]{1,0:T(8,128)(2,1)S(1)}, u32[]{:S(2)}, u32[]{:S(2)}) collective-permute-start(bf16[8,128]{1,0:T(8,128)(2,1)S(1)} %pad_maximum_fusion.11), channel_id=1, source_target_pairs={{0,4},{1,5},{2,6},{3,7},{4,0},{5,1},{6,2},{7,3},{8,12},{9,13},{10,... | collective-permute-start | bytes 6152 | tf_op jit(solution)/shard_map/ppermute | solution.py:56
  14.1 12.8 %collective-permute-start.5 = (bf16[128,1024]{1,0:T(8,128)(2,1)S(1)}, bf16[128,1024]{1,0:T(8,128)(2,1)S(1)}, u32[]{:S(2)}, u32[]{:S(2)}) collective-permute-start(bf16[128,1024]{1,0:T(8,128)(2,1)S(1)} %get-tuple-element.483), channel_id=1, source_target_pairs={{0,4},{1,5},{2,6},{3,7},{4,0},{5,1},{6,2},{7,3},{8,12},{9,13},{10,... | collective-permute-start | bytes 786440 | tf_op jit(solution)/shard_map/ppermute | solution.py:56
  14.2 12.8 %collective-permute-start.6 = (bf16[128,1024]{1,0:T(8,128)(2,1)S(1)}, bf16[128,1024]{1,0:T(8,128)(2,1)S(1)}, u32[]{:S(2)}, u32[]{:S(2)}) collective-permute-start(bf16[128,1024]{1,0:T(8,128)(2,1)S(1)} %get-tuple-element.483), channel_id=1, source_target_pairs={{0,6},{1,7},{2,4},{3,5},{4,2},{5,3},{6,0},{7,1},{8,14},{9,15},{10,... | collective-permute-start | bytes 786440 | tf_op jit(solution)/shard_map/ppermute | solution.py:56
  38.2 13.9 %collective-permute-start.13 = (bf16[128,1024]{1,0:T(8,128)(2,1)S(1)}, bf16[128,1024]{1,0:T(8,128)(2,1)S(1)}, u32[]{:S(2)}, u32[]{:S(2)}) collective-permute-start(bf16[128,1024]{1,0:T(8,128)(2,1)S(1)} %get-tuple-element.237), channel_id=1, source_target_pairs={{0,4},{1,5},{2,6},{3,7},{4,0},{5,1},{6,2},{7,3},{8,12},{9,13},{10,... | collective-permute-start | bytes 786440 | tf_op jit(solution)/shard_map/ppermute | solution.py:56
  38.7 13.4 %collective-permute-start.14 = (bf16[128,1024]{1,0:T(8,128)(2,1)S(1)}, bf16[128,1024]{1,0:T(8,128)(2,1)S(1)}, u32[]{:S(2)}, u32[]{:S(2)}) collective-permute-start(bf16[128,1024]{1,0:T(8,128)(2,1)S(1)} %get-tuple-element.237), channel_id=1, source_target_pairs={{0,6},{1,7},{2,4},{3,5},{4,2},{5,3},{6,0},{7,1},{8,14},{9,15},{10,... | collective-permute-start | bytes 786440 | tf_op jit(solution)/shard_map/ppermute | solution.py:56
  54.9 15.1 %collective-permute-start.16 = (bf16[128,1152]{1,0:T(8,128)(2,1)S(1)}, bf16[128,1152]{1,0:T(8,128)(2,1)S(1)}, u32[]{:S(2)}, u32[]{:S(2)}) collective-permute-start(bf16[128,1152]{1,0:T(8,128)(2,1)S(1)} %concatenate.86), channel_id=1, source_target_pairs={{0,2},{1,3},{2,0},{3,1},{4,6},{5,7},{6,4},{7,5},{8,10},{9,11},{10,... | collective-permute-start | bytes 884744 | tf_op jit(solution)/shard_map/ppermute | solution.py:56
  56.5 13.5 %collective-permute-start.17 = (bf16[128,1152]{1,0:T(8,128)(2,1)S(1)}, bf16[128,1152]{1,0:T(8,128)(2,1)}, u32[]{:S(2)}, u32[]{:S(2)}) collective-permute-start(bf16[128,1152]{1,0:T(8,128)(2,1)S(1)} %concatenate.86), channel_id=1, source_target_pairs={{0,4},{1,5},{2,6},{3,7},{4,0},{5,1},{6,2},{7,3},{8,12},{9,13},{10,... | collective-permute-start | bytes 884744 | tf_op jit(solution)/shard_map/ppermute | solution.py:56
  57.0 19.5 %collective-permute-start.18 = (bf16[128,1152]{1,0:T(8,128)(2,1)S(1)}, bf16[128,1152]{1,0:T(8,128)(2,1)}, u32[]{:S(2)}, u32[]{:S(2)}) collective-permute-start(bf16[128,1152]{1,0:T(8,128)(2,1)S(1)} %concatenate.86), channel_id=1, source_target_pairs={{0,6},{1,7},{2,4},{3,5},{4,2},{5,3},{6,0},{7,1},{8,14},{9,15},{10,... | collective-permute-start | bytes 884744 | tf_op jit(solution)/shard_map/ppermute | solution.py:56
  58.5 24.4 %collective-permute-start.9 = (bf16[128,1024]{1,0:T(8,128)(2,1)}, bf16[128,1024]{1,0:T(8,128)(2,1)S(1)}, u32[]{:S(2)}, u32[]{:S(2)}) collective-permute-start(bf16[128,1024]{1,0:T(8,128)(2,1)} %get-tuple-element.235), channel_id=1, source_target_pairs={{0,4},{1,5},{2,6},{3,7},{4,0},{5,1},{6,2},{7,3},{8,12},{9,13},{10,... | collective-permute-start | bytes 786440 | tf_op jit(solution)/shard_map/ppermute | solution.py:56
  63.7 19.2 %collective-permute-start.10 = (bf16[128,1024]{1,0:T(8,128)(2,1)}, bf16[128,1024]{1,0:T(8,128)(2,1)}, u32[]{:S(2)}, u32[]{:S(2)}) collective-permute-start(bf16[128,1024]{1,0:T(8,128)(2,1)} %get-tuple-element.235), channel_id=1, source_target_pairs={{0,6},{1,7},{2,4},{3,5},{4,2},{5,3},{6,0},{7,1},{8,14},{9,15},{10,... | collective-permute-start | bytes 786440 | tf_op jit(solution)/shard_map/ppermute | solution.py:56
  87.1 12.6 %collective-permute-start.28 = (bf16[32,2048]{1,0:T(8,128)(2,1)S(1)}, bf16[32,2048]{1,0:T(8,128)(2,1)}, u32[]{:S(2)}, u32[]{:S(2)}) collective-permute-start(bf16[32,2048]{1,0:T(8,128)(2,1)S(1)} %dynamic-slice_bitcast_fusion), channel_id=1, source_target_pairs={{0,2},{1,3},{2,0},{3,1},{4,6},{5,7},{6,4},{7,5},{8,10},{9,11},{10,... | collective-permute-start | bytes 393224 | tf_op jit(solution)/shard_map/ppermute | solution.py:56
  101.6 195.9 %all-gather.8.cloned.1.call-start = ((), (), s32[]{:S(2)}) async-start(), calls=%async_computation.1 | async-start | bytes 5898240 | tf_op jit(solution)/shard_map/all_gather | solution.py:116
  102.9 14.5 %collective-permute-start.21 = (bf16[128,1152]{1,0:T(8,128)(2,1)}, bf16[128,1152]{1,0:T(8,128)(2,1)S(1)}, u32[]{:S(2)}, u32[]{:S(2)}) collective-permute-start(bf16[128,1152]{1,0:T(8,128)(2,1)} %get-tuple-element.254), channel_id=1, source_target_pairs={{0,4},{1,5},{2,6},{3,7},{4,0},{5,1},{6,2},{7,3},{8,12},{9,13},{10,... | collective-permute-start | bytes 884744 | tf_op jit(solution)/shard_map/ppermute | solution.py:56
  104.4 14.8 %collective-permute-start.22 = (bf16[128,1152]{1,0:T(8,128)(2,1)S(1)}, bf16[128,1152]{1,0:T(8,128)(2,1)S(1)}, u32[]{:S(2)}, u32[]{:S(2)}) collective-permute-start(bf16[128,1152]{1,0:T(8,128)(2,1)S(1)} %copy-done.27), channel_id=1, source_target_pairs={{0,6},{1,7},{2,4},{3,5},{4,2},{5,3},{6,0},{7,1},{8,14},{9,15},{10,... | collective-permute-start | bytes 884744 | tf_op jit(solution)/shard_map/ppermute | solution.py:56
  120.2 296.8 %all-gather.10.cloned.1.call-start = ((), (), s32[]{:S(2)}) async-start(), calls=%async_computation.2 | async-start | bytes 5898240 | tf_op jit(solution)/shard_map/all_gather | solution.py:116
  149.0 29.5 %collective-permute-start.31 = (bf16[512,2048]{1,0:T(8,128)(2,1)}, bf16[512,2048]{1,0:T(8,128)(2,1)S(1)}, u32[]{:S(2)}, u32[]{:S(2)}) collective-permute-start(bf16[512,2048]{1,0:T(8,128)(2,1)} %all-gather.6.cloned.1.call-done.refs_0_), channel_id=1, source_target_pairs={{0,1},{1,0},{2,3},{3,2},{4,5},{5,4},{6,7},{7,6},{8,9},{9,8},{10,11... | collective-permute-start | bytes 6291464 | tf_op jit(solution)/shard_map/ppermute | solution.py:48
  150.5 14.4 %collective-permute-start.26 = (bf16[128,1024]{1,0:T(8,128)(2,1)}, bf16[128,1024]{1,0:T(8,128)(2,1)}, u32[]{:S(2)}, u32[]{:S(2)}) collective-permute-start(bf16[128,1024]{1,0:T(8,128)(2,1)} %get-tuple-element.259), channel_id=1, source_target_pairs={{0,4},{1,5},{2,6},{3,7},{4,0},{5,1},{6,2},{7,3},{8,12},{9,13},{10,... | collective-permute-start | bytes 786440 | tf_op jit(solution)/shard_map/ppermute | solution.py:107
  152.0 14.5 %collective-permute-start.27 = (bf16[128,1024]{1,0:T(8,128)(2,1)}, bf16[128,1024]{1,0:T(8,128)(2,1)}, u32[]{:S(2)}, u32[]{:S(2)}) collective-permute-start(bf16[128,1024]{1,0:T(8,128)(2,1)} %get-tuple-element.260), channel_id=1, source_target_pairs={{0,6},{1,7},{2,4},{3,5},{4,2},{5,3},{6,0},{7,1},{8,14},{9,15},{10,... | collective-permute-start | bytes 786440 | tf_op jit(solution)/shard_map/ppermute | solution.py:107
  152.8 17.6 %collective-permute-start.36 = (bf16[128,1152]{1,0:T(8,128)(2,1)S(1)}, bf16[128,1152]{1,0:T(8,128)(2,1)S(1)}, u32[]{:S(2)}, u32[]{:S(2)}) collective-permute-start(bf16[128,1152]{1,0:T(8,128)(2,1)S(1)} %concatenate.92), channel_id=1, source_target_pairs={{0,2},{1,3},{2,0},{3,1},{4,6},{5,7},{6,4},{7,5},{8,10},{9,11},{10,... | collective-permute-start | bytes 884744 | tf_op jit(solution)/shard_map/ppermute | solution.py:56
  158.5 19.0 %collective-permute-start.37 = (bf16[128,1152]{1,0:T(8,128)(2,1)S(1)}, bf16[128,1152]{1,0:T(8,128)(2,1)S(1)}, u32[]{:S(2)}, u32[]{:S(2)}) collective-permute-start(bf16[128,1152]{1,0:T(8,128)(2,1)S(1)} %concatenate.92), channel_id=1, source_target_pairs={{0,4},{1,5},{2,6},{3,7},{4,0},{5,1},{6,2},{7,3},{8,12},{9,13},{10,... | collective-permute-start | bytes 884744 | tf_op jit(solution)/shard_map/ppermute | solution.py:56
  185.9 13.6 %collective-permute-start.33 = (bf16[128,1024]{1,0:T(8,128)(2,1)}, bf16[128,1024]{1,0:T(8,128)(2,1)S(1)}, u32[]{:S(2)}, u32[]{:S(2)}) collective-permute-start(bf16[128,1024]{1,0:T(8,128)(2,1)} %get-tuple-element.270), channel_id=1, source_target_pairs={{0,4},{1,5},{2,6},{3,7},{4,0},{5,1},{6,2},{7,3},{8,12},{9,13},{10,... | collective-permute-start | bytes 786440 | tf_op jit(solution)/shard_map/ppermute | solution.py:56
  186.8 17.9 %collective-permute-start.39 = (bf16[512,1152]{1,0:T(8,128)(2,1)S(1)}, bf16[512,1152]{1,0:T(8,128)(2,1)S(1)}, u32[]{:S(2)}, u32[]{:S(2)}) collective-permute-start(bf16[512,1152]{1,0:T(8,128)(2,1)S(1)} %constant_dynamic-update-slice_fusion.20.refs_2_), channel_id=1, source_target_pairs={{0,1},{1,0},{2,3},{3,2},{4,5},{5,4},{6,7},{7,6},{8,9},{9,8},{10,11... | collective-permute-start | bytes 3538952 | tf_op jit(solution)/shard_map/ppermute | solution.py:48
  186.8 12.7 %collective-permute-start.34 = (bf16[128,1024]{1,0:T(8,128)(2,1)}, bf16[128,1024]{1,0:T(8,128)(2,1)S(1)}, u32[]{:S(2)}, u32[]{:S(2)}) collective-permute-start(bf16[128,1024]{1,0:T(8,128)(2,1)} %get-tuple-element.270), channel_id=1, source_target_pairs={{0,6},{1,7},{2,4},{3,5},{4,2},{5,3},{6,0},{7,1},{8,14},{9,15},{10,... | collective-permute-start | bytes 786440 | tf_op jit(solution)/shard_map/ppermute | solution.py:56
  214.9 15.2 %collective-permute-start.44 = (bf16[128,1152]{1,0:T(8,128)(2,1)}, bf16[128,1152]{1,0:T(8,128)(2,1)S(1)}, u32[]{:S(2)}, u32[]{:S(2)}) collective-permute-start(bf16[128,1152]{1,0:T(8,128)(2,1)} %get-tuple-element.280), channel_id=1, source_target_pairs={{0,4},{1,5},{2,6},{3,7},{4,0},{5,1},{6,2},{7,3},{8,12},{9,13},{10,... | collective-permute-start | bytes 884744 | tf_op jit(solution)/shard_map/ppermute | solution.py:56
  217.3 14.5 %collective-permute-start.45 = (bf16[128,1152]{1,0:T(8,128)(2,1)}, bf16[128,1152]{1,0:T(8,128)(2,1)S(1)}, u32[]{:S(2)}, u32[]{:S(2)}) collective-permute-start(bf16[128,1152]{1,0:T(8,128)(2,1)} %get-tuple-element.280), channel_id=1, source_target_pairs={{0,6},{1,7},{2,4},{3,5},{4,2},{5,3},{6,0},{7,1},{8,14},{9,15},{10,... | collective-permute-start | bytes 884744 | tf_op jit(solution)/shard_map/ppermute | solution.py:56
  232.9 184.2 %all-gather.12.cloned.1.call-start = ((), (), s32[]{:S(2)}) async-start(), calls=%async_computation.3 | async-start | bytes 5242880 | tf_op jit(solution)/shard_map/all_gather | solution.py:116
  255.6 15.1 %collective-permute-start.47 = (bf16[512,1024]{1,0:T(8,128)(2,1)}, bf16[512,1024]{1,0:T(8,128)(2,1)S(1)}, u32[]{:S(2)}, u32[]{:S(2)}) collective-permute-start(bf16[512,1024]{1,0:T(8,128)(2,1)} %get-tuple-element.286), channel_id=1, source_target_pairs={{0,1},{1,0},{2,3},{3,2},{4,5},{5,4},{6,7},{7,6},{8,9},{9,8},{10,11... | collective-permute-start | bytes 3145736 | tf_op jit(solution)/shard_map/ppermute | solution.py:48
  256.7 14.0 %collective-permute-start.41 = (bf16[128,1024]{1,0:T(8,128)(2,1)S(1)}, bf16[128,1024]{1,0:T(8,128)(2,1)S(1)}, u32[]{:S(2)}, u32[]{:S(2)}) collective-permute-start(bf16[128,1024]{1,0:T(8,128)(2,1)S(1)} %bitcast.92), channel_id=1, source_target_pairs={{0,4},{1,5},{2,6},{3,7},{4,0},{5,1},{6,2},{7,3},{8,12},{9,13},{10,... | collective-permute-start | bytes 786440 | tf_op jit(solution)/shard_map/ppermute | solution.py:56
  274.6 23.0 %collective-permute-start.49 = (bf16[128,1024]{1,0:T(8,128)(2,1)}, bf16[128,1024]{1,0:T(8,128)(2,1)S(1)}, u32[]{:S(2)}, u32[]{:S(2)}) collective-permute-start(bf16[128,1024]{1,0:T(8,128)(2,1)} %get-tuple-element.298), channel_id=1, source_target_pairs={{0,2},{1,3},{2,0},{3,1},{4,6},{5,7},{6,4},{7,5},{8,10},{9,11},{10,... | collective-permute-start | bytes 786440 | tf_op jit(solution)/shard_map/ppermute | solution.py:107
  276.0 21.6 %collective-permute-start.50 = (bf16[128,1024]{1,0:T(8,128)(2,1)}, bf16[128,1024]{1,0:T(8,128)(2,1)S(1)}, u32[]{:S(2)}, u32[]{:S(2)}) collective-permute-start(bf16[128,1024]{1,0:T(8,128)(2,1)} %get-tuple-element.299), channel_id=1, source_target_pairs={{0,4},{1,5},{2,6},{3,7},{4,0},{5,1},{6,2},{7,3},{8,12},{9,13},{10,... | collective-permute-start | bytes 786440 | tf_op jit(solution)/shard_map/ppermute | solution.py:107
  276.6 21.0 %collective-permute-start.51 = (bf16[128,1024]{1,0:T(8,128)(2,1)}, bf16[128,1024]{1,0:T(8,128)(2,1)S(1)}, u32[]{:S(2)}, u32[]{:S(2)}) collective-permute-start(bf16[128,1024]{1,0:T(8,128)(2,1)} %get-tuple-element.300), channel_id=1, source_target_pairs={{0,6},{1,7},{2,4},{3,5},{4,2},{5,3},{6,0},{7,1},{8,14},{9,15},{10,... | collective-permute-start | bytes 786440 | tf_op jit(solution)/shard_map/ppermute | solution.py:107
  297.7 199.1 %all-gather.14.cloned.1.call-start = ((), (), s32[]{:S(2)}) async-start(), calls=%async_computation.4 | async-start | bytes 5242880 | tf_op jit(solution)/shard_map/all_gather | solution.py:116
  306.1 13.6 %collective-permute-start.54 = (bf16[128,1152]{1,0:T(8,128)(2,1)}, bf16[128,1152]{1,0:T(8,128)(2,1)S(1)}, u32[]{:S(2)}, u32[]{:S(2)}) collective-permute-start(bf16[128,1152]{1,0:T(8,128)(2,1)} %get-tuple-element.309), channel_id=1, source_target_pairs={{0,4},{1,5},{2,6},{3,7},{4,0},{5,1},{6,2},{7,3},{8,12},{9,13},{10,... | collective-permute-start | bytes 884744 | tf_op jit(solution)/shard_map/ppermute | solution.py:107
  306.7 14.7 %collective-permute-start.55 = (bf16[128,1152]{1,0:T(8,128)(2,1)}, bf16[128,1152]{1,0:T(8,128)(2,1)S(1)}, u32[]{:S(2)}, u32[]{:S(2)}) collective-permute-start(bf16[128,1152]{1,0:T(8,128)(2,1)} %get-tuple-element.310), channel_id=1, source_target_pairs={{0,6},{1,7},{2,4},{3,5},{4,2},{5,3},{6,0},{7,1},{8,14},{9,15},{10,... | collective-permute-start | bytes 884744 | tf_op jit(solution)/shard_map/ppermute | solution.py:107
  341.9 14.5 %collective-permute-start.59 = (bf16[128,1024]{1,0:T(8,128)(2,1)}, bf16[128,1024]{1,0:T(8,128)(2,1)S(1)}, u32[]{:S(2)}, u32[]{:S(2)}) collective-permute-start(bf16[128,1024]{1,0:T(8,128)(2,1)} %get-tuple-element.329), channel_id=1, source_target_pairs={{0,4},{1,5},{2,6},{3,7},{4,0},{5,1},{6,2},{7,3},{8,12},{9,13},{10,... | collective-permute-start | bytes 786440 | tf_op jit(solution)/shard_map/ppermute | solution.py:107
  344.4 13.8 %collective-permute-start.60 = (bf16[128,1024]{1,0:T(8,128)(2,1)}, bf16[128,1024]{1,0:T(8,128)(2,1)S(1)}, u32[]{:S(2)}, u32[]{:S(2)}) collective-permute-start(bf16[128,1024]{1,0:T(8,128)(2,1)} %get-tuple-element.330), channel_id=1, source_target_pairs={{0,6},{1,7},{2,4},{3,5},{4,2},{5,3},{6,0},{7,1},{8,14},{9,15},{10,... | collective-permute-start | bytes 786440 | tf_op jit(solution)/shard_map/ppermute | solution.py:107
  369.9 14.8 %collective-permute-start.64 = (bf16[512,2048]{1,0:T(8,128)(2,1)}, bf16[512,2048]{1,0:T(8,128)(2,1)S(1)}, u32[]{:S(2)}, u32[]{:S(2)}) collective-permute-start(bf16[512,2048]{1,0:T(8,128)(2,1)} %convolution_convert_fusion), channel_id=1, source_target_pairs={{0,1},{1,0},{2,3},{3,2},{4,5},{5,4},{6,7},{7,6},{8,9},{9,8},{10,11... | collective-permute-start | bytes 6291464 | tf_op jit(solution)/shard_map/ppermute | solution.py:48
  370.6 14.1 %collective-permute-start.62 = (bf16[128,1024]{1,0:T(8,128)(2,1)S(1)}, bf16[128,1024]{1,0:T(8,128)(2,1)S(1)}, u32[]{:S(2)}, u32[]{:S(2)}) collective-permute-start(bf16[128,1024]{1,0:T(8,128)(2,1)S(1)} %copy-done.72), channel_id=1, source_target_pairs={{0,4},{1,5},{2,6},{3,7},{4,0},{5,1},{6,2},{7,3},{8,12},{9,13},{10,... | collective-permute-start | bytes 786440 | tf_op jit(solution)/shard_map/ppermute | solution.py:56
  390.0 23.0 %collective-permute-start.66 = (bf16[128,2048]{1,0:T(8,128)(2,1)}, bf16[128,2048]{1,0:T(8,128)(2,1)S(1)}, u32[]{:S(2)}, u32[]{:S(2)}) collective-permute-start(bf16[128,2048]{1,0:T(8,128)(2,1)} %get-tuple-element.347), channel_id=1, source_target_pairs={{0,2},{1,3},{2,0},{3,1},{4,6},{5,7},{6,4},{7,5},{8,10},{9,11},{10,... | collective-permute-start | bytes 1572872 | tf_op jit(solution)/shard_map/ppermute | solution.py:107
  391.5 23.7 %collective-permute-start.67 = (bf16[128,2048]{1,0:T(8,128)(2,1)}, bf16[128,2048]{1,0:T(8,128)(2,1)S(1)}, u32[]{:S(2)}, u32[]{:S(2)}) collective-permute-start(bf16[128,2048]{1,0:T(8,128)(2,1)} %get-tuple-element.348), channel_id=1, source_target_pairs={{0,4},{1,5},{2,6},{3,7},{4,0},{5,1},{6,2},{7,3},{8,12},{9,13},{10,... | collective-permute-start | bytes 1572872 | tf_op jit(solution)/shard_map/ppermute | solution.py:107
  392.1 25.0 %collective-permute-start.68 = (bf16[128,2048]{1,0:T(8,128)(2,1)}, bf16[128,2048]{1,0:T(8,128)(2,1)}, u32[]{:S(2)}, u32[]{:S(2)}) collective-permute-start(bf16[128,2048]{1,0:T(8,128)(2,1)} %get-tuple-element.349), channel_id=1, source_target_pairs={{0,6},{1,7},{2,4},{3,5},{4,2},{5,3},{6,0},{7,1},{8,14},{9,15},{10,... | collective-permute-start | bytes 1572872 | tf_op jit(solution)/shard_map/ppermute | solution.py:107
  417.1 18.8 %collective-permute-start.70 = (bf16[2048,1152]{1,0:T(8,128)(2,1)}, bf16[2048,1152]{1,0:T(8,128)(2,1)}, u32[]{:S(2)}, u32[]{:S(2)}) collective-permute-start(bf16[2048,1152]{1,0:T(8,128)(2,1)} %all-gather.10.cloned.1.call-done.refs_0_), channel_id=1, source_target_pairs={{0,1},{1,0},{2,3},{3,2},{4,5},{5,4},{6,7},{7,6},{8,9},{9,8},{10,11... | collective-permute-start | bytes 14155784 | tf_op jit(solution)/shard_map/ppermute | solution.py:48
  417.1 18.8 %collective-permute-start.71 = (bf16[2048,1024]{1,0:T(8,128)(2,1)}, bf16[2048,1024]{1,0:T(8,128)(2,1)}, u32[]{:S(2)}, u32[]{:S(2)}) collective-permute-start(bf16[2048,1024]{1,0:T(8,128)(2,1)} %all-gather.12.cloned.1.call-done.refs_2_), channel_id=1, source_target_pairs={{0,1},{1,0},{2,3},{3,2},{4,5},{5,4},{6,7},{7,6},{8,9},{9,8},{10,11... | collective-permute-start | bytes 12582920 | tf_op jit(solution)/shard_map/ppermute | solution.py:48
  417.6 163.9 %all-reduce.4.cloned.1.call-start = ((), (), s32[]{:S(2)}) async-start(), calls=%async_computation.5 | async-start | bytes 1572864 | tf_op jit(solution)/shard_map/psum | solution.py:1390
  432.4 21.0 %collective-permute-start.75 = (bf16[128,1152]{1,0:T(8,128)(2,1)}, bf16[128,1152]{1,0:T(8,128)(2,1)S(1)}, u32[]{:S(2)}, u32[]{:S(2)}) collective-permute-start(bf16[128,1152]{1,0:T(8,128)(2,1)} %get-tuple-element.356), channel_id=1, source_target_pairs={{0,2},{1,3},{2,0},{3,1},{4,6},{5,7},{6,4},{7,5},{8,10},{9,11},{10,... | collective-permute-start | bytes 884744 | tf_op jit(solution)/shard_map/ppermute | solution.py:107
  432.9 21.7 %collective-permute-start.76 = (bf16[128,1152]{1,0:T(8,128)(2,1)}, bf16[128,1152]{1,0:T(8,128)(2,1)S(1)}, u32[]{:S(2)}, u32[]{:S(2)}) collective-permute-start(bf16[128,1152]{1,0:T(8,128)(2,1)} %get-tuple-element.357), channel_id=1, source_target_pairs={{0,4},{1,5},{2,6},{3,7},{4,0},{5,1},{6,2},{7,3},{8,12},{9,13},{10,... | collective-permute-start | bytes 884744 | tf_op jit(solution)/shard_map/ppermute | solution.py:107
  434.6 20.0 %collective-permute-start.77 = (bf16[128,1152]{1,0:T(8,128)(2,1)}, bf16[128,1152]{1,0:T(8,128)(2,1)S(1)}, u32[]{:S(2)}, u32[]{:S(2)}) collective-permute-start(bf16[128,1152]{1,0:T(8,128)(2,1)} %get-tuple-element.358), channel_id=1, source_target_pairs={{0,6},{1,7},{2,4},{3,5},{4,2},{5,3},{6,0},{7,1},{8,14},{9,15},{10,... | collective-permute-start | bytes 884744 | tf_op jit(solution)/shard_map/ppermute | solution.py:107
  451.0 15.1 %collective-permute-start.72 = (bf16[128,1024]{1,0:T(8,128)(2,1)S(1)}, bf16[128,1024]{1,0:T(8,128)(2,1)S(1)}, u32[]{:S(2)}, u32[]{:S(2)}) collective-permute-start(bf16[128,1024]{1,0:T(8,128)(2,1)S(1)} %copy-done.89), channel_id=1, source_target_pairs={{0,2},{1,3},{2,0},{3,1},{4,6},{5,7},{6,4},{7,5},{8,10},{9,11},{10,... | collective-permute-start | bytes 786440 | tf_op jit(solution)/shard_map/ppermute | solution.py:107
  451.6 14.5 %collective-permute-start.73 = (bf16[128,1024]{1,0:T(8,128)(2,1)S(1)}, bf16[128,1024]{1,0:T(8,128)(2,1)S(1)}, u32[]{:S(2)}, u32[]{:S(2)}) collective-permute-start(bf16[128,1024]{1,0:T(8,128)(2,1)S(1)} %copy-done.88), channel_id=1, source_target_pairs={{0,4},{1,5},{2,6},{3,7},{4,0},{5,1},{6,2},{7,3},{8,12},{9,13},{10,... | collective-permute-start | bytes 786440 | tf_op jit(solution)/shard_map/ppermute | solution.py:107
  453.3 12.8 %collective-permute-start.74 = (bf16[128,1024]{1,0:T(8,128)(2,1)S(1)}, bf16[128,1024]{1,0:T(8,128)(2,1)S(1)}, u32[]{:S(2)}, u32[]{:S(2)}) collective-permute-start(bf16[128,1024]{1,0:T(8,128)(2,1)S(1)} %copy-done.87), channel_id=1, source_target_pairs={{0,6},{1,7},{2,4},{3,5},{4,2},{5,3},{6,0},{7,1},{8,14},{9,15},{10,... | collective-permute-start | bytes 786440 | tf_op jit(solution)/shard_map/ppermute | solution.py:107
  473.3 23.6 %collective-permute-start.79 = (bf16[128,1024]{1,0:T(8,128)(2,1)}, bf16[128,1024]{1,0:T(8,128)(2,1)S(1)}, u32[]{:S(2)}, u32[]{:S(2)}) collective-permute-start(bf16[128,1024]{1,0:T(8,128)(2,1)} %get-tuple-element.387), channel_id=1, source_target_pairs={{0,2},{1,3},{2,0},{3,1},{4,6},{5,7},{6,4},{7,5},{8,10},{9,11},{10,... | collective-permute-start | bytes 786440 | tf_op jit(solution)/shard_map/ppermute | solution.py:107
  475.2 21.7 %collective-permute-start.80 = (bf16[128,1024]{1,0:T(8,128)(2,1)}, bf16[128,1024]{1,0:T(8,128)(2,1)S(1)}, u32[]{:S(2)}, u32[]{:S(2)}) collective-permute-start(bf16[128,1024]{1,0:T(8,128)(2,1)} %get-tuple-element.388), channel_id=1, source_target_pairs={{0,4},{1,5},{2,6},{3,7},{4,0},{5,1},{6,2},{7,3},{8,12},{9,13},{10,... | collective-permute-start | bytes 786440 | tf_op jit(solution)/shard_map/ppermute | solution.py:107
  477.9 19.0 %collective-permute-start.81 = (bf16[128,1024]{1,0:T(8,128)(2,1)}, bf16[128,1024]{1,0:T(8,128)(2,1)S(1)}, u32[]{:S(2)}, u32[]{:S(2)}) collective-permute-start(bf16[128,1024]{1,0:T(8,128)(2,1)} %get-tuple-element.389), channel_id=1, source_target_pairs={{0,6},{1,7},{2,4},{3,5},{4,2},{5,3},{6,0},{7,1},{8,14},{9,15},{10,... | collective-permute-start | bytes 786440 | tf_op jit(solution)/shard_map/ppermute | solution.py:107
  520.3 61.2 %collective-permute-start.83 = (bf16[2048,1152]{1,0:T(8,128)(2,1)}, bf16[2048,1152]{1,0:T(8,128)(2,1)}, u32[]{:S(2)}, u32[]{:S(2)}) collective-permute-start(bf16[2048,1152]{1,0:T(8,128)(2,1)} %all-gather.8.cloned.1.call-done.refs_0_), channel_id=1, source_target_pairs={{0,1},{1,0},{2,3},{3,2},{4,5},{5,4},{6,7},{7,6},{8,9},{9,8},{10,11... | collective-permute-start | bytes 14155784 | tf_op jit(solution)/shard_map/ppermute | solution.py:48
  529.2 14.2 %collective-permute-start.87 = (bf16[128,1024]{1,0:T(8,128)(2,1)}, bf16[128,1024]{1,0:T(8,128)(2,1)S(1)}, u32[]{:S(2)}, u32[]{:S(2)}) collective-permute-start(bf16[128,1024]{1,0:T(8,128)(2,1)} %get-tuple-element.420), channel_id=1, source_target_pairs={{0,4},{1,5},{2,6},{3,7},{4,0},{5,1},{6,2},{7,3},{8,12},{9,13},{10,... | collective-permute-start | bytes 786440 | tf_op jit(solution)/shard_map/ppermute | solution.py:107
  530.7 12.7 %collective-permute-start.88 = (bf16[128,1024]{1,0:T(8,128)(2,1)}, bf16[128,1024]{1,0:T(8,128)(2,1)S(1)}, u32[]{:S(2)}, u32[]{:S(2)}) collective-permute-start(bf16[128,1024]{1,0:T(8,128)(2,1)} %get-tuple-element.421), channel_id=1, source_target_pairs={{0,6},{1,7},{2,4},{3,5},{4,2},{5,3},{6,0},{7,1},{8,14},{9,15},{10,... | collective-permute-start | bytes 786440 | tf_op jit(solution)/shard_map/ppermute | solution.py:107
  531.2 50.3 %collective-permute-start.84 = (bf16[2048,1024]{1,0:T(8,128)(2,1)}, bf16[2048,1024]{1,0:T(8,128)(2,1)}, u32[]{:S(2)}, u32[]{:S(2)}) collective-permute-start(bf16[2048,1024]{1,0:T(8,128)(2,1)} %all-gather.14.cloned.1.call-done.refs_2_), channel_id=1, source_target_pairs={{0,1},{1,0},{2,3},{3,2},{4,5},{5,4},{6,7},{7,6},{8,9},{9,8},{10,11... | collective-permute-start | bytes 12582920 | tf_op jit(solution)/shard_map/ppermute | solution.py:48
  543.4 34.5 %collective-permute-start.89 = (bf16[128,2176]{1,0:T(8,128)(2,1)}, bf16[128,2176]{1,0:T(8,128)(2,1)S(1)}, u32[]{:S(2)}, u32[]{:S(2)}) collective-permute-start(bf16[128,2176]{1,0:T(8,128)(2,1)} %get-tuple-element.423), channel_id=1, source_target_pairs={{0,2},{1,3},{2,0},{3,1},{4,6},{5,7},{6,4},{7,5},{8,10},{9,11},{10,... | collective-permute-start | bytes 1671176 | tf_op jit(solution)/shard_map/ppermute | solution.py:107
  544.6 33.3 %collective-permute-start.90 = (bf16[128,2176]{1,0:T(8,128)(2,1)}, bf16[128,2176]{1,0:T(8,128)(2,1)S(1)}, u32[]{:S(2)}, u32[]{:S(2)}) collective-permute-start(bf16[128,2176]{1,0:T(8,128)(2,1)} %get-tuple-element.424), channel_id=1, source_target_pairs={{0,4},{1,5},{2,6},{3,7},{4,0},{5,1},{6,2},{7,3},{8,12},{9,13},{10,... | collective-permute-start | bytes 1671176 | tf_op jit(solution)/shard_map/ppermute | solution.py:107
  545.5 32.4 %collective-permute-start.91 = (bf16[128,2176]{1,0:T(8,128)(2,1)S(1)}, bf16[128,2176]{1,0:T(8,128)(2,1)S(1)}, u32[]{:S(2)}, u32[]{:S(2)}) collective-permute-start(bf16[128,2176]{1,0:T(8,128)(2,1)S(1)} %copy-done.83), channel_id=1, source_target_pairs={{0,6},{1,7},{2,4},{3,5},{4,2},{5,3},{6,0},{7,1},{8,14},{9,15},{10,... | collective-permute-start | bytes 1671176 | tf_op jit(solution)/shard_map/ppermute | solution.py:107
  579.3 18.9 %collective-permute-start.92 = (bf16[128,3200]{1,0:T(8,128)(2,1)S(1)}, bf16[128,3200]{1,0:T(8,128)(2,1)S(1)}, u32[]{:S(2)}, u32[]{:S(2)}) collective-permute-start(bf16[128,3200]{1,0:T(8,128)(2,1)S(1)} %pad_maximum_fusion.5), channel_id=1, source_target_pairs={{0,8},{8,0},{16,24},{24,16},{1,9},{9,1},{17,25},{25,17},{2,10},{10... | collective-permute-start | bytes 2457608 | tf_op jit(solution)/shard_map/ppermute | solution.py:121
  598.4 39.0 %collective-permute-start.93 = (bf16[128,3200]{1,0:T(8,128)(2,1)S(1)}, bf16[128,3200]{1,0:T(8,128)(2,1)S(1)}, u32[]{:S(2)}, u32[]{:S(2)}) collective-permute-start(bf16[128,3200]{1,0:T(8,128)(2,1)S(1)} %add_convert_fusion), channel_id=1, source_target_pairs={{0,16},{8,24},{16,0},{24,8},{1,17},{9,25},{17,1},{25,9},{2,18},{10... | collective-permute-start | bytes 2457608 | tf_op jit(solution)/shard_map/ppermute | solution.py:121
  (126 other events, 876.8 us)
Sparse Core Ops, SparseCore 0:
  101.8 47.2 all-gather.5
  150.6 88.1 all-gather.7
  240.3 87.8 all-gather.9
  329.7 79.2 all-gather.11
  417.7 79.0 all-gather.13
  532.3 42.3 all-reduce.3
